TPU v7x, 512 devices: a whole 4x4x16 slice. The times are simulated.
512 devices in a mesh: section: 16 (over x, y), expert: 32 (over z, core).
Axes of the slice: x: 4, y: 4, z: 16, core: 2. Of those that a mesh axis runs over, the one named last changes fastest.
Arguments:
- x_fwd: bfloat16 [16, 1024, 3584], P('section', 'expert'), may hold values from -6 to 6
- x_bwd: bfloat16 [16, 1024, 3584], P('section', 'expert'), may hold values from -6 to 6
- grad_out: bfloat16 [16, 1024, 3584], P('section', 'expert'), may hold values from -6 to 6
- norm_gain: float32 [16, 3584], P('section'), may hold values from 0.1 to 1.9
- w_gate: bfloat16 [16, 3584, 4096], P('section', None, 'expert'), may hold values from -0.09375 to 0.09375
- w_up: bfloat16 [16, 3584, 4096], P('section', None, 'expert'), may hold values from -0.09375 to 0.09375
- w_down: bfloat16 [16, 4096, 3584], P('section', 'expert'), may hold values from -0.1875 to 0.1875
- route_fwd: int32 [16, 1024, 1], P('section', 'expert'), may hold values from 0 to 3; in each aligned block of 32 rows (0 to 31, 32 to 63, ..., all dimensions but the last counted through in order) at most 12 rows name the same one
- gate_fwd: int32 [16, 1024, 1], P('section', 'expert'), may hold values from 16 to 255
- route_bwd: int32 [16, 1024, 1], P('section', 'expert'), may hold values from 0 to 3; in each aligned block of 32 rows (0 to 31, 32 to 63, ..., all dimensions but the last counted through in order) at most 12 rows name the same one
- gate_bwd: int32 [16, 1024, 1], P('section', 'expert'), may hold values from 16 to 255
Outputs:
- y_next: bfloat16 [16, 1024, 3584], P('section', 'expert')
- dx_prev: bfloat16 [16, 1024, 3584], P('section', 'expert')
Inputs may be any that keep to these rules, and one draw needn't show every extreme that they name: `route_fwd`: of one device's 32 tokens of a micro-batch at one section, at most 12 go to one expert, and some expert gets exactly 12 in some such block. `route_bwd`: as for route_fwd.
All inputs are finite; a program needn't handle non-finite values.
Results may differ from a plain program's by a relative error of at most 0.0053.
Values may be sent and summed in bfloat16 or wider, within the bound.
No kernel may reach another device: no remote copies, remote signals or barrier semaphores. Data moves between devices by JAX's collectives and lax.ppermute only.
A program may use at most 64 MiB of HBM per device.

v0:
```python
import jax
import jax.numpy as jnp
from jax import lax
from jax.sharding import PartitionSpec as P

EXPERTS = 4
CAP = 12


EPSILON = 1e-06


def passed_along(value, axis, steps):
    count = lax.axis_size(axis)
    pairs = [(source, (source + steps) % count) for source in range(count)]
    return lax.ppermute(value, axis, pairs)


def rms_scale(values):
    return lax.rsqrt(jnp.mean(values * values, axis=-1, keepdims=True) + EPSILON)


def normalize(tokens, gain):
    values = tokens.astype(jnp.float32)
    return (values * rms_scale(values) * gain).astype(jnp.bfloat16)


def norm_backward(tokens, gain, upstream):
    values = tokens.astype(jnp.float32)
    scale = rms_scale(values)
    weighted = upstream * gain
    inner = jnp.mean(values * weighted, axis=-1, keepdims=True)
    return scale * weighted - values * scale * scale * scale * inner


def slot_table(route):
    onehot = (route[:, None] == jnp.arange(EXPERTS, dtype=jnp.int32)[None, :]).astype(jnp.int32)
    rank = jnp.sum(jnp.cumsum(onehot, axis=0) * onehot, axis=1) - 1
    slot = route * CAP + rank
    place = (slot[:, None] == jnp.arange(EXPERTS * CAP, dtype=jnp.int32)[None, :]).astype(
        jnp.bfloat16
    )
    return (slot, place)


def spread(place, rows, split):
    packed = lax.dot_general(
        place, rows, (((0,), (0,)), ((), ())), preferred_element_type=jnp.float32
    )
    packed = packed.astype(jnp.bfloat16).reshape(EXPERTS, CAP, rows.shape[1])
    return jnp.repeat(packed, split, axis=0)


def fold_members(returned, split):
    sources, count, width = returned.shape
    return jnp.sum(returned.astype(jnp.float32).reshape(EXPERTS, split, count, width), axis=1)


def unpack(table, slot):
    flat = table.reshape(EXPERTS * CAP, table.shape[2])
    return jnp.take(flat, slot, axis=0)


def expert_forward(rows, w_gate, w_up, w_down):
    gate = jnp.einsum("scd,dh->sch", rows, w_gate, preferred_element_type=jnp.float32)
    up = jnp.einsum("scd,dh->sch", rows, w_up, preferred_element_type=jnp.float32)
    act = (jax.nn.silu(gate) * up).astype(jnp.bfloat16)
    return jnp.einsum("sch,hd->scd", act, w_down, preferred_element_type=jnp.float32).astype(
        jnp.bfloat16
    )


def expert_backward(rows, grads, w_gate, w_up, w_down):
    gate = jnp.einsum("scd,dh->sch", rows, w_gate, preferred_element_type=jnp.float32)
    up = jnp.einsum("scd,dh->sch", rows, w_up, preferred_element_type=jnp.float32)
    d_act = jnp.einsum("scd,hd->sch", grads, w_down, preferred_element_type=jnp.float32)
    sig = jax.nn.sigmoid(gate)
    d_gate = (d_act * up * sig * (1.0 + gate * (1.0 - sig))).astype(jnp.bfloat16)
    d_up = (d_act * gate * sig).astype(jnp.bfloat16)
    back = jnp.einsum("sch,dh->scd", d_gate, w_gate, preferred_element_type=jnp.float32)
    back = back + jnp.einsum("sch,dh->scd", d_up, w_up, preferred_element_type=jnp.float32)
    return back.astype(jnp.bfloat16)


def per_device(
    x_fwd,
    x_bwd,
    grad_out,
    norm_gain,
    w_gate,
    w_up,
    w_down,
    route_fwd,
    gate_fwd,
    route_bwd,
    gate_bwd,
):
    split = lax.axis_size("expert") // EXPERTS
    gain = norm_gain[0]
    gate_cols = w_gate[0]
    up_cols = w_up[0]
    down_rows = w_down[0]
    inputs_f = x_fwd[0]
    inputs_b = x_bwd[0]
    upstream = grad_out[0]
    slot_f, place_f = slot_table(route_fwd[0, :, 0])
    slot_b, place_b = slot_table(route_bwd[0, :, 0])
    normed_f = normalize(inputs_f, gain)
    normed_b = normalize(inputs_b, gain)
    scale_f = gate_fwd[0].astype(jnp.float32) / 256.0
    scale_b = gate_bwd[0].astype(jnp.float32) / 256.0
    grad_rows = (upstream.astype(jnp.float32) * scale_b).astype(jnp.bfloat16)
    copies_f = spread(place_f, normed_f, split)
    copies_b = spread(place_b, normed_b, split)
    copies_g = spread(place_b, grad_rows, split)
    partial_out = expert_forward(
        lax.all_to_all(copies_f, "expert", split_axis=0, concat_axis=0, tiled=True),
        gate_cols,
        up_cols,
        down_rows,
    )
    returned = lax.all_to_all(partial_out, "expert", split_axis=0, concat_axis=0, tiled=True)
    table_f = fold_members(returned, split)
    partial_grad = expert_backward(
        lax.all_to_all(copies_b, "expert", split_axis=0, concat_axis=0, tiled=True),
        lax.all_to_all(copies_g, "expert", split_axis=0, concat_axis=0, tiled=True),
        gate_cols,
        up_cols,
        down_rows,
    )
    returned = lax.all_to_all(partial_grad, "expert", split_axis=0, concat_axis=0, tiled=True)
    table_b = fold_members(returned, split)
    moe_f = unpack(table_f, slot_f)
    d_normed = unpack(table_b, slot_b)
    y_section = (inputs_f.astype(jnp.float32) + scale_f * moe_f).astype(jnp.bfloat16)
    dx_section = (upstream.astype(jnp.float32) + norm_backward(inputs_b, gain, d_normed)).astype(
        jnp.bfloat16
    )
    y_next = passed_along(y_section, "section", 1)
    dx_prev = passed_along(dx_section, "section", -1)
    return (y_next[None], dx_prev[None])


def solution(mesh):
    in_specs = (
        P("section", "expert", None),
        P("section", "expert", None),
        P("section", "expert", None),
        P("section", None),
        P("section", None, "expert"),
        P("section", None, "expert"),
        P("section", "expert", None),
        P("section", "expert", None),
        P("section", "expert", None),
        P("section", "expert", None),
        P("section", "expert", None),
    )
    out_specs = (P("section", "expert", None), P("section", "expert", None))
    return jax.shard_map(
        per_device, mesh=mesh, in_specs=in_specs, out_specs=out_specs, check_vma=False
    )
```

profile of v0, /device:TPU:6, one launch (start us, length us, event | category | flops | bytes accessed | tf_op | source)
XLA Modules:
  0.0 892.9 jit_solution(12801810400146483325)
XLA Ops:
  0.6 0.0 copy-start
  0.6 1.2 fusion.52
  1.8 0.7 fusion.81
  2.6 0.1 reduce_window_sum.17
  2.6 0.8 select_reduce_fusion.1
  3.5 0.7 compare_and_fusion.1
  4.1 0.8 reduce
  4.9 1.3 convolution_convert_fusion.3
  6.2 0.1 reshape.115
  6.3 2.2 broadcast_in_dim.19
  8.5 15.7 %all-to-all-start = ((bf16[32,12,3584]{2,1,0:T(8,128)(2,1)}), bf16[32,12,3584]{2,1,0:T(8,128)(2,1)}, u32[]{:S(2)}, u32[]{:S(2)}) async-start(bf16[32,12,3584]{2,1,0:T(8,128)(2,1)} %bitcast.69), calls=%async_computation | async-start | bytes 7340032 | tf_op jit(solution)/shard_map/all_to_all | solution.py:117
  24.2 0.0 copy-done.6
  24.2 0.1 fusion.80
  24.3 0.1 reduce_window_sum.18
  24.4 0.2 select_reduce_fusion
  24.5 0.0 copy-done.7
  24.6 0.0 copy-done.5
  24.6 0.4 convolution_convert_fusion.2
  25.0 0.1 reshape.120
  25.0 161.7 %all-to-all-done = bf16[32,12,3584]{2,1,0:T(8,128)(2,1)} async-done(((bf16[32,12,3584]{2,1,0:T(8,128)(2,1)}), bf16[32,12,3584]{2,1,0:T(8,128)(2,1)}, u32[]{:S(2)}, u32[]{:S(2)}) %all-to-all-start) | async-done | bytes 2752544 | tf_op jit(solution)/shard_map/all_to_all | solution.py:117
  186.8 2.3 broadcast_in_dim.36
  189.0 8.9 all-to-all-start.2
  197.9 0.0 copy-done.1
  197.9 0.2 fusion.56
  198.1 0.4 convolution_convert_fusion.1
  198.5 0.1 reshape.122
  198.6 161.9 %all-to-all-done.2 = bf16[32,12,3584]{2,1,0:T(8,128)(2,1)} async-done(((bf16[32,12,3584]{2,1,0:T(8,128)(2,1)}), bf16[32,12,3584]{2,1,0:T(8,128)(2,1)}, u32[]{:S(2)}, u32[]{:S(2)}) %all-to-all-start.2) | async-done | bytes 2752544 | tf_op jit(solution)/shard_map/all_to_all | solution.py:126
  360.4 2.2 broadcast_in_dim.37
  362.7 8.9 all-to-all-start.3
  371.6 0.0 copy-done.3
  371.6 0.0 copy-start.4
  371.6 4.0 fusion.9
  375.6 0.0 copy-done
  375.6 0.0 copy-done.4
  375.6 6.6 convolution_convert_fusion
  382.2 5.1 copy.21
  387.4 146.7 %all-to-all-done.3 = bf16[32,12,3584]{2,1,0:T(8,128)(2,1)} async-done(((bf16[32,12,3584]{2,1,0:T(8,128)(2,1)}), bf16[32,12,3584]{2,1,0:T(8,128)(2,1)}, u32[]{:S(2)}, u32[]{:S(2)}) %all-to-all-start.3) | async-done | bytes 2752544 | tf_op jit(solution)/shard_map/all_to_all | solution.py:125
  534.1 8.9 %all-to-all-start.1 = ((bf16[32,12,3584]{2,1,0:T(8,128)(2,1)}), bf16[32,12,3584]{2,1,0:T(8,128)(2,1)}, u32[]{:S(2)}, u32[]{:S(2)}) async-start(bf16[32,12,3584]{2,1,0:T(8,128)(2,1)} %copy.21), calls=%async_computation.1 | async-start | bytes 7340032 | tf_op jit(solution)/shard_map/all_to_all | solution.py:122
  543.0 3.9 fusion.1
  546.9 3.9 fusion.3
  550.9 7.5 fusion.32
  558.4 3.4 fusion
  561.8 3.4 copy.27
  565.2 140.5 %all-to-all-done.1 = bf16[32,12,3584]{2,1,0:T(8,128)(2,1)} async-done(((bf16[32,12,3584]{2,1,0:T(8,128)(2,1)}), bf16[32,12,3584]{2,1,0:T(8,128)(2,1)}, u32[]{:S(2)}, u32[]{:S(2)}) %all-to-all-start.1) | async-done | bytes 2752544 | tf_op jit(solution)/shard_map/all_to_all | solution.py:122
  705.6 8.5 all-to-all-start.4
  714.2 0.0 copy-done.8
  714.2 2.7 convert_reduce_fusion.1
  717.0 0.0 copy-start.2
  717.0 0.1 reshape.119
  717.1 0.7 gather_fusion
  717.8 0.1 copy-done.2
  717.9 0.8 fusion.55
  718.7 3.5 collective-permute-start
  722.2 154.4 %all-to-all-done.4 = bf16[32,12,3584]{2,1,0:T(8,128)(2,1)} async-done(((bf16[32,12,3584]{2,1,0:T(8,128)(2,1)}), bf16[32,12,3584]{2,1,0:T(8,128)(2,1)}, u32[]{:S(2)}, u32[]{:S(2)}) %all-to-all-start.4) | async-done | bytes 2752544 | tf_op jit(solution)/shard_map/all_to_all | solution.py:131
  876.7 2.7 convert_reduce_fusion
  879.4 0.1 reshape.126
  879.5 0.7 gather_fusion.1
  880.2 0.3 fusion.57
  880.5 0.2 fusion.51
  880.7 5.2 collective-permute-start.1
  885.9 0.0 collective-permute-done
  885.9 4.6 collective-permute-done.1
  890.6 1.6 copy.60
  892.2 0.7 copy.61
  (16 shorter events, 0.1 us)
Async XLA Ops:
  0.6 374.9 %copy-start = (bf16[1,3584,128]{2,1,0:T(8,128)(2,1)S(1)}, bf16[1,3584,128]{2,1,0:T(8,128)(2,1)}, u32[]{:S(2)}) copy-start(bf16[1,3584,128]{2,1,0:T(8,128)(2,1)} %param.18) | copy-start | bytes 2752516
  8.5 15.7 %copy-start.6 = (s32[1,32,1]{1,2,0:T(1,128)S(1)}, s32[1,32,1]{1,2,0:T(1,128)}, u32[]{:S(2)}) copy-start(s32[1,32,1]{1,2,0:T(1,128)} %param.22) | copy-start | bytes 388
  8.5 16.1 %copy-start.7 = (s32[1,32,1]{1,2,0:T(1,128)S(1)}, s32[1,32,1]{1,2,0:T(1,128)}, u32[]{:S(2)}) copy-start(s32[1,32,1]{1,2,0:T(1,128)} %param.23) | copy-start | bytes 388
  8.5 16.1 %copy-start.5 = (bf16[1,32,3584]{2,1,0:T(8,128)(2,1)S(1)}, bf16[1,32,3584]{2,1,0:T(8,128)(2,1)}, u32[]{:S(2)}) copy-start(bf16[1,32,3584]{2,1,0:T(8,128)(2,1)} %param.15) | copy-start | bytes 688132
  8.5 178.3 %all-to-all-start = ((bf16[32,12,3584]{2,1,0:T(8,128)(2,1)}), bf16[32,12,3584]{2,1,0:T(8,128)(2,1)}, u32[]{:S(2)}, u32[]{:S(2)}) async-start(bf16[32,12,3584]{2,1,0:T(8,128)(2,1)} %bitcast.69), calls=%async_computation | async-start | bytes 7340032 | tf_op jit(solution)/shard_map/all_to_all | solution.py:117
  189.0 8.9 copy-start.1
  189.0 171.4 %all-to-all-start.2 = ((bf16[32,12,3584]{2,1,0:T(8,128)(2,1)}), bf16[32,12,3584]{2,1,0:T(8,128)(2,1)}, u32[]{:S(2)}, u32[]{:S(2)}) async-start(bf16[32,12,3584]{2,1,0:T(8,128)(2,1)} %bitcast.70), calls=%async_computation.2 | async-start | bytes 7340032 | tf_op jit(solution)/shard_map/all_to_all | solution.py:126
  362.6 8.9 copy-start.3
  362.7 171.4 %all-to-all-start.3 = ((bf16[32,12,3584]{2,1,0:T(8,128)(2,1)}), bf16[32,12,3584]{2,1,0:T(8,128)(2,1)}, u32[]{:S(2)}, u32[]{:S(2)}) async-start(bf16[32,12,3584]{2,1,0:T(8,128)(2,1)} %bitcast.71), calls=%async_computation.3 | async-start | bytes 7340032 | tf_op jit(solution)/shard_map/all_to_all | solution.py:125
  371.6 4.0 copy-start.4
  534.1 171.6 %all-to-all-start.1 = ((bf16[32,12,3584]{2,1,0:T(8,128)(2,1)}), bf16[32,12,3584]{2,1,0:T(8,128)(2,1)}, u32[]{:S(2)}, u32[]{:S(2)}) async-start(bf16[32,12,3584]{2,1,0:T(8,128)(2,1)} %copy.21), calls=%async_computation.1 | async-start | bytes 7340032 | tf_op jit(solution)/shard_map/all_to_all | solution.py:122
  565.2 149.0 %copy-start.8 = (s32[1,32,1]{1,2,0:T(1,128)S(1)}, s32[1,32,1]{1,2,0:T(1,128)}, u32[]{:S(2)}) copy-start(s32[1,32,1]{1,2,0:T(1,128)} %param.21) | copy-start | bytes 388
  705.6 171.0 %all-to-all-start.4 = ((bf16[32,12,3584]{2,1,0:T(8,128)(2,1)}), bf16[32,12,3584]{2,1,0:T(8,128)(2,1)}, u32[]{:S(2)}, u32[]{:S(2)}) async-start(bf16[32,12,3584]{2,1,0:T(8,128)(2,1)} %copy.27), calls=%async_computation.4 | async-start | bytes 7340032 | tf_op jit(solution)/shard_map/all_to_all | solution.py:131
  717.0 0.9 copy-start.2
  718.7 167.2 %collective-permute-start = (bf16[32,3584]{1,0:T(8,128)(2,1)}, bf16[32,3584]{1,0:T(8,128)(2,1)}, u32[]{:S(2)}, u32[]{:S(2)}) collective-permute-start(bf16[32,3584]{1,0:T(8,128)(2,1)} %fusion.55), channel_id=1, source_target_pairs={{0,32},{32,64},{64,96},{96,128},{128,160},{160,192},{192,224},{224... | collective-permute-start | bytes 688136 | tf_op jit(solution)/shard_map/ppermute | solution.py:16
  880.7 9.8 %collective-permute-start.1 = (bf16[32,3584]{1,0:T(8,128)(2,1)S(1)}, bf16[32,3584]{1,0:T(8,128)(2,1)S(1)}, u32[]{:S(2)}, u32[]{:S(2)}) collective-permute-start(bf16[32,3584]{1,0:T(8,128)(2,1)S(1)} %fusion.51), channel_id=1, source_target_pairs={{0,480},{32,0},{64,32},{96,64},{128,96},{160,128},{192,160},{224,1... | collective-permute-start | bytes 688136 | tf_op jit(solution)/shard_map/ppermute | solution.py:16
where the time goes:
time: 901 us; the launch traced here: 893 us
  waiting for transfers between devices  770 us (85%)
  starting transfers between devices  59.6 us (7%)
  matrix products  31.4 us (3%)
  local copies, waits for them, and re-layouts  19.5 us (2%)
  other arithmetic  11.6 us (1%)
    all_to_all x1, waiting for transfers between devices, per_device(): lax.all_to_all(copies_g, 'expert', split_axis=0, concat_axis=0, tiled=True)  162 us
    all_to_all x1, waiting for transfers between devices, per_device(): lax.all_to_all(copies_f, 'expert', split_axis=0, concat_axis=0, tiled=True)  162 us
    all_to_all x1, waiting for transfers between devices, per_device(): lax.all_to_all(partial_grad, 'expert', split_axis=0, concat_axis=0, tiled...  154 us
    all_to_all x1, waiting for transfers between devices, per_device(): lax.all_to_all(copies_b, 'expert', split_axis=0, concat_axis=0, tiled=True)  147 us
    all_to_all x1, waiting for transfers between devices, per_device(): lax.all_to_all(partial_out, 'expert', split_axis=0, concat_axis=0, tiled=...  140 us
  transfers between devices with their start and end apart: 7, of which 6 were waited for; matrix products, arithmetic and copies ran while one was open for 5% of the time, Pallas kernels for 0%

commit v1 on v0

v1 whole, which is shorter than its diff:
```python
import jax
import jax.numpy as jnp
from jax import lax
from jax.sharding import PartitionSpec as P

EXPERTS = 4
CAP = 12
EPSILON = 1e-06


def passed_along(value, axis, steps):
    count = lax.axis_size(axis)
    pairs = [(source, (source + steps) % count) for source in range(count)]
    return lax.ppermute(value, axis, pairs)


def rms_scale(values):
    return lax.rsqrt(jnp.mean(values * values, axis=-1, keepdims=True) + EPSILON)


def dot(a, b, dims):
    return lax.dot_general(a, b, (dims, ((), ())), preferred_element_type=jnp.float32)


def slots_of(route):
    onehot = (route[:, None] == jnp.arange(EXPERTS, dtype=jnp.int32)[None, :]).astype(jnp.int32)
    rank = jnp.sum(jnp.cumsum(onehot, axis=0) * onehot, axis=1) - 1
    return route * CAP + rank


def half_places(slot):
    expert, rank = slot // CAP, slot % CAP
    base = expert * (2 * CAP) + rank
    return [base + h * CAP for h in range(2)]


def pick_back(table, slot):
    rows = table.reshape(-1, table.shape[-1])
    count = rows.shape[0]
    halves = []
    for place in half_places(slot):
        pick = (place[:, None] == jnp.arange(count, dtype=jnp.int32)[None, :]).astype(jnp.bfloat16)
        halves.append(dot(pick, rows, ((1,), (0,))))
    return jnp.concatenate(halves, axis=1)


def packers(slots, me_expert, side):
    sources, tokens = slots.shape
    groups = sources // side
    expert, rank = slots // CAP, slots % CAP
    source = jnp.arange(sources, dtype=jnp.int32)[:, None]
    base = (source % side) * (groups * 2 * CAP) + (source // side) * (2 * CAP) + rank
    base = jnp.where(expert == me_expert, base, -2 * CAP)
    flat = base.reshape(-1)
    row = jnp.arange(sources * 2 * CAP, dtype=jnp.int32)[:, None]
    return [(flat[None, :] + h * CAP == row).astype(jnp.bfloat16) for h in range(2)]


def pack(places, hidden):
    parts = [dot(place, hidden, ((1,), (0,))).astype(jnp.bfloat16) for place in places]
    return jnp.concatenate(parts, axis=1)


def send_back(partial, side, within, across):
    rows, width = partial.shape
    blocks = partial.astype(jnp.bfloat16).reshape(side, rows // side, width)
    got = lax.all_to_all(
        blocks, "expert", split_axis=0, concat_axis=0, tiled=True, axis_index_groups=within
    )
    total = jnp.sum(got.astype(jnp.float32), axis=0).astype(jnp.bfloat16)
    total = total.reshape(EXPERTS, 2 * CAP, width)
    return lax.all_to_all(
        total, "expert", split_axis=0, concat_axis=0, tiled=True, axis_index_groups=across
    )


def per_device(
    x_fwd,
    x_bwd,
    grad_out,
    norm_gain,
    w_gate,
    w_up,
    w_down,
    route_fwd,
    gate_fwd,
    route_bwd,
    gate_bwd,
):
    count = lax.axis_size("expert")
    ring = count // 2
    side = ring // EXPERTS
    same_core = [[2 * z + c for z in range(ring)] for c in range(2)]
    within = [[2 * (side * g + j) + c for j in range(side)] for g in range(EXPERTS) for c in range(2)]
    across = [[2 * (side * g + j) + c for g in range(EXPERTS)] for j in range(side) for c in range(2)]
    swap = [(i, i ^ 1) for i in range(count)]
    me = lax.axis_index("expert") // (2 * side)

    gain = norm_gain[0]
    tokens, width = x_fwd.shape[1:]
    half = width // 2
    xf = x_fwd[0].astype(jnp.float32)
    xb = x_bwd[0].astype(jnp.float32)
    up32 = grad_out[0].astype(jnp.float32)
    scale_f = gate_fwd[0].astype(jnp.float32) / 256.0
    scale_b = gate_bwd[0].astype(jnp.float32) / 256.0
    r_b = rms_scale(xb)
    normed_f = (xf * rms_scale(xf) * gain).astype(jnp.bfloat16)
    normed_b = (xb * r_b * gain).astype(jnp.bfloat16)
    grad_rows = (up32 * scale_b).astype(jnp.bfloat16)
    slot_f = slots_of(route_fwd[0, :, 0])
    slot_b = slots_of(route_bwd[0, :, 0])

    sent = jnp.concatenate([normed_f, normed_b, grad_rows], axis=0)
    got = lax.all_gather(sent, "expert", axis=0, tiled=False, axis_index_groups=same_core)
    rows_f = got[:, :tokens].reshape(ring * tokens, width)
    rows_b = got[:, tokens : 2 * tokens].reshape(ring * tokens, width)
    rows_g = got[:, 2 * tokens :].reshape(ring * tokens, width)
    both = jnp.concatenate([slot_f, slot_b])
    slots = lax.all_to_all(
        jnp.broadcast_to(both[None, None, :], (ring, 1, 2 * tokens)),
        "expert",
        split_axis=0,
        concat_axis=0,
        tiled=True,
        axis_index_groups=same_core,
    )[:, 0]

    gate_o = lax.ppermute(w_gate[0], "expert", swap)
    up_o = lax.ppermute(w_up[0], "expert", swap)
    down_o = lax.ppermute(w_down[0], "expert", swap)
    w_in = jnp.concatenate([w_gate[0], gate_o, w_up[0], up_o], axis=1)
    w_dn = jnp.concatenate([w_down[0], down_o], axis=0)
    hid = w_dn.shape[0]
    dn_stack = jnp.concatenate([w_dn[:, :half], w_dn[:, half:]], axis=0)
    in_stack = jnp.concatenate([w_in[:half], w_in[half:]], axis=1)

    place_f = packers(slots[:, :tokens], me, side)
    place_b = packers(slots[:, tokens:], me, side)

    pre_f = dot(rows_f, w_in, ((1,), (0,)))
    act = (jax.nn.silu(pre_f[:, :hid]) * pre_f[:, hid:]).astype(jnp.bfloat16)
    part_f = dot(pack(place_f, act), dn_stack, ((1,), (0,)))
    table_f = send_back(part_f, side, within, across)

    pre_b = dot(rows_b, w_in, ((1,), (0,)))
    d_act = dot(rows_g, w_dn, ((1,), (1,)))
    gate, up = pre_b[:, :hid], pre_b[:, hid:]
    sig = jax.nn.sigmoid(gate)
    d_gate = (d_act * up * sig * (1.0 + gate * (1.0 - sig))).astype(jnp.bfloat16)
    d_up = (d_act * gate * sig).astype(jnp.bfloat16)
    part_b = dot(pack(place_b, jnp.concatenate([d_gate, d_up], axis=1)), in_stack, ((1,), (1,)))
    table_b = send_back(part_b, side, within, across)

    moe_f = pick_back(table_f, slot_f)
    y = (xf + scale_f * moe_f).astype(jnp.bfloat16)
    d_normed = pick_back(table_b, slot_b)
    weighted = d_normed * gain
    inner = jnp.mean(xb * weighted, axis=-1, keepdims=True)
    dx = (up32 + (r_b * weighted - xb * r_b * r_b * r_b * inner)).astype(jnp.bfloat16)
    y_next = passed_along(y, "section", 1)
    dx_prev = passed_along(dx, "section", -1)
    return (y_next[None], dx_prev[None])


def solution(mesh):
    in_specs = (
        P("section", "expert", None),
        P("section", "expert", None),
        P("section", "expert", None),
        P("section", None),
        P("section", None, "expert"),
        P("section", None, "expert"),
        P("section", "expert", None),
        P("section", "expert", None),
        P("section", "expert", None),
        P("section", "expert", None),
        P("section", "expert", None),
    )
    out_specs = (P("section", "expert", None), P("section", "expert", None))
    return jax.shard_map(
        per_device, mesh=mesh, in_specs=in_specs, out_specs=out_specs, check_vma=False
    )
```

time: 901 us -> 310 us (0.34)
  waiting for transfers between devices: 770 us -> 200 us
  matrix products: 31.4 us -> 15.6 us
  between operations: 0.96 us -> 14.4 us
    all_to_all x5, waiting for transfers between devices: 765 us -> 95.6 us  [the longest x2 55 us: send_back(): lax.all_to_all(blocks, 'expert', split_axis=0, concat_axis=0, tiled=True,...]
    all_gather x0 -> x1, waiting for transfers between devices: none -> 98.6 us  [per_device(): lax.all_gather(sent, 'expert', axis=0, tiled=False, axis_index_groups=sam...]
    all_to_all x5, starting transfers between devices: 50.9 us -> 34.8 us  [the longest x1 15.2 us: per_device(): lax.all_to_all(jnp.broadcast_to(both[None, None, :], (ring, 1, 2 * tokens...]
    dot_general x9 -> x13, matrix products: 31.4 us -> 15.6 us  [dot(): lax.dot_general(a, b, (dims, ((), ())), preferred_element_type=jnp.float32)]
  transfers between devices with their start and end apart: 7 -> 11, of which waited for: 6 -> 7; matrix products, arithmetic and copies ran while one was open for 5% -> 8% of each run, Pallas kernels for 0% -> 0%
where the time goes in v1:
time: 310 us; the launch traced here: 308 us
  waiting for transfers between devices  200 us (65%)
  starting transfers between devices  51.5 us (17%)
  matrix products  15.6 us (5%)
  between operations  14.4 us (5%)
  other arithmetic  13.6 us (4%)
  local copies, waits for them, and re-layouts  12.9 us (4%)
    all_gather x1, waiting for transfers between devices, per_device(): lax.all_gather(sent, 'expert', axis=0, tiled=False, axis_index_groups=sam...  98.6 us
    all_to_all x2, waiting for transfers between devices, send_back(): lax.all_to_all(blocks, 'expert', split_axis=0, concat_axis=0, tiled=True,...  55 us
    all_to_all x2, waiting for transfers between devices, send_back(): lax.all_to_all(total, 'expert', split_axis=0, concat_axis=0, tiled=True,...  30.1 us
    dot_general x13, matrix products, dot(): lax.dot_general(a, b, (dims, ((), ())), preferred_element_type=jnp.float32)  15.6 us
    all_to_all x1, starting transfers between devices, per_device(): lax.all_to_all(jnp.broadcast_to(both[None, None, :], (ring, 1, 2 * tokens...  15.2 us
    all_to_all x2, starting transfers between devices, send_back(): lax.all_to_all(total, 'expert', split_axis=0, concat_axis=0, tiled=True,...  12.5 us
    all_to_all x1, waiting for transfers between devices, per_device(): lax.all_to_all(jnp.broadcast_to(both[None, None, :], (ring, 1, 2 * tokens...  10.5 us
    ppermute x2, starting transfers between devices, passed_along(): return lax.ppermute(value, axis, pairs)  10.4 us
  transfers between devices with their start and end apart: 11, of which 7 were waited for; matrix products, arithmetic and copies ran while one was open for 8% of the time, Pallas kernels for 0%

profile of v1, /device:TPU:6, one launch (start us, length us, event | category | flops | bytes accessed | tf_op | source)
XLA Modules:
  0.0 308.2 jit_solution(8515189520673345131)
XLA Ops:
  7.2 0.0 all-gather.3.cloned.1.call-start
  7.3 0.8 multiply_bitcast_fusion
  8.1 1.1 fusion.28
  9.2 1.1 fusion.32
  10.3 0.8 reduce.2
  11.0 1.0 fusion.26
  12.1 1.2 fusion.30
  13.3 0.9 pad_maximum_fusion.3
  14.2 0.0 all-gather.3.cloned.1.call-update
  14.2 1.9 collective-permute-start
  16.2 2.4 collective-permute-start.1
  18.6 0.1 fusion.42
  18.7 0.1 reduce_window_sum.17
  18.7 0.1 fusion.41
  18.8 0.1 reduce_window_sum.18
  18.9 0.2 select_reduce_fusion.1
  19.0 0.2 select_reduce_fusion
  19.3 0.1 pad_add_fusion
  19.3 0.6 broadcast_in_dim.11
  19.9 15.2 %all-to-all-start = ((s32[16,1,64]{2,1,0:T(1,128)}), s32[16,1,64]{2,1,0:T(1,128)S(1)}, u32[]{:S(2)}, u32[]{:S(2)}) async-start(s32[16,1,64]{2,1,0:T(1,128)} %broadcast_in_dim.11), calls=%async_computation | async-start | bytes 16384 | tf_op jit(solution)/shard_map/all_to_all | solution.py:120
  35.1 1.9 collective-permute-start.2
  37.1 10.5 %all-to-all-done = s32[16,1,64]{2,1,0:T(1,128)S(1)} async-done(((s32[16,1,64]{2,1,0:T(1,128)}), s32[16,1,64]{2,1,0:T(1,128)S(1)}, u32[]{:S(2)}, u32[]{:S(2)}) %all-to-all-start) | async-done | bytes 4128 | tf_op jit(solution)/shard_map/all_to_all | solution.py:120
  47.6 0.1 fusion.52
  47.7 0.1 eq.178
  47.7 1.7 pad_maximum_fusion
  49.5 1.9 copy-done
  51.4 1.5 fusion.72
  52.8 98.6 %all-gather.3.cloned.1.call-done = bf16[1536,3584]{1,0:T(8,128)(2,1)} async-done(((bf16[96,3584]{1,0:T(8,128)(2,1)}), bf16[1536,3584]{1,0:T(8,128)(2,1)}) %all-gather.3.cloned.1.call-update) | async-done | bytes 11010064 | tf_op jit(solution)/shard_map/all_gather | solution.py:115
  151.4 6.5 %fusion.71 = (bf16[16,32,3584]{2,1,0:T(8,128)(2,1)S(1)}, bf16[16,32,3584]{2,1,0:T(8,128)(2,1)S(1)}, bf16[16,32,3584]{2,1,0:T(8,128)(2,1)}) fusion(bf16[16,96,3584]{2,1,0:T(8,128)(2,1)} %bitcast.52), kind=kLoop, calls=%fused_computation.135 | loop fusion | bytes 22020096 | tf_op jit(solution)/shard_map/slice | solution.py:117
  157.9 2.0 fusion.74
  160.0 2.5 fusion.20
  162.5 0.4 convolution_convert_fusion.2
  162.9 0.4 convolution_convert_fusion.1
  163.3 2.7 fusion.4
  166.0 3.5 %all-to-all-start.3 = ((bf16[4,96,1792]{2,1,0:T(8,128)(2,1)}), bf16[4,96,1792]{2,1,0:T(8,128)(2,1)S(1)}, u32[]{:S(2)}, u32[]{:S(2)}) async-start(bf16[4,96,1792]{2,1,0:T(8,128)(2,1)} %bitcast.22), calls=%async_computation.3 | async-start | bytes 2752512 | tf_op jit(solution)/shard_map/all_to_all | solution.py:67
  169.6 0.1 eq.164
  169.6 1.4 fusion.11
  171.1 0.9 copy-done.2
  171.9 4.1 %fusion.73 = f32[512,512]{1,0:T(8,128)S(1)} fusion(bf16[512,3584]{1,0:T(8,128)(2,1)} %bitcast.53, bf16[3584,512]{1,0:T(8,128)(2,1)S(1)} %copy-done.2), kind=kOutput, calls=%fused_computation.137 | convolution fusion | flops 1879048192 | bytes 8388608 | tf_op jit(solution)/shard_map/dot_general | solution.py:22
  176.0 0.2 fusion.21
  176.2 0.3 convolution_convert_fusion.4
  176.5 0.3 convolution_convert_fusion.3
  176.8 2.0 convolution_convert_fusion
  178.8 23.8 %all-to-all-done.3 = bf16[4,96,1792]{2,1,0:T(8,128)(2,1)S(1)} async-done(((bf16[4,96,1792]{2,1,0:T(8,128)(2,1)}), bf16[4,96,1792]{2,1,0:T(8,128)(2,1)S(1)}, u32[]{:S(2)}, u32[]{:S(2)}) %all-to-all-start.3) | async-done | bytes 1376288 | tf_op jit(solution)/shard_map/all_to_all | solution.py:67
  202.6 3.5 %all-to-all-start.1 = ((bf16[4,96,1792]{2,1,0:T(8,128)(2,1)}), bf16[4,96,1792]{2,1,0:T(8,128)(2,1)S(1)}, u32[]{:S(2)}, u32[]{:S(2)}) async-start(bf16[4,96,1792]{2,1,0:T(8,128)(2,1)} %bitcast.60), calls=%async_computation.1 | async-start | bytes 2752512 | tf_op jit(solution)/shard_map/all_to_all | solution.py:67
  206.2 1.0 reduce_sum.74
  207.2 31.2 %all-to-all-done.1 = bf16[4,96,1792]{2,1,0:T(8,128)(2,1)S(1)} async-done(((bf16[4,96,1792]{2,1,0:T(8,128)(2,1)}), bf16[4,96,1792]{2,1,0:T(8,128)(2,1)S(1)}, u32[]{:S(2)}, u32[]{:S(2)}) %all-to-all-start.1) | async-done | bytes 1376288 | tf_op jit(solution)/shard_map/all_to_all | solution.py:67
  238.4 8.7 %all-to-all-start.4 = ((bf16[4,24,1792]{2,1,0:T(8,128)(2,1)}), bf16[4,24,1792]{2,1,0:T(8,128)(2,1)S(1)}, u32[]{:S(2)}, u32[]{:S(2)}) async-start(bf16[4,24,1792]{2,1,0:T(8,128)(2,1)} %bitcast.23), calls=%async_computation.4 | async-start | bytes 688128 | tf_op jit(solution)/shard_map/all_to_all | solution.py:72
  247.0 1.0 reduce_sum.73
  248.1 20.6 %all-to-all-done.4 = bf16[4,24,1792]{2,1,0:T(8,128)(2,1)S(1)} async-done(((bf16[4,24,1792]{2,1,0:T(8,128)(2,1)}), bf16[4,24,1792]{2,1,0:T(8,128)(2,1)S(1)}, u32[]{:S(2)}, u32[]{:S(2)}) %all-to-all-start.4) | async-done | bytes 344096 | tf_op jit(solution)/shard_map/all_to_all | solution.py:72
  268.6 3.9 %all-to-all-start.2 = ((bf16[4,24,1792]{2,1,0:T(8,128)(2,1)}), bf16[4,24,1792]{2,1,0:T(8,128)(2,1)S(1)}, u32[]{:S(2)}, u32[]{:S(2)}) async-start(bf16[4,24,1792]{2,1,0:T(8,128)(2,1)} %bitcast.16), calls=%async_computation.2 | async-start | bytes 688128 | tf_op jit(solution)/shard_map/all_to_all | solution.py:72
  272.5 0.2 fusion.46
  272.7 0.2 fusion.45
  272.9 0.2 fusion.33
  273.1 0.2 fusion.27
  273.4 5.6 %collective-permute-start.4 = (bf16[32,3584]{1,0:T(8,128)(2,1)S(1)}, bf16[32,3584]{1,0:T(8,128)(2,1)S(1)}, u32[]{:S(2)}, u32[]{:S(2)}) collective-permute-start(bf16[32,3584]{1,0:T(8,128)(2,1)S(1)} %fusion.27), channel_id=1, source_target_pairs={{0,480},{32,0},{64,32},{96,64},{128,96},{160,128},{192,160},{224,1... | collective-permute-start | bytes 688136 | tf_op jit(solution)/shard_map/ppermute | solution.py:14
  278.9 9.6 %all-to-all-done.2 = bf16[4,24,1792]{2,1,0:T(8,128)(2,1)S(1)} async-done(((bf16[4,24,1792]{2,1,0:T(8,128)(2,1)}), bf16[4,24,1792]{2,1,0:T(8,128)(2,1)S(1)}, u32[]{:S(2)}, u32[]{:S(2)}) %all-to-all-start.2) | async-done | bytes 344096 | tf_op jit(solution)/shard_map/all_to_all | solution.py:72
  288.5 0.2 fusion.44
  288.7 0.2 fusion.43
  289.0 0.1 fusion.31
  289.1 4.9 %collective-permute-start.3 = (bf16[32,3584]{1,0:T(8,128)(2,1)S(1)}, bf16[32,3584]{1,0:T(8,128)(2,1)S(1)}, u32[]{:S(2)}, u32[]{:S(2)}) collective-permute-start(bf16[32,3584]{1,0:T(8,128)(2,1)S(1)} %fusion.31), channel_id=1, source_target_pairs={{0,32},{32,64},{64,96},{96,128},{128,160},{160,192},{192,224},{224... | collective-permute-start | bytes 688136 | tf_op jit(solution)/shard_map/ppermute | solution.py:14
  294.0 5.9 %collective-permute-done.3 = bf16[32,3584]{1,0:T(8,128)(2,1)S(1)} collective-permute-done((bf16[32,3584]{1,0:T(8,128)(2,1)S(1)}, bf16[32,3584]{1,0:T(8,128)(2,1)S(1)}, u32[]{:S(2)}, u32[]{:S(2)}) %collective-permute-start.3) | collective-permute-done | bytes 229408 | tf_op jit(solution)/shard_map/ppermute | solution.py:14
  299.9 0.7 copy.21
  300.6 0.7 copy.22
  (35 shorter events, 0.1 us)
Async XLA Ops:
  7.2 7.1 %copy-start.7 = (bf16[1,3584,128]{2,1,0:T(8,128)(2,1)S(1)}, bf16[1,3584,128]{2,1,0:T(8,128)(2,1)}, u32[]{:S(2)}) copy-start(bf16[1,3584,128]{2,1,0:T(8,128)(2,1)} %param.15) | copy-start | bytes 2752516
  7.2 9.0 %copy-start.6 = (bf16[1,3584,128]{2,1,0:T(8,128)(2,1)S(1)}, bf16[1,3584,128]{2,1,0:T(8,128)(2,1)}, u32[]{:S(2)}) copy-start(bf16[1,3584,128]{2,1,0:T(8,128)(2,1)} %param.16) | copy-start | bytes 2752516
  7.2 11.4 %copy-start.10 = (s32[1,32,1]{1,2,0:T(1,128)S(1)}, s32[1,32,1]{1,2,0:T(1,128)}, u32[]{:S(2)}) copy-start(s32[1,32,1]{1,2,0:T(1,128)} %param.18) | copy-start | bytes 388
  7.2 11.5 %copy-start.11 = (s32[1,32,1]{1,2,0:T(1,128)S(1)}, s32[1,32,1]{1,2,0:T(1,128)}, u32[]{:S(2)}) copy-start(s32[1,32,1]{1,2,0:T(1,128)} %param.20) | copy-start | bytes 388
  7.2 27.9 %copy-start.8 = (bf16[1,128,3584]{2,1,0:T(8,128)(2,1)S(1)}, bf16[1,128,3584]{2,1,0:T(8,128)(2,1)}, u32[]{:S(2)}) copy-start(bf16[1,128,3584]{2,1,0:T(8,128)(2,1)} %param.17) | copy-start | bytes 2752516
  7.2 144.2 %all-gather.3.cloned.1.call-start = ((), (), s32[]{:S(2)}) async-start(), calls=%async_computation.5 | async-start | bytes 11698176 | tf_op jit(solution)/shard_map/all_gather | solution.py:115
  14.2 33.5 %collective-permute-start = (bf16[3584,128]{1,0:T(8,128)(2,1)S(1)}, bf16[3584,128]{1,0:T(8,128)(2,1)}, u32[]{:S(2)}, u32[]{:S(2)}) collective-permute-start(bf16[3584,128]{1,0:T(8,128)(2,1)S(1)} %bitcast.63), channel_id=1, source_target_pairs={{0,1},{1,0},{2,3},{3,2},{4,5},{5,4},{6,7},{7,6},{8,9},{9,8},{10,11... | collective-permute-start | bytes 2752520 | tf_op jit(solution)/shard_map/ppermute | solution.py:129
  16.2 31.6 %collective-permute-start.1 = (bf16[3584,128]{1,0:T(8,128)(2,1)S(1)}, bf16[3584,128]{1,0:T(8,128)(2,1)}, u32[]{:S(2)}, u32[]{:S(2)}) collective-permute-start(bf16[3584,128]{1,0:T(8,128)(2,1)S(1)} %bitcast.61), channel_id=1, source_target_pairs={{0,1},{1,0},{2,3},{3,2},{4,5},{5,4},{6,7},{7,6},{8,9},{9,8},{10,11... | collective-permute-start | bytes 2752520 | tf_op jit(solution)/shard_map/ppermute | solution.py:130
  19.9 27.6 %all-to-all-start = ((s32[16,1,64]{2,1,0:T(1,128)}), s32[16,1,64]{2,1,0:T(1,128)S(1)}, u32[]{:S(2)}, u32[]{:S(2)}) async-start(s32[16,1,64]{2,1,0:T(1,128)} %broadcast_in_dim.11), calls=%async_computation | async-start | bytes 16384 | tf_op jit(solution)/shard_map/all_to_all | solution.py:120
  35.1 124.8 %collective-permute-start.2 = (bf16[128,3584]{1,0:T(8,128)(2,1)S(1)}, bf16[128,3584]{1,0:T(8,128)(2,1)}, u32[]{:S(2)}, u32[]{:S(2)}) collective-permute-start(bf16[128,3584]{1,0:T(8,128)(2,1)S(1)} %bitcast.65), channel_id=1, source_target_pairs={{0,1},{1,0},{2,3},{3,2},{4,5},{5,4},{6,7},{7,6},{8,9},{9,8},{10,11... | collective-permute-start | bytes 2752520 | tf_op jit(solution)/shard_map/ppermute | solution.py:131
  49.4 1.9 copy-start
  151.4 6.5 %copy-start.1 = (bf16[3584,512]{1,0:T(8,128)(2,1)S(1)}, bf16[3584,512]{1,0:T(8,128)(2,1)}, u32[]{:S(2)}) copy-start(bf16[3584,512]{1,0:T(8,128)(2,1)} %copy-done) | copy-start | bytes 11010052
  160.0 3.3 %copy-start.5 = (bf16[1792,512]{1,0:T(8,128)(2,1)S(1)}, bf16[1792,512]{1,0:T(8,128)(2,1)}, u32[]{:S(2)}) copy-start(bf16[1792,512]{1,0:T(8,128)(2,1)} %get-tuple-element.12) | copy-start | bytes 5505028
  166.0 36.6 %all-to-all-start.3 = ((bf16[4,96,1792]{2,1,0:T(8,128)(2,1)}), bf16[4,96,1792]{2,1,0:T(8,128)(2,1)S(1)}, u32[]{:S(2)}, u32[]{:S(2)}) async-start(bf16[4,96,1792]{2,1,0:T(8,128)(2,1)} %bitcast.22), calls=%async_computation.3 | async-start | bytes 2752512 | tf_op jit(solution)/shard_map/all_to_all | solution.py:67
  169.6 2.3 copy-start.2
  178.8 68.3 %copy-start.12 = (s32[1,32,1]{1,2,0:T(1,128)S(1)}, s32[1,32,1]{1,2,0:T(1,128)}, u32[]{:S(2)}) copy-start(s32[1,32,1]{1,2,0:T(1,128)} %param.19) | copy-start | bytes 388
  202.6 35.8 %all-to-all-start.1 = ((bf16[4,96,1792]{2,1,0:T(8,128)(2,1)}), bf16[4,96,1792]{2,1,0:T(8,128)(2,1)S(1)}, u32[]{:S(2)}, u32[]{:S(2)}) async-start(bf16[4,96,1792]{2,1,0:T(8,128)(2,1)} %bitcast.60), calls=%async_computation.1 | async-start | bytes 2752512 | tf_op jit(solution)/shard_map/all_to_all | solution.py:67
  206.1 66.8 %copy-start.3 = (bf16[1,32,3584]{2,1,0:T(8,128)(2,1)S(1)}, bf16[1,32,3584]{2,1,0:T(8,128)(2,1)}, u32[]{:S(2)}) copy-start(bf16[1,32,3584]{2,1,0:T(8,128)(2,1)} %param.12) | copy-start | bytes 688132
  206.1 67.0 %copy-start.9 = (bf16[1,32,3584]{2,1,0:T(8,128)(2,1)S(1)}, bf16[1,32,3584]{2,1,0:T(8,128)(2,1)}, u32[]{:S(2)}) copy-start(bf16[1,32,3584]{2,1,0:T(8,128)(2,1)} %param.13) | copy-start | bytes 688132
  207.2 81.8 %copy-start.4 = (bf16[1,32,3584]{2,1,0:T(8,128)(2,1)S(1)}, bf16[1,32,3584]{2,1,0:T(8,128)(2,1)}, u32[]{:S(2)}) copy-start(bf16[1,32,3584]{2,1,0:T(8,128)(2,1)} %param.11) | copy-start | bytes 688132
  238.4 30.2 %all-to-all-start.4 = ((bf16[4,24,1792]{2,1,0:T(8,128)(2,1)}), bf16[4,24,1792]{2,1,0:T(8,128)(2,1)S(1)}, u32[]{:S(2)}, u32[]{:S(2)}) async-start(bf16[4,24,1792]{2,1,0:T(8,128)(2,1)} %bitcast.23), calls=%async_computation.4 | async-start | bytes 688128 | tf_op jit(solution)/shard_map/all_to_all | solution.py:72
  268.6 19.9 %all-to-all-start.2 = ((bf16[4,24,1792]{2,1,0:T(8,128)(2,1)}), bf16[4,24,1792]{2,1,0:T(8,128)(2,1)S(1)}, u32[]{:S(2)}, u32[]{:S(2)}) async-start(bf16[4,24,1792]{2,1,0:T(8,128)(2,1)} %bitcast.16), calls=%async_computation.2 | async-start | bytes 688128 | tf_op jit(solution)/shard_map/all_to_all | solution.py:72
  273.4 20.6 %collective-permute-start.4 = (bf16[32,3584]{1,0:T(8,128)(2,1)S(1)}, bf16[32,3584]{1,0:T(8,128)(2,1)S(1)}, u32[]{:S(2)}, u32[]{:S(2)}) collective-permute-start(bf16[32,3584]{1,0:T(8,128)(2,1)S(1)} %fusion.27), channel_id=1, source_target_pairs={{0,480},{32,0},{64,32},{96,64},{128,96},{160,128},{192,160},{224,1... | collective-permute-start | bytes 688136 | tf_op jit(solution)/shard_map/ppermute | solution.py:14
  289.1 10.8 %collective-permute-start.3 = (bf16[32,3584]{1,0:T(8,128)(2,1)S(1)}, bf16[32,3584]{1,0:T(8,128)(2,1)S(1)}, u32[]{:S(2)}, u32[]{:S(2)}) collective-permute-start(bf16[32,3584]{1,0:T(8,128)(2,1)S(1)} %fusion.31), channel_id=1, source_target_pairs={{0,32},{32,64},{64,96},{96,128},{128,160},{160,192},{192,224},{224... | collective-permute-start | bytes 688136 | tf_op jit(solution)/shard_map/ppermute | solution.py:14
Sparse Core Ops, SparseCore 0:
  14.3 136.9 all-gather.2

commit v2 on v1

--- a/solution.py
+++ b/solution.py
@@ -44,33 +44,42 @@
     return jnp.concatenate(halves, axis=1)
 
 
-def packers(slots, me_expert, side):
-    sources, tokens = slots.shape
+def shifts(count, side, steps):
+    pairs = []
+    for device in range(count):
+        chip, core = device // 2, device % 2
+        place = chip // side * side + (chip % side + steps) % side
+        pairs.append((device, 2 * place + core))
+    return pairs
+
+
+def packers(slots, me_expert, me_place, tokens, side):
+    count = slots.shape[0]
+    sources = count // tokens
     groups = sources // side
     expert, rank = slots // CAP, slots % CAP
-    source = jnp.arange(sources, dtype=jnp.int32)[:, None]
-    base = (source % side) * (groups * 2 * CAP) + (source // side) * (2 * CAP) + rank
+    source = jnp.arange(count, dtype=jnp.int32) // tokens
+    back = (me_place - source % side) % side
+    base = back * (groups * 2 * CAP) + (source // side) * (2 * CAP) + rank
     base = jnp.where(expert == me_expert, base, -2 * CAP)
-    flat = base.reshape(-1)
     row = jnp.arange(sources * 2 * CAP, dtype=jnp.int32)[:, None]
-    return [(flat[None, :] + h * CAP == row).astype(jnp.bfloat16) for h in range(2)]
-
-
-def pack(places, hidden):
-    parts = [dot(place, hidden, ((1,), (0,))).astype(jnp.bfloat16) for place in places]
-    return jnp.concatenate(parts, axis=1)
-
-
-def send_back(partial, side, within, across):
+    return [(base[None, :] + h * CAP == row).astype(jnp.bfloat16) for h in range(2)]
+
+
+def join_group(partial, count, side):
     rows, width = partial.shape
-    blocks = partial.astype(jnp.bfloat16).reshape(side, rows // side, width)
-    got = lax.all_to_all(
-        blocks, "expert", split_axis=0, concat_axis=0, tiled=True, axis_index_groups=within
-    )
-    total = jnp.sum(got.astype(jnp.float32), axis=0).astype(jnp.bfloat16)
-    total = total.reshape(EXPERTS, 2 * CAP, width)
+    part = rows // side
+    blocks = partial.astype(jnp.bfloat16)
+    total = blocks[:part].astype(jnp.float32)
+    for k in range(1, side):
+        got = lax.ppermute(blocks[k * part : (k + 1) * part], "expert", shifts(count, side, -k))
+        total = total + got.astype(jnp.float32)
+    return total.astype(jnp.bfloat16).reshape(EXPERTS, 2 * CAP, width)
+
+
+def across_groups(blocks, across):
     return lax.all_to_all(
-        total, "expert", split_axis=0, concat_axis=0, tiled=True, axis_index_groups=across
+        blocks, "expert", split_axis=0, concat_axis=0, tiled=True, axis_index_groups=across
     )
 
 
@@ -91,10 +100,11 @@
     ring = count // 2
     side = ring // EXPERTS
     same_core = [[2 * z + c for z in range(ring)] for c in range(2)]
-    within = [[2 * (side * g + j) + c for j in range(side)] for g in range(EXPERTS) for c in range(2)]
     across = [[2 * (side * g + j) + c for g in range(EXPERTS)] for j in range(side) for c in range(2)]
     swap = [(i, i ^ 1) for i in range(count)]
-    me = lax.axis_index("expert") // (2 * side)
+    index = lax.axis_index("expert")
+    me_expert = index // (2 * side)
+    me_place = (index // 2) % side
 
     gain = norm_gain[0]
     tokens, width = x_fwd.shape[1:]
@@ -105,26 +115,25 @@
     scale_f = gate_fwd[0].astype(jnp.float32) / 256.0
     scale_b = gate_bwd[0].astype(jnp.float32) / 256.0
     r_b = rms_scale(xb)
-    normed_f = (xf * rms_scale(xf) * gain).astype(jnp.bfloat16)
+    slot_f = slots_of(route_fwd[0, :, 0])
+    slot_b = slots_of(route_bwd[0, :, 0])
+
     normed_b = (xb * r_b * gain).astype(jnp.bfloat16)
     grad_rows = (up32 * scale_b).astype(jnp.bfloat16)
-    slot_f = slots_of(route_fwd[0, :, 0])
-    slot_b = slots_of(route_bwd[0, :, 0])
-
-    sent = jnp.concatenate([normed_f, normed_b, grad_rows], axis=0)
-    got = lax.all_gather(sent, "expert", axis=0, tiled=False, axis_index_groups=same_core)
-    rows_f = got[:, :tokens].reshape(ring * tokens, width)
-    rows_b = got[:, tokens : 2 * tokens].reshape(ring * tokens, width)
-    rows_g = got[:, 2 * tokens :].reshape(ring * tokens, width)
-    both = jnp.concatenate([slot_f, slot_b])
-    slots = lax.all_to_all(
-        jnp.broadcast_to(both[None, None, :], (ring, 1, 2 * tokens)),
-        "expert",
-        split_axis=0,
-        concat_axis=0,
-        tiled=True,
-        axis_index_groups=same_core,
-    )[:, 0]
+    tag = jnp.broadcast_to(slot_b[:, None].astype(jnp.bfloat16), (tokens, 128))
+    sent = jnp.concatenate([normed_b, grad_rows, tag], axis=1)
+    got = lax.all_gather(sent, "expert", axis=0, tiled=True, axis_index_groups=same_core)
+
+    normed_f = (xf * rms_scale(xf) * gain).astype(jnp.bfloat16)
+    place = jnp.concatenate(half_places(slot_f))
+    table_row = jnp.arange(EXPERTS * 2 * CAP, dtype=jnp.int32)[:, None]
+    put = (place[None, :] == table_row).astype(jnp.bfloat16)
+    halves = jnp.concatenate([normed_f[:, :half], normed_f[:, half:]], axis=0)
+    packed = dot(put, halves, ((1,), (0,))).astype(jnp.bfloat16)
+    mine = across_groups(packed.reshape(EXPERTS, 2 * CAP, half), across)
+    mine = mine.reshape(EXPERTS * 2 * CAP, half)
+    blocks = [mine] + [lax.ppermute(mine, "expert", shifts(count, side, k)) for k in range(1, side)]
+    rows_f = jnp.concatenate(blocks, axis=0)
 
     gate_o = lax.ppermute(w_gate[0], "expert", swap)
     up_o = lax.ppermute(w_up[0], "expert", swap)
@@ -135,22 +144,31 @@
     dn_stack = jnp.concatenate([w_dn[:, :half], w_dn[:, half:]], axis=0)
     in_stack = jnp.concatenate([w_in[:half], w_in[half:]], axis=1)
 
-    place_f = packers(slots[:, :tokens], me, side)
-    place_b = packers(slots[:, tokens:], me, side)
-
-    pre_f = dot(rows_f, w_in, ((1,), (0,)))
-    act = (jax.nn.silu(pre_f[:, :hid]) * pre_f[:, hid:]).astype(jnp.bfloat16)
-    part_f = dot(pack(place_f, act), dn_stack, ((1,), (0,)))
-    table_f = send_back(part_f, side, within, across)
-
+    pre_f = dot(rows_f, in_stack, ((1,), (0,))).reshape(ring, 2 * CAP, 4 * hid)
+    pre_f = pre_f[:, :CAP, : 2 * hid] + pre_f[:, CAP:, 2 * hid :]
+    act = (jax.nn.silu(pre_f[..., :hid]) * pre_f[..., hid:]).astype(jnp.bfloat16)
+    lower = jnp.pad(act, ((0, 0), (0, CAP), (0, 0)))
+    upper = jnp.pad(act, ((0, 0), (CAP, 0), (0, 0)))
+    act = jnp.concatenate([lower, upper], axis=2).reshape(ring * 2 * CAP, 2 * hid)
+    part_f = dot(act, dn_stack, ((1,), (0,)))
+    total_f = join_group(part_f, count, side)
+    got, total_f = lax.optimization_barrier((got, total_f))
+    table_f = across_groups(total_f, across)
+
+    rows_b = got[:, :width]
+    rows_g = got[:, width : 2 * width]
+    slots_b = got[:, 2 * width].astype(jnp.int32)
     pre_b = dot(rows_b, w_in, ((1,), (0,)))
     d_act = dot(rows_g, w_dn, ((1,), (1,)))
     gate, up = pre_b[:, :hid], pre_b[:, hid:]
     sig = jax.nn.sigmoid(gate)
     d_gate = (d_act * up * sig * (1.0 + gate * (1.0 - sig))).astype(jnp.bfloat16)
     d_up = (d_act * gate * sig).astype(jnp.bfloat16)
-    part_b = dot(pack(place_b, jnp.concatenate([d_gate, d_up], axis=1)), in_stack, ((1,), (1,)))
-    table_b = send_back(part_b, side, within, across)
+    hidden_b = jnp.concatenate([d_gate, d_up], axis=1)
+    places = packers(slots_b, me_expert, me_place, tokens, side)
+    parts = [dot(p, hidden_b, ((1,), (0,))).astype(jnp.bfloat16) for p in places]
+    part_b = dot(jnp.concatenate(parts, axis=1), in_stack, ((1,), (1,)))
+    table_b = across_groups(join_group(part_b, count, side), across)
 
     moe_f = pick_back(table_f, slot_f)
     y = (xf + scale_f * moe_f).astype(jnp.bfloat16)

time: 310 us -> 311 us (level)
  waiting for transfers between devices: 200 us -> 163 us
  starting transfers between devices: 51.5 us -> 85.4 us
  local copies, waits for them, and re-layouts: 12.9 us -> 4.96 us
  other arithmetic: 13.6 us -> 21.2 us
    ppermute x0 -> x9, waiting for transfers between devices: none -> 102 us  [the longest x6 71.9 us: join_group(): lax.ppermute(blocks[k * part:(k + 1) * part], 'expert', shifts(count, sid...]
    all_gather x1, waiting for transfers between devices: 98.6 us -> 18.7 us  [per_device(): lax.all_gather(sent, 'expert', axis=0, tiled=True, axis_index_groups=same...]
    all_to_all x5 -> x3, waiting for transfers between devices: 95.6 us -> 38.7 us  [across_groups(): lax.all_to_all(blocks, 'expert', split_axis=0, concat_axis=0, tiled=True,...]
    ppermute x0 -> x9, starting transfers between devices: none -> 35.7 us  [the longest x6 24.2 us: join_group(): lax.ppermute(blocks[k * part:(k + 1) * part], 'expert', shifts(count, sid...]
    slice x1 -> x3, local copies, waits for them, and re-layouts: 6.51 us -> 1.09 us  [the longest x2 1.07 us: join_group(): blocks[k * part:(k + 1) * part]]
    dot_general x13 -> x12, matrix products: 15.6 us -> 17.2 us  [dot(): lax.dot_general(a, b, (dims, ((), ())), preferred_element_type=jnp.float32)]
    all_to_all x5 -> x3, starting transfers between devices: 34.8 us -> 34.8 us  [across_groups(): lax.all_to_all(blocks, 'expert', split_axis=0, concat_axis=0, tiled=True,...]
  transfers between devices with their start and end apart: 11 -> 18, of which waited for: 7 -> 11; matrix products, arithmetic and copies ran while one was open for 8% -> 7% of each run, Pallas kernels for 0% -> 0%
where the time goes in v2:
time: 311 us; the launch traced here: 307 us
  waiting for transfers between devices  163 us (52%)
  starting transfers between devices  85.4 us (27%)
  other arithmetic  21.2 us (7%)
  matrix products  17.2 us (6%)
  between operations  14.6 us (5%)
  local copies, waits for them, and re-layouts  4.96 us (2%)
    ppermute x6, waiting for transfers between devices, join_group(): lax.ppermute(blocks[k * part:(k + 1) * part], 'expert', shifts(count, sid...  71.9 us
    all_to_all x3, waiting for transfers between devices, across_groups(): lax.all_to_all(blocks, 'expert', split_axis=0, concat_axis=0, tiled=True,...  38.7 us
    all_to_all x3, starting transfers between devices, across_groups(): lax.all_to_all(blocks, 'expert', split_axis=0, concat_axis=0, tiled=True,...  34.8 us
    ppermute x3, waiting for transfers between devices, per_device(): lax.ppermute(mine, 'expert', shifts(count, side, k))  30.5 us
    ppermute x6, starting transfers between devices, join_group(): lax.ppermute(blocks[k * part:(k + 1) * part], 'expert', shifts(count, sid...  24.2 us
    all_gather x1, waiting for transfers between devices, per_device(): lax.all_gather(sent, 'expert', axis=0, tiled=True, axis_index_groups=same...  18.7 us
    dot_general x12, matrix products, dot(): lax.dot_general(a, b, (dims, ((), ())), preferred_element_type=jnp.float32)  17.2 us
    ppermute x3, starting transfers between devices, per_device(): lax.ppermute(mine, 'expert', shifts(count, side, k))  11.5 us
  transfers between devices with their start and end apart: 18, of which 11 were waited for; matrix products, arithmetic and copies ran while one was open for 7% of the time, Pallas kernels for 0%

profile of v2, /device:TPU:6, one launch (start us, length us, event | category | flops | bytes accessed | tf_op | source)
XLA Modules:
  0.0 306.7 jit_solution(6375939877800164526)
XLA Ops:
  7.3 1.2 fusion.33
  8.5 1.1 fusion.35
  9.6 0.7 fusion.51
  10.4 0.8 select_reduce_fusion
  11.2 1.2 broadcast_add_fusion.1
  12.5 0.7 multiply_bitcast_fusion
  13.1 0.8 reduce
  13.9 1.0 fusion.31
  15.0 1.2 fusion.37
  16.3 0.8 pad_maximum_fusion.7
  17.1 1.9 collective-permute-start.3
  19.0 2.4 collective-permute-start.4
  21.6 0.2 select_reduce_fusion.1
  21.9 1.0 convolution_convert_fusion.2
  22.9 15.1 %all-to-all-start = ((bf16[4,24,1792]{2,1,0:T(8,128)(2,1)}), bf16[4,24,1792]{2,1,0:T(8,128)(2,1)S(1)}, u32[]{:S(2)}, u32[]{:S(2)}) async-start(bf16[4,24,1792]{2,1,0:T(8,128)(2,1)} %bitcast.9), calls=%async_computation | async-start | bytes 688128 | tf_op jit(solution)/shard_map/all_to_all | solution.py:81
  38.0 1.9 collective-permute-start.5
  40.0 3.3 %pad_maximum_fusion = bf16[3584,512]{1,0:T(8,128)(2,1)} fusion(bf16[3584,128]{1,0:T(8,128)(2,1)} %collective-permute-done.4, bf16[3584,128]{1,0:T(8,128)(2,1)S(1)} %bitcast.53, bf16[3584,128]{1,0:T(8,128)(2,1)} %collective-permute-done.3, bf16[3584,128]{1,0:T(8,128)(2,1)S(1)} %bitcast.56), kind=kLoop, calls=%fused_computation | loop fusion | flops 14680064 | bytes 7340032 | tf_op jit(solution)/shard_map/concatenate | solution.py:141
  43.3 23.2 %all-to-all-done = bf16[4,24,1792]{2,1,0:T(8,128)(2,1)S(1)} async-done(((bf16[4,24,1792]{2,1,0:T(8,128)(2,1)}), bf16[4,24,1792]{2,1,0:T(8,128)(2,1)S(1)}, u32[]{:S(2)}, u32[]{:S(2)}) %all-to-all-start) | async-done | bytes 344096 | tf_op jit(solution)/shard_map/all_to_all | solution.py:81
  66.4 3.7 %collective-permute-start = (bf16[96,1792]{1,0:T(8,128)(2,1)S(1)}, bf16[96,1792]{1,0:T(8,128)(2,1)S(1)}, u32[]{:S(2)}, u32[]{:S(2)}) collective-permute-start(bf16[96,1792]{1,0:T(8,128)(2,1)S(1)} %bitcast.62), channel_id=1, source_target_pairs={{0,2},{1,3},{2,4},{3,5},{4,6},{5,7},{6,0},{7,1},{8,10},{9,11},{10,... | collective-permute-start | bytes 1032200 | tf_op jit(solution)/shard_map/ppermute | solution.py:135
  70.1 3.2 %collective-permute-start.1 = (bf16[96,1792]{1,0:T(8,128)(2,1)S(1)}, bf16[96,1792]{1,0:T(8,128)(2,1)S(1)}, u32[]{:S(2)}, u32[]{:S(2)}) collective-permute-start(bf16[96,1792]{1,0:T(8,128)(2,1)S(1)} %bitcast.63), channel_id=1, source_target_pairs={{0,4},{1,5},{2,6},{3,7},{4,0},{5,1},{6,2},{7,3},{8,12},{9,13},{10,... | collective-permute-start | bytes 1032200 | tf_op jit(solution)/shard_map/ppermute | solution.py:135
  73.3 4.5 %collective-permute-start.2 = (bf16[96,1792]{1,0:T(8,128)(2,1)S(1)}, bf16[96,1792]{1,0:T(8,128)(2,1)S(1)}, u32[]{:S(2)}, u32[]{:S(2)}) collective-permute-start(bf16[96,1792]{1,0:T(8,128)(2,1)S(1)} %bitcast.64), channel_id=1, source_target_pairs={{0,6},{1,7},{2,0},{3,1},{4,2},{5,3},{6,4},{7,5},{8,14},{9,15},{10,... | collective-permute-start | bytes 1032200 | tf_op jit(solution)/shard_map/ppermute | solution.py:135
  77.9 2.3 fusion.90
  80.3 1.9 fusion.15
  82.2 5.2 %collective-permute-done = bf16[96,1792]{1,0:T(8,128)(2,1)S(1)} collective-permute-done((bf16[96,1792]{1,0:T(8,128)(2,1)S(1)}, bf16[96,1792]{1,0:T(8,128)(2,1)S(1)}, u32[]{:S(2)}, u32[]{:S(2)}) %collective-permute-start) | collective-permute-done | bytes 344096 | tf_op jit(solution)/shard_map/ppermute | solution.py:135
  87.4 16.8 %collective-permute-done.1 = bf16[96,1792]{1,0:T(8,128)(2,1)S(1)} collective-permute-done((bf16[96,1792]{1,0:T(8,128)(2,1)S(1)}, bf16[96,1792]{1,0:T(8,128)(2,1)S(1)}, u32[]{:S(2)}, u32[]{:S(2)}) %collective-permute-start.1) | collective-permute-done | bytes 344096 | tf_op jit(solution)/shard_map/ppermute | solution.py:135
  104.1 8.6 %collective-permute-done.2 = bf16[96,1792]{1,0:T(8,128)(2,1)S(1)} collective-permute-done((bf16[96,1792]{1,0:T(8,128)(2,1)S(1)}, bf16[96,1792]{1,0:T(8,128)(2,1)S(1)}, u32[]{:S(2)}, u32[]{:S(2)}) %collective-permute-start.2) | collective-permute-done | bytes 344096 | tf_op jit(solution)/shard_map/ppermute | solution.py:135
  112.7 1.6 fusion.4
  114.6 0.9 convolution_convert_fusion
  115.5 1.0 fusion.92
  116.5 8.0 %collective-permute-start.6 = (bf16[96,1792]{1,0:T(8,128)(2,1)}, bf16[96,1792]{1,0:T(8,128)(2,1)S(1)}, u32[]{:S(2)}, u32[]{:S(2)}) collective-permute-start(bf16[96,1792]{1,0:T(8,128)(2,1)} %get-tuple-element.23), channel_id=1, source_target_pairs={{0,6},{1,7},{2,0},{3,1},{4,2},{5,3},{6,4},{7,5},{8,14},{9,15},{10,... | collective-permute-start | bytes 1032200 | tf_op jit(solution)/shard_map/ppermute | solution.py:75
  124.5 3.4 %collective-permute-start.7 = (bf16[96,1792]{1,0:T(8,128)(2,1)}, bf16[96,1792]{1,0:T(8,128)(2,1)}, u32[]{:S(2)}, u32[]{:S(2)}) collective-permute-start(bf16[96,1792]{1,0:T(8,128)(2,1)} %get-tuple-element.25), channel_id=1, source_target_pairs={{0,4},{1,5},{2,6},{3,7},{4,0},{5,1},{6,2},{7,3},{8,12},{9,13},{10,... | collective-permute-start | bytes 1032200 | tf_op jit(solution)/shard_map/ppermute | solution.py:75
  128.0 1.9 collective-permute-start.8
  129.9 10.5 %collective-permute-done.6 = bf16[96,1792]{1,0:T(8,128)(2,1)S(1)} collective-permute-done((bf16[96,1792]{1,0:T(8,128)(2,1)}, bf16[96,1792]{1,0:T(8,128)(2,1)S(1)}, u32[]{:S(2)}, u32[]{:S(2)}) %collective-permute-start.6) | collective-permute-done | bytes 344096 | tf_op jit(solution)/shard_map/ppermute | solution.py:75
  140.4 28.9 %collective-permute-done.7 = bf16[96,1792]{1,0:T(8,128)(2,1)} collective-permute-done((bf16[96,1792]{1,0:T(8,128)(2,1)}, bf16[96,1792]{1,0:T(8,128)(2,1)}, u32[]{:S(2)}, u32[]{:S(2)}) %collective-permute-start.7) | collective-permute-done | bytes 344096 | tf_op jit(solution)/shard_map/ppermute | solution.py:75
  169.3 2.0 add_convert_fusion.1
  171.3 18.7 %all-gather.2.cloned.1.call-done = bf16[512,7296]{1,0:T(8,128)(2,1)} async-done(((bf16[32,7296]{1,0:T(8,128)(2,1)}), bf16[512,7296]{1,0:T(8,128)(2,1)}) %all-gather.2.cloned.1.call-update) | async-done | bytes 7471120 | tf_op jit(solution)/shard_map/all_gather | solution.py:125
  189.9 1.2 fusion.45
  191.1 1.1 fusion.46
  192.2 5.3 %fusion = f32[512,512]{0,1:T(8,128)S(1)} fusion(bf16[512,7296]{1,0:T(8,128)(2,1)} %all-gather.2.cloned.1.call-done, bf16[3584,128]{1,0:T(8,128)(2,1)} %collective-permute-done.4, bf16[3584,128]{1,0:T(8,128)(2,1)} %bitcast.51, bf16[3584,128]{1,0:T(8,128)(2,1)} %collective-permute-done.3, bf16[3584,128]{1,0:T(8,128)(2,1)} %bitcast.54), kind=kOutput, calls=%fused_computation.2 | convolution fusion | flops 1893728256 | bytes 8388608 | tf_op jit(solution)/shard_map/dot_general | solution.py:22
  197.5 3.5 %fusion.26 = (bf16[512,256]{0,1:T(8,128)(2,1)S(1)}, bf16[512,256]{0,1:T(8,128)(2,1)S(1)}) fusion(f32[512,512]{0,1:T(8,128)S(1)} %fusion, bf16[128,3584]{1,0:T(8,128)(2,1)} %collective-permute-done.5, bf16[128,3584]{1,0:T(8,128)(2,1)S(1)} %bitcast.59, bf16[512,7296]{1,0:T(8,128)(2,1)} %all-gather.2.cloned.1.call-done), kind=kOutput, calls=%fused_computation.53 | convolution fusion | flops 944898048 | bytes 7077888 | tf_op jit(solution)/shard_map/dot_general | solution.py:22
  201.0 0.4 convolution_convert_fusion.4
  201.4 0.4 convolution_convert_fusion.3
  201.9 9.0 %all-to-all-start.1 = ((bf16[4,24,1792]{2,1,0:T(8,128)(2,1)}), bf16[4,24,1792]{2,1,0:T(8,128)(2,1)S(1)}, u32[]{:S(2)}, u32[]{:S(2)}) async-start(bf16[4,24,1792]{2,1,0:T(8,128)(2,1)} %bitcast.16), calls=%async_computation.1 | async-start | bytes 688128 | tf_op jit(solution)/shard_map/all_to_all | solution.py:81
  210.9 3.2 %convolution_convert_fusion.1 = bf16[384,1792]{1,0:T(8,128)(2,1)S(1)} fusion(bf16[1792,512]{1,0:T(8,128)(2,1)} %copy-done.2, bf16[1792,512]{1,0:T(8,128)(2,1)S(1)} %get-tuple-element.14, bf16[384,512]{1,0:T(8,128)(2,1)S(1)} %convolution_convert_fusion.3, bf16[384,512]{1,0:T(8,128)(2,1)S(1)} %convolution_convert_fusion.4), kind=kOutput, calls=%fused_computation.7 | convolution fusion | flops 1418887168 | bytes 5832704 | tf_op jit(solution)/shard_map/dot_general | solution.py:22
  214.2 4.0 %collective-permute-start.10 = (bf16[96,1792]{1,0:T(8,128)(2,1)S(1)}, bf16[96,1792]{1,0:T(8,128)(2,1)S(1)}, u32[]{:S(2)}, u32[]{:S(2)}) collective-permute-start(bf16[96,1792]{1,0:T(8,128)(2,1)S(1)} %get-tuple-element.20), channel_id=1, source_target_pairs={{0,6},{1,7},{2,0},{3,1},{4,2},{5,3},{6,4},{7,5},{8,14},{9,15},{10,... | collective-permute-start | bytes 1032200 | tf_op jit(solution)/shard_map/ppermute | solution.py:75
  218.2 3.8 %collective-permute-start.11 = (bf16[96,1792]{1,0:T(8,128)(2,1)S(1)}, bf16[96,1792]{1,0:T(8,128)(2,1)S(1)}, u32[]{:S(2)}, u32[]{:S(2)}) collective-permute-start(bf16[96,1792]{1,0:T(8,128)(2,1)S(1)} %get-tuple-element.22), channel_id=1, source_target_pairs={{0,4},{1,5},{2,6},{3,7},{4,0},{5,1},{6,2},{7,3},{8,12},{9,13},{10,... | collective-permute-start | bytes 1032200 | tf_op jit(solution)/shard_map/ppermute | solution.py:75
  222.1 3.0 collective-permute-start.12
  225.1 11.2 %collective-permute-done.10 = bf16[96,1792]{1,0:T(8,128)(2,1)S(1)} collective-permute-done((bf16[96,1792]{1,0:T(8,128)(2,1)S(1)}, bf16[96,1792]{1,0:T(8,128)(2,1)S(1)}, u32[]{:S(2)}, u32[]{:S(2)}) %collective-permute-start.10) | collective-permute-done | bytes 344096 | tf_op jit(solution)/shard_map/ppermute | solution.py:75
  236.3 21.3 %collective-permute-done.11 = bf16[96,1792]{1,0:T(8,128)(2,1)S(1)} collective-permute-done((bf16[96,1792]{1,0:T(8,128)(2,1)S(1)}, bf16[96,1792]{1,0:T(8,128)(2,1)S(1)}, u32[]{:S(2)}, u32[]{:S(2)}) %collective-permute-start.11) | collective-permute-done | bytes 344096 | tf_op jit(solution)/shard_map/ppermute | solution.py:75
  257.6 0.9 add_convert_fusion
  258.5 10.7 %all-to-all-start.2 = ((bf16[4,24,1792]{2,1,0:T(8,128)(2,1)}), bf16[4,24,1792]{2,1,0:T(8,128)(2,1)S(1)}, u32[]{:S(2)}, u32[]{:S(2)}) async-start(bf16[4,24,1792]{2,1,0:T(8,128)(2,1)} %bitcast.20), calls=%async_computation.2 | async-start | bytes 688128 | tf_op jit(solution)/shard_map/all_to_all | solution.py:81
  269.2 0.2 fusion.53
  269.5 0.2 fusion.54
  269.7 0.1 fusion.38
  269.9 3.5 %collective-permute-start.9 = (bf16[32,3584]{1,0:T(8,128)(2,1)S(1)}, bf16[32,3584]{1,0:T(8,128)(2,1)S(1)}, u32[]{:S(2)}, u32[]{:S(2)}) collective-permute-start(bf16[32,3584]{1,0:T(8,128)(2,1)S(1)} %fusion.38), channel_id=1, source_target_pairs={{0,32},{32,64},{64,96},{96,128},{128,160},{160,192},{192,224},{224... | collective-permute-start | bytes 688136 | tf_op jit(solution)/shard_map/ppermute | solution.py:14
  273.4 15.6 %all-to-all-done.2 = bf16[4,24,1792]{2,1,0:T(8,128)(2,1)S(1)} async-done(((bf16[4,24,1792]{2,1,0:T(8,128)(2,1)}), bf16[4,24,1792]{2,1,0:T(8,128)(2,1)S(1)}, u32[]{:S(2)}, u32[]{:S(2)}) %all-to-all-start.2) | async-done | bytes 344096 | tf_op jit(solution)/shard_map/all_to_all | solution.py:81
  288.9 0.2 fusion.55
  289.2 0.2 fusion.56
  289.4 0.2 fusion.34
  289.6 0.2 fusion.32
  289.9 5.1 %collective-permute-start.13 = (bf16[32,3584]{1,0:T(8,128)(2,1)S(1)}, bf16[32,3584]{1,0:T(8,128)(2,1)S(1)}, u32[]{:S(2)}, u32[]{:S(2)}) collective-permute-start(bf16[32,3584]{1,0:T(8,128)(2,1)S(1)} %fusion.32), channel_id=1, source_target_pairs={{0,480},{32,0},{64,32},{96,64},{128,96},{160,128},{192,160},{224,1... | collective-permute-start | bytes 688136 | tf_op jit(solution)/shard_map/ppermute | solution.py:14
  295.0 3.5 %collective-permute-done.13 = bf16[32,3584]{1,0:T(8,128)(2,1)S(1)} collective-permute-done((bf16[32,3584]{1,0:T(8,128)(2,1)S(1)}, bf16[32,3584]{1,0:T(8,128)(2,1)S(1)}, u32[]{:S(2)}, u32[]{:S(2)}) %collective-permute-start.13) | collective-permute-done | bytes 229408 | tf_op jit(solution)/shard_map/ppermute | solution.py:14
  298.5 0.7 copy.15
  299.2 0.7 copy.16
  (64 shorter events, 0.9 us)
Async XLA Ops:
  7.2 9.9 %copy-start.4 = (bf16[1,3584,128]{2,1,0:T(8,128)(2,1)S(1)}, bf16[1,3584,128]{2,1,0:T(8,128)(2,1)}, u32[]{:S(2)}) copy-start(bf16[1,3584,128]{2,1,0:T(8,128)(2,1)} %param.15) | copy-start | bytes 2752516
  7.2 11.9 %copy-start.3 = (bf16[1,3584,128]{2,1,0:T(8,128)(2,1)S(1)}, bf16[1,3584,128]{2,1,0:T(8,128)(2,1)}, u32[]{:S(2)}) copy-start(bf16[1,3584,128]{2,1,0:T(8,128)(2,1)} %param.16) | copy-start | bytes 2752516
  7.2 14.3 %copy-start.12 = (s32[1,32,1]{1,2,0:T(1,128)S(1)}, s32[1,32,1]{1,2,0:T(1,128)}, u32[]{:S(2)}) copy-start(s32[1,32,1]{1,2,0:T(1,128)} %param.18) | copy-start | bytes 388
  7.2 30.8 %copy-start.5 = (bf16[1,128,3584]{2,1,0:T(8,128)(2,1)S(1)}, bf16[1,128,3584]{2,1,0:T(8,128)(2,1)}, u32[]{:S(2)}) copy-start(bf16[1,128,3584]{2,1,0:T(8,128)(2,1)} %param.17) | copy-start | bytes 2752516
  7.2 182.7 %all-gather.2.cloned.1.call-start = ((), (), s32[]{:S(2)}) async-start(), calls=%async_computation.3 | async-start | bytes 7938048 | tf_op jit(solution)/shard_map/all_gather | solution.py:125
  13.9 9.0 %copy-start.8 = (f32[3584]{0:T(1024)}, f32[3584]{0:T(1024)S(1)}, u32[]{:S(2)}) copy-start(f32[3584]{0:T(1024)S(1)} %reduce) | copy-start | bytes 43012
  13.9 2.3 copy-start.10
  17.1 22.8 %collective-permute-start.3 = (bf16[3584,128]{1,0:T(8,128)(2,1)S(1)}, bf16[3584,128]{1,0:T(8,128)(2,1)}, u32[]{:S(2)}, u32[]{:S(2)}) collective-permute-start(bf16[3584,128]{1,0:T(8,128)(2,1)S(1)} %bitcast.55), channel_id=1, source_target_pairs={{0,1},{1,0},{2,3},{3,2},{4,5},{5,4},{6,7},{7,6},{8,9},{9,8},{10,11... | collective-permute-start | bytes 2752520 | tf_op jit(solution)/shard_map/ppermute | solution.py:138
  19.0 20.9 %collective-permute-start.4 = (bf16[3584,128]{1,0:T(8,128)(2,1)S(1)}, bf16[3584,128]{1,0:T(8,128)(2,1)}, u32[]{:S(2)}, u32[]{:S(2)}) collective-permute-start(bf16[3584,128]{1,0:T(8,128)(2,1)S(1)} %bitcast.52), channel_id=1, source_target_pairs={{0,1},{1,0},{2,3},{3,2},{4,5},{5,4},{6,7},{7,6},{8,9},{9,8},{10,11... | collective-permute-start | bytes 2752520 | tf_op jit(solution)/shard_map/ppermute | solution.py:139
  21.8 1.1 copy-start.15
  21.8 1.1 copy-start.17
  22.9 43.5 %all-to-all-start = ((bf16[4,24,1792]{2,1,0:T(8,128)(2,1)}), bf16[4,24,1792]{2,1,0:T(8,128)(2,1)S(1)}, u32[]{:S(2)}, u32[]{:S(2)}) async-start(bf16[4,24,1792]{2,1,0:T(8,128)(2,1)} %bitcast.9), calls=%async_computation | async-start | bytes 688128 | tf_op jit(solution)/shard_map/all_to_all | solution.py:81
  38.0 42.2 %collective-permute-start.5 = (bf16[128,3584]{1,0:T(8,128)(2,1)S(1)}, bf16[128,3584]{1,0:T(8,128)(2,1)}, u32[]{:S(2)}, u32[]{:S(2)}) collective-permute-start(bf16[128,3584]{1,0:T(8,128)(2,1)S(1)} %bitcast.57), channel_id=1, source_target_pairs={{0,1},{1,0},{2,3},{3,2},{4,5},{5,4},{6,7},{7,6},{8,9},{9,8},{10,11... | collective-permute-start | bytes 2752520 | tf_op jit(solution)/shard_map/ppermute | solution.py:140
  66.4 20.9 %collective-permute-start = (bf16[96,1792]{1,0:T(8,128)(2,1)S(1)}, bf16[96,1792]{1,0:T(8,128)(2,1)S(1)}, u32[]{:S(2)}, u32[]{:S(2)}) collective-permute-start(bf16[96,1792]{1,0:T(8,128)(2,1)S(1)} %bitcast.62), channel_id=1, source_target_pairs={{0,2},{1,3},{2,4},{3,5},{4,6},{5,7},{6,0},{7,1},{8,10},{9,11},{10,... | collective-permute-start | bytes 1032200 | tf_op jit(solution)/shard_map/ppermute | solution.py:135
  70.1 34.0 %collective-permute-start.1 = (bf16[96,1792]{1,0:T(8,128)(2,1)S(1)}, bf16[96,1792]{1,0:T(8,128)(2,1)S(1)}, u32[]{:S(2)}, u32[]{:S(2)}) collective-permute-start(bf16[96,1792]{1,0:T(8,128)(2,1)S(1)} %bitcast.63), channel_id=1, source_target_pairs={{0,4},{1,5},{2,6},{3,7},{4,0},{5,1},{6,2},{7,3},{8,12},{9,13},{10,... | collective-permute-start | bytes 1032200 | tf_op jit(solution)/shard_map/ppermute | solution.py:135
  73.3 39.4 %collective-permute-start.2 = (bf16[96,1792]{1,0:T(8,128)(2,1)S(1)}, bf16[96,1792]{1,0:T(8,128)(2,1)S(1)}, u32[]{:S(2)}, u32[]{:S(2)}) collective-permute-start(bf16[96,1792]{1,0:T(8,128)(2,1)S(1)} %bitcast.64), channel_id=1, source_target_pairs={{0,6},{1,7},{2,0},{3,1},{4,2},{5,3},{6,4},{7,5},{8,14},{9,15},{10,... | collective-permute-start | bytes 1032200 | tf_op jit(solution)/shard_map/ppermute | solution.py:135
  80.2 34.1 %copy-start.2 = (bf16[1792,512]{1,0:T(8,128)(2,1)}, bf16[1792,512]{1,0:T(8,128)(2,1)S(1)}, u32[]{:S(2)}) copy-start(bf16[1792,512]{1,0:T(8,128)(2,1)S(1)} %get-tuple-element.15) | copy-start | bytes 5505028
  116.5 23.9 %collective-permute-start.6 = (bf16[96,1792]{1,0:T(8,128)(2,1)}, bf16[96,1792]{1,0:T(8,128)(2,1)S(1)}, u32[]{:S(2)}, u32[]{:S(2)}) collective-permute-start(bf16[96,1792]{1,0:T(8,128)(2,1)} %get-tuple-element.23), channel_id=1, source_target_pairs={{0,6},{1,7},{2,0},{3,1},{4,2},{5,3},{6,4},{7,5},{8,14},{9,15},{10,... | collective-permute-start | bytes 1032200 | tf_op jit(solution)/shard_map/ppermute | solution.py:75
  124.5 44.7 %collective-permute-start.7 = (bf16[96,1792]{1,0:T(8,128)(2,1)}, bf16[96,1792]{1,0:T(8,128)(2,1)}, u32[]{:S(2)}, u32[]{:S(2)}) collective-permute-start(bf16[96,1792]{1,0:T(8,128)(2,1)} %get-tuple-element.25), channel_id=1, source_target_pairs={{0,4},{1,5},{2,6},{3,7},{4,0},{5,1},{6,2},{7,3},{8,12},{9,13},{10,... | collective-permute-start | bytes 1032200 | tf_op jit(solution)/shard_map/ppermute | solution.py:75
  128.0 41.3 %collective-permute-start.8 = (bf16[96,1792]{1,0:T(8,128)(2,1)}, bf16[96,1792]{1,0:T(8,128)(2,1)}, u32[]{:S(2)}, u32[]{:S(2)}) collective-permute-start(bf16[96,1792]{1,0:T(8,128)(2,1)} %get-tuple-element.24), channel_id=1, source_target_pairs={{0,2},{1,3},{2,4},{3,5},{4,6},{5,7},{6,0},{7,1},{8,10},{9,11},{10,... | collective-permute-start | bytes 1032200 | tf_op jit(solution)/shard_map/ppermute | solution.py:75
  192.2 5.3 %copy-start.6 = (bf16[1,128,3584]{2,1,0:T(8,128)(2,1)S(1)}, bf16[1,128,3584]{2,1,0:T(8,128)(2,1)}, u32[]{:S(2)}) copy-start(bf16[1,128,3584]{2,1,0:T(8,128)(2,1)} %param.17) | copy-start | bytes 2752516
  201.9 56.7 %all-to-all-start.1 = ((bf16[4,24,1792]{2,1,0:T(8,128)(2,1)}), bf16[4,24,1792]{2,1,0:T(8,128)(2,1)S(1)}, u32[]{:S(2)}, u32[]{:S(2)}) async-start(bf16[4,24,1792]{2,1,0:T(8,128)(2,1)} %bitcast.16), calls=%async_computation.1 | async-start | bytes 688128 | tf_op jit(solution)/shard_map/all_to_all | solution.py:81
  210.9 14.2 %copy-start.19 = (s32[1,32,1]{1,2,0:T(1,128)S(1)}, s32[1,32,1]{1,2,0:T(1,128)}, u32[]{:S(2)}) copy-start(s32[1,32,1]{1,2,0:T(1,128)} %param.19) | copy-start | bytes 388
  214.1 55.2 %copy-start.18 = (s32[32]{0:T(128)S(1)}, s32[32]{0:T(128)}, u32[]{:S(2)}) copy-start(s32[32]{0:T(128)} %copy-done.17) | copy-start | bytes 388
  214.1 55.4 %copy-start.16 = (s32[32]{0:T(128)S(1)}, s32[32]{0:T(128)}, u32[]{:S(2)}) copy-start(s32[32]{0:T(128)} %copy-done.15) | copy-start | bytes 388
  214.1 55.6 %copy-start.1 = (bf16[1,32,3584]{2,1,0:T(8,128)(2,1)S(1)}, bf16[1,32,3584]{2,1,0:T(8,128)(2,1)}, u32[]{:S(2)}) copy-start(bf16[1,32,3584]{2,1,0:T(8,128)(2,1)} %param.11) | copy-start | bytes 688132
  214.2 74.7 %copy-start.14 = (s32[32]{0:T(128)S(1)}, s32[32]{0:T(128)}, u32[]{:S(2)}) copy-start(s32[32]{0:T(128)} %get-tuple-element.9) | copy-start | bytes 388
  214.2 75.0 %copy-start.13 = (s32[32]{0:T(128)S(1)}, s32[32]{0:T(128)}, u32[]{:S(2)}) copy-start(s32[32]{0:T(128)} %get-tuple-element.8) | copy-start | bytes 388
  214.2 22.1 %collective-permute-start.10 = (bf16[96,1792]{1,0:T(8,128)(2,1)S(1)}, bf16[96,1792]{1,0:T(8,128)(2,1)S(1)}, u32[]{:S(2)}, u32[]{:S(2)}) collective-permute-start(bf16[96,1792]{1,0:T(8,128)(2,1)S(1)} %get-tuple-element.20), channel_id=1, source_target_pairs={{0,6},{1,7},{2,0},{3,1},{4,2},{5,3},{6,4},{7,5},{8,14},{9,15},{10,... | collective-permute-start | bytes 1032200 | tf_op jit(solution)/shard_map/ppermute | solution.py:75
  218.2 39.4 %collective-permute-start.11 = (bf16[96,1792]{1,0:T(8,128)(2,1)S(1)}, bf16[96,1792]{1,0:T(8,128)(2,1)S(1)}, u32[]{:S(2)}, u32[]{:S(2)}) collective-permute-start(bf16[96,1792]{1,0:T(8,128)(2,1)S(1)} %get-tuple-element.22), channel_id=1, source_target_pairs={{0,4},{1,5},{2,6},{3,7},{4,0},{5,1},{6,2},{7,3},{8,12},{9,13},{10,... | collective-permute-start | bytes 1032200 | tf_op jit(solution)/shard_map/ppermute | solution.py:75
  222.1 35.6 %collective-permute-start.12 = (bf16[96,1792]{1,0:T(8,128)(2,1)S(1)}, bf16[96,1792]{1,0:T(8,128)(2,1)S(1)}, u32[]{:S(2)}, u32[]{:S(2)}) collective-permute-start(bf16[96,1792]{1,0:T(8,128)(2,1)S(1)} %get-tuple-element.21), channel_id=1, source_target_pairs={{0,2},{1,3},{2,4},{3,5},{4,6},{5,7},{6,0},{7,1},{8,10},{9,11},{10,... | collective-permute-start | bytes 1032200 | tf_op jit(solution)/shard_map/ppermute | solution.py:75
  225.1 64.3 %copy-start = (bf16[1,32,3584]{2,1,0:T(8,128)(2,1)S(1)}, bf16[1,32,3584]{2,1,0:T(8,128)(2,1)}, u32[]{:S(2)}) copy-start(bf16[1,32,3584]{2,1,0:T(8,128)(2,1)} %param.12) | copy-start | bytes 688132
  225.1 64.3 %copy-start.9 = (f32[3584]{0:T(1024)S(1)}, f32[3584]{0:T(1024)}, u32[]{:S(2)}) copy-start(f32[3584]{0:T(1024)} %copy-done.8) | copy-start | bytes 43012
  225.1 64.5 %copy-start.7 = (bf16[1,32,3584]{2,1,0:T(8,128)(2,1)S(1)}, bf16[1,32,3584]{2,1,0:T(8,128)(2,1)}, u32[]{:S(2)}) copy-start(bf16[1,32,3584]{2,1,0:T(8,128)(2,1)} %param.13) | copy-start | bytes 688132
  225.1 64.5 %copy-start.11 = (f32[32]{0:T(128)S(1)}, f32[32]{0:T(128)}, u32[]{:S(2)}) copy-start(f32[32]{0:T(128)} %copy-done.10) | copy-start | bytes 388
  258.5 30.4 %all-to-all-start.2 = ((bf16[4,24,1792]{2,1,0:T(8,128)(2,1)}), bf16[4,24,1792]{2,1,0:T(8,128)(2,1)S(1)}, u32[]{:S(2)}, u32[]{:S(2)}) async-start(bf16[4,24,1792]{2,1,0:T(8,128)(2,1)} %bitcast.20), calls=%async_computation.2 | async-start | bytes 688128 | tf_op jit(solution)/shard_map/all_to_all | solution.py:81
  269.9 25.1 %collective-permute-start.9 = (bf16[32,3584]{1,0:T(8,128)(2,1)S(1)}, bf16[32,3584]{1,0:T(8,128)(2,1)S(1)}, u32[]{:S(2)}, u32[]{:S(2)}) collective-permute-start(bf16[32,3584]{1,0:T(8,128)(2,1)S(1)} %fusion.38), channel_id=1, source_target_pairs={{0,32},{32,64},{64,96},{96,128},{128,160},{160,192},{192,224},{224... | collective-permute-start | bytes 688136 | tf_op jit(solution)/shard_map/ppermute | solution.py:14
  289.9 8.6 %collective-permute-start.13 = (bf16[32,3584]{1,0:T(8,128)(2,1)S(1)}, bf16[32,3584]{1,0:T(8,128)(2,1)S(1)}, u32[]{:S(2)}, u32[]{:S(2)}) collective-permute-start(bf16[32,3584]{1,0:T(8,128)(2,1)S(1)} %fusion.32), channel_id=1, source_target_pairs={{0,480},{32,0},{64,32},{96,64},{128,96},{160,128},{192,160},{224,1... | collective-permute-start | bytes 688136 | tf_op jit(solution)/shard_map/ppermute | solution.py:14
Sparse Core Ops, SparseCore 0:
  17.2 172.6 all-gather.1

commit v3 on v2

--- a/solution.py
+++ b/solution.py
@@ -42,6 +42,15 @@
         pick = (place[:, None] == jnp.arange(count, dtype=jnp.int32)[None, :]).astype(jnp.bfloat16)
         halves.append(dot(pick, rows, ((1,), (0,))))
     return jnp.concatenate(halves, axis=1)
+
+
+def shifts(count, side, steps):
+    pairs = []
+    for device in range(count):
+        chip, core = device // 2, device % 2
+        place = chip // side * side + (chip % side + steps) % side
+        pairs.append((device, 2 * place + core))
+    return pairs
 
 
 def shifts(count, side, steps):
@@ -109,57 +118,56 @@
     gain = norm_gain[0]
     tokens, width = x_fwd.shape[1:]
     half = width // 2
+    sent = jnp.concatenate([x_fwd[0], x_bwd[0], grad_out[0]], axis=1)
+    got = lax.all_gather(sent, "expert", axis=0, tiled=True, axis_index_groups=same_core)
+
     xf = x_fwd[0].astype(jnp.float32)
     xb = x_bwd[0].astype(jnp.float32)
     up32 = grad_out[0].astype(jnp.float32)
     scale_f = gate_fwd[0].astype(jnp.float32) / 256.0
     scale_b = gate_bwd[0].astype(jnp.float32) / 256.0
+    r_f = rms_scale(xf)
     r_b = rms_scale(xb)
     slot_f = slots_of(route_fwd[0, :, 0])
     slot_b = slots_of(route_bwd[0, :, 0])
-
-    normed_b = (xb * r_b * gain).astype(jnp.bfloat16)
-    grad_rows = (up32 * scale_b).astype(jnp.bfloat16)
-    tag = jnp.broadcast_to(slot_b[:, None].astype(jnp.bfloat16), (tokens, 128))
-    sent = jnp.concatenate([normed_b, grad_rows, tag], axis=1)
-    got = lax.all_gather(sent, "expert", axis=0, tiled=True, axis_index_groups=same_core)
-
-    normed_f = (xf * rms_scale(xf) * gain).astype(jnp.bfloat16)
-    place = jnp.concatenate(half_places(slot_f))
-    table_row = jnp.arange(EXPERTS * 2 * CAP, dtype=jnp.int32)[:, None]
-    put = (place[None, :] == table_row).astype(jnp.bfloat16)
-    halves = jnp.concatenate([normed_f[:, :half], normed_f[:, half:]], axis=0)
-    packed = dot(put, halves, ((1,), (0,))).astype(jnp.bfloat16)
-    mine = across_groups(packed.reshape(EXPERTS, 2 * CAP, half), across)
-    mine = mine.reshape(EXPERTS * 2 * CAP, half)
-    blocks = [mine] + [lax.ppermute(mine, "expert", shifts(count, side, k)) for k in range(1, side)]
-    rows_f = jnp.concatenate(blocks, axis=0)
+    small = jnp.concatenate(
+        [slot_f.astype(jnp.float32), slot_b.astype(jnp.float32), r_f[:, 0], r_b[:, 0], scale_b[:, 0]]
+    )
+    small = lax.all_to_all(
+        jnp.broadcast_to(small[None, None, :], (ring, 1, 5 * tokens)),
+        "expert",
+        split_axis=0,
+        concat_axis=0,
+        tiled=True,
+        axis_index_groups=same_core,
+    )[:, 0]
+    slots_f, slots_b, rs_f, rs_b, scales_b = [
+        small[:, i * tokens : (i + 1) * tokens].reshape(ring * tokens) for i in range(5)
+    ]
+    slots_f = slots_f.astype(jnp.int32)
+    slots_b = slots_b.astype(jnp.int32)
 
     gate_o = lax.ppermute(w_gate[0], "expert", swap)
     up_o = lax.ppermute(w_up[0], "expert", swap)
     down_o = lax.ppermute(w_down[0], "expert", swap)
     w_in = jnp.concatenate([w_gate[0], gate_o, w_up[0], up_o], axis=1)
+    w_gained = (w_in.astype(jnp.float32) * gain[:, None]).astype(jnp.bfloat16)
     w_dn = jnp.concatenate([w_down[0], down_o], axis=0)
     hid = w_dn.shape[0]
-    dn_stack = jnp.concatenate([w_dn[:, :half], w_dn[:, half:]], axis=0)
     in_stack = jnp.concatenate([w_in[:half], w_in[half:]], axis=1)
-
-    pre_f = dot(rows_f, in_stack, ((1,), (0,))).reshape(ring, 2 * CAP, 4 * hid)
-    pre_f = pre_f[:, :CAP, : 2 * hid] + pre_f[:, CAP:, 2 * hid :]
-    act = (jax.nn.silu(pre_f[..., :hid]) * pre_f[..., hid:]).astype(jnp.bfloat16)
-    lower = jnp.pad(act, ((0, 0), (0, CAP), (0, 0)))
-    upper = jnp.pad(act, ((0, 0), (CAP, 0), (0, 0)))
-    act = jnp.concatenate([lower, upper], axis=2).reshape(ring * 2 * CAP, 2 * hid)
-    part_f = dot(act, dn_stack, ((1,), (0,)))
-    total_f = join_group(part_f, count, side)
-    got, total_f = lax.optimization_barrier((got, total_f))
-    table_f = across_groups(total_f, across)
-
-    rows_b = got[:, :width]
-    rows_g = got[:, width : 2 * width]
-    slots_b = got[:, 2 * width].astype(jnp.int32)
-    pre_b = dot(rows_b, w_in, ((1,), (0,)))
-    d_act = dot(rows_g, w_dn, ((1,), (1,)))
+    w_gained, w_dn, in_stack = lax.optimization_barrier((w_gained, w_dn, in_stack))
+
+    pre_f = dot(got[:, :width], w_gained, ((1,), (0,))) * rs_f[:, None]
+    act = jax.nn.silu(pre_f[:, :hid]) * pre_f[:, hid:]
+    act = jnp.where((slots_f // CAP == me_expert)[:, None], act, 0.0).astype(jnp.bfloat16)
+    part_f = dot(act, w_dn, ((1,), (0,))).astype(jnp.bfloat16)
+    got, part_f = lax.optimization_barrier((got, part_f))
+    moe_f = lax.psum_scatter(
+        part_f, "expert", scatter_dimension=0, tiled=True, axis_index_groups=same_core
+    )
+
+    pre_b = dot(got[:, width : 2 * width], w_gained, ((1,), (0,))) * rs_b[:, None]
+    d_act = dot(got[:, 2 * width :], w_dn, ((1,), (1,))) * scales_b[:, None]
     gate, up = pre_b[:, :hid], pre_b[:, hid:]
     sig = jax.nn.sigmoid(gate)
     d_gate = (d_act * up * sig * (1.0 + gate * (1.0 - sig))).astype(jnp.bfloat16)
@@ -170,8 +178,7 @@
     part_b = dot(jnp.concatenate(parts, axis=1), in_stack, ((1,), (1,)))
     table_b = across_groups(join_group(part_b, count, side), across)
 
-    moe_f = pick_back(table_f, slot_f)
-    y = (xf + scale_f * moe_f).astype(jnp.bfloat16)
+    y = (xf + scale_f * moe_f.astype(jnp.float32)).astype(jnp.bfloat16)
     d_normed = pick_back(table_b, slot_b)
     weighted = d_normed * gain
     inner = jnp.mean(xb * weighted, axis=-1, keepdims=True)

time: 311 us -> 284 us (0.913); the launches traced: 307 us -> 284 us
  starting transfers between devices: 85.4 us -> 49.1 us
  waiting for transfers between devices: 163 us -> 176 us
    all_gather x1, waiting for transfers between devices: 18.7 us -> 93 us  [per_device(): lax.all_gather(sent, 'expert', axis=0, tiled=True, axis_index_groups=same...]
    ppermute x6 -> x3, waiting for transfers between devices: 71.9 us -> 35.4 us  [join_group(): lax.ppermute(blocks[k * part:(k + 1) * part], 'expert', shifts(count, sid...]
    ppermute x3 -> x0, waiting for transfers between devices: 30.5 us -> none  [per_device(): lax.ppermute(mine, 'expert', shifts(count, side, k))]
    all_to_all x3 -> x1, starting transfers between devices: 34.8 us -> 11.5 us  [across_groups(): lax.all_to_all(blocks, 'expert', split_axis=0, concat_axis=0, tiled=True,...]
    ppermute x6 -> x3, starting transfers between devices: 24.2 us -> 8.64 us  [join_group(): lax.ppermute(blocks[k * part:(k + 1) * part], 'expert', shifts(count, sid...]
    all_to_all x0 -> x1, starting transfers between devices: none -> 15.2 us  [per_device(): lax.all_to_all(jnp.broadcast_to(small[None, None, :], (ring, 1, 5 * token...]
    all_to_all x3 -> x1, waiting for transfers between devices: 38.7 us -> 26.9 us  [across_groups(): lax.all_to_all(blocks, 'expert', split_axis=0, concat_axis=0, tiled=True,...]
    ppermute x3 -> x0, starting transfers between devices: 11.5 us -> none  [per_device(): lax.ppermute(mine, 'expert', shifts(count, side, k))]
  transfers between devices with their start and end apart: 18 -> 12, of which waited for: 11 -> 7; matrix products, arithmetic and copies ran while one was open for 7% -> 11% of each run, Pallas kernels for 0% -> 0%
where the time goes in v3:
time: 284 us
  waiting for transfers between devices  176 us (62%)
  starting transfers between devices  49.1 us (17%)
  other arithmetic  20.4 us (7%)
  matrix products  19.7 us (7%)
  between operations  14.4 us (5%)
  local copies, waits for them, and re-layouts  3.89 us (1%)
    all_gather x1, waiting for transfers between devices, per_device(): lax.all_gather(sent, 'expert', axis=0, tiled=True, axis_index_groups=same...  93 us
    ppermute x3, waiting for transfers between devices, join_group(): lax.ppermute(blocks[k * part:(k + 1) * part], 'expert', shifts(count, sid...  35.4 us
    all_to_all x1, waiting for transfers between devices, across_groups(): lax.all_to_all(blocks, 'expert', split_axis=0, concat_axis=0, tiled=True,...  26.9 us
    dot_general x9, matrix products, dot(): lax.dot_general(a, b, (dims, ((), ())), preferred_element_type=jnp.float32)  19.7 us
    all_to_all x1, starting transfers between devices, per_device(): lax.all_to_all(jnp.broadcast_to(small[None, None, :], (ring, 1, 5 * token...  15.2 us
    all_to_all x1, starting transfers between devices, across_groups(): lax.all_to_all(blocks, 'expert', split_axis=0, concat_axis=0, tiled=True,...  11.5 us
    ppermute x3, starting transfers between devices, join_group(): lax.ppermute(blocks[k * part:(k + 1) * part], 'expert', shifts(count, sid...  8.64 us
    reduce_scatter x1, waiting for transfers between devices, per_device(): lax.psum_scatter(part_f, 'expert', scatter_dimension=0, tiled=True, axis_...  8.22 us
  transfers between devices with their start and end apart: 12, of which 7 were waited for; matrix products, arithmetic and copies ran while one was open for 11% of the time, Pallas kernels for 0%

profile of v3, /device:TPU:6, one launch (start us, length us, event | category | flops | bytes accessed | tf_op | source)
XLA Modules:
  0.0 283.6 jit_solution(4865592793996056825)
XLA Ops:
  7.2 2.0 pad_maximum_fusion.3
  9.3 0.7 fusion.40
  10.0 0.1 reduce_window_sum.17
  10.1 0.7 fusion.39
  10.8 0.8 select_reduce_fusion.1
  11.7 0.8 select_reduce_fusion
  12.5 1.1 fusion.23
  13.6 1.1 fusion.25
  14.7 0.7 multiply_bitcast_fusion
  15.4 0.7 broadcast_add_fusion.1
  16.1 0.1 concatenate.25
  16.2 0.6 broadcast_in_dim.22
  16.8 15.2 %all-to-all-start = ((f32[16,1,160]{2,1,0:T(1,128)}), f32[16,1,160]{2,1,0:T(1,128)S(1)}, u32[]{:S(2)}, u32[]{:S(2)}) async-start(f32[16,1,160]{2,1,0:T(1,128)} %broadcast_in_dim.22), calls=%async_computation | async-start | bytes 32768 | tf_op jit(solution)/shard_map/all_to_all | solution.py:136
  32.0 1.9 collective-permute-start
  34.0 2.4 collective-permute-start.1
  36.4 1.9 collective-permute-start.2
  38.3 0.8 reduce
  39.1 5.7 %all-to-all-done = f32[16,1,160]{2,1,0:T(1,128)S(1)} async-done(((f32[16,1,160]{2,1,0:T(1,128)}), f32[16,1,160]{2,1,0:T(1,128)S(1)}, u32[]{:S(2)}, u32[]{:S(2)}) %all-to-all-start) | async-done | bytes 10272 | tf_op jit(solution)/shard_map/all_to_all | solution.py:136
  44.7 0.1 sign_compare_fusion
  44.8 0.1 and.140
  44.9 0.1 fusion.77
  45.0 0.1 mul.192
  45.1 0.1 fusion.47
  45.1 0.1 div.106
  45.2 1.7 pad_maximum_fusion
  46.9 0.2 fusion.75
  47.2 2.4 pad_maximum_fusion.1
  49.6 1.4 pad_maximum_fusion.2
  50.9 0.2 copy-done
  51.1 0.6 copy-done.1
  51.7 2.8 multiply_convert_fusion
  54.5 93.0 %all-gather.2.cloned.1.call-done = bf16[512,10752]{1,0:T(8,128)(2,1)} async-done(((bf16[32,10752]{1,0:T(8,128)(2,1)}), bf16[512,10752]{1,0:T(8,128)(2,1)}) %all-gather.2.cloned.1.call-update) | async-done | bytes 11010064 | tf_op jit(solution)/shard_map/all_gather | solution.py:122
  147.5 5.2 %fusion.9 = f32[512,512]{1,0:T(8,128)S(1)} fusion(bf16[3584,512]{1,0:T(8,128)(2,1)} %multiply_convert_fusion, bf16[512,10752]{1,0:T(8,128)(2,1)} %all-gather.2.cloned.1.call-done, f32[512]{0:T(512)S(1)} %mul.192), kind=kOutput, calls=%fused_computation.13 | convolution fusion | flops 1879310336 | bytes 8390656 | tf_op jit(solution)/shard_map/dot_general | solution.py:22
  152.7 3.0 %convolution_convert_fusion = bf16[512,3584]{1,0:T(8,128)(2,1)} fusion(bf16[256,3584]{1,0:T(8,128)(2,1)S(1)} %copy-done.5, f32[512,512]{1,0:T(8,128)S(1)} %fusion.9, pred[512]{0:T(512)(128)(4,1)S(1)} %fusion.49), kind=kOutput, calls=%fused_computation.1 | convolution fusion | flops 942276608 | bytes 6554112 | tf_op jit(solution)/shard_map/dot_general | solution.py:22
  155.7 0.1 ne.230
  155.8 0.1 mul.208
  155.9 0.1 mul.205
  156.0 0.1 div.113
  156.1 0.1 rem.157
  156.2 5.2 %fusion.6 = f32[512,512]{1,0:T(8,128)S(1)} fusion(bf16[3584,512]{1,0:T(8,128)(2,1)} %multiply_convert_fusion, bf16[512,10752]{1,0:T(8,128)(2,1)} %all-gather.2.cloned.1.call-done, f32[512]{0:T(512)S(1)} %mul.208), kind=kOutput, calls=%fused_computation.12 | convolution fusion | flops 1879310336 | bytes 8390656 | tf_op jit(solution)/shard_map/dot_general | solution.py:22
  161.4 3.4 %fusion.20 = (bf16[512,256]{1,0:T(8,128)(2,1)S(1)}, bf16[512,256]{1,0:T(8,128)(2,1)S(1)}) fusion(f32[512,512]{1,0:T(8,128)S(1)} %fusion.6, f32[512]{0:T(512)S(1)} %mul.205, bf16[256,3584]{1,0:T(8,128)(2,1)S(1)} %copy-done.5, bf16[512,10752]{1,0:T(8,128)(2,1)} %all-gather.2.cloned.1.call-done), kind=kOutput, calls=%fused_computation.32 | convolution fusion | flops 941359104 | bytes 7079936 | tf_op jit(solution)/shard_map/dot_general | solution.py:22
  164.8 0.4 convolution_convert_fusion.2
  165.2 0.4 convolution_convert_fusion.3
  165.6 1.6 convolution_convert_fusion.1
  167.3 0.1 fusion.76
  167.4 4.3 %collective-permute-start.4 = (bf16[96,1792]{1,0:T(8,128)(2,1)S(1)}, bf16[96,1792]{1,0:T(8,128)(2,1)S(1)}, u32[]{:S(2)}, u32[]{:S(2)}) collective-permute-start(bf16[96,1792]{1,0:T(8,128)(2,1)S(1)} %get-tuple-element.20), channel_id=1, source_target_pairs={{0,6},{1,7},{2,0},{3,1},{4,2},{5,3},{6,4},{7,5},{8,14},{9,15},{10,... | collective-permute-start | bytes 1032200 | tf_op jit(solution)/shard_map/ppermute | solution.py:84
  171.6 1.9 collective-permute-start.6
  173.6 2.5 collective-permute-start.5
  176.0 22.7 %collective-permute-done.4 = bf16[96,1792]{1,0:T(8,128)(2,1)S(1)} collective-permute-done((bf16[96,1792]{1,0:T(8,128)(2,1)S(1)}, bf16[96,1792]{1,0:T(8,128)(2,1)S(1)}, u32[]{:S(2)}, u32[]{:S(2)}) %collective-permute-start.4) | collective-permute-done | bytes 344096 | tf_op jit(solution)/shard_map/ppermute | solution.py:84
  198.7 12.7 %collective-permute-done.5 = bf16[96,1792]{1,0:T(8,128)(2,1)S(1)} collective-permute-done((bf16[96,1792]{1,0:T(8,128)(2,1)S(1)}, bf16[96,1792]{1,0:T(8,128)(2,1)S(1)}, u32[]{:S(2)}, u32[]{:S(2)}) %collective-permute-start.5) | collective-permute-done | bytes 344096 | tf_op jit(solution)/shard_map/ppermute | solution.py:84
  211.4 0.9 add_convert_fusion
  212.3 11.5 %all-to-all-start.1 = ((bf16[4,24,1792]{2,1,0:T(8,128)(2,1)}), bf16[4,24,1792]{2,1,0:T(8,128)(2,1)S(1)}, u32[]{:S(2)}, u32[]{:S(2)}) async-start(bf16[4,24,1792]{2,1,0:T(8,128)(2,1)} %bitcast.11), calls=%async_computation.2 | async-start | bytes 688128 | tf_op jit(solution)/shard_map/all_to_all | solution.py:90
  223.8 26.9 %all-to-all-done.1 = bf16[4,24,1792]{2,1,0:T(8,128)(2,1)S(1)} async-done(((bf16[4,24,1792]{2,1,0:T(8,128)(2,1)}), bf16[4,24,1792]{2,1,0:T(8,128)(2,1)S(1)}, u32[]{:S(2)}, u32[]{:S(2)}) %all-to-all-start.1) | async-done | bytes 344096 | tf_op jit(solution)/shard_map/all_to_all | solution.py:90
  250.8 0.2 fusion.42
  251.0 0.2 fusion.41
  251.2 0.2 fusion.32
  251.4 0.2 fusion.31
  251.7 4.4 %collective-permute-start.7 = (bf16[32,3584]{1,0:T(8,128)(2,1)S(1)}, bf16[32,3584]{1,0:T(8,128)(2,1)S(1)}, u32[]{:S(2)}, u32[]{:S(2)}) collective-permute-start(bf16[32,3584]{1,0:T(8,128)(2,1)S(1)} %fusion.31), channel_id=1, source_target_pairs={{0,480},{32,0},{64,32},{96,64},{128,96},{160,128},{192,160},{224,1... | collective-permute-start | bytes 688136 | tf_op jit(solution)/shard_map/ppermute | solution.py:14
  256.0 8.2 %reduce-scatter.2.cloned.1.call-done = bf16[32,3584]{1,0:T(8,128)(2,1)} async-done(((bf16[512,3584]{1,0:T(8,128)(2,1)}), bf16[32,3584]{1,0:T(8,128)(2,1)}) %reduce-scatter.2.cloned.1.call-update) | async-done | bytes 229392 | tf_op jit(solution)/shard_map/reduce_scatter | solution.py:165
  264.2 1.1 fusion.24
  265.3 3.1 %collective-permute-start.3 = (bf16[32,3584]{1,0:T(8,128)(2,1)S(1)}, bf16[32,3584]{1,0:T(8,128)(2,1)S(1)}, u32[]{:S(2)}, u32[]{:S(2)}) collective-permute-start(bf16[32,3584]{1,0:T(8,128)(2,1)S(1)} %fusion.24), channel_id=1, source_target_pairs={{0,32},{32,64},{64,96},{96,128},{128,160},{160,192},{192,224},{224... | collective-permute-start | bytes 688136 | tf_op jit(solution)/shard_map/ppermute | solution.py:14
  268.5 6.9 %collective-permute-done.3 = bf16[32,3584]{1,0:T(8,128)(2,1)S(1)} collective-permute-done((bf16[32,3584]{1,0:T(8,128)(2,1)S(1)}, bf16[32,3584]{1,0:T(8,128)(2,1)S(1)}, u32[]{:S(2)}, u32[]{:S(2)}) %collective-permute-start.3) | collective-permute-done | bytes 229408 | tf_op jit(solution)/shard_map/ppermute | solution.py:14
  275.3 0.7 copy.22
  276.0 0.7 copy.23
  (32 shorter events, 0.3 us)
Async XLA Ops:
  7.2 140.3 %all-gather.2.cloned.1.call-start = ((), (), s32[]{:S(2)}) async-start(), calls=%async_computation.3 | async-start | bytes 11698176 | tf_op jit(solution)/shard_map/all_gather | solution.py:122
  16.8 28.0 %all-to-all-start = ((f32[16,1,160]{2,1,0:T(1,128)}), f32[16,1,160]{2,1,0:T(1,128)S(1)}, u32[]{:S(2)}, u32[]{:S(2)}) async-start(f32[16,1,160]{2,1,0:T(1,128)} %broadcast_in_dim.22), calls=%async_computation | async-start | bytes 32768 | tf_op jit(solution)/shard_map/all_to_all | solution.py:136
  32.0 232.3 %reduce-scatter.2.cloned.1.call-start = ((), (), s32[]{:S(2)}) async-start(), calls=%async_computation.4 | async-start | bytes 3899392 | tf_op jit(solution)/shard_map/reduce_scatter | solution.py:165
  32.0 13.2 %collective-permute-start = (bf16[3584,128]{1,0:T(8,128)(2,1)}, bf16[3584,128]{1,0:T(8,128)(2,1)S(1)}, u32[]{:S(2)}, u32[]{:S(2)}) collective-permute-start(bf16[3584,128]{1,0:T(8,128)(2,1)} %bitcast.42), channel_id=1, source_target_pairs={{0,1},{1,0},{2,3},{3,2},{4,5},{5,4},{6,7},{7,6},{8,9},{9,8},{10,11... | collective-permute-start | bytes 2752520 | tf_op jit(solution)/shard_map/ppermute | solution.py:150
  34.0 11.3 %collective-permute-start.1 = (bf16[3584,128]{1,0:T(8,128)(2,1)}, bf16[3584,128]{1,0:T(8,128)(2,1)S(1)}, u32[]{:S(2)}, u32[]{:S(2)}) collective-permute-start(bf16[3584,128]{1,0:T(8,128)(2,1)} %bitcast.39), channel_id=1, source_target_pairs={{0,1},{1,0},{2,3},{3,2},{4,5},{5,4},{6,7},{7,6},{8,9},{9,8},{10,11... | collective-permute-start | bytes 2752520 | tf_op jit(solution)/shard_map/ppermute | solution.py:151
  36.4 13.2 %collective-permute-start.2 = (bf16[128,3584]{1,0:T(8,128)(2,1)}, bf16[128,3584]{1,0:T(8,128)(2,1)S(1)}, u32[]{:S(2)}, u32[]{:S(2)}) collective-permute-start(bf16[128,3584]{1,0:T(8,128)(2,1)} %bitcast.49), channel_id=1, source_target_pairs={{0,1},{1,0},{2,3},{3,2},{4,5},{5,4},{6,7},{7,6},{8,9},{9,8},{10,11... | collective-permute-start | bytes 2752520 | tf_op jit(solution)/shard_map/ppermute | solution.py:152
  47.2 2.4 copy-start.6
  49.6 1.5 copy-start
  49.6 2.1 copy-start.1
  54.5 98.2 %copy-start.5 = (bf16[256,3584]{1,0:T(8,128)(2,1)S(1)}, bf16[256,3584]{1,0:T(8,128)(2,1)}, u32[]{:S(2)}) copy-start(bf16[256,3584]{1,0:T(8,128)(2,1)} %pad_maximum_fusion.2) | copy-start | bytes 5505028
  161.4 4.2 %copy-start.2 = (bf16[1792,1024]{1,0:T(8,128)(2,1)S(1)}, bf16[1792,1024]{1,0:T(8,128)(2,1)}, u32[]{:S(2)}) copy-start(bf16[1792,1024]{1,0:T(8,128)(2,1)} %pad_maximum_fusion.1) | copy-start | bytes 11010052
  167.2 56.6 %copy-start.8 = (s32[1,32,1]{1,2,0:T(1,128)S(1)}, s32[1,32,1]{1,2,0:T(1,128)}, u32[]{:S(2)}) copy-start(s32[1,32,1]{1,2,0:T(1,128)} %param.19) | copy-start | bytes 388
  167.2 84.0 %copy-start.3 = (bf16[1,32,3584]{2,1,0:T(8,128)(2,1)S(1)}, bf16[1,32,3584]{2,1,0:T(8,128)(2,1)}, u32[]{:S(2)}) copy-start(bf16[1,32,3584]{2,1,0:T(8,128)(2,1)} %param.12) | copy-start | bytes 688132
  167.3 84.2 %copy-start.7 = (bf16[1,32,3584]{2,1,0:T(8,128)(2,1)S(1)}, bf16[1,32,3584]{2,1,0:T(8,128)(2,1)}, u32[]{:S(2)}) copy-start(bf16[1,32,3584]{2,1,0:T(8,128)(2,1)} %param.13) | copy-start | bytes 688132
  167.3 97.0 %copy-start.4 = (bf16[1,32,3584]{2,1,0:T(8,128)(2,1)S(1)}, bf16[1,32,3584]{2,1,0:T(8,128)(2,1)}, u32[]{:S(2)}) copy-start(bf16[1,32,3584]{2,1,0:T(8,128)(2,1)} %param.11) | copy-start | bytes 688132
  167.4 31.4 %collective-permute-start.4 = (bf16[96,1792]{1,0:T(8,128)(2,1)S(1)}, bf16[96,1792]{1,0:T(8,128)(2,1)S(1)}, u32[]{:S(2)}, u32[]{:S(2)}) collective-permute-start(bf16[96,1792]{1,0:T(8,128)(2,1)S(1)} %get-tuple-element.20), channel_id=1, source_target_pairs={{0,6},{1,7},{2,0},{3,1},{4,2},{5,3},{6,4},{7,5},{8,14},{9,15},{10,... | collective-permute-start | bytes 1032200 | tf_op jit(solution)/shard_map/ppermute | solution.py:84
  171.6 27.1 %collective-permute-start.6 = (bf16[96,1792]{1,0:T(8,128)(2,1)S(1)}, bf16[96,1792]{1,0:T(8,128)(2,1)S(1)}, u32[]{:S(2)}, u32[]{:S(2)}) collective-permute-start(bf16[96,1792]{1,0:T(8,128)(2,1)S(1)} %get-tuple-element.21), channel_id=1, source_target_pairs={{0,2},{1,3},{2,4},{3,5},{4,6},{5,7},{6,0},{7,1},{8,10},{9,11},{10,... | collective-permute-start | bytes 1032200 | tf_op jit(solution)/shard_map/ppermute | solution.py:84
  173.6 37.9 %collective-permute-start.5 = (bf16[96,1792]{1,0:T(8,128)(2,1)S(1)}, bf16[96,1792]{1,0:T(8,128)(2,1)S(1)}, u32[]{:S(2)}, u32[]{:S(2)}) collective-permute-start(bf16[96,1792]{1,0:T(8,128)(2,1)S(1)} %get-tuple-element.22), channel_id=1, source_target_pairs={{0,4},{1,5},{2,6},{3,7},{4,0},{5,1},{6,2},{7,3},{8,12},{9,13},{10,... | collective-permute-start | bytes 1032200 | tf_op jit(solution)/shard_map/ppermute | solution.py:84
  212.3 38.4 %all-to-all-start.1 = ((bf16[4,24,1792]{2,1,0:T(8,128)(2,1)}), bf16[4,24,1792]{2,1,0:T(8,128)(2,1)S(1)}, u32[]{:S(2)}, u32[]{:S(2)}) async-start(bf16[4,24,1792]{2,1,0:T(8,128)(2,1)} %bitcast.11), calls=%async_computation.2 | async-start | bytes 688128 | tf_op jit(solution)/shard_map/all_to_all | solution.py:90
  251.7 16.8 %collective-permute-start.7 = (bf16[32,3584]{1,0:T(8,128)(2,1)S(1)}, bf16[32,3584]{1,0:T(8,128)(2,1)S(1)}, u32[]{:S(2)}, u32[]{:S(2)}) collective-permute-start(bf16[32,3584]{1,0:T(8,128)(2,1)S(1)} %fusion.31), channel_id=1, source_target_pairs={{0,480},{32,0},{64,32},{96,64},{128,96},{160,128},{192,160},{224,1... | collective-permute-start | bytes 688136 | tf_op jit(solution)/shard_map/ppermute | solution.py:14
  265.3 10.0 %collective-permute-start.3 = (bf16[32,3584]{1,0:T(8,128)(2,1)S(1)}, bf16[32,3584]{1,0:T(8,128)(2,1)S(1)}, u32[]{:S(2)}, u32[]{:S(2)}) collective-permute-start(bf16[32,3584]{1,0:T(8,128)(2,1)S(1)} %fusion.24), channel_id=1, source_target_pairs={{0,32},{32,64},{64,96},{96,128},{128,160},{160,192},{192,224},{224... | collective-permute-start | bytes 688136 | tf_op jit(solution)/shard_map/ppermute | solution.py:14
Sparse Core Ops, SparseCore 0:
  10.1 137.3 all-gather.1
  155.8 108.3 reduce-scatter.1

commit v4 on v1

v4 whole, which is shorter than its diff:
```python
import jax
import jax.numpy as jnp
import numpy as np
from jax import lax
from jax.sharding import PartitionSpec as P

EXPERTS = 4
CAP = 12
EPSILON = 1e-06


def passed_along(value, axis, steps):
    count = lax.axis_size(axis)
    pairs = [(source, (source + steps) % count) for source in range(count)]
    return lax.ppermute(value, axis, pairs)


def rms_scale(values):
    return lax.rsqrt(jnp.mean(values * values, axis=-1, keepdims=True) + EPSILON)


def dot(a, b, dims):
    return lax.dot_general(a, b, (dims, ((), ())), preferred_element_type=jnp.float32)


def slots_of(route):
    onehot = (route[:, None] == jnp.arange(EXPERTS, dtype=jnp.int32)[None, :]).astype(jnp.int32)
    rank = jnp.sum(jnp.cumsum(onehot, axis=0) * onehot, axis=1) - 1
    return route * CAP + rank


PREFIX = (3, 2, 2, 2, 2, 1, 1, 1, 1)
UNIT = 2 * CAP
SIDE = 4


def right_list(place):
    return [1, 0, -1] if place < SIDE // 2 else [2, 1, 0]


def left_list(place):
    return [3, 0, -1] if place >= SIDE // 2 else [2, 3, 0]


def list_tables():
    sent, valid = [], []
    for place in range(SIDE):
        sent.append(right_list(place) + left_list(place) + [0])
        flags = []
        for step, size in enumerate(PREFIX, 1):
            crossed = max(0, -((place - step) // SIDE))
            units = right_list((place - step) % SIDE)[:size]
            flags += [int(unit == crossed) for unit in units]
        for step, size in enumerate(PREFIX, 1):
            crossed = max(0, (place + step) // SIDE)
            units = left_list((place + step) % SIDE)[:size]
            flags += [int(unit == (EXPERTS - crossed) % EXPERTS) for unit in units]
        both, at = [], 0
        for size in PREFIX:
            both += flags[at : at + size] + flags[at + sum(PREFIX) : at + sum(PREFIX) + size]
            at += size
        valid.append(both + [1])
    return np.array(sent, np.int32), np.array(valid, np.float32)


def along_ring(count, steps):
    chips = count // 2
    return [(d, 2 * ((d // 2 + steps) % chips) + d % 2) for d in range(count)]


def walk_out(units, pairs):
    came = []
    for size in PREFIX:
        units = lax.ppermute(units[: size * UNIT], "expert", pairs)
        came.append(units)
    return came


def walk_back(parts, to_left, to_right):
    total = parts[-1]
    for step in range(len(PREFIX) - 1, -1, -1):
        rows = PREFIX[step] * UNIT
        back_r = lax.ppermute(total[:rows], "expert", to_left)
        back_l = lax.ppermute(total[rows:], "expert", to_right)
        if step > 0:
            extra = (PREFIX[step - 1] - PREFIX[step]) * UNIT
            pad = [jnp.pad(got, ((0, extra), (0, 0))) for got in (back_r, back_l)]
            total = parts[step - 1].astype(jnp.float32) + jnp.concatenate(pad).astype(jnp.float32)
            total = total.astype(jnp.bfloat16)
    return back_r, back_l


def per_device(
    x_fwd,
    x_bwd,
    grad_out,
    norm_gain,
    w_gate,
    w_up,
    w_down,
    route_fwd,
    gate_fwd,
    route_bwd,
    gate_bwd,
):
    count = lax.axis_size("expert")
    ring = count // 2
    same_core = [[2 * z + c for z in range(ring)] for c in range(2)]
    to_right, to_left = along_ring(count, 1), along_ring(count, -1)
    swap = [(i, i ^ 1) for i in range(count)]
    index = lax.axis_index("expert")
    me_expert = index // (2 * SIDE)
    me_place = (index // 2) % SIDE
    sent_table, valid_table = list_tables()
    groups_sent = jnp.asarray(sent_table)[me_place]
    valid = jnp.asarray(valid_table)[me_place]

    gain = norm_gain[0]
    tokens, width = x_fwd.shape[1:]
    half = width // 2
    sent = jnp.concatenate([x_bwd[0], grad_out[0]], axis=1)
    got_b = lax.all_gather(sent, "expert", axis=0, tiled=True, axis_index_groups=same_core)

    xf = x_fwd[0].astype(jnp.float32)
    xb = x_bwd[0].astype(jnp.float32)
    up32 = grad_out[0].astype(jnp.float32)
    scale_f = gate_fwd[0].astype(jnp.float32) / 256.0
    scale_b = gate_bwd[0].astype(jnp.float32) / 256.0

    normed_f = (xf * rms_scale(xf) * gain).astype(jnp.bfloat16)
    slot_f = slots_of(route_fwd[0, :, 0])
    unit_f = (slot_f // CAP - me_expert) % EXPERTS
    rank_f = slot_f % CAP
    row = jnp.arange(7 * UNIT, dtype=jnp.int32)
    row_unit = jnp.repeat(groups_sent, UNIT, total_repeat_length=7 * UNIT)
    row_slot = jnp.where(row_unit < 0, -1, row_unit * UNIT + row % UNIT)
    want = jnp.concatenate([unit_f * UNIT + rank_f, unit_f * UNIT + rank_f + CAP])
    put = (row_slot[:, None] == want[None, :]).astype(jnp.bfloat16)
    halves = jnp.concatenate([normed_f[:, :half], normed_f[:, half:]], axis=0)
    packed = dot(put, halves, ((1,), (0,))).astype(jnp.bfloat16)
    came_r = walk_out(packed[: 3 * UNIT], to_right)
    came_l = walk_out(packed[3 * UNIT : 6 * UNIT], to_left)
    came = [rows for pair in zip(came_r, came_l) for rows in pair]
    rows_f = jnp.concatenate(came + [packed[6 * UNIT :]], axis=0)

    r_b = rms_scale(xb)
    small = jnp.concatenate(
        [route_bwd[0, :, 0].astype(jnp.float32), r_b[:, 0], scale_b[:, 0]]
    )
    small, _ = lax.optimization_barrier((small, came_r[1]))
    small = lax.all_to_all(
        jnp.broadcast_to(small[None, None, :], (ring, 1, 3 * tokens)),
        "expert",
        split_axis=0,
        concat_axis=0,
        tiled=True,
        axis_index_groups=same_core,
    )[:, 0]
    routes_b, rs_b, scales_b = [
        small[:, i * tokens : (i + 1) * tokens].reshape(ring * tokens) for i in range(3)
    ]

    gate_o = lax.ppermute(w_gate[0], "expert", swap)
    up_o = lax.ppermute(w_up[0], "expert", swap)
    down_o = lax.ppermute(w_down[0], "expert", swap)
    w_in = jnp.concatenate([w_gate[0], gate_o, w_up[0], up_o], axis=1)
    w_gained = (w_in.astype(jnp.float32) * gain[:, None]).astype(jnp.bfloat16)
    w_dn = jnp.concatenate([w_down[0], down_o], axis=0)
    hid = w_dn.shape[0]
    dn_stack = jnp.concatenate([w_dn[:, :half], w_dn[:, half:]], axis=0)
    in_stack = jnp.concatenate([w_in[:half], w_in[half:]], axis=1)
    w_in, w_gained, w_dn, in_stack, dn_stack = lax.optimization_barrier(
        (w_in, w_gained, w_dn, in_stack, dn_stack)
    )

    units = valid.shape[0]
    pre_f = dot(rows_f, in_stack, ((1,), (0,))).reshape(units, UNIT, 4 * hid)
    pre_f = pre_f[:, :CAP, : 2 * hid] + pre_f[:, CAP:, 2 * hid :]
    act = jax.nn.silu(pre_f[..., :hid]) * pre_f[..., hid:]
    act = jnp.where(valid[:, None, None] > 0, act, 0.0).astype(jnp.bfloat16)
    lower = jnp.pad(act, ((0, 0), (0, CAP), (0, 0)))
    upper = jnp.pad(act, ((0, 0), (CAP, 0), (0, 0)))
    act = jnp.concatenate([lower, upper], axis=2).reshape(units * UNIT, 2 * hid)
    part_f = dot(act, dn_stack, ((1,), (0,))).astype(jnp.bfloat16)
    got_b, part_f = lax.optimization_barrier((got_b, part_f))

    pre_b = dot(got_b[:, :width], w_gained, ((1,), (0,))) * rs_b[:, None]
    d_act = dot(got_b[:, width:], w_dn, ((1,), (1,))) * scales_b[:, None]
    gate, up = pre_b[:, :hid], pre_b[:, hid:]
    sig = jax.nn.sigmoid(gate)
    mine = (routes_b == me_expert.astype(jnp.float32))[:, None]
    d_gate = jnp.where(mine, d_act * up * sig * (1.0 + gate * (1.0 - sig)), 0.0)
    d_up = jnp.where(mine, d_act * gate * sig, 0.0)
    hidden_b = jnp.concatenate([d_gate.astype(jnp.bfloat16), d_up.astype(jnp.bfloat16)], axis=1)
    part_b = dot(hidden_b, w_in, ((1,), (1,))).astype(jnp.bfloat16)
    d_normed = lax.psum_scatter(
        part_b, "expert", scatter_dimension=0, tiled=True, axis_index_groups=same_core
    ).astype(jnp.float32)

    seen = part_b[0, 0].astype(jnp.float32)
    never = (seen > 1.0) & (seen < -1.0)
    ends = np.cumsum([2 * size * UNIT for size in PREFIX]).tolist()
    starts = [0] + ends[:-1]
    pieces = [part_f[lo:hi] for lo, hi in zip(starts, ends)]
    pieces[-1] = jnp.where(never, 0, pieces[-1])
    back_r, back_l = walk_back(pieces, to_left, to_right)
    table = jnp.concatenate([back_r, back_l, part_f[ends[-1] :]], axis=0)
    moe_f = dot(put, table, ((0,), (0,)))
    moe_f = jnp.concatenate([moe_f[:tokens], moe_f[tokens:]], axis=1)
    y = (xf + scale_f * moe_f).astype(jnp.bfloat16)

    weighted = d_normed * gain
    inner = jnp.mean(xb * weighted, axis=-1, keepdims=True)
    dx = (up32 + (r_b * weighted - xb * r_b * r_b * r_b * inner)).astype(jnp.bfloat16)
    y_next = passed_along(y, "section", 1)
    dx_prev = passed_along(dx, "section", -1)
    return (y_next[None], dx_prev[None])


def solution(mesh):
    in_specs = (
        P("section", "expert", None),
        P("section", "expert", None),
        P("section", "expert", None),
        P("section", None),
        P("section", None, "expert"),
        P("section", None, "expert"),
        P("section", "expert", None),
        P("section", "expert", None),
        P("section", "expert", None),
        P("section", "expert", None),
        P("section", "expert", None),
    )
    out_specs = (P("section", "expert", None), P("section", "expert", None))
    return jax.shard_map(
        per_device, mesh=mesh, in_specs=in_specs, out_specs=out_specs, check_vma=False
    )
```

time: 310 us -> 312 us (level)
  waiting for transfers between devices: 200 us -> 82.9 us
  starting transfers between devices: 51.5 us -> 148 us
  other arithmetic: 13.6 us -> 27 us
  local copies, waits for them, and re-layouts: 12.9 us -> 18.1 us
    ppermute x0 -> x36, starting transfers between devices: none -> 125 us  [the longest x18 70.2 us: walk_out(): units = lax.ppermute(units[:size * UNIT], 'expert', pairs)]
    all_gather x1, waiting for transfers between devices: 98.6 us -> 0.02 us  [per_device(): lax.all_gather(sent, 'expert', axis=0, tiled=True, axis_index_groups=same...]
    all_to_all x5 -> x1, waiting for transfers between devices: 95.6 us -> 2.1 us  [per_device(): lax.all_to_all(jnp.broadcast_to(small[None, None, :], (ring, 1, 3 * token...]
    ppermute x0 -> x36, waiting for transfers between devices: none -> 77.2 us  [the longest x9 37.4 us: walk_back(): back_l = lax.ppermute(total[rows:], 'expert', to_right)]
    all_to_all x5 -> x1, starting transfers between devices: 34.8 us -> 8.58 us  [per_device(): lax.all_to_all(jnp.broadcast_to(small[None, None, :], (ring, 1, 3 * token...]
    unnamed x28 -> x50, local copies, waits for them, and re-layouts: 4.2 us -> 11.6 us
    select_n x1 -> x2, other arithmetic: 0.09 us -> 4.38 us  [the longest x1 4.37 us: per_device(): row_slot = jnp.where(row_unit < 0, -1, row_unit * UNIT + row % UNIT)]
    convert_element_type x2 -> x11, other arithmetic: 1.21 us -> 4.68 us  [the longest x1 3.94 us: per_device(): w_gained = (w_in.astype(jnp.float32) * gain[:, None]).astype(jnp.bfloat16)]
  transfers between devices with their start and end apart: 11 -> 44, of which waited for: 7 -> 29; matrix products, arithmetic and copies ran while one was open for 8% -> 14% of each run, Pallas kernels for 0% -> 0%
where the time goes in v4:
time: 312 us; the launch traced here: 308 us
  starting transfers between devices  148 us (47%)
  waiting for transfers between devices  82.9 us (27%)
  other arithmetic  27 us (9%)
  local copies, waits for them, and re-layouts  18.1 us (6%)
  between operations  16.4 us (5%)
  matrix products  15.9 us (5%)
    ppermute x18, starting transfers between devices, walk_out(): units = lax.ppermute(units[:size * UNIT], 'expert', pairs)  70.2 us
    ppermute x9, waiting for transfers between devices, walk_back(): back_l = lax.ppermute(total[rows:], 'expert', to_right)  37.4 us
    ppermute x9, starting transfers between devices, walk_back(): back_r = lax.ppermute(total[:rows], 'expert', to_left)  27.4 us
    ppermute x9, starting transfers between devices, walk_back(): back_l = lax.ppermute(total[rows:], 'expert', to_right)  27.2 us
    ppermute x9, waiting for transfers between devices, walk_back(): back_r = lax.ppermute(total[:rows], 'expert', to_left)  21.6 us
    ppermute x18, waiting for transfers between devices, walk_out(): units = lax.ppermute(units[:size * UNIT], 'expert', pairs)  18.2 us
    dot_general x7, matrix products, dot(): lax.dot_general(a, b, (dims, ((), ())), preferred_element_type=jnp.float32)  15.9 us
    unnamed x50, local copies, waits for them, and re-layouts  11.6 us
  transfers between devices with their start and end apart: 44, of which 29 were waited for; matrix products, arithmetic and copies ran while one was open for 14% of the time, Pallas kernels for 0%

profile of v4, /device:TPU:6, one launch (start us, length us, event | category | flops | bytes accessed | tf_op | source)
XLA Modules:
  0.0 308.0 jit_solution(14851884940462560309)
XLA Ops:
  7.3 2.0 pad_maximum_fusion.4
  15.7 4.4 %compare_select_fusion.9 = s32[168]{0:T(256)S(1)} fusion(s32[256]{0:T(256)S(1)} %add_bitcast_fusion, s32[]{:T(128)} %bitcast.3, s32[]{:T(128)} %bitcast.4, s32[]{:T(128)} %bitcast.5, s32[]{:T(128)} %bitcast.6, s32[]{:T(128)} %bitcast.7, s32[]{:T(128)} %bitcast.8, s32[]{:T(128)} %bitcast.9), kind=kLoop, calls=%fused_computation.131 | loop fusion | flops 5040 | bytes 1372 | tf_op jit(solution)/shard_map/jit(_where)/select_n | solution.py:136
  22.5 3.8 %collective-permute-start = (bf16[72,1792]{1,0:T(8,128)(2,1)}, bf16[72,1792]{1,0:T(8,128)(2,1)S(1)}, u32[]{:S(2)}, u32[]{:S(2)}) collective-permute-start(bf16[72,1792]{1,0:T(8,128)(2,1)} %get-tuple-element.39), channel_id=1, source_target_pairs={{0,2},{1,3},{2,4},{3,5},{4,6},{5,7},{6,8},{7,9},{8,10},{9,11},{10,... | collective-permute-start | bytes 774152 | tf_op jit(solution)/shard_map/ppermute | solution.py:74
  26.3 9.5 %collective-permute-start.1 = (bf16[72,1792]{1,0:T(8,128)(2,1)}, bf16[72,1792]{1,0:T(8,128)(2,1)S(1)}, u32[]{:S(2)}, u32[]{:S(2)}) collective-permute-start(bf16[72,1792]{1,0:T(8,128)(2,1)} %get-tuple-element.38), channel_id=1, source_target_pairs={{0,30},{1,31},{2,0},{3,1},{4,2},{5,3},{6,4},{7,5},{8,6},{9,7},{10,... | collective-permute-start | bytes 774152 | tf_op jit(solution)/shard_map/ppermute | solution.py:74
  35.8 1.9 collective-permute-start.18
  37.8 2.4 collective-permute-start.19
  40.2 1.9 collective-permute-start.20
  43.1 2.7 collective-permute-done
  45.9 1.9 collective-permute-start.2
  48.5 5.1 %collective-permute-start.3 = (bf16[48,1792]{1,0:T(8,128)(2,1)}, bf16[48,1792]{1,0:T(8,128)(2,1)}, u32[]{:S(2)}, u32[]{:S(2)}) collective-permute-start(bf16[48,1792]{1,0:T(8,128)(2,1)} %slice.263), channel_id=1, source_target_pairs={{0,30},{1,31},{2,0},{3,1},{4,2},{5,3},{6,4},{7,5},{8,6},{9,7},{10,... | collective-permute-start | bytes 516104 | tf_op jit(solution)/shard_map/ppermute | solution.py:74
  55.0 4.2 %collective-permute-done.2 = bf16[48,1792]{1,0:T(8,128)(2,1)} collective-permute-done((bf16[48,1792]{1,0:T(8,128)(2,1)S(1)}, bf16[48,1792]{1,0:T(8,128)(2,1)}, u32[]{:S(2)}, u32[]{:S(2)}) %collective-permute-start.2) | collective-permute-done | bytes 172064 | tf_op jit(solution)/shard_map/ppermute | solution.py:74
  59.9 8.6 %all-to-all-start = ((f32[16,1,96]{2,1,0:T(1,128)}), f32[16,1,96]{2,1,0:T(1,128)S(1)}, u32[]{:S(2)}, u32[]{:S(2)}) async-start(f32[16,1,96]{2,1,0:T(1,128)} %broadcast_in_dim.66), calls=%async_computation | async-start | bytes 16384 | tf_op jit(solution)/shard_map/all_to_all | solution.py:151
  68.5 3.8 %collective-permute-start.4 = (bf16[48,1792]{1,0:T(8,128)(2,1)}, bf16[48,1792]{1,0:T(8,128)(2,1)S(1)}, u32[]{:S(2)}, u32[]{:S(2)}) collective-permute-start(bf16[48,1792]{1,0:T(8,128)(2,1)} %collective-permute-done.2), channel_id=1, source_target_pairs={{0,2},{1,3},{2,4},{3,5},{4,6},{5,7},{6,8},{7,9},{8,10},{9,11},{10,... | collective-permute-start | bytes 516104 | tf_op jit(solution)/shard_map/ppermute | solution.py:74
  72.3 3.2 %collective-permute-start.5 = (bf16[48,1792]{1,0:T(8,128)(2,1)}, bf16[48,1792]{1,0:T(8,128)(2,1)S(1)}, u32[]{:S(2)}, u32[]{:S(2)}) collective-permute-start(bf16[48,1792]{1,0:T(8,128)(2,1)} %collective-permute-done.3), channel_id=1, source_target_pairs={{0,30},{1,31},{2,0},{3,1},{4,2},{5,3},{6,4},{7,5},{8,6},{9,7},{10,... | collective-permute-start | bytes 516104 | tf_op jit(solution)/shard_map/ppermute | solution.py:74
  78.8 2.1 all-to-all-done
  81.7 2.4 collective-permute-start.6
  84.0 4.7 %collective-permute-start.7 = (bf16[48,1792]{1,0:T(8,128)(2,1)S(1)}, bf16[48,1792]{1,0:T(8,128)(2,1)S(1)}, u32[]{:S(2)}, u32[]{:S(2)}) collective-permute-start(bf16[48,1792]{1,0:T(8,128)(2,1)S(1)} %collective-permute-done.5), channel_id=1, source_target_pairs={{0,30},{1,31},{2,0},{3,1},{4,2},{5,3},{6,4},{7,5},{8,6},{9,7},{10,... | collective-permute-start | bytes 516104 | tf_op jit(solution)/shard_map/ppermute | solution.py:74
  90.1 4.2 %collective-permute-done.6 = bf16[48,1792]{1,0:T(8,128)(2,1)S(1)} collective-permute-done((bf16[48,1792]{1,0:T(8,128)(2,1)S(1)}, bf16[48,1792]{1,0:T(8,128)(2,1)S(1)}, u32[]{:S(2)}, u32[]{:S(2)}) %collective-permute-start.6) | collective-permute-done | bytes 172064 | tf_op jit(solution)/shard_map/ppermute | solution.py:74
  96.2 5.1 %collective-permute-start.9 = (bf16[48,1792]{1,0:T(8,128)(2,1)S(1)}, bf16[48,1792]{1,0:T(8,128)(2,1)S(1)}, u32[]{:S(2)}, u32[]{:S(2)}) collective-permute-start(bf16[48,1792]{1,0:T(8,128)(2,1)S(1)} %collective-permute-done.7), channel_id=1, source_target_pairs={{0,30},{1,31},{2,0},{3,1},{4,2},{5,3},{6,4},{7,5},{8,6},{9,7},{10,... | collective-permute-start | bytes 516104 | tf_op jit(solution)/shard_map/ppermute | solution.py:74
  108.1 2.5 pad_maximum_fusion.2
  110.7 3.9 %multiply_convert_fusion = bf16[3584,512]{1,0:T(8,128)(2,1)} fusion(f32[3584]{0:T(1024)S(1)} %reduce.2, bf16[3584,128]{1,0:T(8,128)(2,1)} %collective-permute-done.19, bf16[3584,128]{1,0:T(8,128)(2,1)S(1)} %bitcast.52, bf16[3584,128]{1,0:T(8,128)(2,1)} %collective-permute-done.18, bf16[3584,128]{1,0:T(8,128)(2,1)S(1)} %bitcast.55), kind=kLoop, calls=%fused_computation | loop fusion | flops 18350080 | bytes 7354368 | tf_op jit(solution)/shard_map/convert_element_type | solution.py:167
  114.8 2.1 collective-permute-start.10
  116.8 5.1 %collective-permute-start.11 = (bf16[24,1792]{1,0:T(8,128)(2,1)S(1)}, bf16[24,1792]{1,0:T(8,128)(2,1)S(1)}, u32[]{:S(2)}, u32[]{:S(2)}) collective-permute-start(bf16[24,1792]{1,0:T(8,128)(2,1)S(1)} %slice.265), channel_id=1, source_target_pairs={{0,30},{1,31},{2,0},{3,1},{4,2},{5,3},{6,4},{7,5},{8,6},{9,7},{10,... | collective-permute-start | bytes 258056 | tf_op jit(solution)/shard_map/ppermute | solution.py:74
  122.0 2.3 collective-permute-done.10
  126.2 5.1 %collective-permute-start.13 = (bf16[24,1792]{1,0:T(8,128)(2,1)S(1)}, bf16[24,1792]{1,0:T(8,128)(2,1)S(1)}, u32[]{:S(2)}, u32[]{:S(2)}) collective-permute-start(bf16[24,1792]{1,0:T(8,128)(2,1)S(1)} %collective-permute-done.11), channel_id=1, source_target_pairs={{0,30},{1,31},{2,0},{3,1},{4,2},{5,3},{6,4},{7,5},{8,6},{9,7},{10,... | collective-permute-start | bytes 258056 | tf_op jit(solution)/shard_map/ppermute | solution.py:74
  134.8 5.1 %collective-permute-start.15 = (bf16[24,1792]{1,0:T(8,128)(2,1)S(1)}, bf16[24,1792]{1,0:T(8,128)(2,1)S(1)}, u32[]{:S(2)}, u32[]{:S(2)}) collective-permute-start(bf16[24,1792]{1,0:T(8,128)(2,1)S(1)} %collective-permute-done.13), channel_id=1, source_target_pairs={{0,30},{1,31},{2,0},{3,1},{4,2},{5,3},{6,4},{7,5},{8,6},{9,7},{10,... | collective-permute-start | bytes 258056 | tf_op jit(solution)/shard_map/ppermute | solution.py:74
  143.0 5.5 %collective-permute-start.17 = (bf16[24,1792]{1,0:T(8,128)(2,1)S(1)}, bf16[24,1792]{1,0:T(8,128)(2,1)S(1)}, u32[]{:S(2)}, u32[]{:S(2)}) collective-permute-start(bf16[24,1792]{1,0:T(8,128)(2,1)S(1)} %collective-permute-done.15), channel_id=1, source_target_pairs={{0,30},{1,31},{2,0},{3,1},{4,2},{5,3},{6,4},{7,5},{8,6},{9,7},{10,... | collective-permute-start | bytes 258056 | tf_op jit(solution)/shard_map/ppermute | solution.py:74
  151.3 3.0 fusion.81
  156.4 5.4 %fusion.6 = f32[512,512]{0,1:T(8,128)S(1)} fusion(bf16[3584,512]{1,0:T(8,128)(2,1)} %multiply_convert_fusion, bf16[512,7168]{1,0:T(8,128)(2,1)} %all-gather.2.cloned.1.call-done, f32[512]{0:T(512)S(1)} %mul.166), kind=kOutput, calls=%fused_computation.20 | convolution fusion | flops 1879310336 | bytes 8390656 | tf_op jit(solution)/shard_map/dot_general | solution.py:23
  164.2 3.9 %convolution_convert_fusion = bf16[512,3584]{1,0:T(8,128)(2,1)} fusion(bf16[3584,512]{1,0:T(8,128)(2,1)S(1)} %copy-done.1, bf16[512,256]{0,1:T(8,128)(2,1)S(1)} %get-tuple-element.37, bf16[512,256]{0,1:T(8,128)(2,1)S(1)} %get-tuple-element.36), kind=kOutput, calls=%fused_computation.1 | convolution fusion | flops 1881931776 | bytes 7864320 | tf_op jit(solution)/shard_map/dot_general | solution.py:23
  170.7 5.5 %collective-permute-start.21 = (bf16[24,1792]{1,0:T(8,128)(2,1)S(1)}, bf16[24,1792]{1,0:T(8,128)(2,1)S(1)}, u32[]{:S(2)}, u32[]{:S(2)}) collective-permute-start(bf16[24,1792]{1,0:T(8,128)(2,1)S(1)} %get-tuple-element.60), channel_id=1, source_target_pairs={{0,30},{1,31},{2,0},{3,1},{4,2},{5,3},{6,4},{7,5},{8,6},{9,7},{10,... | collective-permute-start | bytes 258056 | tf_op jit(solution)/shard_map/ppermute | solution.py:83
  176.2 1.9 collective-permute-start.22
  179.1 5.3 %collective-permute-done.22 = bf16[24,1792]{1,0:T(8,128)(2,1)S(1)} collective-permute-done((bf16[24,1792]{1,0:T(8,128)(2,1)S(1)}, bf16[24,1792]{1,0:T(8,128)(2,1)S(1)}, u32[]{:S(2)}, u32[]{:S(2)}) %collective-permute-start.22) | collective-permute-done | bytes 86048 | tf_op jit(solution)/shard_map/ppermute | solution.py:84
  184.5 1.9 collective-permute-start.23
  186.4 3.9 %collective-permute-start.24 = (bf16[24,1792]{1,0:T(8,128)(2,1)S(1)}, bf16[24,1792]{1,0:T(8,128)(2,1)S(1)}, u32[]{:S(2)}, u32[]{:S(2)}) collective-permute-start(bf16[24,1792]{1,0:T(8,128)(2,1)S(1)} %get-tuple-element.59), channel_id=1, source_target_pairs={{0,2},{1,3},{2,4},{3,5},{4,6},{5,7},{6,8},{7,9},{8,10},{9,11},{10,... | collective-permute-start | bytes 258056 | tf_op jit(solution)/shard_map/ppermute | solution.py:84
  190.9 3.1 %collective-permute-done.24 = bf16[24,1792]{1,0:T(8,128)(2,1)S(1)} collective-permute-done((bf16[24,1792]{1,0:T(8,128)(2,1)S(1)}, bf16[24,1792]{1,0:T(8,128)(2,1)S(1)}, u32[]{:S(2)}, u32[]{:S(2)}) %collective-permute-start.24) | collective-permute-done | bytes 86048 | tf_op jit(solution)/shard_map/ppermute | solution.py:84
  194.1 1.9 collective-permute-start.25
  196.0 3.9 %collective-permute-start.26 = (bf16[24,1792]{1,0:T(8,128)(2,1)S(1)}, bf16[24,1792]{1,0:T(8,128)(2,1)S(1)}, u32[]{:S(2)}, u32[]{:S(2)}) collective-permute-start(bf16[24,1792]{1,0:T(8,128)(2,1)S(1)} %get-tuple-element.57), channel_id=1, source_target_pairs={{0,2},{1,3},{2,4},{3,5},{4,6},{5,7},{6,8},{7,9},{8,10},{9,11},{10,... | collective-permute-start | bytes 258056 | tf_op jit(solution)/shard_map/ppermute | solution.py:84
  200.5 3.1 %collective-permute-done.26 = bf16[24,1792]{1,0:T(8,128)(2,1)S(1)} collective-permute-done((bf16[24,1792]{1,0:T(8,128)(2,1)S(1)}, bf16[24,1792]{1,0:T(8,128)(2,1)S(1)}, u32[]{:S(2)}, u32[]{:S(2)}) %collective-permute-start.26) | collective-permute-done | bytes 86048 | tf_op jit(solution)/shard_map/ppermute | solution.py:84
  203.7 3.2 %collective-permute-start.27 = (bf16[24,1792]{1,0:T(8,128)(2,1)S(1)}, bf16[24,1792]{1,0:T(8,128)(2,1)S(1)}, u32[]{:S(2)}, u32[]{:S(2)}) collective-permute-start(bf16[24,1792]{1,0:T(8,128)(2,1)S(1)} %get-tuple-element.54), channel_id=1, source_target_pairs={{0,30},{1,31},{2,0},{3,1},{4,2},{5,3},{6,4},{7,5},{8,6},{9,7},{10,... | collective-permute-start | bytes 258056 | tf_op jit(solution)/shard_map/ppermute | solution.py:83
  206.9 2.6 collective-permute-start.28
  210.1 4.5 %collective-permute-done.28 = bf16[24,1792]{1,0:T(8,128)(2,1)S(1)} collective-permute-done((bf16[24,1792]{1,0:T(8,128)(2,1)S(1)}, bf16[24,1792]{1,0:T(8,128)(2,1)S(1)}, u32[]{:S(2)}, u32[]{:S(2)}) %collective-permute-start.28) | collective-permute-done | bytes 86048 | tf_op jit(solution)/shard_map/ppermute | solution.py:84
  214.6 2.6 collective-permute-start.29
  217.2 3.2 %collective-permute-start.30 = (bf16[48,1792]{1,0:T(8,128)(2,1)S(1)}, bf16[48,1792]{1,0:T(8,128)(2,1)S(1)}, u32[]{:S(2)}, u32[]{:S(2)}) collective-permute-start(bf16[48,1792]{1,0:T(8,128)(2,1)S(1)} %get-tuple-element.51), channel_id=1, source_target_pairs={{0,2},{1,3},{2,4},{3,5},{4,6},{5,7},{6,8},{7,9},{8,10},{9,11},{10,... | collective-permute-start | bytes 516104 | tf_op jit(solution)/shard_map/ppermute | solution.py:84
  220.4 3.7 %collective-permute-done.29 = bf16[48,1792]{1,0:T(8,128)(2,1)S(1)} collective-permute-done((bf16[48,1792]{1,0:T(8,128)(2,1)S(1)}, bf16[48,1792]{1,0:T(8,128)(2,1)S(1)}, u32[]{:S(2)}, u32[]{:S(2)}) %collective-permute-start.29) | collective-permute-done | bytes 172064 | tf_op jit(solution)/shard_map/ppermute | solution.py:83
  224.1 4.9 %collective-permute-done.30 = bf16[48,1792]{1,0:T(8,128)(2,1)S(1)} collective-permute-done((bf16[48,1792]{1,0:T(8,128)(2,1)S(1)}, bf16[48,1792]{1,0:T(8,128)(2,1)S(1)}, u32[]{:S(2)}, u32[]{:S(2)}) %collective-permute-start.30) | collective-permute-done | bytes 172064 | tf_op jit(solution)/shard_map/ppermute | solution.py:84
  229.2 2.7 collective-permute-start.31
  231.9 3.1 %collective-permute-start.32 = (bf16[48,1792]{1,0:T(8,128)(2,1)S(1)}, bf16[48,1792]{1,0:T(8,128)(2,1)S(1)}, u32[]{:S(2)}, u32[]{:S(2)}) collective-permute-start(bf16[48,1792]{1,0:T(8,128)(2,1)S(1)} %get-tuple-element.49), channel_id=1, source_target_pairs={{0,2},{1,3},{2,4},{3,5},{4,6},{5,7},{6,8},{7,9},{8,10},{9,11},{10,... | collective-permute-start | bytes 516104 | tf_op jit(solution)/shard_map/ppermute | solution.py:84
  235.0 4.6 %collective-permute-done.31 = bf16[48,1792]{1,0:T(8,128)(2,1)S(1)} collective-permute-done((bf16[48,1792]{1,0:T(8,128)(2,1)S(1)}, bf16[48,1792]{1,0:T(8,128)(2,1)S(1)}, u32[]{:S(2)}, u32[]{:S(2)}) %collective-permute-start.31) | collective-permute-done | bytes 172064 | tf_op jit(solution)/shard_map/ppermute | solution.py:83
  239.6 3.7 %collective-permute-done.32 = bf16[48,1792]{1,0:T(8,128)(2,1)S(1)} collective-permute-done((bf16[48,1792]{1,0:T(8,128)(2,1)S(1)}, bf16[48,1792]{1,0:T(8,128)(2,1)S(1)}, u32[]{:S(2)}, u32[]{:S(2)}) %collective-permute-start.32) | collective-permute-done | bytes 172064 | tf_op jit(solution)/shard_map/ppermute | solution.py:84
  243.5 4.2 %collective-permute-start.33 = (bf16[48,1792]{1,0:T(8,128)(2,1)S(1)}, bf16[48,1792]{1,0:T(8,128)(2,1)S(1)}, u32[]{:S(2)}, u32[]{:S(2)}) collective-permute-start(bf16[48,1792]{1,0:T(8,128)(2,1)S(1)} %get-tuple-element.46), channel_id=1, source_target_pairs={{0,30},{1,31},{2,0},{3,1},{4,2},{5,3},{6,4},{7,5},{8,6},{9,7},{10,... | collective-permute-start | bytes 516104 | tf_op jit(solution)/shard_map/ppermute | solution.py:83
  249.6 4.1 %collective-permute-done.33 = bf16[48,1792]{1,0:T(8,128)(2,1)S(1)} collective-permute-done((bf16[48,1792]{1,0:T(8,128)(2,1)S(1)}, bf16[48,1792]{1,0:T(8,128)(2,1)S(1)}, u32[]{:S(2)}, u32[]{:S(2)}) %collective-permute-start.33) | collective-permute-done | bytes 172064 | tf_op jit(solution)/shard_map/ppermute | solution.py:83
  253.7 5.2 %collective-permute-done.34 = bf16[48,1792]{1,0:T(8,128)(2,1)S(1)} collective-permute-done((bf16[48,1792]{1,0:T(8,128)(2,1)S(1)}, bf16[48,1792]{1,0:T(8,128)(2,1)S(1)}, u32[]{:S(2)}, u32[]{:S(2)}) %collective-permute-start.34) | collective-permute-done | bytes 172064 | tf_op jit(solution)/shard_map/ppermute | solution.py:84
  259.0 3.3 %collective-permute-start.35 = (bf16[48,1792]{1,0:T(8,128)(2,1)S(1)}, bf16[48,1792]{1,0:T(8,128)(2,1)S(1)}, u32[]{:S(2)}, u32[]{:S(2)}) collective-permute-start(bf16[48,1792]{1,0:T(8,128)(2,1)S(1)} %get-tuple-element.44), channel_id=1, source_target_pairs={{0,30},{1,31},{2,0},{3,1},{4,2},{5,3},{6,4},{7,5},{8,6},{9,7},{10,... | collective-permute-start | bytes 516104 | tf_op jit(solution)/shard_map/ppermute | solution.py:83
  262.3 2.7 collective-permute-start.36
  265.0 4.0 %collective-permute-done.35 = bf16[48,1792]{1,0:T(8,128)(2,1)S(1)} collective-permute-done((bf16[48,1792]{1,0:T(8,128)(2,1)S(1)}, bf16[48,1792]{1,0:T(8,128)(2,1)S(1)}, u32[]{:S(2)}, u32[]{:S(2)}) %collective-permute-start.35) | collective-permute-done | bytes 172064 | tf_op jit(solution)/shard_map/ppermute | solution.py:83
  269.0 4.8 %collective-permute-done.36 = bf16[48,1792]{1,0:T(8,128)(2,1)S(1)} collective-permute-done((bf16[48,1792]{1,0:T(8,128)(2,1)S(1)}, bf16[48,1792]{1,0:T(8,128)(2,1)S(1)}, u32[]{:S(2)}, u32[]{:S(2)}) %collective-permute-start.36) | collective-permute-done | bytes 172064 | tf_op jit(solution)/shard_map/ppermute | solution.py:84
  273.9 2.1 collective-permute-start.37
  276.0 3.9 %collective-permute-start.38 = (bf16[72,1792]{1,0:T(8,128)(2,1)S(1)}, bf16[72,1792]{1,0:T(8,128)(2,1)S(1)}, u32[]{:S(2)}, u32[]{:S(2)}) collective-permute-start(bf16[72,1792]{1,0:T(8,128)(2,1)S(1)} %get-tuple-element.41), channel_id=1, source_target_pairs={{0,2},{1,3},{2,4},{3,5},{4,6},{5,7},{6,8},{7,9},{8,10},{9,11},{10,... | collective-permute-start | bytes 774152 | tf_op jit(solution)/shard_map/ppermute | solution.py:84
  280.0 2.7 collective-permute-done.37
  282.7 2.8 collective-permute-done.38
  286.0 3.6 %collective-permute-start.39 = (bf16[32,3584]{1,0:T(8,128)(2,1)S(1)}, bf16[32,3584]{1,0:T(8,128)(2,1)S(1)}, u32[]{:S(2)}, u32[]{:S(2)}) collective-permute-start(bf16[32,3584]{1,0:T(8,128)(2,1)S(1)} %fusion.46), channel_id=1, source_target_pairs={{0,32},{32,64},{64,96},{96,128},{128,160},{160,192},{192,224},{224... | collective-permute-start | bytes 688136 | tf_op jit(solution)/shard_map/ppermute | solution.py:15
  291.9 4.4 %collective-permute-start.40 = (bf16[32,3584]{1,0:T(8,128)(2,1)S(1)}, bf16[32,3584]{1,0:T(8,128)(2,1)S(1)}, u32[]{:S(2)}, u32[]{:S(2)}) collective-permute-start(bf16[32,3584]{1,0:T(8,128)(2,1)S(1)} %fusion.41), channel_id=1, source_target_pairs={{0,480},{32,0},{64,32},{96,64},{128,96},{160,128},{192,160},{224,1... | collective-permute-start | bytes 688136 | tf_op jit(solution)/shard_map/ppermute | solution.py:15
  296.3 3.5 %collective-permute-done.40 = bf16[32,3584]{1,0:T(8,128)(2,1)S(1)} collective-permute-done((bf16[32,3584]{1,0:T(8,128)(2,1)S(1)}, bf16[32,3584]{1,0:T(8,128)(2,1)S(1)}, u32[]{:S(2)}, u32[]{:S(2)}) %collective-permute-start.40) | collective-permute-done | bytes 229408 | tf_op jit(solution)/shard_map/ppermute | solution.py:15
  (153 shorter events, 53.0 us)
Async XLA Ops:
  7.2 35.0 %copy-start.5 = (bf16[1,32,3584]{2,1,0:T(8,128)(2,1)S(1)}, bf16[1,32,3584]{2,1,0:T(8,128)(2,1)}, u32[]{:S(2)}) copy-start(bf16[1,32,3584]{2,1,0:T(8,128)(2,1)} %param.16) | copy-start | bytes 688132
  7.2 28.7 %copy-start.4 = (bf16[1,3584,128]{2,1,0:T(8,128)(2,1)S(1)}, bf16[1,3584,128]{2,1,0:T(8,128)(2,1)}, u32[]{:S(2)}) copy-start(bf16[1,3584,128]{2,1,0:T(8,128)(2,1)} %param.19) | copy-start | bytes 2752516
  7.2 30.6 %copy-start.3 = (bf16[1,3584,128]{2,1,0:T(8,128)(2,1)S(1)}, bf16[1,3584,128]{2,1,0:T(8,128)(2,1)}, u32[]{:S(2)}) copy-start(bf16[1,3584,128]{2,1,0:T(8,128)(2,1)} %param.20) | copy-start | bytes 2752516
  7.2 33.0 %copy-start.2 = (bf16[1,128,3584]{2,1,0:T(8,128)(2,1)S(1)}, bf16[1,128,3584]{2,1,0:T(8,128)(2,1)}, u32[]{:S(2)}) copy-start(bf16[1,128,3584]{2,1,0:T(8,128)(2,1)} %param.21) | copy-start | bytes 2752516
  7.2 35.1 %copy-start.12 = (s32[1,32,1]{1,2,0:T(1,128)S(1)}, s32[1,32,1]{1,2,0:T(1,128)}, u32[]{:S(2)}) copy-start(s32[1,32,1]{1,2,0:T(1,128)} %param.24) | copy-start | bytes 388
  7.2 35.1 %copy-start.13 = (s32[1,32,1]{1,2,0:T(1,128)S(1)}, s32[1,32,1]{1,2,0:T(1,128)}, u32[]{:S(2)}) copy-start(s32[1,32,1]{1,2,0:T(1,128)} %param.25) | copy-start | bytes 388
  7.2 149.1 %all-gather.2.cloned.1.call-start = ((), (), s32[]{:S(2)}) async-start(), calls=%async_computation.2 | async-start | bytes 7798784 | tf_op jit(solution)/shard_map/all_gather | solution.py:122
  21.5 18.7 %copy-start.6 = (bf16[168,1792]{1,0:T(8,128)(2,1)}, bf16[168,1792]{1,0:T(8,128)(2,1)S(1)}, u32[]{:S(2)}) copy-start(bf16[168,1792]{1,0:T(8,128)(2,1)S(1)} %convolution_convert_fusion.2) | copy-start | bytes 1806340
  22.5 23.3 %collective-permute-start = (bf16[72,1792]{1,0:T(8,128)(2,1)}, bf16[72,1792]{1,0:T(8,128)(2,1)S(1)}, u32[]{:S(2)}, u32[]{:S(2)}) collective-permute-start(bf16[72,1792]{1,0:T(8,128)(2,1)} %get-tuple-element.39), channel_id=1, source_target_pairs={{0,2},{1,3},{2,4},{3,5},{4,6},{5,7},{6,8},{7,9},{8,10},{9,11},{10,... | collective-permute-start | bytes 774152 | tf_op jit(solution)/shard_map/ppermute | solution.py:74
  26.3 21.5 %collective-permute-start.1 = (bf16[72,1792]{1,0:T(8,128)(2,1)}, bf16[72,1792]{1,0:T(8,128)(2,1)S(1)}, u32[]{:S(2)}, u32[]{:S(2)}) collective-permute-start(bf16[72,1792]{1,0:T(8,128)(2,1)} %get-tuple-element.38), channel_id=1, source_target_pairs={{0,30},{1,31},{2,0},{3,1},{4,2},{5,3},{6,4},{7,5},{8,6},{9,7},{10,... | collective-permute-start | bytes 774152 | tf_op jit(solution)/shard_map/ppermute | solution.py:74
  35.8 68.1 %collective-permute-start.18 = (bf16[3584,128]{1,0:T(8,128)(2,1)S(1)}, bf16[3584,128]{1,0:T(8,128)(2,1)}, u32[]{:S(2)}, u32[]{:S(2)}) collective-permute-start(bf16[3584,128]{1,0:T(8,128)(2,1)S(1)} %bitcast.53), channel_id=1, source_target_pairs={{0,1},{1,0},{2,3},{3,2},{4,5},{5,4},{6,7},{7,6},{8,9},{9,8},{10,11... | collective-permute-start | bytes 2752520 | tf_op jit(solution)/shard_map/ppermute | solution.py:163
  37.8 66.2 %collective-permute-start.19 = (bf16[3584,128]{1,0:T(8,128)(2,1)S(1)}, bf16[3584,128]{1,0:T(8,128)(2,1)}, u32[]{:S(2)}, u32[]{:S(2)}) collective-permute-start(bf16[3584,128]{1,0:T(8,128)(2,1)S(1)} %bitcast.50), channel_id=1, source_target_pairs={{0,1},{1,0},{2,3},{3,2},{4,5},{5,4},{6,7},{7,6},{8,9},{9,8},{10,11... | collective-permute-start | bytes 2752520 | tf_op jit(solution)/shard_map/ppermute | solution.py:164
  40.2 62.5 %collective-permute-start.20 = (bf16[128,3584]{1,0:T(8,128)(2,1)S(1)}, bf16[128,3584]{1,0:T(8,128)(2,1)}, u32[]{:S(2)}, u32[]{:S(2)}) collective-permute-start(bf16[128,3584]{1,0:T(8,128)(2,1)S(1)} %bitcast.47), channel_id=1, source_target_pairs={{0,1},{1,0},{2,3},{3,2},{4,5},{5,4},{6,7},{7,6},{8,9},{9,8},{10,11... | collective-permute-start | bytes 2752520 | tf_op jit(solution)/shard_map/ppermute | solution.py:165
  45.9 13.4 %collective-permute-start.2 = (bf16[48,1792]{1,0:T(8,128)(2,1)S(1)}, bf16[48,1792]{1,0:T(8,128)(2,1)}, u32[]{:S(2)}, u32[]{:S(2)}) collective-permute-start(bf16[48,1792]{1,0:T(8,128)(2,1)S(1)} %slice.262), channel_id=1, source_target_pairs={{0,2},{1,3},{2,4},{3,5},{4,6},{5,7},{6,8},{7,9},{8,10},{9,11},{10,... | collective-permute-start | bytes 516104 | tf_op jit(solution)/shard_map/ppermute | solution.py:74
  48.5 23.9 %collective-permute-start.3 = (bf16[48,1792]{1,0:T(8,128)(2,1)}, bf16[48,1792]{1,0:T(8,128)(2,1)}, u32[]{:S(2)}, u32[]{:S(2)}) collective-permute-start(bf16[48,1792]{1,0:T(8,128)(2,1)} %slice.263), channel_id=1, source_target_pairs={{0,30},{1,31},{2,0},{3,1},{4,2},{5,3},{6,4},{7,5},{8,6},{9,7},{10,... | collective-permute-start | bytes 516104 | tf_op jit(solution)/shard_map/ppermute | solution.py:74
  59.9 21.0 %all-to-all-start = ((f32[16,1,96]{2,1,0:T(1,128)}), f32[16,1,96]{2,1,0:T(1,128)S(1)}, u32[]{:S(2)}, u32[]{:S(2)}) async-start(f32[16,1,96]{2,1,0:T(1,128)} %broadcast_in_dim.66), calls=%async_computation | async-start | bytes 16384 | tf_op jit(solution)/shard_map/all_to_all | solution.py:151
  68.4 221.1 %reduce-scatter.2.cloned.1.call-start = ((), (), s32[]{:S(2)}) async-start(), calls=%async_computation.3 | async-start | bytes 3899392 | tf_op jit(solution)/shard_map/reduce_scatter | solution.py:196
  68.5 13.2 %collective-permute-start.4 = (bf16[48,1792]{1,0:T(8,128)(2,1)}, bf16[48,1792]{1,0:T(8,128)(2,1)S(1)}, u32[]{:S(2)}, u32[]{:S(2)}) collective-permute-start(bf16[48,1792]{1,0:T(8,128)(2,1)} %collective-permute-done.2), channel_id=1, source_target_pairs={{0,2},{1,3},{2,4},{3,5},{4,6},{5,7},{6,8},{7,9},{8,10},{9,11},{10,... | collective-permute-start | bytes 516104 | tf_op jit(solution)/shard_map/ppermute | solution.py:74
  72.3 11.7 %collective-permute-start.5 = (bf16[48,1792]{1,0:T(8,128)(2,1)}, bf16[48,1792]{1,0:T(8,128)(2,1)S(1)}, u32[]{:S(2)}, u32[]{:S(2)}) collective-permute-start(bf16[48,1792]{1,0:T(8,128)(2,1)} %collective-permute-done.3), channel_id=1, source_target_pairs={{0,30},{1,31},{2,0},{3,1},{4,2},{5,3},{6,4},{7,5},{8,6},{9,7},{10,... | collective-permute-start | bytes 516104 | tf_op jit(solution)/shard_map/ppermute | solution.py:74
  81.7 12.6 %collective-permute-start.6 = (bf16[48,1792]{1,0:T(8,128)(2,1)S(1)}, bf16[48,1792]{1,0:T(8,128)(2,1)S(1)}, u32[]{:S(2)}, u32[]{:S(2)}) collective-permute-start(bf16[48,1792]{1,0:T(8,128)(2,1)S(1)} %collective-permute-done.4), channel_id=1, source_target_pairs={{0,2},{1,3},{2,4},{3,5},{4,6},{5,7},{6,8},{7,9},{8,10},{9,11},{10,... | collective-permute-start | bytes 516104 | tf_op jit(solution)/shard_map/ppermute | solution.py:74
  84.0 12.1 %collective-permute-start.7 = (bf16[48,1792]{1,0:T(8,128)(2,1)S(1)}, bf16[48,1792]{1,0:T(8,128)(2,1)S(1)}, u32[]{:S(2)}, u32[]{:S(2)}) collective-permute-start(bf16[48,1792]{1,0:T(8,128)(2,1)S(1)} %collective-permute-done.5), channel_id=1, source_target_pairs={{0,30},{1,31},{2,0},{3,1},{4,2},{5,3},{6,4},{7,5},{8,6},{9,7},{10,... | collective-permute-start | bytes 516104 | tf_op jit(solution)/shard_map/ppermute | solution.py:74
  94.2 20.5 %collective-permute-start.8 = (bf16[48,1792]{1,0:T(8,128)(2,1)S(1)}, bf16[48,1792]{1,0:T(8,128)(2,1)S(1)}, u32[]{:S(2)}, u32[]{:S(2)}) collective-permute-start(bf16[48,1792]{1,0:T(8,128)(2,1)S(1)} %collective-permute-done.6), channel_id=1, source_target_pairs={{0,2},{1,3},{2,4},{3,5},{4,6},{5,7},{6,8},{7,9},{8,10},{9,11},{10,... | collective-permute-start | bytes 516104 | tf_op jit(solution)/shard_map/ppermute | solution.py:74
  96.2 20.6 %collective-permute-start.9 = (bf16[48,1792]{1,0:T(8,128)(2,1)S(1)}, bf16[48,1792]{1,0:T(8,128)(2,1)S(1)}, u32[]{:S(2)}, u32[]{:S(2)}) collective-permute-start(bf16[48,1792]{1,0:T(8,128)(2,1)S(1)} %collective-permute-done.7), channel_id=1, source_target_pairs={{0,30},{1,31},{2,0},{3,1},{4,2},{5,3},{6,4},{7,5},{8,6},{9,7},{10,... | collective-permute-start | bytes 516104 | tf_op jit(solution)/shard_map/ppermute | solution.py:74
  105.7 1.9 copy-start
  114.6 7.4 %copy-start.10 = (bf16[744,1792]{1,0:T(8,128)(2,1)S(1)}, bf16[744,1792]{1,0:T(8,128)(2,1)}, u32[]{:S(2)}) copy-start(bf16[744,1792]{1,0:T(8,128)(2,1)} %constant_dynamic-update-slice_fusion.10) | copy-start | bytes 7999492
  114.8 9.5 %collective-permute-start.10 = (bf16[24,1792]{1,0:T(8,128)(2,1)S(1)}, bf16[24,1792]{1,0:T(8,128)(2,1)S(1)}, u32[]{:S(2)}, u32[]{:S(2)}) collective-permute-start(bf16[24,1792]{1,0:T(8,128)(2,1)S(1)} %slice.264), channel_id=1, source_target_pairs={{0,2},{1,3},{2,4},{3,5},{4,6},{5,7},{6,8},{7,9},{8,10},{9,11},{10,... | collective-permute-start | bytes 258056 | tf_op jit(solution)/shard_map/ppermute | solution.py:74
  116.8 9.4 %collective-permute-start.11 = (bf16[24,1792]{1,0:T(8,128)(2,1)S(1)}, bf16[24,1792]{1,0:T(8,128)(2,1)S(1)}, u32[]{:S(2)}, u32[]{:S(2)}) collective-permute-start(bf16[24,1792]{1,0:T(8,128)(2,1)S(1)} %slice.265), channel_id=1, source_target_pairs={{0,30},{1,31},{2,0},{3,1},{4,2},{5,3},{6,4},{7,5},{8,6},{9,7},{10,... | collective-permute-start | bytes 258056 | tf_op jit(solution)/shard_map/ppermute | solution.py:74
  124.3 8.5 %collective-permute-start.12 = (bf16[24,1792]{1,0:T(8,128)(2,1)S(1)}, bf16[24,1792]{1,0:T(8,128)(2,1)S(1)}, u32[]{:S(2)}, u32[]{:S(2)}) collective-permute-start(bf16[24,1792]{1,0:T(8,128)(2,1)S(1)} %collective-permute-done.10), channel_id=1, source_target_pairs={{0,2},{1,3},{2,4},{3,5},{4,6},{5,7},{6,8},{7,9},{8,10},{9,11},{10,... | collective-permute-start | bytes 258056 | tf_op jit(solution)/shard_map/ppermute | solution.py:74
  126.2 8.5 %collective-permute-start.13 = (bf16[24,1792]{1,0:T(8,128)(2,1)S(1)}, bf16[24,1792]{1,0:T(8,128)(2,1)S(1)}, u32[]{:S(2)}, u32[]{:S(2)}) collective-permute-start(bf16[24,1792]{1,0:T(8,128)(2,1)S(1)} %collective-permute-done.11), channel_id=1, source_target_pairs={{0,30},{1,31},{2,0},{3,1},{4,2},{5,3},{6,4},{7,5},{8,6},{9,7},{10,... | collective-permute-start | bytes 258056 | tf_op jit(solution)/shard_map/ppermute | solution.py:74
  132.8 8.2 %collective-permute-start.14 = (bf16[24,1792]{1,0:T(8,128)(2,1)S(1)}, bf16[24,1792]{1,0:T(8,128)(2,1)S(1)}, u32[]{:S(2)}, u32[]{:S(2)}) collective-permute-start(bf16[24,1792]{1,0:T(8,128)(2,1)S(1)} %collective-permute-done.12), channel_id=1, source_target_pairs={{0,2},{1,3},{2,4},{3,5},{4,6},{5,7},{6,8},{7,9},{8,10},{9,11},{10,... | collective-permute-start | bytes 258056 | tf_op jit(solution)/shard_map/ppermute | solution.py:74
  134.8 8.2 %collective-permute-start.15 = (bf16[24,1792]{1,0:T(8,128)(2,1)S(1)}, bf16[24,1792]{1,0:T(8,128)(2,1)S(1)}, u32[]{:S(2)}, u32[]{:S(2)}) collective-permute-start(bf16[24,1792]{1,0:T(8,128)(2,1)S(1)} %collective-permute-done.13), channel_id=1, source_target_pairs={{0,30},{1,31},{2,0},{3,1},{4,2},{5,3},{6,4},{7,5},{8,6},{9,7},{10,... | collective-permute-start | bytes 258056 | tf_op jit(solution)/shard_map/ppermute | solution.py:74
  141.0 7.6 %collective-permute-start.16 = (bf16[24,1792]{1,0:T(8,128)(2,1)S(1)}, bf16[24,1792]{1,0:T(8,128)(2,1)S(1)}, u32[]{:S(2)}, u32[]{:S(2)}) collective-permute-start(bf16[24,1792]{1,0:T(8,128)(2,1)S(1)} %collective-permute-done.14), channel_id=1, source_target_pairs={{0,2},{1,3},{2,4},{3,5},{4,6},{5,7},{6,8},{7,9},{8,10},{9,11},{10,... | collective-permute-start | bytes 258056 | tf_op jit(solution)/shard_map/ppermute | solution.py:74
  143.0 7.4 %collective-permute-start.17 = (bf16[24,1792]{1,0:T(8,128)(2,1)S(1)}, bf16[24,1792]{1,0:T(8,128)(2,1)S(1)}, u32[]{:S(2)}, u32[]{:S(2)}) collective-permute-start(bf16[24,1792]{1,0:T(8,128)(2,1)S(1)} %collective-permute-done.15), channel_id=1, source_target_pairs={{0,30},{1,31},{2,0},{3,1},{4,2},{5,3},{6,4},{7,5},{8,6},{9,7},{10,... | collective-permute-start | bytes 258056 | tf_op jit(solution)/shard_map/ppermute | solution.py:74
  156.4 5.4 %copy-start.8 = (bf16[256,3584]{1,0:T(8,128)(2,1)S(1)}, bf16[256,3584]{1,0:T(8,128)(2,1)}, u32[]{:S(2)}) copy-start(bf16[256,3584]{1,0:T(8,128)(2,1)} %pad_maximum_fusion.2) | copy-start | bytes 5505028
  156.4 5.8 %copy-start.11 = (bf16[512,7168]{1,0:T(8,128)(2,1)S(1)}, bf16[512,7168]{1,0:T(8,128)(2,1)}, u32[]{:S(2)}) copy-start(bf16[512,7168]{1,0:T(8,128)(2,1)} %all-gather.2.cloned.1.call-done) | copy-start | bytes 22020100
  162.2 2.0 copy-start.1
  170.7 8.4 %collective-permute-start.21 = (bf16[24,1792]{1,0:T(8,128)(2,1)S(1)}, bf16[24,1792]{1,0:T(8,128)(2,1)S(1)}, u32[]{:S(2)}, u32[]{:S(2)}) collective-permute-start(bf16[24,1792]{1,0:T(8,128)(2,1)S(1)} %get-tuple-element.60), channel_id=1, source_target_pairs={{0,30},{1,31},{2,0},{3,1},{4,2},{5,3},{6,4},{7,5},{8,6},{9,7},{10,... | collective-permute-start | bytes 258056 | tf_op jit(solution)/shard_map/ppermute | solution.py:83
  176.2 8.2 %collective-permute-start.22 = (bf16[24,1792]{1,0:T(8,128)(2,1)S(1)}, bf16[24,1792]{1,0:T(8,128)(2,1)S(1)}, u32[]{:S(2)}, u32[]{:S(2)}) collective-permute-start(bf16[24,1792]{1,0:T(8,128)(2,1)S(1)} %get-tuple-element.61), channel_id=1, source_target_pairs={{0,2},{1,3},{2,4},{3,5},{4,6},{5,7},{6,8},{7,9},{8,10},{9,11},{10,... | collective-permute-start | bytes 258056 | tf_op jit(solution)/shard_map/ppermute | solution.py:84
  184.5 6.4 %collective-permute-start.23 = (bf16[24,1792]{1,0:T(8,128)(2,1)S(1)}, bf16[24,1792]{1,0:T(8,128)(2,1)S(1)}, u32[]{:S(2)}, u32[]{:S(2)}) collective-permute-start(bf16[24,1792]{1,0:T(8,128)(2,1)S(1)} %get-tuple-element.58), channel_id=1, source_target_pairs={{0,30},{1,31},{2,0},{3,1},{4,2},{5,3},{6,4},{7,5},{8,6},{9,7},{10,... | collective-permute-start | bytes 258056 | tf_op jit(solution)/shard_map/ppermute | solution.py:83
  186.4 7.6 %collective-permute-start.24 = (bf16[24,1792]{1,0:T(8,128)(2,1)S(1)}, bf16[24,1792]{1,0:T(8,128)(2,1)S(1)}, u32[]{:S(2)}, u32[]{:S(2)}) collective-permute-start(bf16[24,1792]{1,0:T(8,128)(2,1)S(1)} %get-tuple-element.59), channel_id=1, source_target_pairs={{0,2},{1,3},{2,4},{3,5},{4,6},{5,7},{6,8},{7,9},{8,10},{9,11},{10,... | collective-permute-start | bytes 258056 | tf_op jit(solution)/shard_map/ppermute | solution.py:84
  194.1 6.4 %collective-permute-start.25 = (bf16[24,1792]{1,0:T(8,128)(2,1)S(1)}, bf16[24,1792]{1,0:T(8,128)(2,1)S(1)}, u32[]{:S(2)}, u32[]{:S(2)}) collective-permute-start(bf16[24,1792]{1,0:T(8,128)(2,1)S(1)} %get-tuple-element.56), channel_id=1, source_target_pairs={{0,30},{1,31},{2,0},{3,1},{4,2},{5,3},{6,4},{7,5},{8,6},{9,7},{10,... | collective-permute-start | bytes 258056 | tf_op jit(solution)/shard_map/ppermute | solution.py:83
  196.0 7.6 %collective-permute-start.26 = (bf16[24,1792]{1,0:T(8,128)(2,1)S(1)}, bf16[24,1792]{1,0:T(8,128)(2,1)S(1)}, u32[]{:S(2)}, u32[]{:S(2)}) collective-permute-start(bf16[24,1792]{1,0:T(8,128)(2,1)S(1)} %get-tuple-element.57), channel_id=1, source_target_pairs={{0,2},{1,3},{2,4},{3,5},{4,6},{5,7},{6,8},{7,9},{8,10},{9,11},{10,... | collective-permute-start | bytes 258056 | tf_op jit(solution)/shard_map/ppermute | solution.py:84
  203.7 6.4 %collective-permute-start.27 = (bf16[24,1792]{1,0:T(8,128)(2,1)S(1)}, bf16[24,1792]{1,0:T(8,128)(2,1)S(1)}, u32[]{:S(2)}, u32[]{:S(2)}) collective-permute-start(bf16[24,1792]{1,0:T(8,128)(2,1)S(1)} %get-tuple-element.54), channel_id=1, source_target_pairs={{0,30},{1,31},{2,0},{3,1},{4,2},{5,3},{6,4},{7,5},{8,6},{9,7},{10,... | collective-permute-start | bytes 258056 | tf_op jit(solution)/shard_map/ppermute | solution.py:83
  206.9 7.6 %collective-permute-start.28 = (bf16[24,1792]{1,0:T(8,128)(2,1)S(1)}, bf16[24,1792]{1,0:T(8,128)(2,1)S(1)}, u32[]{:S(2)}, u32[]{:S(2)}) collective-permute-start(bf16[24,1792]{1,0:T(8,128)(2,1)S(1)} %get-tuple-element.55), channel_id=1, source_target_pairs={{0,2},{1,3},{2,4},{3,5},{4,6},{5,7},{6,8},{7,9},{8,10},{9,11},{10,... | collective-permute-start | bytes 258056 | tf_op jit(solution)/shard_map/ppermute | solution.py:84
  214.6 9.5 %collective-permute-start.29 = (bf16[48,1792]{1,0:T(8,128)(2,1)S(1)}, bf16[48,1792]{1,0:T(8,128)(2,1)S(1)}, u32[]{:S(2)}, u32[]{:S(2)}) collective-permute-start(bf16[48,1792]{1,0:T(8,128)(2,1)S(1)} %get-tuple-element.50), channel_id=1, source_target_pairs={{0,30},{1,31},{2,0},{3,1},{4,2},{5,3},{6,4},{7,5},{8,6},{9,7},{10,... | collective-permute-start | bytes 516104 | tf_op jit(solution)/shard_map/ppermute | solution.py:83
  217.2 11.8 %collective-permute-start.30 = (bf16[48,1792]{1,0:T(8,128)(2,1)S(1)}, bf16[48,1792]{1,0:T(8,128)(2,1)S(1)}, u32[]{:S(2)}, u32[]{:S(2)}) collective-permute-start(bf16[48,1792]{1,0:T(8,128)(2,1)S(1)} %get-tuple-element.51), channel_id=1, source_target_pairs={{0,2},{1,3},{2,4},{3,5},{4,6},{5,7},{6,8},{7,9},{8,10},{9,11},{10,... | collective-permute-start | bytes 516104 | tf_op jit(solution)/shard_map/ppermute | solution.py:84
  229.2 10.5 %collective-permute-start.31 = (bf16[48,1792]{1,0:T(8,128)(2,1)S(1)}, bf16[48,1792]{1,0:T(8,128)(2,1)S(1)}, u32[]{:S(2)}, u32[]{:S(2)}) collective-permute-start(bf16[48,1792]{1,0:T(8,128)(2,1)S(1)} %get-tuple-element.48), channel_id=1, source_target_pairs={{0,30},{1,31},{2,0},{3,1},{4,2},{5,3},{6,4},{7,5},{8,6},{9,7},{10,... | collective-permute-start | bytes 516104 | tf_op jit(solution)/shard_map/ppermute | solution.py:83
  231.9 11.4 %collective-permute-start.32 = (bf16[48,1792]{1,0:T(8,128)(2,1)S(1)}, bf16[48,1792]{1,0:T(8,128)(2,1)S(1)}, u32[]{:S(2)}, u32[]{:S(2)}) collective-permute-start(bf16[48,1792]{1,0:T(8,128)(2,1)S(1)} %get-tuple-element.49), channel_id=1, source_target_pairs={{0,2},{1,3},{2,4},{3,5},{4,6},{5,7},{6,8},{7,9},{8,10},{9,11},{10,... | collective-permute-start | bytes 516104 | tf_op jit(solution)/shard_map/ppermute | solution.py:84
  243.4 36.5 %copy-start.14 = (s32[1,32,1]{1,2,0:T(1,128)S(1)}, s32[1,32,1]{1,2,0:T(1,128)}, u32[]{:S(2)}) copy-start(s32[1,32,1]{1,2,0:T(1,128)} %param.23) | copy-start | bytes 388
  243.5 10.2 %collective-permute-start.33 = (bf16[48,1792]{1,0:T(8,128)(2,1)S(1)}, bf16[48,1792]{1,0:T(8,128)(2,1)S(1)}, u32[]{:S(2)}, u32[]{:S(2)}) collective-permute-start(bf16[48,1792]{1,0:T(8,128)(2,1)S(1)} %get-tuple-element.46), channel_id=1, source_target_pairs={{0,30},{1,31},{2,0},{3,1},{4,2},{5,3},{6,4},{7,5},{8,6},{9,7},{10,... | collective-permute-start | bytes 516104 | tf_op jit(solution)/shard_map/ppermute | solution.py:83
  247.6 11.2 %collective-permute-start.34 = (bf16[48,1792]{1,0:T(8,128)(2,1)S(1)}, bf16[48,1792]{1,0:T(8,128)(2,1)S(1)}, u32[]{:S(2)}, u32[]{:S(2)}) collective-permute-start(bf16[48,1792]{1,0:T(8,128)(2,1)S(1)} %get-tuple-element.47), channel_id=1, source_target_pairs={{0,2},{1,3},{2,4},{3,5},{4,6},{5,7},{6,8},{7,9},{8,10},{9,11},{10,... | collective-permute-start | bytes 516104 | tf_op jit(solution)/shard_map/ppermute | solution.py:84
  259.0 26.8 %copy-start.7 = (bf16[1,32,3584]{2,1,0:T(8,128)(2,1)S(1)}, bf16[1,32,3584]{2,1,0:T(8,128)(2,1)}, u32[]{:S(2)}) copy-start(bf16[1,32,3584]{2,1,0:T(8,128)(2,1)} %param.15) | copy-start | bytes 688132
  259.0 10.0 %collective-permute-start.35 = (bf16[48,1792]{1,0:T(8,128)(2,1)S(1)}, bf16[48,1792]{1,0:T(8,128)(2,1)S(1)}, u32[]{:S(2)}, u32[]{:S(2)}) collective-permute-start(bf16[48,1792]{1,0:T(8,128)(2,1)S(1)} %get-tuple-element.44), channel_id=1, source_target_pairs={{0,30},{1,31},{2,0},{3,1},{4,2},{5,3},{6,4},{7,5},{8,6},{9,7},{10,... | collective-permute-start | bytes 516104 | tf_op jit(solution)/shard_map/ppermute | solution.py:83
  262.3 11.5 %collective-permute-start.36 = (bf16[48,1792]{1,0:T(8,128)(2,1)S(1)}, bf16[48,1792]{1,0:T(8,128)(2,1)S(1)}, u32[]{:S(2)}, u32[]{:S(2)}) collective-permute-start(bf16[48,1792]{1,0:T(8,128)(2,1)S(1)} %get-tuple-element.45), channel_id=1, source_target_pairs={{0,2},{1,3},{2,4},{3,5},{4,6},{5,7},{6,8},{7,9},{8,10},{9,11},{10,... | collective-permute-start | bytes 516104 | tf_op jit(solution)/shard_map/ppermute | solution.py:84
  273.9 16.9 %copy-start.9 = (bf16[1,32,3584]{2,1,0:T(8,128)(2,1)S(1)}, bf16[1,32,3584]{2,1,0:T(8,128)(2,1)}, u32[]{:S(2)}) copy-start(bf16[1,32,3584]{2,1,0:T(8,128)(2,1)} %param.17) | copy-start | bytes 688132
  273.9 8.7 %collective-permute-start.37 = (bf16[72,1792]{1,0:T(8,128)(2,1)S(1)}, bf16[72,1792]{1,0:T(8,128)(2,1)S(1)}, u32[]{:S(2)}, u32[]{:S(2)}) collective-permute-start(bf16[72,1792]{1,0:T(8,128)(2,1)S(1)} %get-tuple-element.40), channel_id=1, source_target_pairs={{0,30},{1,31},{2,0},{3,1},{4,2},{5,3},{6,4},{7,5},{8,6},{9,7},{10,... | collective-permute-start | bytes 774152 | tf_op jit(solution)/shard_map/ppermute | solution.py:83
  276.0 9.4 %collective-permute-start.38 = (bf16[72,1792]{1,0:T(8,128)(2,1)S(1)}, bf16[72,1792]{1,0:T(8,128)(2,1)S(1)}, u32[]{:S(2)}, u32[]{:S(2)}) collective-permute-start(bf16[72,1792]{1,0:T(8,128)(2,1)S(1)} %get-tuple-element.41), channel_id=1, source_target_pairs={{0,2},{1,3},{2,4},{3,5},{4,6},{5,7},{6,8},{7,9},{8,10},{9,11},{10,... | collective-permute-start | bytes 774152 | tf_op jit(solution)/shard_map/ppermute | solution.py:84
  286.0 10.3 %collective-permute-start.39 = (bf16[32,3584]{1,0:T(8,128)(2,1)S(1)}, bf16[32,3584]{1,0:T(8,128)(2,1)S(1)}, u32[]{:S(2)}, u32[]{:S(2)}) collective-permute-start(bf16[32,3584]{1,0:T(8,128)(2,1)S(1)} %fusion.46), channel_id=1, source_target_pairs={{0,32},{32,64},{64,96},{96,128},{128,160},{160,192},{192,224},{224... | collective-permute-start | bytes 688136 | tf_op jit(solution)/shard_map/ppermute | solution.py:15
  291.9 7.9 %collective-permute-start.40 = (bf16[32,3584]{1,0:T(8,128)(2,1)S(1)}, bf16[32,3584]{1,0:T(8,128)(2,1)S(1)}, u32[]{:S(2)}, u32[]{:S(2)}) collective-permute-start(bf16[32,3584]{1,0:T(8,128)(2,1)S(1)} %fusion.41), channel_id=1, source_target_pairs={{0,480},{32,0},{64,32},{96,64},{128,96},{160,128},{192,160},{224,1... | collective-permute-start | bytes 688136 | tf_op jit(solution)/shard_map/ppermute | solution.py:15
Sparse Core Ops, SparseCore 0:
  10.1 123.1 all-gather.1
  200.1 82.3 reduce-scatter.1

commit v5 on v3

v5 whole, which is shorter than its diff:
```python
import jax
import jax.numpy as jnp
from jax import lax
from jax.sharding import PartitionSpec as P

EXPERTS = 4
CAP = 12
EPSILON = 1e-06


def passed_along(value, axis, steps):
    count = lax.axis_size(axis)
    pairs = [(source, (source + steps) % count) for source in range(count)]
    return lax.ppermute(value, axis, pairs)


def rms_scale(values):
    return lax.rsqrt(jnp.mean(values * values, axis=-1, keepdims=True) + EPSILON)


def dot(a, b, dims):
    return lax.dot_general(a, b, (dims, ((), ())), preferred_element_type=jnp.float32)


def slots_of(route):
    onehot = (route[:, None] == jnp.arange(EXPERTS, dtype=jnp.int32)[None, :]).astype(jnp.int32)
    rank = jnp.sum(jnp.cumsum(onehot, axis=0) * onehot, axis=1) - 1
    return route * CAP + rank


def along(count, chip_of):
    return [(d, 2 * chip_of(d // 2) + d % 2) for d in range(count)]


def in_group(count, side, place_of):
    return along(count, lambda chip: chip // side * side + place_of(chip % side))


def to_section(value, sections, count, steps, hop, chips):
    pairs = []
    for s in range(sections):
        for d in range(count):
            chip = (d // 2 + hop) % chips
            pairs.append((s * count + d, (s + steps) % sections * count + 2 * chip + d % 2))
    return lax.ppermute(value, ("section", "expert"), pairs)


def pick_rows(route, me_group):
    slot = slots_of(route)
    place = (slot // CAP - me_group) % EXPERTS * (2 * CAP) + slot % CAP
    want = jnp.concatenate([place, place + CAP])
    row = jnp.arange(EXPERTS * 2 * CAP, dtype=jnp.int32)[:, None]
    return (row == want[None, :]).astype(jnp.bfloat16)


def packers(slots, me_group, me_place, tokens, side):
    count = slots.shape[0]
    sources = count // tokens
    groups = sources // side
    expert, rank = slots // CAP, slots % CAP
    source = jnp.arange(count, dtype=jnp.int32) // tokens
    back = (me_place - source % side) % side
    base = (back * groups + (me_group - source // side) % groups) * (2 * CAP) + rank
    base = jnp.where(expert == me_group, base, -2 * CAP)
    row = jnp.arange(sources * 2 * CAP, dtype=jnp.int32)[:, None]
    return [(base[None, :] + h * CAP == row).astype(jnp.bfloat16) for h in range(2)]


def add(a, b):
    return (a.astype(jnp.float32) + b.astype(jnp.float32)).astype(jnp.bfloat16)


def per_device(
    x_fwd,
    x_bwd,
    grad_out,
    norm_gain,
    w_gate,
    w_up,
    w_down,
    route_fwd,
    gate_fwd,
    route_bwd,
    gate_bwd,
):
    sections = lax.axis_size("section")
    count = lax.axis_size("expert")
    ring = count // 2
    side = ring // EXPERTS
    unit = 2 * CAP
    part = EXPERTS * unit
    same_core = [[2 * z + c for z in range(ring)] for c in range(2)]
    near = in_group(count, side, lambda j: j ^ 1)
    far = in_group(count, side, lambda j: j ^ 2)
    swap = [(i, i ^ 1) for i in range(count)]
    index = lax.axis_index("expert")
    me_group = index // (2 * side)
    me_place = (index // 2) % side

    gain = norm_gain[0]
    tokens, width = x_fwd.shape[1:]
    half = width // 2
    sent = jnp.concatenate([x_bwd[0], grad_out[0]], axis=1)
    got_b = lax.all_gather(sent, "expert", axis=0, tiled=True, axis_index_groups=same_core)

    xf = x_fwd[0].astype(jnp.float32)
    normed_f = (xf * rms_scale(xf) * gain).astype(jnp.bfloat16)
    put = pick_rows(route_fwd[0, :, 0], me_group)
    halves = jnp.concatenate([normed_f[:, :half], normed_f[:, half:]], axis=0)
    packed = dot(put, halves, ((1,), (0,))).astype(jnp.bfloat16)
    blocks = [packed[:unit]]
    for k in range(1, EXPERTS):
        hop = along(count, lambda chip: (chip + side * k) % ring)
        blocks.append(lax.ppermute(packed[k * unit : (k + 1) * unit], "expert", hop))
    mine = jnp.concatenate(blocks, axis=0)
    pair = jnp.concatenate([mine, lax.ppermute(mine, "expert", far)], axis=0)
    rows_f = jnp.concatenate([pair, lax.ppermute(pair, "expert", near)], axis=0)

    xb = x_bwd[0].astype(jnp.float32)
    r_b = rms_scale(xb)
    small = jnp.concatenate(
        [
            slots_of(route_bwd[0, :, 0]).astype(jnp.float32),
            r_b[:, 0],
            gate_bwd[0, :, 0].astype(jnp.float32) / 256.0,
        ]
    )
    small = lax.all_to_all(
        jnp.broadcast_to(small[None, None, :], (ring, 1, 3 * tokens)),
        "expert",
        split_axis=0,
        concat_axis=0,
        tiled=True,
        axis_index_groups=same_core,
    )[:, 0]
    slots_b, rs_b, scales_b = [
        small[:, i * tokens : (i + 1) * tokens].reshape(ring * tokens) for i in range(3)
    ]
    slots_b = slots_b.astype(jnp.int32)

    gate_o = lax.ppermute(w_gate[0], "expert", swap)
    up_o = lax.ppermute(w_up[0], "expert", swap)
    down_o = lax.ppermute(w_down[0], "expert", swap)
    last_f = passed_along(x_fwd[0], "section", 1).astype(jnp.float32)
    last_b = passed_along(sent, "section", -1).astype(jnp.float32)
    last_gain = passed_along(norm_gain, "section", -1)
    whole = jnp.concatenate([route_fwd[0, :, 0], gate_fwd[0, :, 0]])[None, :]
    whole = passed_along(whole, "section", 1)[0]
    last_put_f = pick_rows(whole[:tokens], me_group)
    last_scale_f = whole[tokens:, None].astype(jnp.float32) / 256.0
    last_put_b = pick_rows(passed_along(route_bwd[0, :, 0][None, :], "section", -1)[0], me_group)

    w_in = jnp.concatenate([w_gate[0], gate_o, w_up[0], up_o], axis=1)
    w_gained = (w_in.astype(jnp.float32) * gain[:, None]).astype(jnp.bfloat16)
    w_dn = jnp.concatenate([w_down[0], down_o], axis=0)
    hid = w_dn.shape[0]
    dn_stack = jnp.concatenate([w_dn[:, :half], w_dn[:, half:]], axis=0)
    in_stack = jnp.concatenate([w_in[:half], w_in[half:]], axis=1)
    w_gained, w_dn, in_stack, dn_stack = lax.optimization_barrier(
        (w_gained, w_dn, in_stack, dn_stack)
    )

    pre_f = dot(rows_f, in_stack, ((1,), (0,))).reshape(ring, unit, 4 * hid)
    pre_f = pre_f[:, :CAP, : 2 * hid] + pre_f[:, CAP:, 2 * hid :]
    act = (jax.nn.silu(pre_f[..., :hid]) * pre_f[..., hid:]).astype(jnp.bfloat16)
    lower = jnp.pad(act, ((0, 0), (0, CAP), (0, 0)))
    upper = jnp.pad(act, ((0, 0), (CAP, 0), (0, 0)))
    act = jnp.concatenate([lower, upper], axis=2).reshape(ring * unit, 2 * hid)
    part_f = dot(act, dn_stack, ((1,), (0,))).astype(jnp.bfloat16)
    pair = add(part_f[: 2 * part], lax.ppermute(part_f[2 * part :], "expert", near))
    total_f = add(pair[:part], lax.ppermute(pair[part:], "expert", far))
    got_b, total_f = lax.optimization_barrier((got_b, total_f))
    table_f = [
        to_section(total_f[k * unit : (k + 1) * unit], sections, count, 1, -side * k, ring)
        for k in range(EXPERTS)
    ]

    pre_b = dot(got_b[:, :width], w_gained, ((1,), (0,))) * rs_b[:, None]
    d_act = dot(got_b[:, width:], w_dn, ((1,), (1,))) * scales_b[:, None]
    gate, up = pre_b[:, :hid], pre_b[:, hid:]
    sig = jax.nn.sigmoid(gate)
    d_gate = (d_act * up * sig * (1.0 + gate * (1.0 - sig))).astype(jnp.bfloat16)
    d_up = (d_act * gate * sig).astype(jnp.bfloat16)
    hidden_b = jnp.concatenate([d_gate, d_up], axis=1)
    places = packers(slots_b, me_group, me_place, tokens, side)
    parts = [dot(p, hidden_b, ((1,), (0,))).astype(jnp.bfloat16) for p in places]
    part_b = dot(jnp.concatenate(parts, axis=1), in_stack, ((1,), (1,))).astype(jnp.bfloat16)
    total_b = part_b[:part].astype(jnp.float32)
    for k in range(1, side):
        hop = in_group(count, side, lambda j: (j - k) % side)
        back = lax.ppermute(part_b[k * part : (k + 1) * part], "expert", hop)
        total_b = total_b + back.astype(jnp.float32)
    total_b = total_b.astype(jnp.bfloat16)
    table_b = [
        to_section(total_b[k * unit : (k + 1) * unit], sections, count, -1, -side * k, ring)
        for k in range(EXPERTS)
    ]

    moe_f = dot(last_put_f, jnp.concatenate(table_f, axis=0), ((0,), (0,)))
    moe_f = jnp.concatenate([moe_f[:tokens], moe_f[tokens:]], axis=1)
    y_next = (last_f + last_scale_f * moe_f).astype(jnp.bfloat16)

    d_normed = dot(last_put_b, jnp.concatenate(table_b, axis=0), ((0,), (0,)))
    d_normed = jnp.concatenate([d_normed[:tokens], d_normed[tokens:]], axis=1)
    last_x, last_g = last_b[:, :width], last_b[:, width:]
    r = rms_scale(last_x)
    weighted = d_normed * last_gain
    inner = jnp.mean(last_x * weighted, axis=-1, keepdims=True)
    dx_prev = (last_g + (r * weighted - last_x * r * r * r * inner)).astype(jnp.bfloat16)
    return (y_next[None], dx_prev[None])


def solution(mesh):
    in_specs = (
        P("section", "expert", None),
        P("section", "expert", None),
        P("section", "expert", None),
        P("section", None),
        P("section", None, "expert"),
        P("section", None, "expert"),
        P("section", "expert", None),
        P("section", "expert", None),
        P("section", "expert", None),
        P("section", "expert", None),
        P("section", "expert", None),
    )
    out_specs = (P("section", "expert", None), P("section", "expert", None))
    return jax.shard_map(
        per_device, mesh=mesh, in_specs=in_specs, out_specs=out_specs, check_vma=False
    )
```

time: 284 us -> 300 us (1.056)
  the two profiles are of different devices: /device:TPU:6 before, /device:TPU:64 now
where the time goes in v5:
time: 300 us; the launch traced here: 299 us
  starting transfers between devices  134 us (45%)
  waiting for transfers between devices  105 us (35%)
  other arithmetic  24.8 us (8%)
  between operations  14.9 us (5%)
  matrix products  12.5 us (4%)
  local copies, waits for them, and re-layouts  8.22 us (3%)
    ppermute x8, starting transfers between devices, to_section(): return lax.ppermute(value, ('section', 'expert'), pairs)  49.2 us
    ppermute x3, starting transfers between devices, per_device(): blocks.append(lax.ppermute(packed[k * unit:(k + 1) * unit], 'expert', hop))  23.7 us
    ppermute x3, waiting for transfers between devices, per_device(): back = lax.ppermute(part_b[k * part:(k + 1) * part], 'expert', hop)  23.5 us
    ppermute x1, waiting for transfers between devices, per_device(): rows_f = jnp.concatenate([pair, lax.ppermute(pair, 'expert', near)], axis=0)  22.2 us
    ppermute x1, waiting for transfers between devices, per_device(): pair = jnp.concatenate([mine, lax.ppermute(mine, 'expert', far)], axis=0)  21 us
    ppermute x5, starting transfers between devices, passed_along(): return lax.ppermute(value, axis, pairs)  17.9 us
    ppermute x3, starting transfers between devices, per_device(): back = lax.ppermute(part_b[k * part:(k + 1) * part], 'expert', hop)  13.5 us
    dot_general x10, matrix products, dot(): lax.dot_general(a, b, (dims, ((), ())), preferred_element_type=jnp.float32)  12.5 us
  transfers between devices with their start and end apart: 28, of which 10 were waited for; matrix products, arithmetic and copies ran while one was open for 14% of the time, Pallas kernels for 0%

profile of v5, /device:TPU:64, one launch (start us, length us, event | category | flops | bytes accessed | tf_op | source)
XLA Modules:
  0.0 298.9 jit_solution(4796499624586504349)
XLA Ops:
  7.2 1.9 pad_maximum_fusion.5
  9.2 7.4 %collective-permute-start.16 = (bf16[32,7168]{1,0:T(8,128)(2,1)}, bf16[32,7168]{1,0:T(8,128)(2,1)}, u32[]{:S(2)}, u32[]{:S(2)}) collective-permute-start(bf16[32,7168]{1,0:T(8,128)(2,1)} %pad_maximum_fusion.5), channel_id=1, source_target_pairs={{0,480},{32,0},{64,32},{96,64},{128,96},{160,128},{192,160},{224,1... | collective-permute-start | bytes 1376264 | tf_op jit(solution)/shard_map/ppermute | solution.py:14
  16.6 0.7 fusion.56
  17.4 0.8 select_reduce_fusion.2
  18.2 0.7 broadcast_add_fusion.3
  18.9 0.8 reduce
  19.8 1.1 fusion.20
  21.3 0.8 constant_dynamic-update-slice_fusion.4
  22.1 9.1 %collective-permute-start.2 = (bf16[24,1792]{1,0:T(8,128)(2,1)}, bf16[24,1792]{1,0:T(8,128)(2,1)S(1)}, u32[]{:S(2)}, u32[]{:S(2)}) collective-permute-start(bf16[24,1792]{1,0:T(8,128)(2,1)} %get-tuple-element.51), channel_id=1, source_target_pairs={{0,8},{1,9},{2,10},{3,11},{4,12},{5,13},{6,14},{7,15},{8,16},{9,17... | collective-permute-start | bytes 258056 | tf_op jit(solution)/shard_map/ppermute | solution.py:114
  31.2 9.1 %collective-permute-start.3 = (bf16[24,1792]{1,0:T(8,128)(2,1)}, bf16[24,1792]{1,0:T(8,128)(2,1)S(1)}, u32[]{:S(2)}, u32[]{:S(2)}) collective-permute-start(bf16[24,1792]{1,0:T(8,128)(2,1)} %get-tuple-element.50), channel_id=1, source_target_pairs={{0,16},{1,17},{2,18},{3,19},{4,20},{5,21},{6,22},{7,23},{8,24},{9,... | collective-permute-start | bytes 258056 | tf_op jit(solution)/shard_map/ppermute | solution.py:114
  40.3 5.5 %collective-permute-start.4 = (bf16[24,1792]{1,0:T(8,128)(2,1)}, bf16[24,1792]{1,0:T(8,128)(2,1)S(1)}, u32[]{:S(2)}, u32[]{:S(2)}) collective-permute-start(bf16[24,1792]{1,0:T(8,128)(2,1)} %get-tuple-element.49), channel_id=1, source_target_pairs={{0,24},{1,25},{2,26},{3,27},{4,28},{5,29},{6,30},{7,31},{8,0},{9,1... | collective-permute-start | bytes 258056 | tf_op jit(solution)/shard_map/ppermute | solution.py:114
  47.0 6.5 %all-to-all-start = ((f32[16,1,96]{2,1,0:T(1,128)}), f32[16,1,96]{2,1,0:T(1,128)S(1)}, u32[]{:S(2)}, u32[]{:S(2)}) async-start(f32[16,1,96]{2,1,0:T(1,128)} %broadcast_in_dim.13), calls=%async_computation | async-start | bytes 16384 | tf_op jit(solution)/shard_map/all_to_all | solution.py:128
  53.5 2.6 collective-permute-start.17
  56.2 2.7 collective-permute-done.17
  58.9 1.9 collective-permute-start.1
  61.1 6.5 %collective-permute-done.1 = s32[1,64]{1,0:T(1,128)S(1)} collective-permute-done((s32[1,64]{1,0:T(1,128)S(1)}, s32[1,64]{1,0:T(1,128)S(1)}, u32[]{:S(2)}, u32[]{:S(2)}) %collective-permute-start.1) | collective-permute-done | bytes 288 | tf_op jit(solution)/shard_map/ppermute | solution.py:14
  67.6 1.9 collective-permute-start.7
  69.9 2.4 collective-permute-start.8
  72.4 1.9 collective-permute-start.9
  74.3 0.9 pad_maximum_fusion.6
  75.2 2.0 collective-permute-start.5
  77.3 0.7 constant_dynamic-update-slice_fusion.3
  77.9 0.7 constant_dynamic-update-slice_fusion.2
  78.6 0.7 constant_dynamic-update-slice_fusion.1
  79.3 21.0 %collective-permute-done.5 = bf16[96,1792]{1,0:T(8,128)(2,1)S(1)} collective-permute-done((bf16[96,1792]{1,0:T(8,128)(2,1)S(1)}, bf16[96,1792]{1,0:T(8,128)(2,1)S(1)}, u32[]{:S(2)}, u32[]{:S(2)}) %collective-permute-start.5) | collective-permute-done | bytes 344096 | tf_op jit(solution)/shard_map/ppermute | solution.py:116
  100.3 2.5 collective-permute-start.25
  102.8 0.9 constant_dynamic-update-slice_fusion
  103.7 3.5 %collective-permute-start = (bf16[32,3584]{1,0:T(8,128)(2,1)S(1)}, bf16[32,3584]{1,0:T(8,128)(2,1)S(1)}, u32[]{:S(2)}, u32[]{:S(2)}) collective-permute-start(bf16[32,3584]{1,0:T(8,128)(2,1)S(1)} %bitcast.54), channel_id=1, source_target_pairs={{0,32},{32,64},{64,96},{96,128},{128,160},{160,192},{192,224},{224... | collective-permute-start | bytes 688136 | tf_op jit(solution)/shard_map/ppermute | solution.py:14
  107.3 6.1 %collective-permute-start.6 = (bf16[192,1792]{1,0:T(8,128)(2,1)S(1)}, bf16[192,1792]{1,0:T(8,128)(2,1)S(1)}, u32[]{:S(2)}, u32[]{:S(2)}) collective-permute-start(bf16[192,1792]{1,0:T(8,128)(2,1)S(1)} %copy-done.13), channel_id=1, source_target_pairs={{0,2},{1,3},{2,0},{3,1},{4,6},{5,7},{6,4},{7,5},{8,10},{9,11},{10,... | collective-permute-start | bytes 2064392 | tf_op jit(solution)/shard_map/ppermute | solution.py:117
  113.4 1.5 pad_maximum_fusion
  115.9 4.1 %multiply_convert_fusion = bf16[3584,512]{1,0:T(8,128)(2,1)} fusion(f32[3584]{0:T(1024)S(1)} %copy-done.12, bf16[3584,128]{1,0:T(8,128)(2,1)S(1)} %collective-permute-done.8, bf16[3584,128]{1,0:T(8,128)(2,1)S(1)} %bitcast.46, bf16[3584,128]{1,0:T(8,128)(2,1)} %collective-permute-done.7, bf16[3584,128]{1,0:T(8,128)(2,1)S(1)} %bitcast.49), kind=kLoop, calls=%fused_computation | loop fusion | flops 18350080 | bytes 7354368 | tf_op jit(solution)/shard_map/convert_element_type | solution.py:154
  120.2 1.3 pad_maximum_fusion.2
  121.5 22.2 %collective-permute-done.6 = bf16[192,1792]{1,0:T(8,128)(2,1)S(1)} collective-permute-done((bf16[192,1792]{1,0:T(8,128)(2,1)S(1)}, bf16[192,1792]{1,0:T(8,128)(2,1)S(1)}, u32[]{:S(2)}, u32[]{:S(2)}) %collective-permute-start.6) | collective-permute-done | bytes 688160 | tf_op jit(solution)/shard_map/ppermute | solution.py:117
  143.8 1.6 fusion.105
  145.6 0.9 convolution_convert_fusion
  146.5 1.1 copy-done.6
  147.6 4.0 %collective-permute-start.10 = (bf16[192,1792]{1,0:T(8,128)(2,1)S(1)}, bf16[192,1792]{1,0:T(8,128)(2,1)S(1)}, u32[]{:S(2)}, u32[]{:S(2)}) collective-permute-start(bf16[192,1792]{1,0:T(8,128)(2,1)S(1)} %slice.202), channel_id=1, source_target_pairs={{0,2},{1,3},{2,0},{3,1},{4,6},{5,7},{6,4},{7,5},{8,10},{9,11},{10,... | collective-permute-start | bytes 2064392 | tf_op jit(solution)/shard_map/ppermute | solution.py:170
  152.9 0.7 pad_add_fusion
  155.7 9.9 %collective-permute-done.10 = bf16[192,1792]{1,0:T(8,128)(2,1)S(1)} collective-permute-done((bf16[192,1792]{1,0:T(8,128)(2,1)S(1)}, bf16[192,1792]{1,0:T(8,128)(2,1)S(1)}, u32[]{:S(2)}, u32[]{:S(2)}) %collective-permute-start.10) | collective-permute-done | bytes 688160 | tf_op jit(solution)/shard_map/ppermute | solution.py:170
  165.6 1.3 add_convert_fusion
  166.9 4.8 %collective-permute-start.11 = (bf16[96,1792]{1,0:T(8,128)(2,1)S(1)}, bf16[96,1792]{1,0:T(8,128)(2,1)S(1)}, u32[]{:S(2)}, u32[]{:S(2)}) collective-permute-start(bf16[96,1792]{1,0:T(8,128)(2,1)S(1)} %slice.204), channel_id=1, source_target_pairs={{0,4},{1,5},{2,6},{3,7},{4,0},{5,1},{6,2},{7,3},{8,12},{9,13},{10,... | collective-permute-start | bytes 1032200 | tf_op jit(solution)/shard_map/ppermute | solution.py:171
  171.8 0.7 sign_compare_fusion
  173.2 1.1 convert_element_type.150
  174.3 10.4 %collective-permute-done.11 = bf16[96,1792]{1,0:T(8,128)(2,1)S(1)} collective-permute-done((bf16[96,1792]{1,0:T(8,128)(2,1)S(1)}, bf16[96,1792]{1,0:T(8,128)(2,1)S(1)}, u32[]{:S(2)}, u32[]{:S(2)}) %collective-permute-start.11) | collective-permute-done | bytes 344096 | tf_op jit(solution)/shard_map/ppermute | solution.py:171
  184.8 5.4 %fusion.4 = f32[512,512]{0,1:T(8,128)S(1)} fusion(bf16[3584,512]{1,0:T(8,128)(2,1)} %multiply_convert_fusion, bf16[512,7168]{1,0:T(8,128)(2,1)} %all-gather.2.cloned.1.call-done, f32[512]{0:T(512)} %mul.224), kind=kOutput, calls=%fused_computation.17 | convolution fusion | flops 1879310336 | bytes 8390656 | tf_op jit(solution)/shard_map/dot_general | solution.py:22
  190.6 1.4 fusion.19
  192.9 2.1 collective-permute-start.12
  194.9 5.5 %collective-permute-start.13 = (bf16[24,1792]{1,0:T(8,128)(2,1)S(1)}, bf16[24,1792]{1,0:T(8,128)(2,1)S(1)}, u32[]{:S(2)}, u32[]{:S(2)}) collective-permute-start(bf16[24,1792]{1,0:T(8,128)(2,1)S(1)} %get-tuple-element.44), channel_id=1, source_target_pairs={{0,56},{1,57},{2,58},{3,59},{4,60},{5,61},{6,62},{7,63},{8,32},{9,... | collective-permute-start | bytes 258056 | tf_op jit(solution)/shard_map/ppermute | solution.py:45
  200.5 8.7 %collective-permute-start.14 = (bf16[24,1792]{1,0:T(8,128)(2,1)S(1)}, bf16[24,1792]{1,0:T(8,128)(2,1)S(1)}, u32[]{:S(2)}, u32[]{:S(2)}) collective-permute-start(bf16[24,1792]{1,0:T(8,128)(2,1)S(1)} %get-tuple-element.43), channel_id=1, source_target_pairs={{0,48},{1,49},{2,50},{3,51},{4,52},{5,53},{6,54},{7,55},{8,56},{9,... | collective-permute-start | bytes 258056 | tf_op jit(solution)/shard_map/ppermute | solution.py:45
  209.2 6.3 %collective-permute-start.15 = (bf16[24,1792]{1,0:T(8,128)(2,1)S(1)}, bf16[24,1792]{1,0:T(8,128)(2,1)S(1)}, u32[]{:S(2)}, u32[]{:S(2)}) collective-permute-start(bf16[24,1792]{1,0:T(8,128)(2,1)S(1)} %get-tuple-element.42), channel_id=1, source_target_pairs={{0,40},{1,41},{2,42},{3,43},{4,44},{5,45},{6,46},{7,47},{8,48},{9,... | collective-permute-start | bytes 258056 | tf_op jit(solution)/shard_map/ppermute | solution.py:45
  215.5 1.7 convolution_convert_fusion.1
  217.2 1.9 collective-permute-start.18
  219.2 5.6 %collective-permute-start.19 = (bf16[96,1792]{1,0:T(8,128)(2,1)S(1)}, bf16[96,1792]{1,0:T(8,128)(2,1)S(1)}, u32[]{:S(2)}, u32[]{:S(2)}) collective-permute-start(bf16[96,1792]{1,0:T(8,128)(2,1)S(1)} %get-tuple-element.32), channel_id=1, source_target_pairs={{0,4},{1,5},{2,6},{3,7},{4,0},{5,1},{6,2},{7,3},{8,12},{9,13},{10,... | collective-permute-start | bytes 1032200 | tf_op jit(solution)/shard_map/ppermute | solution.py:191
  224.8 6.0 %collective-permute-start.20 = (bf16[96,1792]{1,0:T(8,128)(2,1)S(1)}, bf16[96,1792]{1,0:T(8,128)(2,1)S(1)}, u32[]{:S(2)}, u32[]{:S(2)}) collective-permute-start(bf16[96,1792]{1,0:T(8,128)(2,1)S(1)} %get-tuple-element.31), channel_id=1, source_target_pairs={{0,2},{1,3},{2,4},{3,5},{4,6},{5,7},{6,0},{7,1},{8,10},{9,11},{10,... | collective-permute-start | bytes 1032200 | tf_op jit(solution)/shard_map/ppermute | solution.py:191
  231.1 11.2 %collective-permute-done.18 = bf16[96,1792]{1,0:T(8,128)(2,1)S(1)} collective-permute-done((bf16[96,1792]{1,0:T(8,128)(2,1)S(1)}, bf16[96,1792]{1,0:T(8,128)(2,1)S(1)}, u32[]{:S(2)}, u32[]{:S(2)}) %collective-permute-start.18) | collective-permute-done | bytes 344096 | tf_op jit(solution)/shard_map/ppermute | solution.py:191
  242.3 5.7 %collective-permute-done.19 = bf16[96,1792]{1,0:T(8,128)(2,1)S(1)} collective-permute-done((bf16[96,1792]{1,0:T(8,128)(2,1)S(1)}, bf16[96,1792]{1,0:T(8,128)(2,1)S(1)}, u32[]{:S(2)}, u32[]{:S(2)}) %collective-permute-start.19) | collective-permute-done | bytes 344096 | tf_op jit(solution)/shard_map/ppermute | solution.py:191
  247.9 6.6 %collective-permute-done.20 = bf16[96,1792]{1,0:T(8,128)(2,1)S(1)} collective-permute-done((bf16[96,1792]{1,0:T(8,128)(2,1)S(1)}, bf16[96,1792]{1,0:T(8,128)(2,1)S(1)}, u32[]{:S(2)}, u32[]{:S(2)}) %collective-permute-start.20) | collective-permute-done | bytes 344096 | tf_op jit(solution)/shard_map/ppermute | solution.py:191
  254.8 6.6 %collective-permute-start.21 = (bf16[24,1792]{1,0:T(8,128)(2,1)S(1)}, bf16[24,1792]{1,0:T(8,128)(2,1)S(1)}, u32[]{:S(2)}, u32[]{:S(2)}) collective-permute-start(bf16[24,1792]{1,0:T(8,128)(2,1)S(1)} %get-tuple-element.37), channel_id=1, source_target_pairs={{0,480},{1,481},{2,482},{3,483},{4,484},{5,485},{6,486},{7,487},{8... | collective-permute-start | bytes 258056 | tf_op jit(solution)/shard_map/ppermute | solution.py:45
  261.3 5.8 %collective-permute-start.22 = (bf16[24,1792]{1,0:T(8,128)(2,1)S(1)}, bf16[24,1792]{1,0:T(8,128)(2,1)S(1)}, u32[]{:S(2)}, u32[]{:S(2)}) collective-permute-start(bf16[24,1792]{1,0:T(8,128)(2,1)S(1)} %get-tuple-element.40), channel_id=1, source_target_pairs={{0,504},{1,505},{2,506},{3,507},{4,508},{5,509},{6,510},{7,511},{8... | collective-permute-start | bytes 258056 | tf_op jit(solution)/shard_map/ppermute | solution.py:45
  267.2 9.6 %collective-permute-start.23 = (bf16[24,1792]{1,0:T(8,128)(2,1)S(1)}, bf16[24,1792]{1,0:T(8,128)(2,1)S(1)}, u32[]{:S(2)}, u32[]{:S(2)}) collective-permute-start(bf16[24,1792]{1,0:T(8,128)(2,1)S(1)} %get-tuple-element.39), channel_id=1, source_target_pairs={{0,496},{1,497},{2,498},{3,499},{4,500},{5,501},{6,502},{7,503},{8... | collective-permute-start | bytes 258056 | tf_op jit(solution)/shard_map/ppermute | solution.py:45
  276.8 4.6 %collective-permute-start.24 = (bf16[24,1792]{1,0:T(8,128)(2,1)S(1)}, bf16[24,1792]{1,0:T(8,128)(2,1)S(1)}, u32[]{:S(2)}, u32[]{:S(2)}) collective-permute-start(bf16[24,1792]{1,0:T(8,128)(2,1)S(1)} %get-tuple-element.38), channel_id=1, source_target_pairs={{0,488},{1,489},{2,490},{3,491},{4,492},{5,493},{6,494},{7,495},{8... | collective-permute-start | bytes 258056 | tf_op jit(solution)/shard_map/ppermute | solution.py:45
  281.5 0.8 fusion.46
  282.3 8.4 %collective-permute-done.23 = bf16[24,1792]{1,0:T(8,128)(2,1)S(1)} collective-permute-done((bf16[24,1792]{1,0:T(8,128)(2,1)S(1)}, bf16[24,1792]{1,0:T(8,128)(2,1)S(1)}, u32[]{:S(2)}, u32[]{:S(2)}) %collective-permute-start.23) | collective-permute-done | bytes 86048 | tf_op jit(solution)/shard_map/ppermute | solution.py:45
  291.2 0.9 fusion.50
  (130 shorter events, 10.6 us)
Async XLA Ops:
  7.2 13.7 %copy-start.8 = (bf16[1,32,3584]{2,1,0:T(8,128)(2,1)S(1)}, bf16[1,32,3584]{2,1,0:T(8,128)(2,1)}, u32[]{:S(2)}) copy-start(bf16[1,32,3584]{2,1,0:T(8,128)(2,1)} %param.11) | copy-start | bytes 688132
  7.2 177.6 %all-gather.2.cloned.1.call-start = ((), (), s32[]{:S(2)}) async-start(), calls=%async_computation.1 | async-start | bytes 7798784 | tf_op jit(solution)/shard_map/all_gather | solution.py:104
  9.1 36.7 %copy-start.19 = (s32[1,32,1]{1,2,0:T(1,128)S(1)}, s32[1,32,1]{1,2,0:T(1,128)}, u32[]{:S(2)}) copy-start(s32[1,32,1]{1,2,0:T(1,128)} %param.20) | copy-start | bytes 388
  9.1 37.0 %copy-start.7 = (bf16[1,32,3584]{2,1,0:T(8,128)(2,1)S(1)}, bf16[1,32,3584]{2,1,0:T(8,128)(2,1)}, u32[]{:S(2)}) copy-start(bf16[1,32,3584]{2,1,0:T(8,128)(2,1)} %param.12) | copy-start | bytes 688132
  9.1 37.2 %copy-start.22 = (s32[1,32,1]{1,2,0:T(1,128)S(1)}, s32[1,32,1]{1,2,0:T(1,128)}, u32[]{:S(2)}) copy-start(s32[1,32,1]{1,2,0:T(1,128)} %param.21) | copy-start | bytes 388
  9.1 47.0 %copy-start.15 = (s32[1,32,1]{1,2,0:T(1,128)S(1)}, s32[1,32,1]{1,2,0:T(1,128)}, u32[]{:S(2)}) copy-start(s32[1,32,1]{1,2,0:T(1,128)} %param.18) | copy-start | bytes 388
  9.1 47.0 %copy-start.23 = (s32[1,32,1]{1,2,0:T(1,128)S(1)}, s32[1,32,1]{1,2,0:T(1,128)}, u32[]{:S(2)}) copy-start(s32[1,32,1]{1,2,0:T(1,128)} %param.19) | copy-start | bytes 388
  9.1 58.5 %copy-start.1 = (bf16[1,3584,128]{2,1,0:T(8,128)(2,1)S(1)}, bf16[1,3584,128]{2,1,0:T(8,128)(2,1)}, u32[]{:S(2)}) copy-start(bf16[1,3584,128]{2,1,0:T(8,128)(2,1)} %param.15) | copy-start | bytes 2752516
  9.2 60.8 %copy-start = (bf16[1,3584,128]{2,1,0:T(8,128)(2,1)S(1)}, bf16[1,3584,128]{2,1,0:T(8,128)(2,1)}, u32[]{:S(2)}) copy-start(bf16[1,3584,128]{2,1,0:T(8,128)(2,1)} %param.16) | copy-start | bytes 2752516
  9.2 63.2 %copy-start.2 = (bf16[1,128,3584]{2,1,0:T(8,128)(2,1)S(1)}, bf16[1,128,3584]{2,1,0:T(8,128)(2,1)}, u32[]{:S(2)}) copy-start(bf16[1,128,3584]{2,1,0:T(8,128)(2,1)} %param.17) | copy-start | bytes 2752516
  9.2 164.0 %collective-permute-start.16 = (bf16[32,7168]{1,0:T(8,128)(2,1)}, bf16[32,7168]{1,0:T(8,128)(2,1)}, u32[]{:S(2)}, u32[]{:S(2)}) collective-permute-start(bf16[32,7168]{1,0:T(8,128)(2,1)} %pad_maximum_fusion.5), channel_id=1, source_target_pairs={{0,480},{32,0},{64,32},{96,64},{128,96},{160,128},{192,160},{224,1... | collective-permute-start | bytes 1376264 | tf_op jit(solution)/shard_map/ppermute | solution.py:14
  19.7 1.2 copy-start.11
  22.1 47.8 %collective-permute-start.2 = (bf16[24,1792]{1,0:T(8,128)(2,1)}, bf16[24,1792]{1,0:T(8,128)(2,1)S(1)}, u32[]{:S(2)}, u32[]{:S(2)}) collective-permute-start(bf16[24,1792]{1,0:T(8,128)(2,1)} %get-tuple-element.51), channel_id=1, source_target_pairs={{0,8},{1,9},{2,10},{3,11},{4,12},{5,13},{6,14},{7,15},{8,16},{9,17... | collective-permute-start | bytes 258056 | tf_op jit(solution)/shard_map/ppermute | solution.py:114
  31.2 41.2 %collective-permute-start.3 = (bf16[24,1792]{1,0:T(8,128)(2,1)}, bf16[24,1792]{1,0:T(8,128)(2,1)S(1)}, u32[]{:S(2)}, u32[]{:S(2)}) collective-permute-start(bf16[24,1792]{1,0:T(8,128)(2,1)} %get-tuple-element.50), channel_id=1, source_target_pairs={{0,16},{1,17},{2,18},{3,19},{4,20},{5,21},{6,22},{7,23},{8,24},{9,... | collective-permute-start | bytes 258056 | tf_op jit(solution)/shard_map/ppermute | solution.py:114
  40.3 34.0 %collective-permute-start.4 = (bf16[24,1792]{1,0:T(8,128)(2,1)}, bf16[24,1792]{1,0:T(8,128)(2,1)S(1)}, u32[]{:S(2)}, u32[]{:S(2)}) collective-permute-start(bf16[24,1792]{1,0:T(8,128)(2,1)} %get-tuple-element.49), channel_id=1, source_target_pairs={{0,24},{1,25},{2,26},{3,27},{4,28},{5,29},{6,30},{7,31},{8,0},{9,1... | collective-permute-start | bytes 258056 | tf_op jit(solution)/shard_map/ppermute | solution.py:114
  47.0 107.2 %all-to-all-start = ((f32[16,1,96]{2,1,0:T(1,128)}), f32[16,1,96]{2,1,0:T(1,128)S(1)}, u32[]{:S(2)}, u32[]{:S(2)}) async-start(f32[16,1,96]{2,1,0:T(1,128)} %broadcast_in_dim.13), calls=%async_computation | async-start | bytes 16384 | tf_op jit(solution)/shard_map/all_to_all | solution.py:128
  53.5 5.4 %collective-permute-start.17 = (s32[1,32]{1,0:T(1,128)S(1)}, s32[1,32]{1,0:T(1,128)S(1)}, u32[]{:S(2)}, u32[]{:S(2)}) collective-permute-start(s32[1,32]{1,0:T(1,128)S(1)} %bitcast.68), channel_id=1, source_target_pairs={{0,480},{32,0},{64,32},{96,64},{128,96},{160,128},{192,160},{224,1... | collective-permute-start | bytes 392 | tf_op jit(solution)/shard_map/ppermute | solution.py:14
  58.9 8.7 %collective-permute-start.1 = (s32[1,64]{1,0:T(1,128)S(1)}, s32[1,64]{1,0:T(1,128)S(1)}, u32[]{:S(2)}, u32[]{:S(2)}) collective-permute-start(s32[1,64]{1,0:T(1,128)S(1)} %add_bitcast_fusion), channel_id=1, source_target_pairs={{0,32},{32,64},{64,96},{96,128},{128,160},{160,192},{192,224},{224... | collective-permute-start | bytes 776 | tf_op jit(solution)/shard_map/ppermute | solution.py:14
  67.6 39.7 %collective-permute-start.7 = (bf16[3584,128]{1,0:T(8,128)(2,1)S(1)}, bf16[3584,128]{1,0:T(8,128)(2,1)}, u32[]{:S(2)}, u32[]{:S(2)}) collective-permute-start(bf16[3584,128]{1,0:T(8,128)(2,1)S(1)} %bitcast.47), channel_id=1, source_target_pairs={{0,1},{1,0},{2,3},{3,2},{4,5},{5,4},{6,7},{7,6},{8,9},{9,8},{10,11... | collective-permute-start | bytes 2752520 | tf_op jit(solution)/shard_map/ppermute | solution.py:141
  69.9 43.5 %collective-permute-start.8 = (bf16[3584,128]{1,0:T(8,128)(2,1)S(1)}, bf16[3584,128]{1,0:T(8,128)(2,1)S(1)}, u32[]{:S(2)}, u32[]{:S(2)}) collective-permute-start(bf16[3584,128]{1,0:T(8,128)(2,1)S(1)} %bitcast.44), channel_id=1, source_target_pairs={{0,1},{1,0},{2,3},{3,2},{4,5},{5,4},{6,7},{7,6},{8,9},{9,8},{10,11... | collective-permute-start | bytes 2752520 | tf_op jit(solution)/shard_map/ppermute | solution.py:142
  72.4 31.3 %collective-permute-start.9 = (bf16[128,3584]{1,0:T(8,128)(2,1)S(1)}, bf16[128,3584]{1,0:T(8,128)(2,1)S(1)}, u32[]{:S(2)}, u32[]{:S(2)}) collective-permute-start(bf16[128,3584]{1,0:T(8,128)(2,1)S(1)} %bitcast.50), channel_id=1, source_target_pairs={{0,1},{1,0},{2,3},{3,2},{4,5},{5,4},{6,7},{7,6},{8,9},{9,8},{10,11... | collective-permute-start | bytes 2752520 | tf_op jit(solution)/shard_map/ppermute | solution.py:143
  75.2 25.1 %collective-permute-start.5 = (bf16[96,1792]{1,0:T(8,128)(2,1)S(1)}, bf16[96,1792]{1,0:T(8,128)(2,1)S(1)}, u32[]{:S(2)}, u32[]{:S(2)}) collective-permute-start(bf16[96,1792]{1,0:T(8,128)(2,1)S(1)} %pad_maximum_fusion.6), channel_id=1, source_target_pairs={{0,4},{1,5},{2,6},{3,7},{4,0},{5,1},{6,2},{7,3},{8,12},{9,13},{10,... | collective-permute-start | bytes 1032200 | tf_op jit(solution)/shard_map/ppermute | solution.py:116
  100.3 53.2 %collective-permute-start.25 = (f32[1,3584]{1,0:T(1,128)}, f32[1,3584]{1,0:T(1,128)S(1)}, u32[]{:S(2)}, u32[]{:S(2)}) collective-permute-start(f32[1,3584]{1,0:T(1,128)} %param.14), channel_id=1, source_target_pairs={{0,480},{32,0},{64,32},{96,64},{128,96},{160,128},{192,160},{224,1... | collective-permute-start | bytes 43016 | tf_op jit(solution)/shard_map/ppermute | solution.py:14
  103.7 3.6 %copy-start.13 = (bf16[192,1792]{1,0:T(8,128)(2,1)S(1)}, bf16[192,1792]{1,0:T(8,128)(2,1)}, u32[]{:S(2)}) copy-start(bf16[192,1792]{1,0:T(8,128)(2,1)} %get-tuple-element.45) | copy-start | bytes 2064388
  103.7 177.8 %collective-permute-start = (bf16[32,3584]{1,0:T(8,128)(2,1)S(1)}, bf16[32,3584]{1,0:T(8,128)(2,1)S(1)}, u32[]{:S(2)}, u32[]{:S(2)}) collective-permute-start(bf16[32,3584]{1,0:T(8,128)(2,1)S(1)} %bitcast.54), channel_id=1, source_target_pairs={{0,32},{32,64},{64,96},{96,128},{128,160},{160,192},{192,224},{224... | collective-permute-start | bytes 688136 | tf_op jit(solution)/shard_map/ppermute | solution.py:14
  107.3 36.4 %collective-permute-start.6 = (bf16[192,1792]{1,0:T(8,128)(2,1)S(1)}, bf16[192,1792]{1,0:T(8,128)(2,1)S(1)}, u32[]{:S(2)}, u32[]{:S(2)}) collective-permute-start(bf16[192,1792]{1,0:T(8,128)(2,1)S(1)} %copy-done.13), channel_id=1, source_target_pairs={{0,2},{1,3},{2,0},{3,1},{4,6},{5,7},{6,4},{7,5},{8,10},{9,11},{10,... | collective-permute-start | bytes 2064392 | tf_op jit(solution)/shard_map/ppermute | solution.py:117
  115.2 0.7 copy-start.12
  115.9 27.9 %copy-start.3 = (bf16[1792,1024]{1,0:T(8,128)(2,1)}, bf16[1792,1024]{1,0:T(8,128)(2,1)S(1)}, u32[]{:S(2)}) copy-start(bf16[1792,1024]{1,0:T(8,128)(2,1)S(1)} %pad_maximum_fusion.1) | copy-start | bytes 11010052
  120.1 23.6 %copy-start.14 = (bf16[384,1792]{1,0:T(8,128)(2,1)S(1)}, bf16[384,1792]{1,0:T(8,128)(2,1)}, u32[]{:S(2)}) copy-start(bf16[384,1792]{1,0:T(8,128)(2,1)} %get-tuple-element.46) | copy-start | bytes 4128772
  146.5 1.1 copy-start.6
  147.6 18.0 %collective-permute-start.10 = (bf16[192,1792]{1,0:T(8,128)(2,1)S(1)}, bf16[192,1792]{1,0:T(8,128)(2,1)S(1)}, u32[]{:S(2)}, u32[]{:S(2)}) collective-permute-start(bf16[192,1792]{1,0:T(8,128)(2,1)S(1)} %slice.202), channel_id=1, source_target_pairs={{0,2},{1,3},{2,0},{3,1},{4,6},{5,7},{6,4},{7,5},{8,10},{9,11},{10,... | collective-permute-start | bytes 2064392 | tf_op jit(solution)/shard_map/ppermute | solution.py:170
  154.2 11.5 %copy-start.9 = (f32[16,1,96]{2,1,0:T(1,128)}, f32[16,1,96]{2,1,0:T(1,128)S(1)}, u32[]{:S(2)}) copy-start(f32[16,1,96]{2,1,0:T(1,128)S(1)} %all-to-all-done) | copy-start | bytes 18436
  166.9 17.8 %collective-permute-start.11 = (bf16[96,1792]{1,0:T(8,128)(2,1)S(1)}, bf16[96,1792]{1,0:T(8,128)(2,1)S(1)}, u32[]{:S(2)}, u32[]{:S(2)}) collective-permute-start(bf16[96,1792]{1,0:T(8,128)(2,1)S(1)} %slice.204), channel_id=1, source_target_pairs={{0,4},{1,5},{2,6},{3,7},{4,0},{5,1},{6,2},{7,3},{8,12},{9,13},{10,... | collective-permute-start | bytes 1032200 | tf_op jit(solution)/shard_map/ppermute | solution.py:171
  184.8 5.5 %copy-start.5 = (bf16[256,3584]{1,0:T(8,128)(2,1)S(1)}, bf16[256,3584]{1,0:T(8,128)(2,1)}, u32[]{:S(2)}) copy-start(bf16[256,3584]{1,0:T(8,128)(2,1)} %pad_maximum_fusion.2) | copy-start | bytes 5505028
  184.8 5.4 %copy-start.16 = (f32[512]{0:T(512)S(1)}, f32[512]{0:T(512)}, u32[]{:S(2)}) copy-start(f32[512]{0:T(512)} %mul.221) | copy-start | bytes 6148
  184.8 5.8 %copy-start.21 = (bf16[512,7168]{1,0:T(8,128)(2,1)S(1)}, bf16[512,7168]{1,0:T(8,128)(2,1)}, u32[]{:S(2)}) copy-start(bf16[512,7168]{1,0:T(8,128)(2,1)} %all-gather.2.cloned.1.call-done) | copy-start | bytes 22020100
  190.6 1.4 copy-start.18
  190.6 1.8 copy-start.17
  192.0 23.5 %copy-start.4 = (bf16[1792,1024]{1,0:T(8,128)(2,1)S(1)}, bf16[1792,1024]{1,0:T(8,128)(2,1)}, u32[]{:S(2)}) copy-start(bf16[1792,1024]{1,0:T(8,128)(2,1)} %copy-done.3) | copy-start | bytes 11010052
  192.9 24.4 %collective-permute-start.12 = (bf16[24,1792]{1,0:T(8,128)(2,1)S(1)}, bf16[24,1792]{1,0:T(8,128)(2,1)S(1)}, u32[]{:S(2)}, u32[]{:S(2)}) collective-permute-start(bf16[24,1792]{1,0:T(8,128)(2,1)S(1)} %get-tuple-element.41), channel_id=1, source_target_pairs={{0,32},{1,33},{2,34},{3,35},{4,36},{5,37},{6,38},{7,39},{8,40},{9,... | collective-permute-start | bytes 258056 | tf_op jit(solution)/shard_map/ppermute | solution.py:45
  194.9 24.2 %collective-permute-start.13 = (bf16[24,1792]{1,0:T(8,128)(2,1)S(1)}, bf16[24,1792]{1,0:T(8,128)(2,1)S(1)}, u32[]{:S(2)}, u32[]{:S(2)}) collective-permute-start(bf16[24,1792]{1,0:T(8,128)(2,1)S(1)} %get-tuple-element.44), channel_id=1, source_target_pairs={{0,56},{1,57},{2,58},{3,59},{4,60},{5,61},{6,62},{7,63},{8,32},{9,... | collective-permute-start | bytes 258056 | tf_op jit(solution)/shard_map/ppermute | solution.py:45
  200.5 24.3 %collective-permute-start.14 = (bf16[24,1792]{1,0:T(8,128)(2,1)S(1)}, bf16[24,1792]{1,0:T(8,128)(2,1)S(1)}, u32[]{:S(2)}, u32[]{:S(2)}) collective-permute-start(bf16[24,1792]{1,0:T(8,128)(2,1)S(1)} %get-tuple-element.43), channel_id=1, source_target_pairs={{0,48},{1,49},{2,50},{3,51},{4,52},{5,53},{6,54},{7,55},{8,56},{9,... | collective-permute-start | bytes 258056 | tf_op jit(solution)/shard_map/ppermute | solution.py:45
  209.2 21.6 %collective-permute-start.15 = (bf16[24,1792]{1,0:T(8,128)(2,1)S(1)}, bf16[24,1792]{1,0:T(8,128)(2,1)S(1)}, u32[]{:S(2)}, u32[]{:S(2)}) collective-permute-start(bf16[24,1792]{1,0:T(8,128)(2,1)S(1)} %get-tuple-element.42), channel_id=1, source_target_pairs={{0,40},{1,41},{2,42},{3,43},{4,44},{5,45},{6,46},{7,47},{8,48},{9,... | collective-permute-start | bytes 258056 | tf_op jit(solution)/shard_map/ppermute | solution.py:45
  217.1 13.6 %copy-start.25 = (s32[64]{0:T(128)S(1)}, s32[64]{0:T(128)}, u32[]{:S(2)}) copy-start(s32[64]{0:T(128)} %pad_add_fusion) | copy-start | bytes 772
  217.2 25.0 %collective-permute-start.18 = (bf16[96,1792]{1,0:T(8,128)(2,1)S(1)}, bf16[96,1792]{1,0:T(8,128)(2,1)S(1)}, u32[]{:S(2)}, u32[]{:S(2)}) collective-permute-start(bf16[96,1792]{1,0:T(8,128)(2,1)S(1)} %get-tuple-element.30), channel_id=1, source_target_pairs={{0,6},{1,7},{2,0},{3,1},{4,2},{5,3},{6,4},{7,5},{8,14},{9,15},{10,... | collective-permute-start | bytes 1032200 | tf_op jit(solution)/shard_map/ppermute | solution.py:191
  219.2 28.7 %collective-permute-start.19 = (bf16[96,1792]{1,0:T(8,128)(2,1)S(1)}, bf16[96,1792]{1,0:T(8,128)(2,1)S(1)}, u32[]{:S(2)}, u32[]{:S(2)}) collective-permute-start(bf16[96,1792]{1,0:T(8,128)(2,1)S(1)} %get-tuple-element.32), channel_id=1, source_target_pairs={{0,4},{1,5},{2,6},{3,7},{4,0},{5,1},{6,2},{7,3},{8,12},{9,13},{10,... | collective-permute-start | bytes 1032200 | tf_op jit(solution)/shard_map/ppermute | solution.py:191
  224.8 29.8 %collective-permute-start.20 = (bf16[96,1792]{1,0:T(8,128)(2,1)S(1)}, bf16[96,1792]{1,0:T(8,128)(2,1)S(1)}, u32[]{:S(2)}, u32[]{:S(2)}) collective-permute-start(bf16[96,1792]{1,0:T(8,128)(2,1)S(1)} %get-tuple-element.31), channel_id=1, source_target_pairs={{0,2},{1,3},{2,4},{3,5},{4,6},{5,7},{6,0},{7,1},{8,10},{9,11},{10,... | collective-permute-start | bytes 1032200 | tf_op jit(solution)/shard_map/ppermute | solution.py:191
  231.0 50.4 %copy-start.20 = (f32[32]{0:T(128)S(1)}, f32[32]{0:T(128)}, u32[]{:S(2)}) copy-start(f32[32]{0:T(128)} %multiply_bitcast_fusion.1) | copy-start | bytes 388
  231.1 59.6 %copy-start.24 = (s32[64]{0:T(128)S(1)}, s32[64]{0:T(128)}, u32[]{:S(2)}) copy-start(s32[64]{0:T(128)} %pad_add_fusion.2) | copy-start | bytes 772
  254.7 36.3 %copy-start.10 = (f32[3584]{0:T(1024)S(1)}, f32[3584]{0:T(1024)}, u32[]{:S(2)}) copy-start(f32[3584]{0:T(1024)} %reduce.1) | copy-start | bytes 43012
  254.8 27.5 %collective-permute-start.21 = (bf16[24,1792]{1,0:T(8,128)(2,1)S(1)}, bf16[24,1792]{1,0:T(8,128)(2,1)S(1)}, u32[]{:S(2)}, u32[]{:S(2)}) collective-permute-start(bf16[24,1792]{1,0:T(8,128)(2,1)S(1)} %get-tuple-element.37), channel_id=1, source_target_pairs={{0,480},{1,481},{2,482},{3,483},{4,484},{5,485},{6,486},{7,487},{8... | collective-permute-start | bytes 258056 | tf_op jit(solution)/shard_map/ppermute | solution.py:45
  261.3 20.9 %collective-permute-start.22 = (bf16[24,1792]{1,0:T(8,128)(2,1)S(1)}, bf16[24,1792]{1,0:T(8,128)(2,1)S(1)}, u32[]{:S(2)}, u32[]{:S(2)}) collective-permute-start(bf16[24,1792]{1,0:T(8,128)(2,1)S(1)} %get-tuple-element.40), channel_id=1, source_target_pairs={{0,504},{1,505},{2,506},{3,507},{4,508},{5,509},{6,510},{7,511},{8... | collective-permute-start | bytes 258056 | tf_op jit(solution)/shard_map/ppermute | solution.py:45
  267.2 23.5 %collective-permute-start.23 = (bf16[24,1792]{1,0:T(8,128)(2,1)S(1)}, bf16[24,1792]{1,0:T(8,128)(2,1)S(1)}, u32[]{:S(2)}, u32[]{:S(2)}) collective-permute-start(bf16[24,1792]{1,0:T(8,128)(2,1)S(1)} %get-tuple-element.39), channel_id=1, source_target_pairs={{0,496},{1,497},{2,498},{3,499},{4,500},{5,501},{6,502},{7,503},{8... | collective-permute-start | bytes 258056 | tf_op jit(solution)/shard_map/ppermute | solution.py:45
  276.8 13.9 %collective-permute-start.24 = (bf16[24,1792]{1,0:T(8,128)(2,1)S(1)}, bf16[24,1792]{1,0:T(8,128)(2,1)S(1)}, u32[]{:S(2)}, u32[]{:S(2)}) collective-permute-start(bf16[24,1792]{1,0:T(8,128)(2,1)S(1)} %get-tuple-element.38), channel_id=1, source_target_pairs={{0,488},{1,489},{2,490},{3,491},{4,492},{5,493},{6,494},{7,495},{8... | collective-permute-start | bytes 258056 | tf_op jit(solution)/shard_map/ppermute | solution.py:45
Sparse Core Ops, SparseCore 0:
  10.1 140.3 all-gather.1

commit v6 on v3

v6 whole, which is shorter than its diff:
```python
import jax
import jax.numpy as jnp
from jax import lax
from jax.sharding import PartitionSpec as P

EXPERTS = 4
CAP = 12
EPSILON = 1e-06


def passed_along(value, axis, steps):
    count = lax.axis_size(axis)
    pairs = [(source, (source + steps) % count) for source in range(count)]
    return lax.ppermute(value, axis, pairs)


def rms_scale(values):
    return lax.rsqrt(jnp.mean(values * values, axis=-1, keepdims=True) + EPSILON)


def dot(a, b, dims):
    return lax.dot_general(a, b, (dims, ((), ())), preferred_element_type=jnp.float32)


def slots_of(route):
    onehot = (route[:, None] == jnp.arange(EXPERTS, dtype=jnp.int32)[None, :]).astype(jnp.int32)
    rank = jnp.sum(jnp.cumsum(onehot, axis=0) * onehot, axis=1) - 1
    return route * CAP + rank


def half_places(slot):
    expert, rank = slot // CAP, slot % CAP
    base = expert * (2 * CAP) + rank
    return [base + h * CAP for h in range(2)]


def pick_back(table, slot):
    rows = table.reshape(-1, table.shape[-1])
    count = rows.shape[0]
    halves = []
    for place in half_places(slot):
        pick = (place[:, None] == jnp.arange(count, dtype=jnp.int32)[None, :]).astype(jnp.bfloat16)
        halves.append(dot(pick, rows, ((1,), (0,))))
    return jnp.concatenate(halves, axis=1)


def group_to_section(value, sections, count, side, steps, hop):
    pairs = []
    for s in range(sections):
        for d in range(count):
            chip, core = d // 2, d % 2
            chip = chip // side * side + (chip % side + hop) % side
            pairs.append((s * count + d, (s + steps) % sections * count + 2 * chip + core))
    return lax.ppermute(value, ("section", "expert"), pairs)


def packers(slots, me_expert, first_place, tokens, side, turn):
    count = slots.shape[0]
    sources = count // tokens
    groups = sources // side
    expert, rank = slots // CAP, slots % CAP
    source = jnp.arange(count, dtype=jnp.int32) // tokens
    place = (turn * (source % side - first_place)) % side
    base = (place * groups + source // side) * (2 * CAP) + rank
    base = jnp.where(expert == me_expert, base, -2 * CAP)
    row = jnp.arange(sources * 2 * CAP, dtype=jnp.int32)[:, None]
    return [(base[None, :] + h * CAP == row).astype(jnp.bfloat16) for h in range(2)]


def pack(places, hidden):
    parts = [dot(place, hidden, ((1,), (0,))).astype(jnp.bfloat16) for place in places]
    return jnp.concatenate(parts, axis=1)


def across_groups(rows, across):
    return lax.all_to_all(
        rows.reshape(EXPERTS, 2 * CAP, rows.shape[1]),
        "expert",
        split_axis=0,
        concat_axis=0,
        tiled=True,
        axis_index_groups=across,
    )


def per_device(
    x_fwd,
    x_bwd,
    grad_out,
    norm_gain,
    w_gate,
    w_up,
    w_down,
    route_fwd,
    gate_fwd,
    route_bwd,
    gate_bwd,
):
    sections = lax.axis_size("section")
    count = lax.axis_size("expert")
    ring = count // 2
    side = ring // EXPERTS
    same_core = [[2 * z + c for z in range(ring)] for c in range(2)]
    within = [[2 * (side * g + j) + c for j in range(side)] for g in range(EXPERTS) for c in range(2)]
    across = [[2 * (side * g + j) + c for g in range(EXPERTS)] for j in range(side) for c in range(2)]
    swap = [(i, i ^ 1) for i in range(count)]
    index = lax.axis_index("expert")
    me_expert = index // (2 * side)
    me_place = (index // 2) % side

    gain = norm_gain[0]
    tokens, width = x_fwd.shape[1:]
    half = width // 2
    sent_b = jnp.concatenate([x_bwd[0], grad_out[0]], axis=1)
    sent = jnp.concatenate([x_fwd[0], x_bwd[0], grad_out[0]], axis=1)
    got = lax.all_gather(sent, "expert", axis=0, tiled=True, axis_index_groups=same_core)

    xf = x_fwd[0].astype(jnp.float32)
    xb = x_bwd[0].astype(jnp.float32)
    scale_f = gate_fwd[0].astype(jnp.float32) / 256.0
    slot_f = slots_of(route_fwd[0, :, 0])
    slot_b = slots_of(route_bwd[0, :, 0])
    small = jnp.concatenate(
        [
            slot_f.astype(jnp.float32),
            slot_b.astype(jnp.float32),
            rms_scale(xf)[:, 0],
            rms_scale(xb)[:, 0],
            gate_bwd[0, :, 0].astype(jnp.float32) / 256.0,
        ]
    )
    small = lax.all_to_all(
        jnp.broadcast_to(small[None, None, :], (ring, 1, 5 * tokens)),
        "expert",
        split_axis=0,
        concat_axis=0,
        tiled=True,
        axis_index_groups=same_core,
    )[:, 0]
    slots_f, slots_b, rs_f, rs_b, scales_b = [
        small[:, i * tokens : (i + 1) * tokens].reshape(ring * tokens) for i in range(5)
    ]
    slots_f = slots_f.astype(jnp.int32)
    slots_b = slots_b.astype(jnp.int32)
    places_f = packers(slots_f, me_expert, 0, tokens, side, 1)
    places_b = packers(slots_b, me_expert, me_place, tokens, side, -1)

    gate_o = lax.ppermute(w_gate[0], "expert", swap)
    up_o = lax.ppermute(w_up[0], "expert", swap)
    down_o = lax.ppermute(w_down[0], "expert", swap)
    w_in = jnp.concatenate([w_gate[0], gate_o, w_up[0], up_o], axis=1)
    w_gained = (w_in.astype(jnp.float32) * gain[:, None]).astype(jnp.bfloat16)
    w_dn = jnp.concatenate([w_down[0], down_o], axis=0)
    hid = w_dn.shape[0]
    dn_stack = jnp.concatenate([w_dn[:, :half], w_dn[:, half:]], axis=0)
    in_stack = jnp.concatenate([w_in[:half], w_in[half:]], axis=1)
    w_gained, w_dn, in_stack, dn_stack = lax.optimization_barrier(
        (w_gained, w_dn, in_stack, dn_stack)
    )

    last_b = passed_along(sent_b, "section", -1).astype(jnp.float32)
    last_gain = passed_along(norm_gain, "section", -1)
    last_slot = passed_along(slot_b[None, :], "section", -1)[0]

    pre_f = dot(got[:, :width], w_gained, ((1,), (0,))) * rs_f[:, None]
    act = (jax.nn.silu(pre_f[:, :hid]) * pre_f[:, hid:]).astype(jnp.bfloat16)
    part_f = dot(pack(places_f, act), dn_stack, ((1,), (0,))).astype(jnp.bfloat16)
    got, part_f = lax.optimization_barrier((got, part_f))
    total_f = lax.psum_scatter(
        part_f, "expert", scatter_dimension=0, tiled=True, axis_index_groups=within
    )

    pre_b = dot(got[:, width : 2 * width], w_gained, ((1,), (0,))) * rs_b[:, None]
    d_act = dot(got[:, 2 * width :], w_dn, ((1,), (1,))) * scales_b[:, None]
    gate, up = pre_b[:, :hid], pre_b[:, hid:]
    sig = jax.nn.sigmoid(gate)
    d_gate = (d_act * up * sig * (1.0 + gate * (1.0 - sig))).astype(jnp.bfloat16)
    d_up = (d_act * gate * sig).astype(jnp.bfloat16)
    hidden_b = pack(places_b, jnp.concatenate([d_gate, d_up], axis=1))
    part_b = dot(hidden_b, in_stack, ((1,), (1,))).astype(jnp.bfloat16)
    rows = part_b.shape[0] // side
    total_b = sum(
        group_to_section(
            part_b[k * rows : (k + 1) * rows], sections, count, side, -1, -k
        ).astype(jnp.float32)
        for k in range(side)
    ).astype(jnp.bfloat16)

    table_f = across_groups(total_f, across)
    seen = table_f[0, 0, 0].astype(jnp.float32)
    total_b = jnp.where((seen > 1.0) & (seen < -1.0), 0, total_b)
    moe_f = pick_back(table_f, slot_f)
    y = (xf + scale_f * moe_f).astype(jnp.bfloat16)
    y_next = passed_along(y, "section", 1)

    d_normed = pick_back(across_groups(total_b, across), last_slot)
    last_x, last_g = last_b[:, :width], last_b[:, width:]
    r = rms_scale(last_x)
    weighted = d_normed * last_gain
    inner = jnp.mean(last_x * weighted, axis=-1, keepdims=True)
    dx_prev = (last_g + (r * weighted - last_x * r * r * r * inner)).astype(jnp.bfloat16)
    return (y_next[None], dx_prev[None])


def solution(mesh):
    in_specs = (
        P("section", "expert", None),
        P("section", "expert", None),
        P("section", "expert", None),
        P("section", None),
        P("section", None, "expert"),
        P("section", None, "expert"),
        P("section", "expert", None),
        P("section", "expert", None),
        P("section", "expert", None),
        P("section", "expert", None),
        P("section", "expert", None),
    )
    out_specs = (P("section", "expert", None), P("section", "expert", None))
    return jax.shard_map(
        per_device, mesh=mesh, in_specs=in_specs, out_specs=out_specs, check_vma=False
    )
```

time: 284 us -> 296 us (1.042)
  starting transfers between devices: 49.1 us -> 69.7 us
  waiting for transfers between devices: 176 us -> 158 us
  other arithmetic: 20.4 us -> 25.1 us
    all_to_all x1 -> x2, waiting for transfers between devices: 26.9 us -> 3.3 us  [across_groups(): lax.all_to_all(rows.reshape(EXPERTS, 2 * CAP, rows.shape[1]), 'expert', s...]
    reduce_scatter x1, waiting for transfers between devices: 8.22 us -> 29 us  [per_device(): lax.psum_scatter(part_f, 'expert', scatter_dimension=0, tiled=True, axis_...]
    ppermute x3 -> x4, waiting for transfers between devices: 35.4 us -> 26.7 us  [group_to_section(): return lax.ppermute(value, ('section', 'expert'), pairs)]
    all_to_all x1 -> x2, starting transfers between devices: 11.5 us -> 19.4 us  [across_groups(): lax.all_to_all(rows.reshape(EXPERTS, 2 * CAP, rows.shape[1]), 'expert', s...]
    ppermute x2 -> x4, starting transfers between devices: 7.46 us -> 14.2 us  [passed_along(): return lax.ppermute(value, axis, pairs)]
    ppermute x3 -> x4, starting transfers between devices: 8.64 us -> 14.6 us  [group_to_section(): return lax.ppermute(value, ('section', 'expert'), pairs)]
    ppermute x2 -> x4, waiting for transfers between devices: 6.9 us -> 2.98 us  [passed_along(): return lax.ppermute(value, axis, pairs)]
    dot_general x9 -> x13, matrix products: 19.7 us -> 21.1 us  [dot(): lax.dot_general(a, b, (dims, ((), ())), preferred_element_type=jnp.float32)]
  transfers between devices with their start and end apart: 12 -> 16, of which waited for: 7 -> 7; matrix products, arithmetic and copies ran while one was open for 11% -> 13% of each run, Pallas kernels for 0% -> 0%
where the time goes in v6:
time: 296 us; the launch traced here: 294 us
  waiting for transfers between devices  158 us (53%)
  starting transfers between devices  69.7 us (24%)
  other arithmetic  25.1 us (8%)
  matrix products  21.1 us (7%)
  between operations  15.8 us (5%)
  local copies, waits for them, and re-layouts  3.95 us (1%)
    all_gather x1, waiting for transfers between devices, per_device(): lax.all_gather(sent, 'expert', axis=0, tiled=True, axis_index_groups=same...  90.9 us
    reduce_scatter x1, waiting for transfers between devices, per_device(): lax.psum_scatter(part_f, 'expert', scatter_dimension=0, tiled=True, axis_...  29 us
    ppermute x4, waiting for transfers between devices, group_to_section(): return lax.ppermute(value, ('section', 'expert'), pairs)  26.7 us
    dot_general x13, matrix products, dot(): lax.dot_general(a, b, (dims, ((), ())), preferred_element_type=jnp.float32)  21.1 us
    all_to_all x2, starting transfers between devices, across_groups(): lax.all_to_all(rows.reshape(EXPERTS, 2 * CAP, rows.shape[1]), 'expert', s...  19.4 us
    all_to_all x1, starting transfers between devices, per_device(): lax.all_to_all(jnp.broadcast_to(small[None, None, :], (ring, 1, 5 * token...  15.2 us
    ppermute x4, starting transfers between devices, group_to_section(): return lax.ppermute(value, ('section', 'expert'), pairs)  14.6 us
    ppermute x4, starting transfers between devices, passed_along(): return lax.ppermute(value, axis, pairs)  14.2 us
  transfers between devices with their start and end apart: 16, of which 7 were waited for; matrix products, arithmetic and copies ran while one was open for 13% of the time, Pallas kernels for 0%

profile of v6, /device:TPU:6, one launch (start us, length us, event | category | flops | bytes accessed | tf_op | source)
XLA Modules:
  0.0 294.2 jit_solution(12728066303120833165)
XLA Ops:
  7.2 2.1 pad_maximum_fusion.4
  9.3 0.7 fusion.37
  10.1 0.7 fusion.36
  10.9 0.8 select_reduce_fusion.1
  11.7 0.8 select_reduce_fusion
  12.6 1.1 multiply_reduce_fusion.2
  13.7 1.1 fusion.24
  14.8 0.7 multiply_bitcast_fusion
  15.4 0.7 add_convert_fusion.1
  16.1 1.2 broadcast_add_fusion.2
  17.4 0.6 broadcast_in_dim.14
  18.1 15.2 %all-to-all-start = ((f32[16,1,160]{2,1,0:T(1,128)}), f32[16,1,160]{2,1,0:T(1,128)S(1)}, u32[]{:S(2)}, u32[]{:S(2)}) async-start(f32[16,1,160]{2,1,0:T(1,128)} %broadcast_in_dim.14), calls=%async_computation | async-start | bytes 32768 | tf_op jit(solution)/shard_map/all_to_all | solution.py:132
  33.3 1.9 collective-permute-start.2
  35.2 2.4 collective-permute-start
  37.6 1.9 collective-permute-start.1
  39.6 0.8 reduce
  40.4 5.6 %all-to-all-done = f32[16,1,160]{2,1,0:T(1,128)S(1)} async-done(((f32[16,1,160]{2,1,0:T(1,128)}), f32[16,1,160]{2,1,0:T(1,128)S(1)}, u32[]{:S(2)}, u32[]{:S(2)}) %all-to-all-start) | async-done | bytes 10272 | tf_op jit(solution)/shard_map/all_to_all | solution.py:132
  45.9 0.1 fusion.48
  46.2 0.1 ne.355
  46.5 1.4 fusion.15
  48.0 1.4 pad_maximum_fusion.3
  49.3 0.4 pad_maximum_fusion
  49.8 0.2 fusion.83
  50.0 2.4 pad_maximum_fusion.1
  52.4 1.4 pad_maximum_fusion.2
  53.8 2.8 multiply_convert_fusion
  56.6 90.9 %all-gather.2.cloned.1.call-done = bf16[512,10752]{1,0:T(8,128)(2,1)} async-done(((bf16[32,10752]{1,0:T(8,128)(2,1)}), bf16[512,10752]{1,0:T(8,128)(2,1)}) %all-gather.2.cloned.1.call-update) | async-done | bytes 11010064 | tf_op jit(solution)/shard_map/all_gather | solution.py:116
  147.5 5.2 %fusion.9 = f32[512,512]{1,0:T(8,128)S(1)} fusion(bf16[3584,512]{1,0:T(8,128)(2,1)} %multiply_convert_fusion, bf16[512,10752]{1,0:T(8,128)(2,1)} %all-gather.2.cloned.1.call-done, f32[512]{0:T(512)S(1)} %mul.244), kind=kOutput, calls=%fused_computation.18 | convolution fusion | flops 1879310336 | bytes 8390656 | tf_op jit(solution)/shard_map/dot_general | solution.py:22
  152.7 0.2 fusion.23
  152.9 0.3 convolution_convert_fusion.5
  153.2 0.3 convolution_convert_fusion.4
  153.5 2.0 convolution_convert_fusion
  155.9 5.3 %fusion.6 = f32[512,512]{1,0:T(8,128)S(1)} fusion(bf16[3584,512]{1,0:T(8,128)(2,1)} %multiply_convert_fusion, bf16[512,10752]{1,0:T(8,128)(2,1)} %all-gather.2.cloned.1.call-done, f32[512]{0:T(512)S(1)} %mul.261), kind=kOutput, calls=%fused_computation.17 | convolution fusion | flops 1879310336 | bytes 8390656 | tf_op jit(solution)/shard_map/dot_general | solution.py:22
  161.3 3.4 %fusion.22 = (bf16[512,256]{1,0:T(8,128)(2,1)S(1)}, bf16[512,256]{1,0:T(8,128)(2,1)S(1)}) fusion(f32[512,512]{1,0:T(8,128)S(1)} %fusion.6, f32[512]{0:T(512)S(1)} %mul.258, bf16[256,3584]{1,0:T(8,128)(2,1)S(1)} %copy-done.6, bf16[512,10752]{1,0:T(8,128)(2,1)} %all-gather.2.cloned.1.call-done), kind=kOutput, calls=%fused_computation.40 | convolution fusion | flops 941359104 | bytes 7079936 | tf_op jit(solution)/shard_map/dot_general | solution.py:22
  164.7 0.4 convolution_convert_fusion.3
  165.1 0.4 convolution_convert_fusion.2
  165.5 1.6 convolution_convert_fusion.1
  167.2 29.0 %reduce-scatter.2.cloned.1.call-done = bf16[96,1792]{1,0:T(8,128)(2,1)} async-done(((bf16[384,1792]{1,0:T(8,128)(2,1)}), bf16[96,1792]{1,0:T(8,128)(2,1)}) %reduce-scatter.2.cloned.1.call-update) | async-done | bytes 344080 | tf_op jit(solution)/shard_map/reduce_scatter | solution.py:169
  196.2 10.0 %all-to-all-start.1 = ((bf16[4,24,1792]{2,1,0:T(8,128)(2,1)}), bf16[4,24,1792]{2,1,0:T(8,128)(2,1)S(1)}, u32[]{:S(2)}, u32[]{:S(2)}) async-start(bf16[4,24,1792]{2,1,0:T(8,128)(2,1)} %bitcast.84), calls=%async_computation.2 | async-start | bytes 688128 | tf_op jit(solution)/shard_map/all_to_all | solution.py:76
  206.2 0.9 fusion.84
  207.1 4.9 %collective-permute-start.6 = (bf16[96,1792]{1,0:T(8,128)(2,1)}, bf16[96,1792]{1,0:T(8,128)(2,1)S(1)}, u32[]{:S(2)}, u32[]{:S(2)}) collective-permute-start(bf16[96,1792]{1,0:T(8,128)(2,1)} %get-tuple-element.30), channel_id=1, source_target_pairs={{0,480},{1,481},{2,482},{3,483},{4,484},{5,485},{6,486},{7,487},{8... | collective-permute-start | bytes 1032200 | tf_op jit(solution)/shard_map/ppermute | solution.py:54
  212.0 5.4 %collective-permute-start.7 = (bf16[96,1792]{1,0:T(8,128)(2,1)}, bf16[96,1792]{1,0:T(8,128)(2,1)S(1)}, u32[]{:S(2)}, u32[]{:S(2)}) collective-permute-start(bf16[96,1792]{1,0:T(8,128)(2,1)} %get-tuple-element.33), channel_id=1, source_target_pairs={{0,486},{1,487},{2,480},{3,481},{4,482},{5,483},{6,484},{7,485},{8... | collective-permute-start | bytes 1032200 | tf_op jit(solution)/shard_map/ppermute | solution.py:54
  217.4 1.9 collective-permute-start.8
  219.3 2.4 collective-permute-start.9
  221.9 3.7 %collective-permute-start.4 = (bf16[32,7168]{1,0:T(8,128)(2,1)S(1)}, bf16[32,7168]{1,0:T(8,128)(2,1)S(1)}, u32[]{:S(2)}, u32[]{:S(2)}) collective-permute-start(bf16[32,7168]{1,0:T(8,128)(2,1)S(1)} %pad_maximum_fusion.6), channel_id=1, source_target_pairs={{0,480},{32,0},{64,32},{96,64},{128,96},{160,128},{192,160},{224,1... | collective-permute-start | bytes 1376264 | tf_op jit(solution)/shard_map/ppermute | solution.py:14
  225.5 1.2 multiply_bitcast_fusion.1
  226.7 0.5 slice.105
  228.5 2.2 collective-permute-done.7
  230.8 24.5 %collective-permute-done.8 = bf16[96,1792]{1,0:T(8,128)(2,1)S(1)} collective-permute-done((bf16[96,1792]{1,0:T(8,128)(2,1)S(1)}, bf16[96,1792]{1,0:T(8,128)(2,1)S(1)}, u32[]{:S(2)}, u32[]{:S(2)}) %collective-permute-start.8) | collective-permute-done | bytes 344096 | tf_op jit(solution)/shard_map/ppermute | solution.py:54
  255.2 0.9 fusion.34
  256.1 9.4 %all-to-all-start.2 = ((bf16[4,24,1792]{2,1,0:T(8,128)(2,1)}), bf16[4,24,1792]{2,1,0:T(8,128)(2,1)S(1)}, u32[]{:S(2)}, u32[]{:S(2)}) async-start(bf16[4,24,1792]{2,1,0:T(8,128)(2,1)} %bitcast.19), calls=%async_computation.3 | async-start | bytes 688128 | tf_op jit(solution)/shard_map/all_to_all | solution.py:76
  265.5 0.9 fusion.38
  266.4 0.9 fusion.39
  267.3 0.8 fusion.25
  268.1 3.3 %collective-permute-start.3 = (bf16[32,3584]{1,0:T(8,128)(2,1)S(1)}, bf16[32,3584]{1,0:T(8,128)(2,1)S(1)}, u32[]{:S(2)}, u32[]{:S(2)}) collective-permute-start(bf16[32,3584]{1,0:T(8,128)(2,1)S(1)} %fusion.25), channel_id=1, source_target_pairs={{0,32},{32,64},{64,96},{96,128},{128,160},{160,192},{192,224},{224... | collective-permute-start | bytes 688136 | tf_op jit(solution)/shard_map/ppermute | solution.py:14
  271.5 4.6 %collective-permute-start.5 = (s32[1,32]{1,0:T(1,128)S(1)}, s32[1,32]{1,0:T(1,128)S(1)}, u32[]{:S(2)}, u32[]{:S(2)}) collective-permute-start(s32[1,32]{1,0:T(1,128)S(1)} %bitcast_add_fusion), channel_id=1, source_target_pairs={{0,480},{32,0},{64,32},{96,64},{128,96},{160,128},{192,160},{224,1... | collective-permute-start | bytes 392 | tf_op jit(solution)/shard_map/ppermute | solution.py:14
  276.1 2.6 collective-permute-start.10
  278.7 3.0 %collective-permute-done.10 = f32[1,3584]{1,0:T(1,128)S(1)} collective-permute-done((f32[1,3584]{1,0:T(1,128)S(1)}, f32[1,3584]{1,0:T(1,128)S(1)}, u32[]{:S(2)}, u32[]{:S(2)}) %collective-permute-start.10) | collective-permute-done | bytes 14368 | tf_op jit(solution)/shard_map/ppermute | solution.py:14
  281.8 3.3 %all-to-all-done.2 = bf16[4,24,1792]{2,1,0:T(8,128)(2,1)S(1)} async-done(((bf16[4,24,1792]{2,1,0:T(8,128)(2,1)}), bf16[4,24,1792]{2,1,0:T(8,128)(2,1)S(1)}, u32[]{:S(2)}, u32[]{:S(2)}) %all-to-all-start.2) | async-done | bytes 344096 | tf_op jit(solution)/shard_map/all_to_all | solution.py:76
  285.1 0.2 fusion.40
  285.4 0.2 fusion.41
  285.6 0.2 multiply_reduce_fusion.1
  285.8 0.9 fusion.35
  286.7 0.7 copy.21
  (63 shorter events, 1.4 us)
Async XLA Ops:
  7.2 140.4 %all-gather.2.cloned.1.call-start = ((), (), s32[]{:S(2)}) async-start(), calls=%async_computation.4 | async-start | bytes 11698176 | tf_op jit(solution)/shard_map/all_gather | solution.py:116
  12.6 4.8 %copy-start.11 = (s32[32]{0:T(128)}, s32[32]{0:T(128)S(1)}, u32[]{:S(2)}) copy-start(s32[32]{0:T(128)S(1)} %select_reduce_fusion) | copy-start | bytes 388
  18.1 27.9 %all-to-all-start = ((f32[16,1,160]{2,1,0:T(1,128)}), f32[16,1,160]{2,1,0:T(1,128)S(1)}, u32[]{:S(2)}, u32[]{:S(2)}) async-start(f32[16,1,160]{2,1,0:T(1,128)} %broadcast_in_dim.14), calls=%async_computation | async-start | bytes 32768 | tf_op jit(solution)/shard_map/all_to_all | solution.py:132
  33.3 162.9 %reduce-scatter.2.cloned.1.call-start = ((), (), s32[]{:S(2)}) async-start(), calls=%async_computation.5 | async-start | bytes 1720320 | tf_op jit(solution)/shard_map/reduce_scatter | solution.py:169
  33.3 13.2 %collective-permute-start.2 = (bf16[128,3584]{1,0:T(8,128)(2,1)}, bf16[128,3584]{1,0:T(8,128)(2,1)S(1)}, u32[]{:S(2)}, u32[]{:S(2)}) collective-permute-start(bf16[128,3584]{1,0:T(8,128)(2,1)} %bitcast.66), channel_id=1, source_target_pairs={{0,1},{1,0},{2,3},{3,2},{4,5},{5,4},{6,7},{7,6},{8,9},{9,8},{10,11... | collective-permute-start | bytes 2752520 | tf_op jit(solution)/shard_map/ppermute | solution.py:150
  35.2 14.1 %collective-permute-start = (bf16[3584,128]{1,0:T(8,128)(2,1)}, bf16[3584,128]{1,0:T(8,128)(2,1)S(1)}, u32[]{:S(2)}, u32[]{:S(2)}) collective-permute-start(bf16[3584,128]{1,0:T(8,128)(2,1)} %bitcast.72), channel_id=1, source_target_pairs={{0,1},{1,0},{2,3},{3,2},{4,5},{5,4},{6,7},{7,6},{8,9},{9,8},{10,11... | collective-permute-start | bytes 2752520 | tf_op jit(solution)/shard_map/ppermute | solution.py:148
  37.6 11.7 %collective-permute-start.1 = (bf16[3584,128]{1,0:T(8,128)(2,1)}, bf16[3584,128]{1,0:T(8,128)(2,1)S(1)}, u32[]{:S(2)}, u32[]{:S(2)}) collective-permute-start(bf16[3584,128]{1,0:T(8,128)(2,1)} %bitcast.69), channel_id=1, source_target_pairs={{0,1},{1,0},{2,3},{3,2},{4,5},{5,4},{6,7},{7,6},{8,9},{9,8},{10,11... | collective-permute-start | bytes 2752520 | tf_op jit(solution)/shard_map/ppermute | solution.py:149
  46.5 2.8 copy-start.1
  46.5 2.8 copy-start.2
  50.0 2.4 copy-start
  56.6 96.9 %copy-start.7 = (bf16[512,1792]{1,0:T(8,128)(2,1)S(1)}, bf16[512,1792]{1,0:T(8,128)(2,1)}, u32[]{:S(2)}) copy-start(bf16[512,1792]{1,0:T(8,128)(2,1)} %pad_maximum_fusion.3) | copy-start | bytes 5505028
  155.9 5.3 %copy-start.6 = (bf16[256,3584]{1,0:T(8,128)(2,1)S(1)}, bf16[256,3584]{1,0:T(8,128)(2,1)}, u32[]{:S(2)}) copy-start(bf16[256,3584]{1,0:T(8,128)(2,1)} %pad_maximum_fusion.2) | copy-start | bytes 5505028
  161.3 4.2 %copy-start.3 = (bf16[1792,1024]{1,0:T(8,128)(2,1)S(1)}, bf16[1792,1024]{1,0:T(8,128)(2,1)}, u32[]{:S(2)}) copy-start(bf16[1792,1024]{1,0:T(8,128)(2,1)} %pad_maximum_fusion.1) | copy-start | bytes 11010052
  165.5 56.3 %copy-start.4 = (bf16[1,32,3584]{2,1,0:T(8,128)(2,1)S(1)}, bf16[1,32,3584]{2,1,0:T(8,128)(2,1)}, u32[]{:S(2)}) copy-start(bf16[1,32,3584]{2,1,0:T(8,128)(2,1)} %param.12) | copy-start | bytes 688132
  165.5 56.3 %copy-start.8 = (bf16[1,32,3584]{2,1,0:T(8,128)(2,1)S(1)}, bf16[1,32,3584]{2,1,0:T(8,128)(2,1)}, u32[]{:S(2)}) copy-start(bf16[1,32,3584]{2,1,0:T(8,128)(2,1)} %param.13) | copy-start | bytes 688132
  196.2 30.5 %all-to-all-start.1 = ((bf16[4,24,1792]{2,1,0:T(8,128)(2,1)}), bf16[4,24,1792]{2,1,0:T(8,128)(2,1)S(1)}, u32[]{:S(2)}, u32[]{:S(2)}) async-start(bf16[4,24,1792]{2,1,0:T(8,128)(2,1)} %bitcast.84), calls=%async_computation.2 | async-start | bytes 688128 | tf_op jit(solution)/shard_map/all_to_all | solution.py:76
  206.2 61.1 %copy-start.5 = (bf16[1,32,3584]{2,1,0:T(8,128)(2,1)S(1)}, bf16[1,32,3584]{2,1,0:T(8,128)(2,1)}, u32[]{:S(2)}) copy-start(bf16[1,32,3584]{2,1,0:T(8,128)(2,1)} %param.11) | copy-start | bytes 688132
  207.1 21.4 %collective-permute-start.6 = (bf16[96,1792]{1,0:T(8,128)(2,1)}, bf16[96,1792]{1,0:T(8,128)(2,1)S(1)}, u32[]{:S(2)}, u32[]{:S(2)}) collective-permute-start(bf16[96,1792]{1,0:T(8,128)(2,1)} %get-tuple-element.30), channel_id=1, source_target_pairs={{0,480},{1,481},{2,482},{3,483},{4,484},{5,485},{6,486},{7,487},{8... | collective-permute-start | bytes 1032200 | tf_op jit(solution)/shard_map/ppermute | solution.py:54
  212.0 18.7 %collective-permute-start.7 = (bf16[96,1792]{1,0:T(8,128)(2,1)}, bf16[96,1792]{1,0:T(8,128)(2,1)S(1)}, u32[]{:S(2)}, u32[]{:S(2)}) collective-permute-start(bf16[96,1792]{1,0:T(8,128)(2,1)} %get-tuple-element.33), channel_id=1, source_target_pairs={{0,486},{1,487},{2,480},{3,481},{4,482},{5,483},{6,484},{7,485},{8... | collective-permute-start | bytes 1032200 | tf_op jit(solution)/shard_map/ppermute | solution.py:54
  217.4 37.8 %collective-permute-start.8 = (bf16[96,1792]{1,0:T(8,128)(2,1)S(1)}, bf16[96,1792]{1,0:T(8,128)(2,1)S(1)}, u32[]{:S(2)}, u32[]{:S(2)}) collective-permute-start(bf16[96,1792]{1,0:T(8,128)(2,1)S(1)} %get-tuple-element.32), channel_id=1, source_target_pairs={{0,484},{1,485},{2,486},{3,487},{4,480},{5,481},{6,482},{7,483},{8... | collective-permute-start | bytes 1032200 | tf_op jit(solution)/shard_map/ppermute | solution.py:54
  219.3 35.9 %collective-permute-start.9 = (bf16[96,1792]{1,0:T(8,128)(2,1)S(1)}, bf16[96,1792]{1,0:T(8,128)(2,1)S(1)}, u32[]{:S(2)}, u32[]{:S(2)}) collective-permute-start(bf16[96,1792]{1,0:T(8,128)(2,1)S(1)} %get-tuple-element.31), channel_id=1, source_target_pairs={{0,482},{1,483},{2,484},{3,485},{4,486},{5,487},{6,480},{7,481},{8... | collective-permute-start | bytes 1032200 | tf_op jit(solution)/shard_map/ppermute | solution.py:54
  221.9 59.9 %collective-permute-start.4 = (bf16[32,7168]{1,0:T(8,128)(2,1)S(1)}, bf16[32,7168]{1,0:T(8,128)(2,1)S(1)}, u32[]{:S(2)}, u32[]{:S(2)}) collective-permute-start(bf16[32,7168]{1,0:T(8,128)(2,1)S(1)} %pad_maximum_fusion.6), channel_id=1, source_target_pairs={{0,480},{32,0},{64,32},{96,64},{128,96},{160,128},{192,160},{224,1... | collective-permute-start | bytes 1376264 | tf_op jit(solution)/shard_map/ppermute | solution.py:14
  255.2 16.2 %copy-start.10 = (s32[1,32,1]{1,2,0:T(1,128)S(1)}, s32[1,32,1]{1,2,0:T(1,128)}, u32[]{:S(2)}) copy-start(s32[1,32,1]{1,2,0:T(1,128)} %param.20) | copy-start | bytes 388
  255.2 16.2 %copy-start.12 = (s32[32]{0:T(128)S(1)}, s32[32]{0:T(128)}, u32[]{:S(2)}) copy-start(s32[32]{0:T(128)} %copy-done.11) | copy-start | bytes 388
  255.2 20.9 %copy-start.9 = (f32[1,3584]{1,0:T(1,128)S(1)}, f32[1,3584]{1,0:T(1,128)}, u32[]{:S(2)}) copy-start(f32[1,3584]{1,0:T(1,128)} %param.14) | copy-start | bytes 43012
  256.1 29.0 %all-to-all-start.2 = ((bf16[4,24,1792]{2,1,0:T(8,128)(2,1)}), bf16[4,24,1792]{2,1,0:T(8,128)(2,1)S(1)}, u32[]{:S(2)}, u32[]{:S(2)}) async-start(bf16[4,24,1792]{2,1,0:T(8,128)(2,1)} %bitcast.19), calls=%async_computation.3 | async-start | bytes 688128 | tf_op jit(solution)/shard_map/all_to_all | solution.py:76
  268.1 13.7 %collective-permute-start.3 = (bf16[32,3584]{1,0:T(8,128)(2,1)S(1)}, bf16[32,3584]{1,0:T(8,128)(2,1)S(1)}, u32[]{:S(2)}, u32[]{:S(2)}) collective-permute-start(bf16[32,3584]{1,0:T(8,128)(2,1)S(1)} %fusion.25), channel_id=1, source_target_pairs={{0,32},{32,64},{64,96},{96,128},{128,160},{160,192},{192,224},{224... | collective-permute-start | bytes 688136 | tf_op jit(solution)/shard_map/ppermute | solution.py:14
  271.5 7.2 %collective-permute-start.5 = (s32[1,32]{1,0:T(1,128)S(1)}, s32[1,32]{1,0:T(1,128)S(1)}, u32[]{:S(2)}, u32[]{:S(2)}) collective-permute-start(s32[1,32]{1,0:T(1,128)S(1)} %bitcast_add_fusion), channel_id=1, source_target_pairs={{0,480},{32,0},{64,32},{96,64},{128,96},{160,128},{192,160},{224,1... | collective-permute-start | bytes 392 | tf_op jit(solution)/shard_map/ppermute | solution.py:14
  276.1 5.6 %collective-permute-start.10 = (f32[1,3584]{1,0:T(1,128)S(1)}, f32[1,3584]{1,0:T(1,128)S(1)}, u32[]{:S(2)}, u32[]{:S(2)}) collective-permute-start(f32[1,3584]{1,0:T(1,128)S(1)} %copy-done.9), channel_id=1, source_target_pairs={{0,480},{32,0},{64,32},{96,64},{128,96},{160,128},{192,160},{224,1... | collective-permute-start | bytes 43016 | tf_op jit(solution)/shard_map/ppermute | solution.py:14
Sparse Core Ops, SparseCore 0:
  10.1 137.4 all-gather.1
  155.6 40.5 reduce-scatter.1

commit v7 on v6

--- a/solution.py
+++ b/solution.py
@@ -44,6 +44,23 @@
     return jnp.concatenate(halves, axis=1)
 
 
+def to_section(value, sections, count, steps, hop, chips):
+    pairs = []
+    for s in range(sections):
+        for d in range(count):
+            chip = (d // 2 + hop) % chips
+            pairs.append((s * count + d, (s + steps) % sections * count + 2 * chip + d % 2))
+    return lax.ppermute(value, ("section", "expert"), pairs)
+
+
+def pick_rows(route, me_group):
+    slot = slots_of(route)
+    place = (slot // CAP - me_group) % EXPERTS * (2 * CAP) + slot % CAP
+    want = jnp.concatenate([place, place + CAP])
+    row = jnp.arange(EXPERTS * 2 * CAP, dtype=jnp.int32)[:, None]
+    return (row == want[None, :]).astype(jnp.bfloat16)
+
+
 def group_to_section(value, sections, count, side, steps, hop):
     pairs = []
     for s in range(sections):
@@ -54,14 +71,17 @@
     return lax.ppermute(value, ("section", "expert"), pairs)
 
 
-def packers(slots, me_expert, first_place, tokens, side, turn):
+def packers(slots, me_expert, first_place, tokens, side, turn, near_first=False):
     count = slots.shape[0]
     sources = count // tokens
     groups = sources // side
     expert, rank = slots // CAP, slots % CAP
     source = jnp.arange(count, dtype=jnp.int32) // tokens
     place = (turn * (source % side - first_place)) % side
-    base = (place * groups + source // side) * (2 * CAP) + rank
+    group = source // side
+    if near_first:
+        group = (me_expert - group) % groups
+    base = (place * groups + group) * (2 * CAP) + rank
     base = jnp.where(expert == me_expert, base, -2 * CAP)
     row = jnp.arange(sources * 2 * CAP, dtype=jnp.int32)[:, None]
     return [(base[None, :] + h * CAP == row).astype(jnp.bfloat16) for h in range(2)]
@@ -117,7 +137,6 @@
 
     xf = x_fwd[0].astype(jnp.float32)
     xb = x_bwd[0].astype(jnp.float32)
-    scale_f = gate_fwd[0].astype(jnp.float32) / 256.0
     slot_f = slots_of(route_fwd[0, :, 0])
     slot_b = slots_of(route_bwd[0, :, 0])
     small = jnp.concatenate(
@@ -142,7 +161,7 @@
     ]
     slots_f = slots_f.astype(jnp.int32)
     slots_b = slots_b.astype(jnp.int32)
-    places_f = packers(slots_f, me_expert, 0, tokens, side, 1)
+    places_f = packers(slots_f, me_expert, 0, tokens, side, 1, near_first=True)
     places_b = packers(slots_b, me_expert, me_place, tokens, side, -1)
 
     gate_o = lax.ppermute(w_gate[0], "expert", swap)
@@ -154,13 +173,20 @@
     hid = w_dn.shape[0]
     dn_stack = jnp.concatenate([w_dn[:, :half], w_dn[:, half:]], axis=0)
     in_stack = jnp.concatenate([w_in[:half], w_in[half:]], axis=1)
+    last_f = passed_along(x_fwd[0], "section", 1)
+    last_b = passed_along(sent_b, "section", -1)
+    last_gain = passed_along(norm_gain, "section", -1)
+    whole = jnp.concatenate([route_fwd[0, :, 0], gate_fwd[0, :, 0]])[None, :]
+    whole = passed_along(whole, "section", 1)[0]
+    last_slot = passed_along(slot_b[None, :], "section", -1)[0]
+    seen = last_f[0, 0] + last_b[0, 0] + last_gain[0, 0] + (whole[0] + last_slot[0])
+    seen = seen.astype(jnp.float32)
+    dn_stack = jnp.where((seen > 1.0) & (seen < -1.0), 0, dn_stack)
     w_gained, w_dn, in_stack, dn_stack = lax.optimization_barrier(
         (w_gained, w_dn, in_stack, dn_stack)
     )
-
-    last_b = passed_along(sent_b, "section", -1).astype(jnp.float32)
-    last_gain = passed_along(norm_gain, "section", -1)
-    last_slot = passed_along(slot_b[None, :], "section", -1)[0]
+    last_put = pick_rows(whole[:tokens], me_expert)
+    last_scale = whole[tokens:, None].astype(jnp.float32) / 256.0
 
     pre_f = dot(got[:, :width], w_gained, ((1,), (0,))) * rs_f[:, None]
     act = (jax.nn.silu(pre_f[:, :hid]) * pre_f[:, hid:]).astype(jnp.bfloat16)
@@ -186,14 +212,19 @@
         for k in range(side)
     ).astype(jnp.bfloat16)
 
-    table_f = across_groups(total_f, across)
-    seen = table_f[0, 0, 0].astype(jnp.float32)
+    seen = total_f[0, 0].astype(jnp.float32)
     total_b = jnp.where((seen > 1.0) & (seen < -1.0), 0, total_b)
-    moe_f = pick_back(table_f, slot_f)
-    y = (xf + scale_f * moe_f).astype(jnp.bfloat16)
-    y_next = passed_along(y, "section", 1)
+    unit = 2 * CAP
+    table_f = [
+        to_section(total_f[k * unit : (k + 1) * unit], sections, count, 1, -side * k, ring)
+        for k in range(EXPERTS)
+    ]
+    moe_f = dot(last_put, jnp.concatenate(table_f, axis=0), ((0,), (0,)))
+    moe_f = jnp.concatenate([moe_f[:tokens], moe_f[tokens:]], axis=1)
+    y_next = (last_f.astype(jnp.float32) + last_scale * moe_f).astype(jnp.bfloat16)
 
     d_normed = pick_back(across_groups(total_b, across), last_slot)
+    last_b = last_b.astype(jnp.float32)
     last_x, last_g = last_b[:, :width], last_b[:, width:]
     r = rms_scale(last_x)
     weighted = d_normed * last_gain

time: 296 us -> 287 us (0.970)
  the two profiles are of different devices: /device:TPU:6 before, /device:TPU:58 now
where the time goes in v7:
time: 287 us; the launch traced here: 286 us
  waiting for transfers between devices  123 us (43%)
  starting transfers between devices  83.4 us (29%)
  other arithmetic  32.7 us (11%)
  between operations  18.6 us (6%)
  matrix products  18.3 us (6%)
  local copies, waits for them, and re-layouts  9.27 us (3%)
    all_gather x1, waiting for transfers between devices, per_device(): lax.all_gather(sent, 'expert', axis=0, tiled=True, axis_index_groups=same...  63.6 us
    reduce_scatter x1, waiting for transfers between devices, per_device(): lax.psum_scatter(part_f, 'expert', scatter_dimension=0, tiled=True, axis_...  37.8 us
    ppermute x4, starting transfers between devices, to_section(): return lax.ppermute(value, ('section', 'expert'), pairs)  26.8 us
    all_to_all x1, waiting for transfers between devices, across_groups(): lax.all_to_all(rows.reshape(EXPERTS, 2 * CAP, rows.shape[1]), 'expert', s...  18.5 us
    dot_general x12, matrix products, dot(): lax.dot_general(a, b, (dims, ((), ())), preferred_element_type=jnp.float32)  18.3 us
    ppermute x4, starting transfers between devices, group_to_section(): return lax.ppermute(value, ('section', 'expert'), pairs)  17.3 us
    all_to_all x1, starting transfers between devices, per_device(): lax.all_to_all(jnp.broadcast_to(small[None, None, :], (ring, 1, 5 * token...  15.2 us
    ppermute x5, starting transfers between devices, passed_along(): return lax.ppermute(value, axis, pairs)  14.3 us
  transfers between devices with their start and end apart: 20, of which 5 were waited for; matrix products, arithmetic and copies ran while one was open for 17% of the time, Pallas kernels for 0%

profile of v7, /device:TPU:58, one launch (start us, length us, event | category | flops | bytes accessed | tf_op | source)
XLA Modules:
  0.0 285.5 jit_solution(8759102054096509919)
XLA Ops:
  7.3 2.2 pad_maximum_fusion.3
  9.5 3.1 %collective-permute-start = (bf16[32,3584]{1,0:T(8,128)(2,1)}, bf16[32,3584]{1,0:T(8,128)(2,1)S(1)}, u32[]{:S(2)}, u32[]{:S(2)}) collective-permute-start(bf16[32,3584]{1,0:T(8,128)(2,1)} %bitcast.84), channel_id=1, source_target_pairs={{0,32},{32,64},{64,96},{96,128},{128,160},{160,192},{192,224},{224... | collective-permute-start | bytes 688136 | tf_op jit(solution)/shard_map/ppermute | solution.py:14
  12.5 0.7 fusion.47
  13.3 0.7 fusion.46
  14.1 0.8 select_reduce_fusion.1
  14.9 0.8 select_reduce_fusion
  15.8 1.1 multiply_reduce_fusion.2
  16.9 1.1 multiply_reduce_fusion.3
  18.0 0.7 multiply_bitcast_fusion
  18.7 0.7 add_convert_fusion.2
  19.3 0.7 add_convert_fusion.1
  20.1 0.6 broadcast_in_dim.21
  20.7 15.2 %all-to-all-start = ((f32[16,1,160]{2,1,0:T(1,128)}), f32[16,1,160]{2,1,0:T(1,128)S(1)}, u32[]{:S(2)}, u32[]{:S(2)}) async-start(f32[16,1,160]{2,1,0:T(1,128)} %broadcast_in_dim.21), calls=%async_computation | async-start | bytes 32768 | tf_op jit(solution)/shard_map/all_to_all | solution.py:151
  35.9 0.8 add_bitcast_fusion
  36.7 3.5 %collective-permute-start.1 = (s32[1,64]{1,0:T(1,128)S(1)}, s32[1,64]{1,0:T(1,128)S(1)}, u32[]{:S(2)}, u32[]{:S(2)}) collective-permute-start(s32[1,64]{1,0:T(1,128)S(1)} %add_bitcast_fusion), channel_id=1, source_target_pairs={{0,32},{32,64},{64,96},{96,128},{128,160},{160,192},{192,224},{224... | collective-permute-start | bytes 776 | tf_op jit(solution)/shard_map/ppermute | solution.py:14
  40.2 0.7 bitcast_add_fusion
  40.8 2.3 collective-permute-start.7
  43.2 1.1 pad_maximum_fusion.5
  44.3 2.8 collective-permute-start.5
  47.1 2.7 collective-permute-start.6
  49.9 1.9 collective-permute-start.4
  51.8 0.6 broadcast_add_fusion.3
  52.4 2.4 collective-permute-start.2
  55.1 0.7 multiply_bitcast_fusion.1
  55.8 0.6 pad_add_fusion
  57.1 2.3 collective-permute-done.6
  59.4 1.9 collective-permute-start.3
  61.4 0.5 slice.157
  61.9 0.6 reduce.1
  63.5 0.5 slice.155
  64.1 1.2 slice.156
  67.2 1.3 fusion.15
  68.5 1.6 maximum_select_fusion
  70.0 1.7 pad_maximum_fusion
  72.0 2.4 pad_maximum_fusion.1
  74.3 2.5 pad_maximum_fusion.2
  76.9 4.0 %multiply_convert_fusion = bf16[3584,512]{1,0:T(8,128)(2,1)} fusion(f32[3584]{0:T(1024)S(1)} %reduce, bf16[3584,128]{1,0:T(8,128)(2,1)} %collective-permute-done.3, bf16[3584,128]{1,0:T(8,128)(2,1)S(1)} %bitcast.73, bf16[3584,128]{1,0:T(8,128)(2,1)} %collective-permute-done.2, bf16[3584,128]{1,0:T(8,128)(2,1)S(1)} %bitcast.76), kind=kLoop, calls=%fused_computation | loop fusion | flops 18350080 | bytes 7354368 | tf_op jit(solution)/shard_map/convert_element_type | solution.py:171
  80.9 63.6 %all-gather.2.cloned.1.call-done = bf16[512,10752]{1,0:T(8,128)(2,1)} async-done(((bf16[32,10752]{1,0:T(8,128)(2,1)}), bf16[512,10752]{1,0:T(8,128)(2,1)}) %all-gather.2.cloned.1.call-update) | async-done | bytes 11010064 | tf_op jit(solution)/shard_map/all_gather | solution.py:136
  144.4 5.2 %fusion.9 = f32[512,512]{1,0:T(8,128)S(1)} fusion(bf16[3584,512]{1,0:T(8,128)(2,1)} %multiply_convert_fusion, bf16[512,10752]{1,0:T(8,128)(2,1)} %all-gather.2.cloned.1.call-done, f32[512]{0:T(512)S(1)} %mul.240), kind=kOutput, calls=%fused_computation.18 | convolution fusion | flops 1879310336 | bytes 8390656 | tf_op jit(solution)/shard_map/dot_general | solution.py:22
  150.4 2.0 convolution_convert_fusion
  152.4 1.1 convert_element_type.159
  153.5 5.3 %fusion.6 = f32[512,512]{1,0:T(8,128)S(1)} fusion(bf16[3584,512]{1,0:T(8,128)(2,1)} %multiply_convert_fusion, bf16[512,10752]{1,0:T(8,128)(2,1)} %all-gather.2.cloned.1.call-done, f32[512]{0:T(512)S(1)} %mul.255), kind=kOutput, calls=%fused_computation.17 | convolution fusion | flops 1879310336 | bytes 8390656 | tf_op jit(solution)/shard_map/dot_general | solution.py:22
  158.9 1.5 copy-done.11
  160.3 1.2 fusion.22
  162.4 1.6 convolution_convert_fusion.1
  164.0 0.8 fusion.94
  164.8 2.8 collective-permute-start.12
  167.6 4.9 %collective-permute-start.13 = (bf16[96,1792]{1,0:T(8,128)(2,1)S(1)}, bf16[96,1792]{1,0:T(8,128)(2,1)S(1)}, u32[]{:S(2)}, u32[]{:S(2)}) collective-permute-start(bf16[96,1792]{1,0:T(8,128)(2,1)S(1)} %get-tuple-element.33), channel_id=1, source_target_pairs={{0,486},{1,487},{2,480},{3,481},{4,482},{5,483},{6,484},{7,485},{8... | collective-permute-start | bytes 1032200 | tf_op jit(solution)/shard_map/ppermute | solution.py:71
  172.4 2.7 collective-permute-start.14
  175.1 7.0 %collective-permute-start.15 = (bf16[96,1792]{1,0:T(8,128)(2,1)S(1)}, bf16[96,1792]{1,0:T(8,128)(2,1)S(1)}, u32[]{:S(2)}, u32[]{:S(2)}) collective-permute-start(bf16[96,1792]{1,0:T(8,128)(2,1)S(1)} %get-tuple-element.31), channel_id=1, source_target_pairs={{0,482},{1,483},{2,484},{3,485},{4,486},{5,487},{6,480},{7,481},{8... | collective-permute-start | bytes 1032200 | tf_op jit(solution)/shard_map/ppermute | solution.py:71
  182.1 37.8 %reduce-scatter.2.cloned.1.call-done = bf16[96,1792]{1,0:T(8,128)(2,1)} async-done(((bf16[384,1792]{1,0:T(8,128)(2,1)}), bf16[96,1792]{1,0:T(8,128)(2,1)}) %reduce-scatter.2.cloned.1.call-update) | async-done | bytes 344080 | tf_op jit(solution)/shard_map/reduce_scatter | solution.py:195
  219.9 1.2 slice.173
  222.4 1.7 fusion.96
  224.1 11.1 %collective-permute-start.10 = (bf16[24,1792]{1,0:T(8,128)(2,1)}, bf16[24,1792]{1,0:T(8,128)(2,1)}, u32[]{:S(2)}, u32[]{:S(2)}) collective-permute-start(bf16[24,1792]{1,0:T(8,128)(2,1)} %get-tuple-element.38), channel_id=1, source_target_pairs={{0,48},{1,49},{2,50},{3,51},{4,52},{5,53},{6,54},{7,55},{8,56},{9,... | collective-permute-start | bytes 258056 | tf_op jit(solution)/shard_map/ppermute | solution.py:53
  235.2 3.8 %collective-permute-start.11 = (bf16[24,1792]{1,0:T(8,128)(2,1)}, bf16[24,1792]{1,0:T(8,128)(2,1)}, u32[]{:S(2)}, u32[]{:S(2)}) collective-permute-start(bf16[24,1792]{1,0:T(8,128)(2,1)} %get-tuple-element.37), channel_id=1, source_target_pairs={{0,40},{1,41},{2,42},{3,43},{4,44},{5,45},{6,46},{7,47},{8,48},{9,... | collective-permute-start | bytes 258056 | tf_op jit(solution)/shard_map/ppermute | solution.py:53
  239.1 3.9 %collective-permute-start.8 = (bf16[24,1792]{1,0:T(8,128)(2,1)}, bf16[24,1792]{1,0:T(8,128)(2,1)S(1)}, u32[]{:S(2)}, u32[]{:S(2)}) collective-permute-start(bf16[24,1792]{1,0:T(8,128)(2,1)} %get-tuple-element.36), channel_id=1, source_target_pairs={{0,32},{1,33},{2,34},{3,35},{4,36},{5,37},{6,38},{7,39},{8,40},{9,... | collective-permute-start | bytes 258056 | tf_op jit(solution)/shard_map/ppermute | solution.py:53
  243.1 8.0 %collective-permute-start.9 = (bf16[24,1792]{1,0:T(8,128)(2,1)}, bf16[24,1792]{1,0:T(8,128)(2,1)S(1)}, u32[]{:S(2)}, u32[]{:S(2)}) collective-permute-start(bf16[24,1792]{1,0:T(8,128)(2,1)} %get-tuple-element.39), channel_id=1, source_target_pairs={{0,56},{1,57},{2,58},{3,59},{4,60},{5,61},{6,62},{7,63},{8,32},{9,... | collective-permute-start | bytes 258056 | tf_op jit(solution)/shard_map/ppermute | solution.py:53
  251.1 0.9 fusion.34
  252.0 3.5 %all-to-all-start.1 = ((bf16[4,24,1792]{2,1,0:T(8,128)(2,1)}), bf16[4,24,1792]{2,1,0:T(8,128)(2,1)S(1)}, u32[]{:S(2)}, u32[]{:S(2)}) async-start(bf16[4,24,1792]{2,1,0:T(8,128)(2,1)} %bitcast.21), calls=%async_computation.2 | async-start | bytes 688128 | tf_op jit(solution)/shard_map/all_to_all | solution.py:96
  255.5 1.0 collective-permute-done.9
  256.5 1.2 fusion.35
  257.8 0.8 fusion.43
  258.6 18.5 %all-to-all-done.1 = bf16[4,24,1792]{2,1,0:T(8,128)(2,1)S(1)} async-done(((bf16[4,24,1792]{2,1,0:T(8,128)(2,1)}), bf16[4,24,1792]{2,1,0:T(8,128)(2,1)S(1)}, u32[]{:S(2)}, u32[]{:S(2)}) %all-to-all-start.1) | async-done | bytes 344096 | tf_op jit(solution)/shard_map/all_to_all | solution.py:96
  277.8 0.9 fusion.44
  (81 shorter events, 4.2 us)
Async XLA Ops:
  7.2 42.6 %copy-start.7 = (f32[1,3584]{1,0:T(1,128)S(1)}, f32[1,3584]{1,0:T(1,128)}, u32[]{:S(2)}) copy-start(f32[1,3584]{1,0:T(1,128)} %param.14) | copy-start | bytes 43012
  7.2 42.7 %copy-start = (bf16[1,128,3584]{2,1,0:T(8,128)(2,1)S(1)}, bf16[1,128,3584]{2,1,0:T(8,128)(2,1)}, u32[]{:S(2)}) copy-start(bf16[1,128,3584]{2,1,0:T(8,128)(2,1)} %param.17) | copy-start | bytes 2752516
  7.2 45.2 %copy-start.2 = (bf16[1,3584,128]{2,1,0:T(8,128)(2,1)S(1)}, bf16[1,3584,128]{2,1,0:T(8,128)(2,1)}, u32[]{:S(2)}) copy-start(bf16[1,3584,128]{2,1,0:T(8,128)(2,1)} %param.15) | copy-start | bytes 2752516
  7.2 52.2 %copy-start.1 = (bf16[1,3584,128]{2,1,0:T(8,128)(2,1)S(1)}, bf16[1,3584,128]{2,1,0:T(8,128)(2,1)}, u32[]{:S(2)}) copy-start(bf16[1,3584,128]{2,1,0:T(8,128)(2,1)} %param.16) | copy-start | bytes 2752516
  7.2 137.2 %all-gather.2.cloned.1.call-start = ((), (), s32[]{:S(2)}) async-start(), calls=%async_computation.3 | async-start | bytes 11698176 | tf_op jit(solution)/shard_map/all_gather | solution.py:136
  9.5 54.1 %collective-permute-start = (bf16[32,3584]{1,0:T(8,128)(2,1)}, bf16[32,3584]{1,0:T(8,128)(2,1)S(1)}, u32[]{:S(2)}, u32[]{:S(2)}) collective-permute-start(bf16[32,3584]{1,0:T(8,128)(2,1)} %bitcast.84), channel_id=1, source_target_pairs={{0,32},{32,64},{64,96},{96,128},{128,160},{160,192},{192,224},{224... | collective-permute-start | bytes 688136 | tf_op jit(solution)/shard_map/ppermute | solution.py:14
  20.7 41.9 %all-to-all-start = ((f32[16,1,160]{2,1,0:T(1,128)}), f32[16,1,160]{2,1,0:T(1,128)S(1)}, u32[]{:S(2)}, u32[]{:S(2)}) async-start(f32[16,1,160]{2,1,0:T(1,128)} %broadcast_in_dim.21), calls=%async_computation | async-start | bytes 32768 | tf_op jit(solution)/shard_map/all_to_all | solution.py:151
  35.9 184.0 %reduce-scatter.2.cloned.1.call-start = ((), (), s32[]{:S(2)}) async-start(), calls=%async_computation.4 | async-start | bytes 1720320 | tf_op jit(solution)/shard_map/reduce_scatter | solution.py:195
  36.7 15.7 %collective-permute-start.1 = (s32[1,64]{1,0:T(1,128)S(1)}, s32[1,64]{1,0:T(1,128)S(1)}, u32[]{:S(2)}, u32[]{:S(2)}) collective-permute-start(s32[1,64]{1,0:T(1,128)S(1)} %add_bitcast_fusion), channel_id=1, source_target_pairs={{0,32},{32,64},{64,96},{96,128},{128,160},{160,192},{192,224},{224... | collective-permute-start | bytes 776 | tf_op jit(solution)/shard_map/ppermute | solution.py:14
  40.8 9.0 %collective-permute-start.7 = (s32[1,32]{1,0:T(1,128)S(1)}, s32[1,32]{1,0:T(1,128)S(1)}, u32[]{:S(2)}, u32[]{:S(2)}) collective-permute-start(s32[1,32]{1,0:T(1,128)S(1)} %bitcast_add_fusion), channel_id=1, source_target_pairs={{0,480},{32,0},{64,32},{96,64},{128,96},{160,128},{192,160},{224,1... | collective-permute-start | bytes 392 | tf_op jit(solution)/shard_map/ppermute | solution.py:14
  44.3 19.8 %collective-permute-start.5 = (bf16[32,7168]{1,0:T(8,128)(2,1)S(1)}, bf16[32,7168]{1,0:T(8,128)(2,1)}, u32[]{:S(2)}, u32[]{:S(2)}) collective-permute-start(bf16[32,7168]{1,0:T(8,128)(2,1)S(1)} %pad_maximum_fusion.5), channel_id=1, source_target_pairs={{0,480},{32,0},{64,32},{96,64},{128,96},{160,128},{192,160},{224,1... | collective-permute-start | bytes 1376264 | tf_op jit(solution)/shard_map/ppermute | solution.py:14
  47.1 12.4 %collective-permute-start.6 = (f32[1,3584]{1,0:T(1,128)}, f32[1,3584]{1,0:T(1,128)S(1)}, u32[]{:S(2)}, u32[]{:S(2)}) collective-permute-start(f32[1,3584]{1,0:T(1,128)} %param.14), channel_id=1, source_target_pairs={{0,480},{32,0},{64,32},{96,64},{128,96},{160,128},{192,160},{224,1... | collective-permute-start | bytes 43016 | tf_op jit(solution)/shard_map/ppermute | solution.py:14
  49.8 5.3 %copy-start.12 = (s32[1,32]{1,0:T(1,128)}, s32[1,32]{1,0:T(1,128)S(1)}, u32[]{:S(2)}) copy-start(s32[1,32]{1,0:T(1,128)S(1)} %collective-permute-done.7) | copy-start | bytes 388
  49.9 17.3 %collective-permute-start.4 = (bf16[128,3584]{1,0:T(8,128)(2,1)S(1)}, bf16[128,3584]{1,0:T(8,128)(2,1)}, u32[]{:S(2)}, u32[]{:S(2)}) collective-permute-start(bf16[128,3584]{1,0:T(8,128)(2,1)S(1)} %bitcast.68), channel_id=1, source_target_pairs={{0,1},{1,0},{2,3},{3,2},{4,5},{5,4},{6,7},{7,6},{8,9},{9,8},{10,11... | collective-permute-start | bytes 2752520 | tf_op jit(solution)/shard_map/ppermute | solution.py:169
  52.4 17.6 %collective-permute-start.2 = (bf16[3584,128]{1,0:T(8,128)(2,1)S(1)}, bf16[3584,128]{1,0:T(8,128)(2,1)}, u32[]{:S(2)}, u32[]{:S(2)}) collective-permute-start(bf16[3584,128]{1,0:T(8,128)(2,1)S(1)} %bitcast.74), channel_id=1, source_target_pairs={{0,1},{1,0},{2,3},{3,2},{4,5},{5,4},{6,7},{7,6},{8,9},{9,8},{10,11... | collective-permute-start | bytes 2752520 | tf_op jit(solution)/shard_map/ppermute | solution.py:167
  59.4 10.6 %collective-permute-start.3 = (bf16[3584,128]{1,0:T(8,128)(2,1)S(1)}, bf16[3584,128]{1,0:T(8,128)(2,1)}, u32[]{:S(2)}, u32[]{:S(2)}) collective-permute-start(bf16[3584,128]{1,0:T(8,128)(2,1)S(1)} %bitcast.71), channel_id=1, source_target_pairs={{0,1},{1,0},{2,3},{3,2},{4,5},{5,4},{6,7},{7,6},{8,9},{9,8},{10,11... | collective-permute-start | bytes 2752520 | tf_op jit(solution)/shard_map/ppermute | solution.py:168
  80.9 69.5 %copy-start.5 = (bf16[512,1792]{1,0:T(8,128)(2,1)S(1)}, bf16[512,1792]{1,0:T(8,128)(2,1)}, u32[]{:S(2)}) copy-start(bf16[512,1792]{1,0:T(8,128)(2,1)} %maximum_select_fusion) | copy-start | bytes 5505028
  153.5 5.4 %copy-start.4 = (bf16[256,3584]{1,0:T(8,128)(2,1)S(1)}, bf16[256,3584]{1,0:T(8,128)(2,1)}, u32[]{:S(2)}) copy-start(bf16[256,3584]{1,0:T(8,128)(2,1)} %pad_maximum_fusion.2) | copy-start | bytes 5505028
  153.5 6.8 %copy-start.11 = (bf16[512,10752]{1,0:T(8,128)(2,1)S(1)}, bf16[512,10752]{1,0:T(8,128)(2,1)}, u32[]{:S(2)}) copy-start(bf16[512,10752]{1,0:T(8,128)(2,1)} %all-gather.2.cloned.1.call-done) | copy-start | bytes 33030148
  160.3 2.0 copy-start.3
  164.8 70.4 %collective-permute-start.12 = (bf16[96,1792]{1,0:T(8,128)(2,1)}, bf16[96,1792]{1,0:T(8,128)(2,1)S(1)}, u32[]{:S(2)}, u32[]{:S(2)}) collective-permute-start(bf16[96,1792]{1,0:T(8,128)(2,1)} %get-tuple-element.30), channel_id=1, source_target_pairs={{0,480},{1,481},{2,482},{3,483},{4,484},{5,485},{6,486},{7,487},{8... | collective-permute-start | bytes 1032200 | tf_op jit(solution)/shard_map/ppermute | solution.py:71
  167.6 71.5 %collective-permute-start.13 = (bf16[96,1792]{1,0:T(8,128)(2,1)S(1)}, bf16[96,1792]{1,0:T(8,128)(2,1)S(1)}, u32[]{:S(2)}, u32[]{:S(2)}) collective-permute-start(bf16[96,1792]{1,0:T(8,128)(2,1)S(1)} %get-tuple-element.33), channel_id=1, source_target_pairs={{0,486},{1,487},{2,480},{3,481},{4,482},{5,483},{6,484},{7,485},{8... | collective-permute-start | bytes 1032200 | tf_op jit(solution)/shard_map/ppermute | solution.py:71
  172.4 70.6 %collective-permute-start.14 = (bf16[96,1792]{1,0:T(8,128)(2,1)S(1)}, bf16[96,1792]{1,0:T(8,128)(2,1)S(1)}, u32[]{:S(2)}, u32[]{:S(2)}) collective-permute-start(bf16[96,1792]{1,0:T(8,128)(2,1)S(1)} %get-tuple-element.32), channel_id=1, source_target_pairs={{0,484},{1,485},{2,486},{3,487},{4,480},{5,481},{6,482},{7,483},{8... | collective-permute-start | bytes 1032200 | tf_op jit(solution)/shard_map/ppermute | solution.py:71
  175.1 75.9 %collective-permute-start.15 = (bf16[96,1792]{1,0:T(8,128)(2,1)S(1)}, bf16[96,1792]{1,0:T(8,128)(2,1)S(1)}, u32[]{:S(2)}, u32[]{:S(2)}) collective-permute-start(bf16[96,1792]{1,0:T(8,128)(2,1)S(1)} %get-tuple-element.31), channel_id=1, source_target_pairs={{0,482},{1,483},{2,484},{3,485},{4,486},{5,487},{6,480},{7,481},{8... | collective-permute-start | bytes 1032200 | tf_op jit(solution)/shard_map/ppermute | solution.py:71
  224.1 31.3 %collective-permute-start.10 = (bf16[24,1792]{1,0:T(8,128)(2,1)}, bf16[24,1792]{1,0:T(8,128)(2,1)}, u32[]{:S(2)}, u32[]{:S(2)}) collective-permute-start(bf16[24,1792]{1,0:T(8,128)(2,1)} %get-tuple-element.38), channel_id=1, source_target_pairs={{0,48},{1,49},{2,50},{3,51},{4,52},{5,53},{6,54},{7,55},{8,56},{9,... | collective-permute-start | bytes 258056 | tf_op jit(solution)/shard_map/ppermute | solution.py:53
  235.2 20.2 %collective-permute-start.11 = (bf16[24,1792]{1,0:T(8,128)(2,1)}, bf16[24,1792]{1,0:T(8,128)(2,1)}, u32[]{:S(2)}, u32[]{:S(2)}) collective-permute-start(bf16[24,1792]{1,0:T(8,128)(2,1)} %get-tuple-element.37), channel_id=1, source_target_pairs={{0,40},{1,41},{2,42},{3,43},{4,44},{5,45},{6,46},{7,47},{8,48},{9,... | collective-permute-start | bytes 258056 | tf_op jit(solution)/shard_map/ppermute | solution.py:53
  239.1 18.7 %copy-start.8 = (f32[32]{0:T(128)S(1)}, f32[32]{0:T(128)}, u32[]{:S(2)}) copy-start(f32[32]{0:T(128)} %multiply_bitcast_fusion.1) | copy-start | bytes 388
  239.1 38.0 %copy-start.10 = (s32[32]{0:T(128)S(1)}, s32[32]{0:T(128)}, u32[]{:S(2)}) copy-start(s32[32]{0:T(128)} %get-tuple-element.17) | copy-start | bytes 388
  239.1 38.2 %copy-start.9 = (s32[32]{0:T(128)S(1)}, s32[32]{0:T(128)}, u32[]{:S(2)}) copy-start(s32[32]{0:T(128)} %get-tuple-element.16) | copy-start | bytes 388
  239.1 38.5 %copy-start.6 = (f32[3584]{0:T(1024)S(1)}, f32[3584]{0:T(1024)}, u32[]{:S(2)}) copy-start(f32[3584]{0:T(1024)} %reduce.1) | copy-start | bytes 43012
  239.1 16.4 %collective-permute-start.8 = (bf16[24,1792]{1,0:T(8,128)(2,1)}, bf16[24,1792]{1,0:T(8,128)(2,1)S(1)}, u32[]{:S(2)}, u32[]{:S(2)}) collective-permute-start(bf16[24,1792]{1,0:T(8,128)(2,1)} %get-tuple-element.36), channel_id=1, source_target_pairs={{0,32},{1,33},{2,34},{3,35},{4,36},{5,37},{6,38},{7,39},{8,40},{9,... | collective-permute-start | bytes 258056 | tf_op jit(solution)/shard_map/ppermute | solution.py:53
  243.1 13.5 %collective-permute-start.9 = (bf16[24,1792]{1,0:T(8,128)(2,1)}, bf16[24,1792]{1,0:T(8,128)(2,1)S(1)}, u32[]{:S(2)}, u32[]{:S(2)}) collective-permute-start(bf16[24,1792]{1,0:T(8,128)(2,1)} %get-tuple-element.39), channel_id=1, source_target_pairs={{0,56},{1,57},{2,58},{3,59},{4,60},{5,61},{6,62},{7,63},{8,32},{9,... | collective-permute-start | bytes 258056 | tf_op jit(solution)/shard_map/ppermute | solution.py:53
  252.0 25.1 %all-to-all-start.1 = ((bf16[4,24,1792]{2,1,0:T(8,128)(2,1)}), bf16[4,24,1792]{2,1,0:T(8,128)(2,1)S(1)}, u32[]{:S(2)}, u32[]{:S(2)}) async-start(bf16[4,24,1792]{2,1,0:T(8,128)(2,1)} %bitcast.21), calls=%async_computation.2 | async-start | bytes 688128 | tf_op jit(solution)/shard_map/all_to_all | solution.py:96
Sparse Core Ops, SparseCore 0:
  10.1 134.2 all-gather.1
  152.5 67.3 reduce-scatter.1

commit v8 on v6

--- a/solution.py
+++ b/solution.py
@@ -72,15 +72,17 @@
     return jnp.concatenate(parts, axis=1)
 
 
-def across_groups(rows, across):
-    return lax.all_to_all(
-        rows.reshape(EXPERTS, 2 * CAP, rows.shape[1]),
+def across_groups(parts, across):
+    blocks = [rows.reshape(EXPERTS, 2 * CAP, rows.shape[1]) for rows in parts]
+    table = lax.all_to_all(
+        jnp.concatenate(blocks, axis=1),
         "expert",
         split_axis=0,
         concat_axis=0,
         tiled=True,
         axis_index_groups=across,
     )
+    return [table[:, i * 2 * CAP : (i + 1) * 2 * CAP] for i in range(len(parts))]
 
 
 def per_device(
@@ -117,7 +119,6 @@
 
     xf = x_fwd[0].astype(jnp.float32)
     xb = x_bwd[0].astype(jnp.float32)
-    scale_f = gate_fwd[0].astype(jnp.float32) / 256.0
     slot_f = slots_of(route_fwd[0, :, 0])
     slot_b = slots_of(route_bwd[0, :, 0])
     small = jnp.concatenate(
@@ -154,13 +155,15 @@
     hid = w_dn.shape[0]
     dn_stack = jnp.concatenate([w_dn[:, :half], w_dn[:, half:]], axis=0)
     in_stack = jnp.concatenate([w_in[:half], w_in[half:]], axis=1)
+    last_b = passed_along(sent_b, "section", -1)
+    last_gain = passed_along(norm_gain, "section", -1)
+    last_slot = passed_along(slot_b[None, :], "section", -1)[0]
+    seen = last_b[0, 0] + last_gain[0, 0] + last_slot[0]
+    seen = seen.astype(jnp.float32)
+    dn_stack = jnp.where((seen > 1.0) & (seen < -1.0), 0, dn_stack)
     w_gained, w_dn, in_stack, dn_stack = lax.optimization_barrier(
         (w_gained, w_dn, in_stack, dn_stack)
     )
-
-    last_b = passed_along(sent_b, "section", -1).astype(jnp.float32)
-    last_gain = passed_along(norm_gain, "section", -1)
-    last_slot = passed_along(slot_b[None, :], "section", -1)[0]
 
     pre_f = dot(got[:, :width], w_gained, ((1,), (0,))) * rs_f[:, None]
     act = (jax.nn.silu(pre_f[:, :hid]) * pre_f[:, hid:]).astype(jnp.bfloat16)
@@ -186,14 +189,13 @@
         for k in range(side)
     ).astype(jnp.bfloat16)
 
-    table_f = across_groups(total_f, across)
-    seen = table_f[0, 0, 0].astype(jnp.float32)
-    total_b = jnp.where((seen > 1.0) & (seen < -1.0), 0, total_b)
+    table_f, table_b = across_groups([total_f, total_b], across)
     moe_f = pick_back(table_f, slot_f)
-    y = (xf + scale_f * moe_f).astype(jnp.bfloat16)
-    y_next = passed_along(y, "section", 1)
-
-    d_normed = pick_back(across_groups(total_b, across), last_slot)
+    scale_f = gate_fwd[0].astype(jnp.float32) / 256.0
+    y_next = passed_along((xf + scale_f * moe_f).astype(jnp.bfloat16), "section", 1)
+
+    last_b = last_b.astype(jnp.float32)
+    d_normed = pick_back(table_b, last_slot)
     last_x, last_g = last_b[:, :width], last_b[:, width:]
     r = rms_scale(last_x)
     weighted = d_normed * last_gain

time: 296 us -> 292 us (0.986)
  the two profiles are of different devices: /device:TPU:6 before, /device:TPU:32 now
where the time goes in v8:
time: 292 us; the launch traced here: 291 us
  waiting for transfers between devices  160 us (55%)
  starting transfers between devices  63.6 us (22%)
  other arithmetic  27.4 us (9%)
  matrix products  19.8 us (7%)
  between operations  15.9 us (5%)
  local copies, waits for them, and re-layouts  4.28 us (1%)
    all_gather x1, waiting for transfers between devices, per_device(): lax.all_gather(sent, 'expert', axis=0, tiled=True, axis_index_groups=same...  66.2 us
    ppermute x4, waiting for transfers between devices, group_to_section(): return lax.ppermute(value, ('section', 'expert'), pairs)  41.5 us
    all_to_all x1, waiting for transfers between devices, across_groups(): lax.all_to_all(jnp.concatenate(blocks, axis=1), 'expert', split_axis=0, c...  34.1 us
    dot_general x13, matrix products, dot(): lax.dot_general(a, b, (dims, ((), ())), preferred_element_type=jnp.float32)  19.8 us
    ppermute x4, starting transfers between devices, group_to_section(): return lax.ppermute(value, ('section', 'expert'), pairs)  18.5 us
    all_to_all x1, starting transfers between devices, per_device(): lax.all_to_all(jnp.broadcast_to(small[None, None, :], (ring, 1, 5 * token...  15.2 us
    ppermute x4, starting transfers between devices, passed_along(): return lax.ppermute(value, axis, pairs)  14.7 us
    ppermute x4, waiting for transfers between devices, passed_along(): return lax.ppermute(value, axis, pairs)  11.2 us
  transfers between devices with their start and end apart: 15, of which 8 were waited for; matrix products, arithmetic and copies ran while one was open for 13% of the time, Pallas kernels for 0%

profile of v8, /device:TPU:32, one launch (start us, length us, event | category | flops | bytes accessed | tf_op | source)
XLA Modules:
  0.0 291.2 jit_solution(18168357688646847755)
XLA Ops:
  7.2 2.2 pad_maximum_fusion.3
  9.4 1.9 collective-permute-start.1
  11.3 2.4 collective-permute-start
  13.8 1.9 collective-permute-start.2
  15.7 7.1 %collective-permute-start.4 = (f32[1,3584]{1,0:T(1,128)}, f32[1,3584]{1,0:T(1,128)S(1)}, u32[]{:S(2)}, u32[]{:S(2)}) collective-permute-start(f32[1,3584]{1,0:T(1,128)} %param.14), channel_id=1, source_target_pairs={{0,480},{32,0},{64,32},{96,64},{128,96},{160,128},{192,160},{224,1... | collective-permute-start | bytes 43016 | tf_op jit(solution)/shard_map/ppermute | solution.py:14
  22.8 0.7 fusion.35
  23.6 0.8 select_reduce_fusion
  24.4 0.7 bitcast_add_fusion
  25.1 2.6 collective-permute-start.5
  27.8 0.7 fusion.36
  28.5 0.8 select_reduce_fusion.1
  29.4 1.1 fusion.24
  30.5 1.1 multiply_reduce_fusion.2
  31.6 0.7 multiply_bitcast_fusion
  32.3 0.7 add_convert_fusion.1
  33.0 0.7 broadcast_add_fusion.2
  33.7 0.6 broadcast_in_dim.14
  34.3 15.2 %all-to-all-start = ((f32[16,1,160]{2,1,0:T(1,128)}), f32[16,1,160]{2,1,0:T(1,128)S(1)}, u32[]{:S(2)}, u32[]{:S(2)}) async-start(f32[16,1,160]{2,1,0:T(1,128)} %broadcast_in_dim.14), calls=%async_computation | async-start | bytes 32768 | tf_op jit(solution)/shard_map/all_to_all | solution.py:133
  49.5 1.1 pad_maximum_fusion.6
  50.7 2.4 collective-permute-start.3
  53.2 0.5 slice.114
  53.7 7.2 %all-to-all-done = f32[16,1,160]{2,1,0:T(1,128)S(1)} async-done(((f32[16,1,160]{2,1,0:T(1,128)}), f32[16,1,160]{2,1,0:T(1,128)S(1)}, u32[]{:S(2)}, u32[]{:S(2)}) %all-to-all-start) | async-done | bytes 10272 | tf_op jit(solution)/shard_map/all_to_all | solution.py:133
  61.9 2.7 collective-permute-done.3
  64.6 1.2 slice.113
  67.1 1.4 fusion.15
  68.5 1.6 maximum_select_fusion
  70.1 0.4 pad_maximum_fusion
  70.5 0.2 fusion.82
  70.8 2.4 pad_maximum_fusion.1
  73.1 2.6 pad_maximum_fusion.2
  75.7 2.8 multiply_convert_fusion
  78.5 66.2 %all-gather.2.cloned.1.call-done = bf16[512,10752]{1,0:T(8,128)(2,1)} async-done(((bf16[32,10752]{1,0:T(8,128)(2,1)}), bf16[512,10752]{1,0:T(8,128)(2,1)}) %all-gather.2.cloned.1.call-update) | async-done | bytes 11010064 | tf_op jit(solution)/shard_map/all_gather | solution.py:118
  144.7 5.2 %fusion.9 = f32[512,512]{1,0:T(8,128)S(1)} fusion(bf16[3584,512]{1,0:T(8,128)(2,1)} %multiply_convert_fusion, bf16[512,10752]{1,0:T(8,128)(2,1)} %all-gather.2.cloned.1.call-done, f32[512]{0:T(512)S(1)} %mul.246), kind=kOutput, calls=%fused_computation.18 | convolution fusion | flops 1879310336 | bytes 8390656 | tf_op jit(solution)/shard_map/dot_general | solution.py:22
  149.9 0.2 fusion.23
  150.1 0.3 convolution_convert_fusion.4
  150.4 0.3 convolution_convert_fusion.5
  150.7 2.0 convolution_convert_fusion
  152.7 5.3 %fusion.6 = f32[512,512]{1,0:T(8,128)S(1)} fusion(bf16[3584,512]{1,0:T(8,128)(2,1)} %multiply_convert_fusion, bf16[512,10752]{1,0:T(8,128)(2,1)} %all-gather.2.cloned.1.call-done, f32[512]{0:T(512)S(1)} %mul.257), kind=kOutput, calls=%fused_computation.17 | convolution fusion | flops 1879310336 | bytes 8390656 | tf_op jit(solution)/shard_map/dot_general | solution.py:22
  158.0 3.4 %fusion.22 = (bf16[512,256]{1,0:T(8,128)(2,1)S(1)}, bf16[512,256]{1,0:T(8,128)(2,1)S(1)}) fusion(f32[512,512]{1,0:T(8,128)S(1)} %fusion.6, f32[512]{0:T(512)S(1)} %mul.254, bf16[256,3584]{1,0:T(8,128)(2,1)S(1)} %copy-done.5, bf16[512,10752]{1,0:T(8,128)(2,1)} %all-gather.2.cloned.1.call-done), kind=kOutput, calls=%fused_computation.41 | convolution fusion | flops 941359104 | bytes 7079936 | tf_op jit(solution)/shard_map/dot_general | solution.py:22
  161.5 0.4 convolution_convert_fusion.2
  161.9 0.4 convolution_convert_fusion.3
  162.2 1.6 convolution_convert_fusion.1
  164.0 7.7 %collective-permute-start.9 = (bf16[96,1792]{1,0:T(8,128)(2,1)S(1)}, bf16[96,1792]{1,0:T(8,128)(2,1)S(1)}, u32[]{:S(2)}, u32[]{:S(2)}) collective-permute-start(bf16[96,1792]{1,0:T(8,128)(2,1)S(1)} %get-tuple-element.31), channel_id=1, source_target_pairs={{0,482},{1,483},{2,484},{3,485},{4,486},{5,487},{6,480},{7,481},{8... | collective-permute-start | bytes 1032200 | tf_op jit(solution)/shard_map/ppermute | solution.py:54
  171.7 6.0 %collective-permute-start.8 = (bf16[96,1792]{1,0:T(8,128)(2,1)S(1)}, bf16[96,1792]{1,0:T(8,128)(2,1)S(1)}, u32[]{:S(2)}, u32[]{:S(2)}) collective-permute-start(bf16[96,1792]{1,0:T(8,128)(2,1)S(1)} %get-tuple-element.32), channel_id=1, source_target_pairs={{0,484},{1,485},{2,486},{3,487},{4,480},{5,481},{6,482},{7,483},{8... | collective-permute-start | bytes 1032200 | tf_op jit(solution)/shard_map/ppermute | solution.py:54
  177.7 2.3 collective-permute-start.7
  180.1 2.5 collective-permute-start.6
  182.5 15.7 %collective-permute-done.9 = bf16[96,1792]{1,0:T(8,128)(2,1)S(1)} collective-permute-done((bf16[96,1792]{1,0:T(8,128)(2,1)S(1)}, bf16[96,1792]{1,0:T(8,128)(2,1)S(1)}, u32[]{:S(2)}, u32[]{:S(2)}) %collective-permute-start.9) | collective-permute-done | bytes 344096 | tf_op jit(solution)/shard_map/ppermute | solution.py:54
  198.2 22.9 %collective-permute-done.8 = bf16[96,1792]{1,0:T(8,128)(2,1)S(1)} collective-permute-done((bf16[96,1792]{1,0:T(8,128)(2,1)S(1)}, bf16[96,1792]{1,0:T(8,128)(2,1)S(1)}, u32[]{:S(2)}, u32[]{:S(2)}) %collective-permute-start.8) | collective-permute-done | bytes 344096 | tf_op jit(solution)/shard_map/ppermute | solution.py:54
  221.1 2.9 %collective-permute-done.7 = bf16[96,1792]{1,0:T(8,128)(2,1)S(1)} collective-permute-done((bf16[96,1792]{1,0:T(8,128)(2,1)S(1)}, bf16[96,1792]{1,0:T(8,128)(2,1)S(1)}, u32[]{:S(2)}, u32[]{:S(2)}) %collective-permute-start.7) | collective-permute-done | bytes 344096 | tf_op jit(solution)/shard_map/ppermute | solution.py:54
  224.0 0.2 add_convert_fusion
  224.3 1.9 pad_maximum_fusion.4
  226.2 8.8 %all-to-all-start.1 = ((bf16[4,48,1792]{2,1,0:T(8,128)(2,1)}), bf16[4,48,1792]{2,1,0:T(8,128)(2,1)S(1)}, u32[]{:S(2)}, u32[]{:S(2)}) async-start(bf16[4,48,1792]{2,1,0:T(8,128)(2,1)} %pad_maximum_fusion.4), calls=%async_computation.2 | async-start | bytes 1376256 | tf_op jit(solution)/shard_map/all_to_all | solution.py:77
  235.1 1.1 convert_element_type.157
  236.2 34.1 %all-to-all-done.1 = bf16[4,48,1792]{2,1,0:T(8,128)(2,1)S(1)} async-done(((bf16[4,48,1792]{2,1,0:T(8,128)(2,1)}), bf16[4,48,1792]{2,1,0:T(8,128)(2,1)S(1)}, u32[]{:S(2)}, u32[]{:S(2)}) %all-to-all-start.1) | async-done | bytes 688160 | tf_op jit(solution)/shard_map/all_to_all | solution.py:77
  270.4 0.2 fusion.38
  270.6 0.2 fusion.37
  270.8 0.1 fusion.25
  271.0 2.6 collective-permute-start.10
  273.6 0.2 fusion.40
  273.8 0.2 fusion.39
  274.1 0.2 multiply_reduce_fusion.1
  274.3 0.9 fusion.34
  275.2 8.5 %collective-permute-done.10 = bf16[32,3584]{1,0:T(8,128)(2,1)S(1)} collective-permute-done((bf16[32,3584]{1,0:T(8,128)(2,1)S(1)}, bf16[32,3584]{1,0:T(8,128)(2,1)S(1)}, u32[]{:S(2)}, u32[]{:S(2)}) %collective-permute-start.10) | collective-permute-done | bytes 229408 | tf_op jit(solution)/shard_map/ppermute | solution.py:14
  283.7 0.7 copy.21
  (56 shorter events, 1.6 us)
Async XLA Ops:
  7.2 59.9 %copy-start = (bf16[1,128,3584]{2,1,0:T(8,128)(2,1)S(1)}, bf16[1,128,3584]{2,1,0:T(8,128)(2,1)}, u32[]{:S(2)}) copy-start(bf16[1,128,3584]{2,1,0:T(8,128)(2,1)} %param.17) | copy-start | bytes 2752516
  7.2 43.5 %copy-start.7 = (f32[1,3584]{1,0:T(1,128)S(1)}, f32[1,3584]{1,0:T(1,128)}, u32[]{:S(2)}) copy-start(f32[1,3584]{1,0:T(1,128)} %param.14) | copy-start | bytes 43012
  7.2 137.5 %all-gather.2.cloned.1.call-start = ((), (), s32[]{:S(2)}) async-start(), calls=%async_computation.3 | async-start | bytes 11698176 | tf_op jit(solution)/shard_map/all_gather | solution.py:118
  9.4 60.6 %collective-permute-start.1 = (bf16[3584,128]{1,0:T(8,128)(2,1)}, bf16[3584,128]{1,0:T(8,128)(2,1)S(1)}, u32[]{:S(2)}, u32[]{:S(2)}) collective-permute-start(bf16[3584,128]{1,0:T(8,128)(2,1)} %bitcast.70), channel_id=1, source_target_pairs={{0,1},{1,0},{2,3},{3,2},{4,5},{5,4},{6,7},{7,6},{8,9},{9,8},{10,11... | collective-permute-start | bytes 2752520 | tf_op jit(solution)/shard_map/ppermute | solution.py:150
  11.3 58.7 %collective-permute-start = (bf16[3584,128]{1,0:T(8,128)(2,1)}, bf16[3584,128]{1,0:T(8,128)(2,1)S(1)}, u32[]{:S(2)}, u32[]{:S(2)}) collective-permute-start(bf16[3584,128]{1,0:T(8,128)(2,1)} %bitcast.73), channel_id=1, source_target_pairs={{0,1},{1,0},{2,3},{3,2},{4,5},{5,4},{6,7},{7,6},{8,9},{9,8},{10,11... | collective-permute-start | bytes 2752520 | tf_op jit(solution)/shard_map/ppermute | solution.py:149
  13.8 53.3 %collective-permute-start.2 = (bf16[128,3584]{1,0:T(8,128)(2,1)}, bf16[128,3584]{1,0:T(8,128)(2,1)}, u32[]{:S(2)}, u32[]{:S(2)}) collective-permute-start(bf16[128,3584]{1,0:T(8,128)(2,1)} %bitcast.67), channel_id=1, source_target_pairs={{0,1},{1,0},{2,3},{3,2},{4,5},{5,4},{6,7},{7,6},{8,9},{9,8},{10,11... | collective-permute-start | bytes 2752520 | tf_op jit(solution)/shard_map/ppermute | solution.py:151
  15.7 37.5 %collective-permute-start.4 = (f32[1,3584]{1,0:T(1,128)}, f32[1,3584]{1,0:T(1,128)S(1)}, u32[]{:S(2)}, u32[]{:S(2)}) collective-permute-start(f32[1,3584]{1,0:T(1,128)} %param.14), channel_id=1, source_target_pairs={{0,480},{32,0},{64,32},{96,64},{128,96},{160,128},{192,160},{224,1... | collective-permute-start | bytes 43016 | tf_op jit(solution)/shard_map/ppermute | solution.py:14
  25.1 25.6 %collective-permute-start.5 = (s32[1,32]{1,0:T(1,128)S(1)}, s32[1,32]{1,0:T(1,128)S(1)}, u32[]{:S(2)}, u32[]{:S(2)}) collective-permute-start(s32[1,32]{1,0:T(1,128)S(1)} %bitcast_add_fusion), channel_id=1, source_target_pairs={{0,480},{32,0},{64,32},{96,64},{128,96},{160,128},{192,160},{224,1... | collective-permute-start | bytes 392 | tf_op jit(solution)/shard_map/ppermute | solution.py:14
  34.3 26.5 %all-to-all-start = ((f32[16,1,160]{2,1,0:T(1,128)}), f32[16,1,160]{2,1,0:T(1,128)S(1)}, u32[]{:S(2)}, u32[]{:S(2)}) async-start(f32[16,1,160]{2,1,0:T(1,128)} %broadcast_in_dim.14), calls=%async_computation | async-start | bytes 32768 | tf_op jit(solution)/shard_map/all_to_all | solution.py:133
  49.5 174.7 %reduce-scatter.2.cloned.1.call-start = ((), (), s32[]{:S(2)}) async-start(), calls=%async_computation.4 | async-start | bytes 1720320 | tf_op jit(solution)/shard_map/reduce_scatter | solution.py:172
  50.7 13.8 %collective-permute-start.3 = (bf16[32,7168]{1,0:T(8,128)(2,1)S(1)}, bf16[32,7168]{1,0:T(8,128)(2,1)}, u32[]{:S(2)}, u32[]{:S(2)}) collective-permute-start(bf16[32,7168]{1,0:T(8,128)(2,1)S(1)} %pad_maximum_fusion.6), channel_id=1, source_target_pairs={{0,480},{32,0},{64,32},{96,64},{128,96},{160,128},{192,160},{224,1... | collective-permute-start | bytes 1376264 | tf_op jit(solution)/shard_map/ppermute | solution.py:14
  67.0 3.0 %copy-start.1 = (bf16[1,3584,128]{2,1,0:T(8,128)(2,1)S(1)}, bf16[1,3584,128]{2,1,0:T(8,128)(2,1)}, u32[]{:S(2)}) copy-start(bf16[1,3584,128]{2,1,0:T(8,128)(2,1)} %param.16) | copy-start | bytes 2752516
  67.0 3.0 %copy-start.2 = (bf16[1,3584,128]{2,1,0:T(8,128)(2,1)S(1)}, bf16[1,3584,128]{2,1,0:T(8,128)(2,1)}, u32[]{:S(2)}) copy-start(bf16[1,3584,128]{2,1,0:T(8,128)(2,1)} %param.15) | copy-start | bytes 2752516
  78.5 72.2 %copy-start.6 = (bf16[512,1792]{1,0:T(8,128)(2,1)S(1)}, bf16[512,1792]{1,0:T(8,128)(2,1)}, u32[]{:S(2)}) copy-start(bf16[512,1792]{1,0:T(8,128)(2,1)} %maximum_select_fusion) | copy-start | bytes 5505028
  152.7 5.3 %copy-start.5 = (bf16[256,3584]{1,0:T(8,128)(2,1)S(1)}, bf16[256,3584]{1,0:T(8,128)(2,1)}, u32[]{:S(2)}) copy-start(bf16[256,3584]{1,0:T(8,128)(2,1)} %pad_maximum_fusion.2) | copy-start | bytes 5505028
  158.0 4.2 %copy-start.3 = (bf16[1792,1024]{1,0:T(8,128)(2,1)S(1)}, bf16[1792,1024]{1,0:T(8,128)(2,1)}, u32[]{:S(2)}) copy-start(bf16[1792,1024]{1,0:T(8,128)(2,1)} %pad_maximum_fusion.1) | copy-start | bytes 11010052
  163.9 71.2 %copy-start.8 = (s32[1,32,1]{1,2,0:T(1,128)S(1)}, s32[1,32,1]{1,2,0:T(1,128)}, u32[]{:S(2)}) copy-start(s32[1,32,1]{1,2,0:T(1,128)} %param.19) | copy-start | bytes 388
  164.0 34.3 %collective-permute-start.9 = (bf16[96,1792]{1,0:T(8,128)(2,1)S(1)}, bf16[96,1792]{1,0:T(8,128)(2,1)S(1)}, u32[]{:S(2)}, u32[]{:S(2)}) collective-permute-start(bf16[96,1792]{1,0:T(8,128)(2,1)S(1)} %get-tuple-element.31), channel_id=1, source_target_pairs={{0,482},{1,483},{2,484},{3,485},{4,486},{5,487},{6,480},{7,481},{8... | collective-permute-start | bytes 1032200 | tf_op jit(solution)/shard_map/ppermute | solution.py:54
  171.7 49.4 %collective-permute-start.8 = (bf16[96,1792]{1,0:T(8,128)(2,1)S(1)}, bf16[96,1792]{1,0:T(8,128)(2,1)S(1)}, u32[]{:S(2)}, u32[]{:S(2)}) collective-permute-start(bf16[96,1792]{1,0:T(8,128)(2,1)S(1)} %get-tuple-element.32), channel_id=1, source_target_pairs={{0,484},{1,485},{2,486},{3,487},{4,480},{5,481},{6,482},{7,483},{8... | collective-permute-start | bytes 1032200 | tf_op jit(solution)/shard_map/ppermute | solution.py:54
  177.7 46.3 %collective-permute-start.7 = (bf16[96,1792]{1,0:T(8,128)(2,1)S(1)}, bf16[96,1792]{1,0:T(8,128)(2,1)S(1)}, u32[]{:S(2)}, u32[]{:S(2)}) collective-permute-start(bf16[96,1792]{1,0:T(8,128)(2,1)S(1)} %get-tuple-element.33), channel_id=1, source_target_pairs={{0,486},{1,487},{2,480},{3,481},{4,482},{5,483},{6,484},{7,485},{8... | collective-permute-start | bytes 1032200 | tf_op jit(solution)/shard_map/ppermute | solution.py:54
  180.1 44.0 %collective-permute-start.6 = (bf16[96,1792]{1,0:T(8,128)(2,1)S(1)}, bf16[96,1792]{1,0:T(8,128)(2,1)S(1)}, u32[]{:S(2)}, u32[]{:S(2)}) collective-permute-start(bf16[96,1792]{1,0:T(8,128)(2,1)S(1)} %get-tuple-element.30), channel_id=1, source_target_pairs={{0,480},{1,481},{2,482},{3,483},{4,484},{5,485},{6,486},{7,487},{8... | collective-permute-start | bytes 1032200 | tf_op jit(solution)/shard_map/ppermute | solution.py:54
  224.2 46.6 %copy-start.4 = (bf16[1,32,3584]{2,1,0:T(8,128)(2,1)S(1)}, bf16[1,32,3584]{2,1,0:T(8,128)(2,1)}, u32[]{:S(2)}) copy-start(bf16[1,32,3584]{2,1,0:T(8,128)(2,1)} %param.11) | copy-start | bytes 688132
  226.2 44.1 %all-to-all-start.1 = ((bf16[4,48,1792]{2,1,0:T(8,128)(2,1)}), bf16[4,48,1792]{2,1,0:T(8,128)(2,1)S(1)}, u32[]{:S(2)}, u32[]{:S(2)}) async-start(bf16[4,48,1792]{2,1,0:T(8,128)(2,1)} %pad_maximum_fusion.4), calls=%async_computation.2 | async-start | bytes 1376256 | tf_op jit(solution)/shard_map/all_to_all | solution.py:77
  271.0 12.7 %collective-permute-start.10 = (bf16[32,3584]{1,0:T(8,128)(2,1)S(1)}, bf16[32,3584]{1,0:T(8,128)(2,1)S(1)}, u32[]{:S(2)}, u32[]{:S(2)}) collective-permute-start(bf16[32,3584]{1,0:T(8,128)(2,1)S(1)} %fusion.25), channel_id=1, source_target_pairs={{0,32},{32,64},{64,96},{96,128},{128,160},{160,192},{192,224},{224... | collective-permute-start | bytes 688136 | tf_op jit(solution)/shard_map/ppermute | solution.py:14
Sparse Core Ops, SparseCore 0:
  10.1 134.5 all-gather.1
  152.8 65.1 reduce-scatter.1

commit v9 on v3

--- a/solution.py
+++ b/solution.py
@@ -44,21 +44,11 @@
     return jnp.concatenate(halves, axis=1)
 
 
-def shifts(count, side, steps):
+def partners(count, side, bits):
     pairs = []
     for device in range(count):
         chip, core = device // 2, device % 2
-        place = chip // side * side + (chip % side + steps) % side
-        pairs.append((device, 2 * place + core))
-    return pairs
-
-
-def shifts(count, side, steps):
-    pairs = []
-    for device in range(count):
-        chip, core = device // 2, device % 2
-        place = chip // side * side + (chip % side + steps) % side
-        pairs.append((device, 2 * place + core))
+        pairs.append((device, 2 * (chip // side * side + (chip % side ^ bits)) + core))
     return pairs
 
 
@@ -68,8 +58,9 @@
     groups = sources // side
     expert, rank = slots // CAP, slots % CAP
     source = jnp.arange(count, dtype=jnp.int32) // tokens
-    back = (me_place - source % side) % side
-    base = back * (groups * 2 * CAP) + (source // side) * (2 * CAP) + rank
+    differs = source % side ^ me_place
+    block = differs // 2 + differs % 2 * 2
+    base = block * (groups * 2 * CAP) + (source // side) * (2 * CAP) + rank
     base = jnp.where(expert == me_expert, base, -2 * CAP)
     row = jnp.arange(sources * 2 * CAP, dtype=jnp.int32)[:, None]
     return [(base[None, :] + h * CAP == row).astype(jnp.bfloat16) for h in range(2)]
@@ -77,13 +68,12 @@
 
 def join_group(partial, count, side):
     rows, width = partial.shape
-    part = rows // side
     blocks = partial.astype(jnp.bfloat16)
-    total = blocks[:part].astype(jnp.float32)
-    for k in range(1, side):
-        got = lax.ppermute(blocks[k * part : (k + 1) * part], "expert", shifts(count, side, -k))
-        total = total + got.astype(jnp.float32)
-    return total.astype(jnp.bfloat16).reshape(EXPERTS, 2 * CAP, width)
+    for part, bits in ((rows // 2, 1), (rows // 4, 2)):
+        got = lax.ppermute(blocks[part:], "expert", partners(count, side, bits))
+        total = blocks[:part].astype(jnp.float32) + got.astype(jnp.float32)
+        blocks = total.astype(jnp.bfloat16)
+    return blocks.reshape(EXPERTS, 2 * CAP, width)
 
 
 def across_groups(blocks, across):

time: 284 us -> 288 us (1.014)
  waiting for transfers between devices: 176 us -> 189 us
  starting transfers between devices: 49.1 us -> 37.4 us
    ppermute x3 -> x2, waiting for transfers between devices: 35.4 us -> 56.9 us  [join_group(): got = lax.ppermute(blocks[part:], 'expert', partners(count, side, bits))]
    reduce_scatter x1, waiting for transfers between devices: 8.22 us -> 0.02 us  [per_device(): lax.psum_scatter(part_f, 'expert', scatter_dimension=0, tiled=True, axis_...]
    all_to_all x1, starting transfers between devices: 11.5 us -> 5.55 us  [across_groups(): lax.all_to_all(blocks, 'expert', split_axis=0, concat_axis=0, tiled=True,...]
    ppermute x3 -> x2, starting transfers between devices: 8.64 us -> 4 us  [join_group(): got = lax.ppermute(blocks[part:], 'expert', partners(count, side, bits))]
  transfers between devices with their start and end apart: 12 -> 11, of which waited for: 7 -> 7; matrix products, arithmetic and copies ran while one was open for 11% -> 11% of each run, Pallas kernels for 0% -> 0%
where the time goes in v9:
time: 288 us; the launch traced here: 285 us
  waiting for transfers between devices  189 us (66%)
  starting transfers between devices  37.4 us (13%)
  other arithmetic  20.4 us (7%)
  matrix products  19.6 us (7%)
  between operations  14.4 us (5%)
  local copies, waits for them, and re-layouts  3.9 us (1%)
    all_gather x1, waiting for transfers between devices, per_device(): lax.all_gather(sent, 'expert', axis=0, tiled=True, axis_index_groups=same...  93.1 us
    ppermute x2, waiting for transfers between devices, join_group(): got = lax.ppermute(blocks[part:], 'expert', partners(count, side, bits))  56.9 us
    all_to_all x1, waiting for transfers between devices, across_groups(): lax.all_to_all(blocks, 'expert', split_axis=0, concat_axis=0, tiled=True,...  25.6 us
    dot_general x9, matrix products, dot(): lax.dot_general(a, b, (dims, ((), ())), preferred_element_type=jnp.float32)  19.6 us
    all_to_all x1, starting transfers between devices, per_device(): lax.all_to_all(jnp.broadcast_to(small[None, None, :], (ring, 1, 5 * token...  15.2 us
    ppermute x2, waiting for transfers between devices, passed_along(): return lax.ppermute(value, axis, pairs)  8.12 us
    ppermute x2, starting transfers between devices, passed_along(): return lax.ppermute(value, axis, pairs)  6.31 us
  transfers between devices with their start and end apart: 11, of which 7 were waited for; matrix products, arithmetic and copies ran while one was open for 11% of the time, Pallas kernels for 0%

profile of v9, /device:TPU:6, one launch (start us, length us, event | category | flops | bytes accessed | tf_op | source)
XLA Modules:
  0.0 285.1 jit_solution(2649954291766978756)
XLA Ops:
  7.2 2.1 pad_maximum_fusion.3
  9.3 0.7 fusion.40
  10.0 0.1 reduce_window_sum.17
  10.1 0.7 fusion.39
  10.8 0.1 reduce_window_sum.18
  10.9 0.8 select_reduce_fusion.1
  11.7 0.8 select_reduce_fusion
  12.5 1.1 fusion.23
  13.6 1.1 fusion.25
  14.7 0.7 multiply_bitcast_fusion
  15.4 0.7 broadcast_add_fusion.1
  16.1 0.1 concatenate.25
  16.2 0.6 broadcast_in_dim.22
  16.8 15.2 %all-to-all-start = ((f32[16,1,160]{2,1,0:T(1,128)}), f32[16,1,160]{2,1,0:T(1,128)S(1)}, u32[]{:S(2)}, u32[]{:S(2)}) async-start(f32[16,1,160]{2,1,0:T(1,128)} %broadcast_in_dim.22), calls=%async_computation | async-start | bytes 32768 | tf_op jit(solution)/shard_map/all_to_all | solution.py:126
  32.0 1.9 collective-permute-start
  34.0 2.4 collective-permute-start.1
  36.4 1.9 collective-permute-start.2
  38.3 0.8 reduce
  39.1 5.6 %all-to-all-done = f32[16,1,160]{2,1,0:T(1,128)S(1)} async-done(((f32[16,1,160]{2,1,0:T(1,128)}), f32[16,1,160]{2,1,0:T(1,128)S(1)}, u32[]{:S(2)}, u32[]{:S(2)}) %all-to-all-start) | async-done | bytes 10272 | tf_op jit(solution)/shard_map/all_to_all | solution.py:126
  44.6 0.1 sign_compare_fusion
  44.7 0.1 and.158
  44.8 0.1 fusion.79
  44.9 0.1 mul.203
  45.0 0.1 fusion.47
  45.1 0.1 div.112
  45.2 1.7 pad_maximum_fusion
  46.8 0.2 fusion.78
  47.1 2.4 pad_maximum_fusion.1
  49.5 1.4 pad_maximum_fusion.2
  50.8 0.2 copy-done
  51.0 0.6 copy-done.1
  51.6 2.8 multiply_convert_fusion
  54.4 93.1 %all-gather.2.cloned.1.call-done = bf16[512,10752]{1,0:T(8,128)(2,1)} async-done(((bf16[32,10752]{1,0:T(8,128)(2,1)}), bf16[512,10752]{1,0:T(8,128)(2,1)}) %all-gather.2.cloned.1.call-update) | async-done | bytes 11010064 | tf_op jit(solution)/shard_map/all_gather | solution.py:112
  147.5 5.2 %fusion.9 = f32[512,512]{1,0:T(8,128)S(1)} fusion(bf16[3584,512]{1,0:T(8,128)(2,1)} %multiply_convert_fusion, bf16[512,10752]{1,0:T(8,128)(2,1)} %all-gather.2.cloned.1.call-done, f32[512]{0:T(512)S(1)} %mul.203), kind=kOutput, calls=%fused_computation.14 | convolution fusion | flops 1879310336 | bytes 8390656 | tf_op jit(solution)/shard_map/dot_general | solution.py:22
  152.7 3.0 %convolution_convert_fusion = bf16[512,3584]{1,0:T(8,128)(2,1)} fusion(bf16[256,3584]{1,0:T(8,128)(2,1)S(1)} %copy-done.5, f32[512,512]{1,0:T(8,128)S(1)} %fusion.9, pred[512]{0:T(512)(128)(4,1)S(1)} %fusion.49), kind=kOutput, calls=%fused_computation.1 | convolution fusion | flops 942276608 | bytes 6554112 | tf_op jit(solution)/shard_map/dot_general | solution.py:22
  155.7 0.1 ne.250
  155.8 0.1 mul.220
  155.9 0.1 mul.217
  156.0 0.1 div.119
  156.1 0.1 rem.161
  156.2 5.2 %fusion.6 = f32[512,512]{1,0:T(8,128)S(1)} fusion(bf16[3584,512]{1,0:T(8,128)(2,1)} %multiply_convert_fusion, bf16[512,10752]{1,0:T(8,128)(2,1)} %all-gather.2.cloned.1.call-done, f32[512]{0:T(512)S(1)} %mul.220), kind=kOutput, calls=%fused_computation.13 | convolution fusion | flops 1879310336 | bytes 8390656 | tf_op jit(solution)/shard_map/dot_general | solution.py:22
  161.4 3.4 %fusion.20 = (bf16[512,256]{1,0:T(8,128)(2,1)S(1)}, bf16[512,256]{1,0:T(8,128)(2,1)S(1)}) fusion(f32[512,512]{1,0:T(8,128)S(1)} %fusion.6, f32[512]{0:T(512)S(1)} %mul.217, bf16[256,3584]{1,0:T(8,128)(2,1)S(1)} %copy-done.5, bf16[512,10752]{1,0:T(8,128)(2,1)} %all-gather.2.cloned.1.call-done), kind=kOutput, calls=%fused_computation.33 | convolution fusion | flops 941359104 | bytes 7079936 | tf_op jit(solution)/shard_map/dot_general | solution.py:22
  164.8 0.4 convolution_convert_fusion.2
  165.2 0.4 convolution_convert_fusion.3
  165.6 1.6 convolution_convert_fusion.1
  167.3 2.1 collective-permute-start.4
  169.4 32.1 %collective-permute-done.4 = bf16[192,1792]{1,0:T(8,128)(2,1)S(1)} collective-permute-done((bf16[192,1792]{1,0:T(8,128)(2,1)S(1)}, bf16[192,1792]{1,0:T(8,128)(2,1)S(1)}, u32[]{:S(2)}, u32[]{:S(2)}) %collective-permute-start.4) | collective-permute-done | bytes 688160 | tf_op jit(solution)/shard_map/ppermute | solution.py:73
  201.5 0.2 add_convert_fusion
  201.7 2.0 collective-permute-start.5
  203.6 24.8 %collective-permute-done.5 = bf16[96,1792]{1,0:T(8,128)(2,1)S(1)} collective-permute-done((bf16[96,1792]{1,0:T(8,128)(2,1)S(1)}, bf16[96,1792]{1,0:T(8,128)(2,1)S(1)}, u32[]{:S(2)}, u32[]{:S(2)}) %collective-permute-start.5) | collective-permute-done | bytes 344096 | tf_op jit(solution)/shard_map/ppermute | solution.py:73
  228.5 0.8 add_convert_fusion.1
  229.3 5.6 %all-to-all-start.1 = ((bf16[4,24,1792]{2,1,0:T(8,128)(2,1)}), bf16[4,24,1792]{2,1,0:T(8,128)(2,1)S(1)}, u32[]{:S(2)}, u32[]{:S(2)}) async-start(bf16[4,24,1792]{2,1,0:T(8,128)(2,1)} %bitcast.11), calls=%async_computation.2 | async-start | bytes 688128 | tf_op jit(solution)/shard_map/all_to_all | solution.py:80
  234.9 25.6 %all-to-all-done.1 = bf16[4,24,1792]{2,1,0:T(8,128)(2,1)S(1)} async-done(((bf16[4,24,1792]{2,1,0:T(8,128)(2,1)}), bf16[4,24,1792]{2,1,0:T(8,128)(2,1)S(1)}, u32[]{:S(2)}, u32[]{:S(2)}) %all-to-all-start.1) | async-done | bytes 344096 | tf_op jit(solution)/shard_map/all_to_all | solution.py:80
  260.4 0.2 fusion.42
  260.6 0.2 fusion.41
  260.9 0.2 fusion.32
  261.1 0.2 fusion.31
  261.3 4.4 %collective-permute-start.6 = (bf16[32,3584]{1,0:T(8,128)(2,1)S(1)}, bf16[32,3584]{1,0:T(8,128)(2,1)S(1)}, u32[]{:S(2)}, u32[]{:S(2)}) collective-permute-start(bf16[32,3584]{1,0:T(8,128)(2,1)S(1)} %fusion.31), channel_id=1, source_target_pairs={{0,480},{32,0},{64,32},{96,64},{128,96},{160,128},{192,160},{224,1... | collective-permute-start | bytes 688136 | tf_op jit(solution)/shard_map/ppermute | solution.py:14
  265.8 1.1 fusion.24
  266.8 1.9 collective-permute-start.3
  268.8 0.8 collective-permute-done.6
  269.6 7.3 %collective-permute-done.3 = bf16[32,3584]{1,0:T(8,128)(2,1)S(1)} collective-permute-done((bf16[32,3584]{1,0:T(8,128)(2,1)S(1)}, bf16[32,3584]{1,0:T(8,128)(2,1)S(1)}, u32[]{:S(2)}, u32[]{:S(2)}) %collective-permute-start.3) | collective-permute-done | bytes 229408 | tf_op jit(solution)/shard_map/ppermute | solution.py:14
  276.9 0.7 copy.22
  277.6 0.7 copy.23
  (32 shorter events, 0.3 us)
Async XLA Ops:
  7.2 140.3 %all-gather.2.cloned.1.call-start = ((), (), s32[]{:S(2)}) async-start(), calls=%async_computation.3 | async-start | bytes 11698176 | tf_op jit(solution)/shard_map/all_gather | solution.py:112
  16.8 27.9 %all-to-all-start = ((f32[16,1,160]{2,1,0:T(1,128)}), f32[16,1,160]{2,1,0:T(1,128)S(1)}, u32[]{:S(2)}, u32[]{:S(2)}) async-start(f32[16,1,160]{2,1,0:T(1,128)} %broadcast_in_dim.22), calls=%async_computation | async-start | bytes 32768 | tf_op jit(solution)/shard_map/all_to_all | solution.py:126
  32.0 233.7 %reduce-scatter.2.cloned.1.call-start = ((), (), s32[]{:S(2)}) async-start(), calls=%async_computation.4 | async-start | bytes 3899392 | tf_op jit(solution)/shard_map/reduce_scatter | solution.py:155
  32.0 13.1 %collective-permute-start = (bf16[3584,128]{1,0:T(8,128)(2,1)}, bf16[3584,128]{1,0:T(8,128)(2,1)S(1)}, u32[]{:S(2)}, u32[]{:S(2)}) collective-permute-start(bf16[3584,128]{1,0:T(8,128)(2,1)} %bitcast.42), channel_id=1, source_target_pairs={{0,1},{1,0},{2,3},{3,2},{4,5},{5,4},{6,7},{7,6},{8,9},{9,8},{10,11... | collective-permute-start | bytes 2752520 | tf_op jit(solution)/shard_map/ppermute | solution.py:140
  34.0 11.2 %collective-permute-start.1 = (bf16[3584,128]{1,0:T(8,128)(2,1)}, bf16[3584,128]{1,0:T(8,128)(2,1)S(1)}, u32[]{:S(2)}, u32[]{:S(2)}) collective-permute-start(bf16[3584,128]{1,0:T(8,128)(2,1)} %bitcast.39), channel_id=1, source_target_pairs={{0,1},{1,0},{2,3},{3,2},{4,5},{5,4},{6,7},{7,6},{8,9},{9,8},{10,11... | collective-permute-start | bytes 2752520 | tf_op jit(solution)/shard_map/ppermute | solution.py:141
  36.4 13.1 %collective-permute-start.2 = (bf16[128,3584]{1,0:T(8,128)(2,1)}, bf16[128,3584]{1,0:T(8,128)(2,1)S(1)}, u32[]{:S(2)}, u32[]{:S(2)}) collective-permute-start(bf16[128,3584]{1,0:T(8,128)(2,1)} %bitcast.49), channel_id=1, source_target_pairs={{0,1},{1,0},{2,3},{3,2},{4,5},{5,4},{6,7},{7,6},{8,9},{9,8},{10,11... | collective-permute-start | bytes 2752520 | tf_op jit(solution)/shard_map/ppermute | solution.py:142
  47.1 2.4 copy-start.6
  49.5 1.5 copy-start
  49.5 2.1 copy-start.1
  54.4 98.3 %copy-start.5 = (bf16[256,3584]{1,0:T(8,128)(2,1)S(1)}, bf16[256,3584]{1,0:T(8,128)(2,1)}, u32[]{:S(2)}) copy-start(bf16[256,3584]{1,0:T(8,128)(2,1)} %pad_maximum_fusion.2) | copy-start | bytes 5505028
  161.4 4.2 %copy-start.2 = (bf16[1792,1024]{1,0:T(8,128)(2,1)S(1)}, bf16[1792,1024]{1,0:T(8,128)(2,1)}, u32[]{:S(2)}) copy-start(bf16[1792,1024]{1,0:T(8,128)(2,1)} %pad_maximum_fusion.1) | copy-start | bytes 11010052
  167.2 67.6 %copy-start.8 = (s32[1,32,1]{1,2,0:T(1,128)S(1)}, s32[1,32,1]{1,2,0:T(1,128)}, u32[]{:S(2)}) copy-start(s32[1,32,1]{1,2,0:T(1,128)} %param.19) | copy-start | bytes 388
  167.2 93.6 %copy-start.3 = (bf16[1,32,3584]{2,1,0:T(8,128)(2,1)S(1)}, bf16[1,32,3584]{2,1,0:T(8,128)(2,1)}, u32[]{:S(2)}) copy-start(bf16[1,32,3584]{2,1,0:T(8,128)(2,1)} %param.12) | copy-start | bytes 688132
  167.3 93.8 %copy-start.7 = (bf16[1,32,3584]{2,1,0:T(8,128)(2,1)S(1)}, bf16[1,32,3584]{2,1,0:T(8,128)(2,1)}, u32[]{:S(2)}) copy-start(bf16[1,32,3584]{2,1,0:T(8,128)(2,1)} %param.13) | copy-start | bytes 688132
  167.3 98.4 %copy-start.4 = (bf16[1,32,3584]{2,1,0:T(8,128)(2,1)S(1)}, bf16[1,32,3584]{2,1,0:T(8,128)(2,1)}, u32[]{:S(2)}) copy-start(bf16[1,32,3584]{2,1,0:T(8,128)(2,1)} %param.11) | copy-start | bytes 688132
  167.3 34.2 %collective-permute-start.4 = (bf16[192,1792]{1,0:T(8,128)(2,1)S(1)}, bf16[192,1792]{1,0:T(8,128)(2,1)S(1)}, u32[]{:S(2)}, u32[]{:S(2)}) collective-permute-start(bf16[192,1792]{1,0:T(8,128)(2,1)S(1)} %slice.85), channel_id=1, source_target_pairs={{0,2},{1,3},{2,0},{3,1},{4,6},{5,7},{6,4},{7,5},{8,10},{9,11},{10,... | collective-permute-start | bytes 2064392 | tf_op jit(solution)/shard_map/ppermute | solution.py:73
  201.7 26.8 %collective-permute-start.5 = (bf16[96,1792]{1,0:T(8,128)(2,1)S(1)}, bf16[96,1792]{1,0:T(8,128)(2,1)S(1)}, u32[]{:S(2)}, u32[]{:S(2)}) collective-permute-start(bf16[96,1792]{1,0:T(8,128)(2,1)S(1)} %slice.87), channel_id=1, source_target_pairs={{0,4},{1,5},{2,6},{3,7},{4,0},{5,1},{6,2},{7,3},{8,12},{9,13},{10,... | collective-permute-start | bytes 1032200 | tf_op jit(solution)/shard_map/ppermute | solution.py:73
  229.3 31.1 %all-to-all-start.1 = ((bf16[4,24,1792]{2,1,0:T(8,128)(2,1)}), bf16[4,24,1792]{2,1,0:T(8,128)(2,1)S(1)}, u32[]{:S(2)}, u32[]{:S(2)}) async-start(bf16[4,24,1792]{2,1,0:T(8,128)(2,1)} %bitcast.11), calls=%async_computation.2 | async-start | bytes 688128 | tf_op jit(solution)/shard_map/all_to_all | solution.py:80
  261.3 8.3 %collective-permute-start.6 = (bf16[32,3584]{1,0:T(8,128)(2,1)S(1)}, bf16[32,3584]{1,0:T(8,128)(2,1)S(1)}, u32[]{:S(2)}, u32[]{:S(2)}) collective-permute-start(bf16[32,3584]{1,0:T(8,128)(2,1)S(1)} %fusion.31), channel_id=1, source_target_pairs={{0,480},{32,0},{64,32},{96,64},{128,96},{160,128},{192,160},{224,1... | collective-permute-start | bytes 688136 | tf_op jit(solution)/shard_map/ppermute | solution.py:14
  266.8 10.1 %collective-permute-start.3 = (bf16[32,3584]{1,0:T(8,128)(2,1)S(1)}, bf16[32,3584]{1,0:T(8,128)(2,1)S(1)}, u32[]{:S(2)}, u32[]{:S(2)}) collective-permute-start(bf16[32,3584]{1,0:T(8,128)(2,1)S(1)} %fusion.24), channel_id=1, source_target_pairs={{0,32},{32,64},{64,96},{96,128},{128,160},{160,192},{192,224},{224... | collective-permute-start | bytes 688136 | tf_op jit(solution)/shard_map/ppermute | solution.py:14
Sparse Core Ops, SparseCore 0:
  10.1 137.3 all-gather.1
  155.8 100.6 reduce-scatter.1

commit v10 on v9

--- a/solution.py
+++ b/solution.py
@@ -169,6 +169,8 @@
     table_b = across_groups(join_group(part_b, count, side), across)
 
     y = (xf + scale_f * moe_f.astype(jnp.float32)).astype(jnp.bfloat16)
+    seen = y[0, 0].astype(jnp.float32)
+    slot_b = jnp.where((seen > 1.0) & (seen < -1.0), 0, slot_b)
     d_normed = pick_back(table_b, slot_b)
     weighted = d_normed * gain
     inner = jnp.mean(xb * weighted, axis=-1, keepdims=True)

time: 288 us -> 284 us (0.986)
  waiting for transfers between devices: 189 us -> 181 us
    all_to_all x1, waiting for transfers between devices: 25.6 us -> 0.01 us  [across_groups(): lax.all_to_all(blocks, 'expert', split_axis=0, concat_axis=0, tiled=True,...]
    reduce_scatter x1, waiting for transfers between devices: 0.02 us -> 21.8 us  [per_device(): lax.psum_scatter(part_f, 'expert', scatter_dimension=0, tiled=True, axis_...]
    ppermute x2, waiting for transfers between devices: 8.12 us -> 3.51 us  [passed_along(): return lax.ppermute(value, axis, pairs)]
  transfers between devices with their start and end apart: 11 -> 11, of which waited for: 7 -> 6; matrix products, arithmetic and copies ran while one was open for 11% -> 11% of each run, Pallas kernels for 0% -> 0%
where the time goes in v10:
time: 284 us; the launch traced here: 280 us
  waiting for transfers between devices  181 us (64%)
  starting transfers between devices  39 us (14%)
  other arithmetic  20.5 us (7%)
  matrix products  19.6 us (7%)
  between operations  15.7 us (6%)
  local copies, waits for them, and re-layouts  4.41 us (2%)
    all_gather x1, waiting for transfers between devices, per_device(): lax.all_gather(sent, 'expert', axis=0, tiled=True, axis_index_groups=same...  93 us
    ppermute x2, waiting for transfers between devices, join_group(): got = lax.ppermute(blocks[part:], 'expert', partners(count, side, bits))  56.9 us
    reduce_scatter x1, waiting for transfers between devices, per_device(): lax.psum_scatter(part_f, 'expert', scatter_dimension=0, tiled=True, axis_...  21.8 us
    dot_general x9, matrix products, dot(): lax.dot_general(a, b, (dims, ((), ())), preferred_element_type=jnp.float32)  19.6 us
    all_to_all x1, starting transfers between devices, per_device(): lax.all_to_all(jnp.broadcast_to(small[None, None, :], (ring, 1, 5 * token...  15.2 us
    ppermute x2, starting transfers between devices, passed_along(): return lax.ppermute(value, axis, pairs)  7.94 us
  transfers between devices with their start and end apart: 11, of which 6 were waited for; matrix products, arithmetic and copies ran while one was open for 11% of the time, Pallas kernels for 0%

profile of v10, /device:TPU:6, one launch (start us, length us, event | category | flops | bytes accessed | tf_op | source)
XLA Modules:
  0.0 280.2 jit_solution(12842327533011000543)
XLA Ops:
  7.2 2.0 pad_maximum_fusion.3
  9.3 0.7 fusion.40
  10.0 0.1 reduce_window_sum.17
  10.1 0.7 fusion.39
  10.8 0.1 reduce_window_sum.18
  10.8 0.8 select_reduce_fusion.1
  11.7 0.8 select_reduce_fusion
  12.5 1.1 fusion.23
  13.6 1.1 fusion.25
  14.7 0.7 multiply_bitcast_fusion
  15.4 0.7 add_convert_fusion.2
  16.1 0.1 concatenate.25
  16.1 0.6 broadcast_in_dim.26
  16.8 15.2 %all-to-all-start = ((f32[16,1,160]{2,1,0:T(1,128)}), f32[16,1,160]{2,1,0:T(1,128)S(1)}, u32[]{:S(2)}, u32[]{:S(2)}) async-start(f32[16,1,160]{2,1,0:T(1,128)} %broadcast_in_dim.26), calls=%async_computation | async-start | bytes 32768 | tf_op jit(solution)/shard_map/all_to_all | solution.py:126
  32.0 1.9 collective-permute-start
  33.9 2.4 collective-permute-start.1
  36.4 1.9 collective-permute-start.2
  38.3 0.8 reduce
  39.1 5.7 %all-to-all-done = f32[16,1,160]{2,1,0:T(1,128)S(1)} async-done(((f32[16,1,160]{2,1,0:T(1,128)}), f32[16,1,160]{2,1,0:T(1,128)S(1)}, u32[]{:S(2)}, u32[]{:S(2)}) %all-to-all-start) | async-done | bytes 10272 | tf_op jit(solution)/shard_map/all_to_all | solution.py:126
  44.7 0.1 sign_compare_fusion
  44.8 0.1 and.164
  44.9 0.1 fusion.79
  45.0 0.1 mul.203
  45.0 0.1 fusion.47
  45.1 0.1 div.112
  45.2 1.7 pad_maximum_fusion
  46.9 0.2 fusion.78
  47.2 2.4 pad_maximum_fusion.1
  49.6 1.4 pad_maximum_fusion.2
  50.9 0.2 copy-done
  51.1 0.6 copy-done.1
  51.7 2.8 multiply_convert_fusion
  54.5 93.0 %all-gather.2.cloned.1.call-done = bf16[512,10752]{1,0:T(8,128)(2,1)} async-done(((bf16[32,10752]{1,0:T(8,128)(2,1)}), bf16[512,10752]{1,0:T(8,128)(2,1)}) %all-gather.2.cloned.1.call-update) | async-done | bytes 11010064 | tf_op jit(solution)/shard_map/all_gather | solution.py:112
  147.5 5.2 %fusion.9 = f32[512,512]{1,0:T(8,128)S(1)} fusion(bf16[3584,512]{1,0:T(8,128)(2,1)} %multiply_convert_fusion, bf16[512,10752]{1,0:T(8,128)(2,1)} %all-gather.2.cloned.1.call-done, f32[512]{0:T(512)S(1)} %mul.203), kind=kOutput, calls=%fused_computation.14 | convolution fusion | flops 1879310336 | bytes 8390656 | tf_op jit(solution)/shard_map/dot_general | solution.py:22
  152.7 3.0 %convolution_convert_fusion = bf16[512,3584]{1,0:T(8,128)(2,1)} fusion(bf16[256,3584]{1,0:T(8,128)(2,1)S(1)} %copy-done.5, f32[512,512]{1,0:T(8,128)S(1)} %fusion.9, pred[512]{0:T(512)(128)(4,1)S(1)} %fusion.49), kind=kOutput, calls=%fused_computation.1 | convolution fusion | flops 942276608 | bytes 6554112 | tf_op jit(solution)/shard_map/dot_general | solution.py:22
  155.7 0.1 ne.247
  155.8 0.1 mul.220
  155.9 0.1 mul.217
  156.0 0.1 div.119
  156.1 0.1 rem.161
  156.2 5.2 %fusion.6 = f32[512,512]{1,0:T(8,128)S(1)} fusion(bf16[3584,512]{1,0:T(8,128)(2,1)} %multiply_convert_fusion, bf16[512,10752]{1,0:T(8,128)(2,1)} %all-gather.2.cloned.1.call-done, f32[512]{0:T(512)S(1)} %mul.220), kind=kOutput, calls=%fused_computation.13 | convolution fusion | flops 1879310336 | bytes 8390656 | tf_op jit(solution)/shard_map/dot_general | solution.py:22
  161.4 3.4 %fusion.20 = (bf16[512,256]{1,0:T(8,128)(2,1)S(1)}, bf16[512,256]{1,0:T(8,128)(2,1)S(1)}) fusion(f32[512,512]{1,0:T(8,128)S(1)} %fusion.6, f32[512]{0:T(512)S(1)} %mul.217, bf16[256,3584]{1,0:T(8,128)(2,1)S(1)} %copy-done.5, bf16[512,10752]{1,0:T(8,128)(2,1)} %all-gather.2.cloned.1.call-done), kind=kOutput, calls=%fused_computation.33 | convolution fusion | flops 941359104 | bytes 7079936 | tf_op jit(solution)/shard_map/dot_general | solution.py:22
  164.8 0.4 convolution_convert_fusion.2
  165.2 0.4 convolution_convert_fusion.3
  165.6 1.6 convolution_convert_fusion.1
  167.3 2.1 collective-permute-start.4
  169.4 32.1 %collective-permute-done.4 = bf16[192,1792]{1,0:T(8,128)(2,1)S(1)} collective-permute-done((bf16[192,1792]{1,0:T(8,128)(2,1)S(1)}, bf16[192,1792]{1,0:T(8,128)(2,1)S(1)}, u32[]{:S(2)}, u32[]{:S(2)}) %collective-permute-start.4) | collective-permute-done | bytes 688160 | tf_op jit(solution)/shard_map/ppermute | solution.py:73
  201.5 0.2 add_convert_fusion
  201.7 2.0 collective-permute-start.5
  203.7 24.8 %collective-permute-done.5 = bf16[96,1792]{1,0:T(8,128)(2,1)S(1)} collective-permute-done((bf16[96,1792]{1,0:T(8,128)(2,1)S(1)}, bf16[96,1792]{1,0:T(8,128)(2,1)S(1)}, u32[]{:S(2)}, u32[]{:S(2)}) %collective-permute-start.5) | collective-permute-done | bytes 344096 | tf_op jit(solution)/shard_map/ppermute | solution.py:73
  228.5 0.8 add_convert_fusion.1
  229.3 5.5 %all-to-all-start.1 = ((bf16[4,24,1792]{2,1,0:T(8,128)(2,1)}), bf16[4,24,1792]{2,1,0:T(8,128)(2,1)S(1)}, u32[]{:S(2)}, u32[]{:S(2)}) async-start(bf16[4,24,1792]{2,1,0:T(8,128)(2,1)} %bitcast.12), calls=%async_computation.2 | async-start | bytes 688128 | tf_op jit(solution)/shard_map/all_to_all | solution.py:80
  234.8 21.8 %reduce-scatter.2.cloned.1.call-done = bf16[32,3584]{1,0:T(8,128)(2,1)} async-done(((bf16[512,3584]{1,0:T(8,128)(2,1)}), bf16[32,3584]{1,0:T(8,128)(2,1)}) %reduce-scatter.2.cloned.1.call-update) | async-done | bytes 229392 | tf_op jit(solution)/shard_map/reduce_scatter | solution.py:155
  256.7 1.1 fusion.24
  257.7 0.5 slice.83
  258.2 3.5 %collective-permute-start.3 = (bf16[32,3584]{1,0:T(8,128)(2,1)S(1)}, bf16[32,3584]{1,0:T(8,128)(2,1)S(1)}, u32[]{:S(2)}, u32[]{:S(2)}) collective-permute-start(bf16[32,3584]{1,0:T(8,128)(2,1)S(1)} %fusion.24), channel_id=1, source_target_pairs={{0,32},{32,64},{64,96},{96,128},{128,160},{160,192},{192,224},{224... | collective-permute-start | bytes 688136 | tf_op jit(solution)/shard_map/ppermute | solution.py:14
  263.1 0.2 fusion.42
  263.3 0.2 fusion.41
  263.6 0.2 fusion.32
  263.8 0.2 fusion.31
  264.0 4.4 %collective-permute-start.6 = (bf16[32,3584]{1,0:T(8,128)(2,1)S(1)}, bf16[32,3584]{1,0:T(8,128)(2,1)S(1)}, u32[]{:S(2)}, u32[]{:S(2)}) collective-permute-start(bf16[32,3584]{1,0:T(8,128)(2,1)S(1)} %fusion.31), channel_id=1, source_target_pairs={{0,480},{32,0},{64,32},{96,64},{128,96},{160,128},{192,160},{224,1... | collective-permute-start | bytes 688136 | tf_op jit(solution)/shard_map/ppermute | solution.py:14
  268.5 3.5 %collective-permute-done.6 = bf16[32,3584]{1,0:T(8,128)(2,1)S(1)} collective-permute-done((bf16[32,3584]{1,0:T(8,128)(2,1)S(1)}, bf16[32,3584]{1,0:T(8,128)(2,1)S(1)}, u32[]{:S(2)}, u32[]{:S(2)}) %collective-permute-start.6) | collective-permute-done | bytes 229408 | tf_op jit(solution)/shard_map/ppermute | solution.py:14
  272.0 0.7 copy.22
  272.7 0.7 copy.23
  (36 shorter events, 0.3 us)
Async XLA Ops:
  7.2 140.3 %all-gather.2.cloned.1.call-start = ((), (), s32[]{:S(2)}) async-start(), calls=%async_computation.3 | async-start | bytes 11698176 | tf_op jit(solution)/shard_map/all_gather | solution.py:112
  16.8 28.0 %all-to-all-start = ((f32[16,1,160]{2,1,0:T(1,128)}), f32[16,1,160]{2,1,0:T(1,128)S(1)}, u32[]{:S(2)}, u32[]{:S(2)}) async-start(f32[16,1,160]{2,1,0:T(1,128)} %broadcast_in_dim.26), calls=%async_computation | async-start | bytes 32768 | tf_op jit(solution)/shard_map/all_to_all | solution.py:126
  32.0 224.7 %reduce-scatter.2.cloned.1.call-start = ((), (), s32[]{:S(2)}) async-start(), calls=%async_computation.4 | async-start | bytes 3899392 | tf_op jit(solution)/shard_map/reduce_scatter | solution.py:155
  32.0 13.2 %collective-permute-start = (bf16[3584,128]{1,0:T(8,128)(2,1)}, bf16[3584,128]{1,0:T(8,128)(2,1)S(1)}, u32[]{:S(2)}, u32[]{:S(2)}) collective-permute-start(bf16[3584,128]{1,0:T(8,128)(2,1)} %bitcast.43), channel_id=1, source_target_pairs={{0,1},{1,0},{2,3},{3,2},{4,5},{5,4},{6,7},{7,6},{8,9},{9,8},{10,11... | collective-permute-start | bytes 2752520 | tf_op jit(solution)/shard_map/ppermute | solution.py:140
  33.9 11.3 %collective-permute-start.1 = (bf16[3584,128]{1,0:T(8,128)(2,1)}, bf16[3584,128]{1,0:T(8,128)(2,1)S(1)}, u32[]{:S(2)}, u32[]{:S(2)}) collective-permute-start(bf16[3584,128]{1,0:T(8,128)(2,1)} %bitcast.40), channel_id=1, source_target_pairs={{0,1},{1,0},{2,3},{3,2},{4,5},{5,4},{6,7},{7,6},{8,9},{9,8},{10,11... | collective-permute-start | bytes 2752520 | tf_op jit(solution)/shard_map/ppermute | solution.py:141
  36.4 13.2 %collective-permute-start.2 = (bf16[128,3584]{1,0:T(8,128)(2,1)}, bf16[128,3584]{1,0:T(8,128)(2,1)S(1)}, u32[]{:S(2)}, u32[]{:S(2)}) collective-permute-start(bf16[128,3584]{1,0:T(8,128)(2,1)} %bitcast.50), channel_id=1, source_target_pairs={{0,1},{1,0},{2,3},{3,2},{4,5},{5,4},{6,7},{7,6},{8,9},{9,8},{10,11... | collective-permute-start | bytes 2752520 | tf_op jit(solution)/shard_map/ppermute | solution.py:142
  47.2 2.4 copy-start.6
  49.5 1.6 copy-start
  49.5 2.1 copy-start.1
  54.5 98.2 %copy-start.5 = (bf16[256,3584]{1,0:T(8,128)(2,1)S(1)}, bf16[256,3584]{1,0:T(8,128)(2,1)}, u32[]{:S(2)}) copy-start(bf16[256,3584]{1,0:T(8,128)(2,1)} %pad_maximum_fusion.2) | copy-start | bytes 5505028
  161.4 4.2 %copy-start.2 = (bf16[1792,1024]{1,0:T(8,128)(2,1)S(1)}, bf16[1792,1024]{1,0:T(8,128)(2,1)}, u32[]{:S(2)}) copy-start(bf16[1792,1024]{1,0:T(8,128)(2,1)} %pad_maximum_fusion.1) | copy-start | bytes 11010052
  167.2 36.4 %copy-start.9 = (s32[1,32,1]{1,2,0:T(1,128)S(1)}, s32[1,32,1]{1,2,0:T(1,128)}, u32[]{:S(2)}) copy-start(s32[1,32,1]{1,2,0:T(1,128)} %param.19) | copy-start | bytes 388
  167.2 89.4 %copy-start.4 = (bf16[1,32,3584]{2,1,0:T(8,128)(2,1)S(1)}, bf16[1,32,3584]{2,1,0:T(8,128)(2,1)}, u32[]{:S(2)}) copy-start(bf16[1,32,3584]{2,1,0:T(8,128)(2,1)} %param.11) | copy-start | bytes 688132
  167.2 95.8 %copy-start.8 = (s32[1,32,1]{1,2,0:T(1,128)S(1)}, s32[1,32,1]{1,2,0:T(1,128)}, u32[]{:S(2)}) copy-start(s32[1,32,1]{1,2,0:T(1,128)} %param.20) | copy-start | bytes 388
  167.3 96.3 %copy-start.3 = (bf16[1,32,3584]{2,1,0:T(8,128)(2,1)S(1)}, bf16[1,32,3584]{2,1,0:T(8,128)(2,1)}, u32[]{:S(2)}) copy-start(bf16[1,32,3584]{2,1,0:T(8,128)(2,1)} %param.12) | copy-start | bytes 688132
  167.3 96.4 %copy-start.7 = (bf16[1,32,3584]{2,1,0:T(8,128)(2,1)S(1)}, bf16[1,32,3584]{2,1,0:T(8,128)(2,1)}, u32[]{:S(2)}) copy-start(bf16[1,32,3584]{2,1,0:T(8,128)(2,1)} %param.13) | copy-start | bytes 688132
  167.3 34.1 %collective-permute-start.4 = (bf16[192,1792]{1,0:T(8,128)(2,1)S(1)}, bf16[192,1792]{1,0:T(8,128)(2,1)S(1)}, u32[]{:S(2)}, u32[]{:S(2)}) collective-permute-start(bf16[192,1792]{1,0:T(8,128)(2,1)S(1)} %slice.90), channel_id=1, source_target_pairs={{0,2},{1,3},{2,0},{3,1},{4,6},{5,7},{6,4},{7,5},{8,10},{9,11},{10,... | collective-permute-start | bytes 2064392 | tf_op jit(solution)/shard_map/ppermute | solution.py:73
  201.7 26.8 %collective-permute-start.5 = (bf16[96,1792]{1,0:T(8,128)(2,1)S(1)}, bf16[96,1792]{1,0:T(8,128)(2,1)S(1)}, u32[]{:S(2)}, u32[]{:S(2)}) collective-permute-start(bf16[96,1792]{1,0:T(8,128)(2,1)S(1)} %slice.92), channel_id=1, source_target_pairs={{0,4},{1,5},{2,6},{3,7},{4,0},{5,1},{6,2},{7,3},{8,12},{9,13},{10,... | collective-permute-start | bytes 1032200 | tf_op jit(solution)/shard_map/ppermute | solution.py:73
  229.3 33.8 %all-to-all-start.1 = ((bf16[4,24,1792]{2,1,0:T(8,128)(2,1)}), bf16[4,24,1792]{2,1,0:T(8,128)(2,1)S(1)}, u32[]{:S(2)}, u32[]{:S(2)}) async-start(bf16[4,24,1792]{2,1,0:T(8,128)(2,1)} %bitcast.12), calls=%async_computation.2 | async-start | bytes 688128 | tf_op jit(solution)/shard_map/all_to_all | solution.py:80
  258.2 10.2 %collective-permute-start.3 = (bf16[32,3584]{1,0:T(8,128)(2,1)S(1)}, bf16[32,3584]{1,0:T(8,128)(2,1)S(1)}, u32[]{:S(2)}, u32[]{:S(2)}) collective-permute-start(bf16[32,3584]{1,0:T(8,128)(2,1)S(1)} %fusion.24), channel_id=1, source_target_pairs={{0,32},{32,64},{64,96},{96,128},{128,160},{160,192},{192,224},{224... | collective-permute-start | bytes 688136 | tf_op jit(solution)/shard_map/ppermute | solution.py:14
  264.0 8.0 %collective-permute-start.6 = (bf16[32,3584]{1,0:T(8,128)(2,1)S(1)}, bf16[32,3584]{1,0:T(8,128)(2,1)S(1)}, u32[]{:S(2)}, u32[]{:S(2)}) collective-permute-start(bf16[32,3584]{1,0:T(8,128)(2,1)S(1)} %fusion.31), channel_id=1, source_target_pairs={{0,480},{32,0},{64,32},{96,64},{128,96},{160,128},{192,160},{224,1... | collective-permute-start | bytes 688136 | tf_op jit(solution)/shard_map/ppermute | solution.py:14
Sparse Core Ops, SparseCore 0:
  10.1 137.3 all-gather.1
  155.8 100.7 reduce-scatter.1

commit v11 on v10

--- a/solution.py
+++ b/solution.py
@@ -66,14 +66,29 @@
     return [(base[None, :] + h * CAP == row).astype(jnp.bfloat16) for h in range(2)]
 
 
-def join_group(partial, count, side):
+def far_in_section(value, sections, count, side, steps):
+    far = dict(partners(count, side, 2))
+    pairs = [
+        (s * count + d, (s + steps) % sections * count + far[d])
+        for s in range(sections)
+        for d in range(count)
+    ]
+    return lax.ppermute(value, ("section", "expert"), pairs)
+
+
+def add(a, b):
+    return (a.astype(jnp.float32) + b.astype(jnp.float32)).astype(jnp.bfloat16)
+
+
+def join_group(partial, sections, count, side, steps):
     rows, width = partial.shape
     blocks = partial.astype(jnp.bfloat16)
-    for part, bits in ((rows // 2, 1), (rows // 4, 2)):
-        got = lax.ppermute(blocks[part:], "expert", partners(count, side, bits))
-        total = blocks[:part].astype(jnp.float32) + got.astype(jnp.float32)
-        blocks = total.astype(jnp.bfloat16)
-    return blocks.reshape(EXPERTS, 2 * CAP, width)
+    got = lax.ppermute(blocks[rows // 2 :], "expert", partners(count, side, 1))
+    blocks = add(blocks[: rows // 2], got)
+    part = rows // 4
+    own = passed_along(blocks[:part], "section", steps)
+    got = far_in_section(blocks[part:], sections, count, side, steps)
+    return add(own, got).reshape(EXPERTS, 2 * CAP, width)
 
 
 def across_groups(blocks, across):
@@ -113,7 +128,6 @@
 
     xf = x_fwd[0].astype(jnp.float32)
     xb = x_bwd[0].astype(jnp.float32)
-    up32 = grad_out[0].astype(jnp.float32)
     scale_f = gate_fwd[0].astype(jnp.float32) / 256.0
     scale_b = gate_bwd[0].astype(jnp.float32) / 256.0
     r_f = rms_scale(xf)
@@ -145,6 +159,11 @@
     w_dn = jnp.concatenate([w_down[0], down_o], axis=0)
     hid = w_dn.shape[0]
     in_stack = jnp.concatenate([w_in[:half], w_in[half:]], axis=1)
+    last_b = passed_along(sent[:, width:], "section", -1)
+    last_gain = passed_along(norm_gain, "section", -1)
+    last_slot = passed_along(slot_b[None, :], "section", -1)[0]
+    seen = last_b[0, 0].astype(jnp.float32) + last_gain[0, 0] + last_slot[0].astype(jnp.float32)
+    w_dn = jnp.where((seen > 1.0) & (seen < -1.0), 0, w_dn)
     w_gained, w_dn, in_stack = lax.optimization_barrier((w_gained, w_dn, in_stack))
 
     pre_f = dot(got[:, :width], w_gained, ((1,), (0,))) * rs_f[:, None]
@@ -166,17 +185,19 @@
     places = packers(slots_b, me_expert, me_place, tokens, side)
     parts = [dot(p, hidden_b, ((1,), (0,))).astype(jnp.bfloat16) for p in places]
     part_b = dot(jnp.concatenate(parts, axis=1), in_stack, ((1,), (1,)))
-    table_b = across_groups(join_group(part_b, count, side), across)
+    table_b = across_groups(join_group(part_b, lax.axis_size("section"), count, side, -1), across)
 
     y = (xf + scale_f * moe_f.astype(jnp.float32)).astype(jnp.bfloat16)
     seen = y[0, 0].astype(jnp.float32)
-    slot_b = jnp.where((seen > 1.0) & (seen < -1.0), 0, slot_b)
-    d_normed = pick_back(table_b, slot_b)
-    weighted = d_normed * gain
-    inner = jnp.mean(xb * weighted, axis=-1, keepdims=True)
-    dx = (up32 + (r_b * weighted - xb * r_b * r_b * r_b * inner)).astype(jnp.bfloat16)
+    last_slot = jnp.where((seen > 1.0) & (seen < -1.0), 0, last_slot)
+    d_normed = pick_back(table_b, last_slot)
+    last_b = last_b.astype(jnp.float32)
+    last_x, last_g = last_b[:, :width], last_b[:, width:]
+    r = rms_scale(last_x)
+    weighted = d_normed * last_gain
+    inner = jnp.mean(last_x * weighted, axis=-1, keepdims=True)
+    dx_prev = (last_g + (r * weighted - last_x * r * r * r * inner)).astype(jnp.bfloat16)
     y_next = passed_along(y, "section", 1)
-    dx_prev = passed_along(dx, "section", -1)
     return (y_next[None], dx_prev[None])
 
 

time: 284 us -> 278 us (0.979); the launches traced: 280 us -> 277 us
  waiting for transfers between devices: 181 us -> 159 us
  starting transfers between devices: 39 us -> 50.5 us
  other arithmetic: 20.5 us -> 26.4 us
    all_gather x1, waiting for transfers between devices: 93 us -> 77.5 us  [per_device(): lax.all_gather(sent, 'expert', axis=0, tiled=True, axis_index_groups=same...]
    ppermute x2 -> x5, starting transfers between devices: 7.94 us -> 18.3 us  [passed_along(): return lax.ppermute(value, axis, pairs)]
    ppermute x2 -> x5, waiting for transfers between devices: 3.51 us -> 13.6 us  [passed_along(): return lax.ppermute(value, axis, pairs)]
    reduce_scatter x1, waiting for transfers between devices: 21.8 us -> 15.6 us  [per_device(): lax.psum_scatter(part_f, 'expert', scatter_dimension=0, tiled=True, axis_...]
    all_to_all x1, waiting for transfers between devices: 5.65 us -> 0.01 us  [per_device(): lax.all_to_all(jnp.broadcast_to(small[None, None, :], (ring, 1, 5 * token...]
    ppermute x2, waiting for transfers between devices: 56.9 us -> 52.1 us  [the longest x1 32 us: join_group(): got = lax.ppermute(blocks[rows // 2:], 'expert', partners(count, side, 1))]
  transfers between devices with their start and end apart: 11 -> 14, of which waited for: 6 -> 7; matrix products, arithmetic and copies ran while one was open for 11% -> 14% of each run, Pallas kernels for 0% -> 0%
where the time goes in v11:
time: 278 us; the launch traced here: 277 us
  waiting for transfers between devices  159 us (57%)
  starting transfers between devices  50.5 us (18%)
  other arithmetic  26.4 us (9%)
  matrix products  19.7 us (7%)
  between operations  17.1 us (6%)
  local copies, waits for them, and re-layouts  4.64 us (2%)
    all_gather x1, waiting for transfers between devices, per_device(): lax.all_gather(sent, 'expert', axis=0, tiled=True, axis_index_groups=same...  77.5 us
    ppermute x1, waiting for transfers between devices, join_group(): got = lax.ppermute(blocks[rows // 2:], 'expert', partners(count, side, 1))  32 us
    ppermute x1, waiting for transfers between devices, far_in_section(): return lax.ppermute(value, ('section', 'expert'), pairs)  20.2 us
    dot_general x9, matrix products, dot(): lax.dot_general(a, b, (dims, ((), ())), preferred_element_type=jnp.float32)  19.7 us
    ppermute x5, starting transfers between devices, passed_along(): return lax.ppermute(value, axis, pairs)  18.3 us
    reduce_scatter x1, waiting for transfers between devices, per_device(): lax.psum_scatter(part_f, 'expert', scatter_dimension=0, tiled=True, axis_...  15.6 us
    all_to_all x1, starting transfers between devices, per_device(): lax.all_to_all(jnp.broadcast_to(small[None, None, :], (ring, 1, 5 * token...  15.2 us
    ppermute x5, waiting for transfers between devices, passed_along(): return lax.ppermute(value, axis, pairs)  13.6 us
  transfers between devices with their start and end apart: 14, of which 7 were waited for; matrix products, arithmetic and copies ran while one was open for 14% of the time, Pallas kernels for 0%

profile of v11, /device:TPU:6, one launch (start us, length us, event | category | flops | bytes accessed | tf_op | source)
XLA Modules:
  0.0 277.4 jit_solution(12141473423291379400)
XLA Ops:
  7.2 2.2 pad_maximum_fusion.2
  9.4 0.7 fusion.33
  10.2 0.7 fusion.34
  11.0 0.8 select_reduce_fusion
  11.9 0.8 select_reduce_fusion.1
  12.7 1.1 multiply_reduce_fusion.2
  13.8 1.1 fusion.23
  14.9 0.7 multiply_bitcast_fusion
  15.6 0.7 add_convert_fusion.2
  16.2 0.7 add_convert_fusion.3
  16.9 0.1 concatenate.28
  17.0 0.6 broadcast_in_dim.32
  17.6 15.2 %all-to-all-start = ((f32[16,1,160]{2,1,0:T(1,128)}), f32[16,1,160]{2,1,0:T(1,128)S(1)}, u32[]{:S(2)}, u32[]{:S(2)}) async-start(f32[16,1,160]{2,1,0:T(1,128)} %broadcast_in_dim.32), calls=%async_computation | async-start | bytes 32768 | tf_op jit(solution)/shard_map/all_to_all | solution.py:140
  32.8 1.9 collective-permute-start
  34.8 2.4 collective-permute-start.1
  37.2 1.1 pad_maximum_fusion.4
  38.3 5.2 %collective-permute-start.2 = (bf16[32,7168]{1,0:T(8,128)(2,1)S(1)}, bf16[32,7168]{1,0:T(8,128)(2,1)}, u32[]{:S(2)}, u32[]{:S(2)}) collective-permute-start(bf16[32,7168]{1,0:T(8,128)(2,1)S(1)} %pad_maximum_fusion.4), channel_id=1, source_target_pairs={{0,480},{32,0},{64,32},{96,64},{128,96},{160,128},{192,160},{224,1... | collective-permute-start | bytes 1376264 | tf_op jit(solution)/shard_map/ppermute | solution.py:14
  43.5 2.7 collective-permute-start.3
  46.1 0.7 bitcast_add_fusion
  46.8 2.3 collective-permute-start.4
  49.2 4.5 %collective-permute-done.4 = s32[1,32]{1,0:T(1,128)S(1)} collective-permute-done((s32[1,32]{1,0:T(1,128)S(1)}, s32[1,32]{1,0:T(1,128)S(1)}, u32[]{:S(2)}, u32[]{:S(2)}) %collective-permute-start.4) | collective-permute-done | bytes 160 | tf_op jit(solution)/shard_map/ppermute | solution.py:14
  53.8 1.9 collective-permute-start.5
  55.7 0.5 slice.102
  56.2 0.1 fusion.41
  56.3 0.1 sign_compare_fusion
  56.4 0.1 div.118
  56.5 0.1 and.167
  56.7 0.1 mul.215
  56.8 1.1 slice.101
  59.2 1.6 pad_maximum_fusion
  60.8 0.2 fusion.72
  61.1 2.3 pad_maximum_fusion.1
  63.4 2.7 maximum_select_fusion
  66.2 3.9 %multiply_convert_fusion = bf16[3584,512]{1,0:T(8,128)(2,1)} fusion(f32[3584]{0:T(1024)S(1)} %reduce, bf16[3584,128]{1,0:T(8,128)(2,1)} %collective-permute-done.1, bf16[3584,128]{1,0:T(8,128)(2,1)S(1)} %bitcast.59, bf16[3584,128]{1,0:T(8,128)(2,1)S(1)} %collective-permute-done, bf16[3584,128]{1,0:T(8,128)(2,1)S(1)} %bitcast.62), kind=kLoop, calls=%fused_computation | loop fusion | flops 18350080 | bytes 7354368 | tf_op jit(solution)/shard_map/convert_element_type | solution.py:158
  70.0 77.5 %all-gather.2.cloned.1.call-done = bf16[512,10752]{1,0:T(8,128)(2,1)} async-done(((bf16[32,10752]{1,0:T(8,128)(2,1)}), bf16[512,10752]{1,0:T(8,128)(2,1)}) %all-gather.2.cloned.1.call-update) | async-done | bytes 11010064 | tf_op jit(solution)/shard_map/all_gather | solution.py:127
  147.5 5.2 %fusion.9 = f32[512,512]{1,0:T(8,128)S(1)} fusion(bf16[3584,512]{1,0:T(8,128)(2,1)} %multiply_convert_fusion, bf16[512,10752]{1,0:T(8,128)(2,1)} %all-gather.2.cloned.1.call-done, f32[512]{0:T(512)S(1)} %mul.215), kind=kOutput, calls=%fused_computation.14 | convolution fusion | flops 1879310336 | bytes 8390656 | tf_op jit(solution)/shard_map/dot_general | solution.py:22
  152.8 3.0 %convolution_convert_fusion = bf16[512,3584]{1,0:T(8,128)(2,1)} fusion(bf16[256,3584]{1,0:T(8,128)(2,1)S(1)} %copy-done.4, f32[512,512]{1,0:T(8,128)S(1)} %fusion.9, pred[512]{0:T(512)(128)(4,1)S(1)} %fusion.43), kind=kOutput, calls=%fused_computation.1 | convolution fusion | flops 942276608 | bytes 6554112 | tf_op jit(solution)/shard_map/dot_general | solution.py:22
  155.8 0.1 mul.233
  156.1 0.1 ne.251
  156.2 5.2 %fusion.6 = f32[512,512]{1,0:T(8,128)S(1)} fusion(bf16[3584,512]{1,0:T(8,128)(2,1)} %multiply_convert_fusion, bf16[512,10752]{1,0:T(8,128)(2,1)} %all-gather.2.cloned.1.call-done, f32[512]{0:T(512)S(1)} %mul.233), kind=kOutput, calls=%fused_computation.13 | convolution fusion | flops 1879310336 | bytes 8390656 | tf_op jit(solution)/shard_map/dot_general | solution.py:22
  161.5 3.4 %fusion.20 = (bf16[512,256]{1,0:T(8,128)(2,1)S(1)}, bf16[512,256]{1,0:T(8,128)(2,1)S(1)}) fusion(f32[512,512]{1,0:T(8,128)S(1)} %fusion.6, f32[512]{0:T(512)S(1)} %mul.230, bf16[256,3584]{1,0:T(8,128)(2,1)S(1)} %copy-done.4, bf16[512,10752]{1,0:T(8,128)(2,1)} %all-gather.2.cloned.1.call-done), kind=kOutput, calls=%fused_computation.30 | convolution fusion | flops 941359104 | bytes 7079936 | tf_op jit(solution)/shard_map/dot_general | solution.py:22
  164.9 0.4 convolution_convert_fusion.3
  165.3 0.4 convolution_convert_fusion.2
  165.7 1.6 convolution_convert_fusion.1
  167.4 2.1 collective-permute-start.7
  169.4 32.0 %collective-permute-done.7 = bf16[192,1792]{1,0:T(8,128)(2,1)S(1)} collective-permute-done((bf16[192,1792]{1,0:T(8,128)(2,1)S(1)}, bf16[192,1792]{1,0:T(8,128)(2,1)S(1)}, u32[]{:S(2)}, u32[]{:S(2)}) %collective-permute-start.7) | collective-permute-done | bytes 688160 | tf_op jit(solution)/shard_map/ppermute | solution.py:86
  201.4 0.2 add_convert_fusion
  201.7 4.9 %collective-permute-start.8 = (bf16[96,1792]{1,0:T(8,128)(2,1)S(1)}, bf16[96,1792]{1,0:T(8,128)(2,1)S(1)}, u32[]{:S(2)}, u32[]{:S(2)}) collective-permute-start(bf16[96,1792]{1,0:T(8,128)(2,1)S(1)} %get-tuple-element.22), channel_id=1, source_target_pairs={{0,480},{32,0},{64,32},{96,64},{128,96},{160,128},{192,160},{224,1... | collective-permute-start | bytes 1032200 | tf_op jit(solution)/shard_map/ppermute | solution.py:14
  206.6 2.3 collective-permute-start.9
  209.0 1.1 convert_element_type.145
  210.1 3.9 %collective-permute-done.8 = bf16[96,1792]{1,0:T(8,128)(2,1)S(1)} collective-permute-done((bf16[96,1792]{1,0:T(8,128)(2,1)S(1)}, bf16[96,1792]{1,0:T(8,128)(2,1)S(1)}, u32[]{:S(2)}, u32[]{:S(2)}) %collective-permute-start.8) | collective-permute-done | bytes 344096 | tf_op jit(solution)/shard_map/ppermute | solution.py:14
  213.9 20.2 %collective-permute-done.9 = bf16[96,1792]{1,0:T(8,128)(2,1)S(1)} collective-permute-done((bf16[96,1792]{1,0:T(8,128)(2,1)S(1)}, bf16[96,1792]{1,0:T(8,128)(2,1)S(1)}, u32[]{:S(2)}, u32[]{:S(2)}) %collective-permute-start.9) | collective-permute-done | bytes 344096 | tf_op jit(solution)/shard_map/ppermute | solution.py:76
  234.1 0.8 add_convert_fusion.1
  234.9 6.3 %all-to-all-start.1 = ((bf16[4,24,1792]{2,1,0:T(8,128)(2,1)}), bf16[4,24,1792]{2,1,0:T(8,128)(2,1)S(1)}, u32[]{:S(2)}, u32[]{:S(2)}) async-start(bf16[4,24,1792]{2,1,0:T(8,128)(2,1)} %bitcast.18), calls=%async_computation.2 | async-start | bytes 688128 | tf_op jit(solution)/shard_map/all_to_all | solution.py:95
  241.2 15.6 %reduce-scatter.2.cloned.1.call-done = bf16[32,3584]{1,0:T(8,128)(2,1)} async-done(((bf16[512,3584]{1,0:T(8,128)(2,1)}), bf16[32,3584]{1,0:T(8,128)(2,1)}) %reduce-scatter.2.cloned.1.call-update) | async-done | bytes 229392 | tf_op jit(solution)/shard_map/reduce_scatter | solution.py:174
  256.9 1.1 fusion.24
  258.0 0.5 slice.110
  259.8 3.2 %collective-permute-start.6 = (bf16[32,3584]{1,0:T(8,128)(2,1)S(1)}, bf16[32,3584]{1,0:T(8,128)(2,1)S(1)}, u32[]{:S(2)}, u32[]{:S(2)}) collective-permute-start(bf16[32,3584]{1,0:T(8,128)(2,1)S(1)} %fusion.24), channel_id=1, source_target_pairs={{0,32},{32,64},{64,96},{96,128},{128,160},{160,192},{192,224},{224... | collective-permute-start | bytes 688136 | tf_op jit(solution)/shard_map/ppermute | solution.py:14
  263.0 0.2 fusion.35
  263.2 0.2 fusion.36
  263.5 0.2 multiply_reduce_fusion.1
  263.7 0.9 fusion.32
  264.6 5.2 %collective-permute-done.6 = bf16[32,3584]{1,0:T(8,128)(2,1)S(1)} collective-permute-done((bf16[32,3584]{1,0:T(8,128)(2,1)S(1)}, bf16[32,3584]{1,0:T(8,128)(2,1)S(1)}, u32[]{:S(2)}, u32[]{:S(2)}) %collective-permute-start.6) | collective-permute-done | bytes 229408 | tf_op jit(solution)/shard_map/ppermute | solution.py:14
  269.8 0.7 copy.21
  (45 shorter events, 0.8 us)
Async XLA Ops:
  7.2 52.1 %copy-start.1 = (bf16[1,3584,128]{2,1,0:T(8,128)(2,1)S(1)}, bf16[1,3584,128]{2,1,0:T(8,128)(2,1)}, u32[]{:S(2)}) copy-start(bf16[1,3584,128]{2,1,0:T(8,128)(2,1)} %param.15) | copy-start | bytes 2752516
  7.2 52.1 %copy-start = (bf16[1,3584,128]{2,1,0:T(8,128)(2,1)S(1)}, bf16[1,3584,128]{2,1,0:T(8,128)(2,1)}, u32[]{:S(2)}) copy-start(bf16[1,3584,128]{2,1,0:T(8,128)(2,1)} %param.16) | copy-start | bytes 2752516
  7.2 42.0 %copy-start.6 = (f32[1,3584]{1,0:T(1,128)S(1)}, f32[1,3584]{1,0:T(1,128)}, u32[]{:S(2)}) copy-start(f32[1,3584]{1,0:T(1,128)} %param.14) | copy-start | bytes 43012
  7.2 140.3 %all-gather.2.cloned.1.call-start = ((), (), s32[]{:S(2)}) async-start(), calls=%async_computation.3 | async-start | bytes 11698176 | tf_op jit(solution)/shard_map/all_gather | solution.py:127
  17.6 38.7 %all-to-all-start = ((f32[16,1,160]{2,1,0:T(1,128)}), f32[16,1,160]{2,1,0:T(1,128)S(1)}, u32[]{:S(2)}, u32[]{:S(2)}) async-start(f32[16,1,160]{2,1,0:T(1,128)} %broadcast_in_dim.32), calls=%async_computation | async-start | bytes 32768 | tf_op jit(solution)/shard_map/all_to_all | solution.py:140
  32.8 224.1 %reduce-scatter.2.cloned.1.call-start = ((), (), s32[]{:S(2)}) async-start(), calls=%async_computation.4 | async-start | bytes 3899392 | tf_op jit(solution)/shard_map/reduce_scatter | solution.py:174
  32.8 26.4 %collective-permute-start = (bf16[3584,128]{1,0:T(8,128)(2,1)}, bf16[3584,128]{1,0:T(8,128)(2,1)S(1)}, u32[]{:S(2)}, u32[]{:S(2)}) collective-permute-start(bf16[3584,128]{1,0:T(8,128)(2,1)} %bitcast.60), channel_id=1, source_target_pairs={{0,1},{1,0},{2,3},{3,2},{4,5},{5,4},{6,7},{7,6},{8,9},{9,8},{10,11... | collective-permute-start | bytes 2752520 | tf_op jit(solution)/shard_map/ppermute | solution.py:154
  34.8 24.4 %collective-permute-start.1 = (bf16[3584,128]{1,0:T(8,128)(2,1)}, bf16[3584,128]{1,0:T(8,128)(2,1)}, u32[]{:S(2)}, u32[]{:S(2)}) collective-permute-start(bf16[3584,128]{1,0:T(8,128)(2,1)} %bitcast.57), channel_id=1, source_target_pairs={{0,1},{1,0},{2,3},{3,2},{4,5},{5,4},{6,7},{7,6},{8,9},{9,8},{10,11... | collective-permute-start | bytes 2752520 | tf_op jit(solution)/shard_map/ppermute | solution.py:155
  38.3 18.5 %collective-permute-start.2 = (bf16[32,7168]{1,0:T(8,128)(2,1)S(1)}, bf16[32,7168]{1,0:T(8,128)(2,1)}, u32[]{:S(2)}, u32[]{:S(2)}) collective-permute-start(bf16[32,7168]{1,0:T(8,128)(2,1)S(1)} %pad_maximum_fusion.4), channel_id=1, source_target_pairs={{0,480},{32,0},{64,32},{96,64},{128,96},{160,128},{192,160},{224,1... | collective-permute-start | bytes 1376264 | tf_op jit(solution)/shard_map/ppermute | solution.py:14
  43.5 12.3 %collective-permute-start.3 = (f32[1,3584]{1,0:T(1,128)}, f32[1,3584]{1,0:T(1,128)S(1)}, u32[]{:S(2)}, u32[]{:S(2)}) collective-permute-start(f32[1,3584]{1,0:T(1,128)} %param.14), channel_id=1, source_target_pairs={{0,480},{32,0},{64,32},{96,64},{128,96},{160,128},{192,160},{224,1... | collective-permute-start | bytes 43016 | tf_op jit(solution)/shard_map/ppermute | solution.py:14
  46.8 7.0 %collective-permute-start.4 = (s32[1,32]{1,0:T(1,128)S(1)}, s32[1,32]{1,0:T(1,128)S(1)}, u32[]{:S(2)}, u32[]{:S(2)}) collective-permute-start(s32[1,32]{1,0:T(1,128)S(1)} %bitcast_add_fusion), channel_id=1, source_target_pairs={{0,480},{32,0},{64,32},{96,64},{128,96},{160,128},{192,160},{224,1... | collective-permute-start | bytes 392 | tf_op jit(solution)/shard_map/ppermute | solution.py:14
  53.8 9.7 %collective-permute-start.5 = (bf16[128,3584]{1,0:T(8,128)(2,1)}, bf16[128,3584]{1,0:T(8,128)(2,1)}, u32[]{:S(2)}, u32[]{:S(2)}) collective-permute-start(bf16[128,3584]{1,0:T(8,128)(2,1)} %bitcast.70), channel_id=1, source_target_pairs={{0,1},{1,0},{2,3},{3,2},{4,5},{5,4},{6,7},{7,6},{8,9},{9,8},{10,11... | collective-permute-start | bytes 2752520 | tf_op jit(solution)/shard_map/ppermute | solution.py:156
  61.1 2.3 copy-start.5
  70.0 82.7 %copy-start.4 = (bf16[256,3584]{1,0:T(8,128)(2,1)S(1)}, bf16[256,3584]{1,0:T(8,128)(2,1)}, u32[]{:S(2)}) copy-start(bf16[256,3584]{1,0:T(8,128)(2,1)} %maximum_select_fusion) | copy-start | bytes 5505028
  161.5 4.2 %copy-start.2 = (bf16[1792,1024]{1,0:T(8,128)(2,1)S(1)}, bf16[1792,1024]{1,0:T(8,128)(2,1)}, u32[]{:S(2)}) copy-start(bf16[1792,1024]{1,0:T(8,128)(2,1)} %pad_maximum_fusion.1) | copy-start | bytes 11010052
  167.3 41.6 %copy-start.7 = (s32[1,32,1]{1,2,0:T(1,128)S(1)}, s32[1,32,1]{1,2,0:T(1,128)}, u32[]{:S(2)}) copy-start(s32[1,32,1]{1,2,0:T(1,128)} %param.19) | copy-start | bytes 388
  167.3 89.6 %copy-start.3 = (bf16[1,32,3584]{2,1,0:T(8,128)(2,1)S(1)}, bf16[1,32,3584]{2,1,0:T(8,128)(2,1)}, u32[]{:S(2)}) copy-start(bf16[1,32,3584]{2,1,0:T(8,128)(2,1)} %param.11) | copy-start | bytes 688132
  167.4 34.1 %collective-permute-start.7 = (bf16[192,1792]{1,0:T(8,128)(2,1)S(1)}, bf16[192,1792]{1,0:T(8,128)(2,1)S(1)}, u32[]{:S(2)}, u32[]{:S(2)}) collective-permute-start(bf16[192,1792]{1,0:T(8,128)(2,1)S(1)} %slice.117), channel_id=1, source_target_pairs={{0,2},{1,3},{2,0},{3,1},{4,6},{5,7},{6,4},{7,5},{8,10},{9,11},{10,... | collective-permute-start | bytes 2064392 | tf_op jit(solution)/shard_map/ppermute | solution.py:86
  201.7 12.3 %collective-permute-start.8 = (bf16[96,1792]{1,0:T(8,128)(2,1)S(1)}, bf16[96,1792]{1,0:T(8,128)(2,1)S(1)}, u32[]{:S(2)}, u32[]{:S(2)}) collective-permute-start(bf16[96,1792]{1,0:T(8,128)(2,1)S(1)} %get-tuple-element.22), channel_id=1, source_target_pairs={{0,480},{32,0},{64,32},{96,64},{128,96},{160,128},{192,160},{224,1... | collective-permute-start | bytes 1032200 | tf_op jit(solution)/shard_map/ppermute | solution.py:14
  206.6 27.5 %collective-permute-start.9 = (bf16[96,1792]{1,0:T(8,128)(2,1)S(1)}, bf16[96,1792]{1,0:T(8,128)(2,1)S(1)}, u32[]{:S(2)}, u32[]{:S(2)}) collective-permute-start(bf16[96,1792]{1,0:T(8,128)(2,1)S(1)} %get-tuple-element.23), channel_id=1, source_target_pairs={{0,484},{1,485},{2,486},{3,487},{4,480},{5,481},{6,482},{7,483},{8... | collective-permute-start | bytes 1032200 | tf_op jit(solution)/shard_map/ppermute | solution.py:76
  234.9 28.1 %all-to-all-start.1 = ((bf16[4,24,1792]{2,1,0:T(8,128)(2,1)}), bf16[4,24,1792]{2,1,0:T(8,128)(2,1)S(1)}, u32[]{:S(2)}, u32[]{:S(2)}) async-start(bf16[4,24,1792]{2,1,0:T(8,128)(2,1)} %bitcast.18), calls=%async_computation.2 | async-start | bytes 688128 | tf_op jit(solution)/shard_map/all_to_all | solution.py:95
  259.8 10.0 %collective-permute-start.6 = (bf16[32,3584]{1,0:T(8,128)(2,1)S(1)}, bf16[32,3584]{1,0:T(8,128)(2,1)S(1)}, u32[]{:S(2)}, u32[]{:S(2)}) collective-permute-start(bf16[32,3584]{1,0:T(8,128)(2,1)S(1)} %fusion.24), channel_id=1, source_target_pairs={{0,32},{32,64},{64,96},{96,128},{128,160},{160,192},{192,224},{224... | collective-permute-start | bytes 688136 | tf_op jit(solution)/shard_map/ppermute | solution.py:14
Sparse Core Ops, SparseCore 0:
  10.1 137.3 all-gather.1
  155.9 100.9 reduce-scatter.1
